TPU v7x, 32 devices: a whole 2x2x4 slice. The times are simulated.
32 devices in a mesh: seq: 8 (over z, y), tensor: 4 (over x, core).
Axes of the slice: x: 2, y: 2, z: 4, core: 2. Of those that a mesh axis runs over, the one named last changes fastest.
Arguments:
- layer_in: bfloat16 [6, 1024, 2048], P(None, ('seq', 'tensor')), may hold values from -6 to 6
- cotangent: bfloat16 [6, 1024, 2048], P(None, ('seq', 'tensor')), may hold values from -6 to 6
- doc_lengths: int32 [6, 8], replicated, may hold values from 1 to 768, 1024 in all within a row
- pad_counts: int32 [6], replicated, may hold values from 0 to 127
- gain_attn: float32 [2048], replicated, may hold values from 0.5 to 1.5
- gain_ffn: float32 [2048], replicated, may hold values from 0.5 to 1.5
- w_qkv: bfloat16 [3, 2048, 2048], P(None, None, 'tensor'), may hold values from -0.125 to 0.125
- a_qkv: bfloat16 [3, 2048, 16], replicated, may hold values from -0.125 to 0.125
- b_qkv: bfloat16 [3, 16, 2048], P(None, None, 'tensor'), may hold values from -0.75 to 0.75
- m_qkv: float32 [3, 2048], P(None, 'tensor'), may hold values from 0.6 to 1.6
- w_out: bfloat16 [2048, 2048], P('tensor'), may hold values from -0.1875 to 0.1875
- a_out: bfloat16 [2048, 16], P('tensor'), may hold values from -0.125 to 0.125
- b_out: bfloat16 [16, 2048], replicated, may hold values from -0.75 to 0.75
- m_out: float32 [2048], replicated, may hold values from 3 to 30
- w_gateup: bfloat16 [2, 2048, 5632], P(None, None, 'tensor'), may hold values from -0.125 to 0.125
- a_gateup: bfloat16 [2, 2048, 16], replicated, may hold values from -0.125 to 0.125
- b_gateup: bfloat16 [2, 16, 5632], P(None, None, 'tensor'), may hold values from -0.75 to 0.75
- m_gateup: float32 [2, 5632], P(None, 'tensor'), may hold values from 0.5 to 3
- w_down: bfloat16 [5632, 2048], P('tensor'), may hold values from -0.109375 to 0.109375
- a_down: bfloat16 [5632, 16], P('tensor'), may hold values from -0.078125 to 0.078125
- b_down: bfloat16 [16, 2048], replicated, may hold values from -0.75 to 0.75
- m_down: float32 [2048], replicated, may hold values from 0.5 to 4
Outputs:
- layer_out: bfloat16 [6, 1024, 2048], P(None, ('seq', 'tensor'))
- grad_in: float32 [6, 1024, 2048], P(None, ('seq', 'tensor'))
- grad_a_qkv: float32 [3, 2048, 16], replicated
- grad_b_qkv: float32 [3, 16, 2048], P(None, None, 'tensor')
- grad_m_qkv: float32 [3, 2048], P(None, 'tensor')
- grad_a_out: float32 [2048, 16], P('tensor')
- grad_b_out: float32 [16, 2048], replicated
- grad_m_out: float32 [2048], replicated
- grad_a_gateup: float32 [2, 2048, 16], replicated
- grad_b_gateup: float32 [2, 16, 5632], P(None, None, 'tensor')
- grad_m_gateup: float32 [2, 5632], P(None, 'tensor')
- grad_a_down: float32 [5632, 16], P('tensor')
- grad_b_down: float32 [16, 2048], replicated
- grad_m_down: float32 [2048], replicated
Inputs may be any that keep to these rules, and one draw needn't show every extreme that they name: `doc_lengths`: each row's 8 document lengths sum to 1024.
All inputs are finite; a program needn't handle non-finite values.
Results may differ from a plain program's by a relative error of at most 0.03.
Values may be sent and summed in bfloat16 or wider, within the bound.
No kernel may reach another device: no remote copies, remote signals or barrier semaphores. Data moves between devices by JAX's collectives and lax.ppermute only.
A program may use at most 512 MiB of HBM per device.

v0:
```python
from functools import partial
import math

import jax
import jax.numpy as jnp
from jax import lax
from jax.sharding import PartitionSpec as P

HEAD_DIM = 128


epsilon = 1e-05
adapter_scale = 2.0
rope_base = 10000.0
maximal_precision = lax.Precision.HIGHEST
score_block = 512


def rms_norm(values, gain):
    return values * lax.rsqrt(jnp.mean(values * values, axis=-1, keepdims=True) + epsilon) * gain


def rotary_tables(positions, head_size):
    half_size = head_size // 2
    frequency = rope_base ** (-(2.0 * jnp.arange(half_size, dtype=jnp.float32)) / head_size)
    angles = positions.astype(jnp.float32)[:, None] * frequency[None, :]
    cosine = jnp.concatenate([jnp.cos(angles), jnp.cos(angles)], axis=-1)
    sine_table = jnp.concatenate([jnp.sin(angles), jnp.sin(angles)], axis=-1)
    return (cosine, sine_table)


def rotate(values, cosine, sine_table):
    half_size = values.shape[-1] // 2
    turned = jnp.concatenate([-values[..., half_size:], values[..., :half_size]], axis=-1)
    return values * cosine[None, :, None, :] + turned * sine_table[None, :, None, :]


def rotate_back(grads, cosine, sine_table):
    half_size = grads.shape[-1] // 2
    scaled = grads * sine_table[None, :, None, :]
    turned = jnp.concatenate([scaled[..., half_size:], -scaled[..., :half_size]], axis=-1)
    return grads * cosine[None, :, None, :] + turned


def keep_state(inner_state):
    return inner_state


def doc_index(offsets, positions):
    return jnp.sum((offsets[:, None, :] <= positions[None, :, None]).astype(jnp.int32), axis=-1)


def block_active(offsets, key_first, key_last, query_first, query_last):
    probe_pos = jnp.stack([jnp.minimum(key_last, query_last), query_first])
    doc_pair = doc_index(offsets, probe_pos)
    return jnp.logical_and(key_first <= query_last, jnp.any(doc_pair[:, 0] >= doc_pair[:, 1]))


def block_weights(queries, key_heads, offsets, query_first, key_first):
    score_scale = 1.0 / math.sqrt(queries.shape[-1])
    raw_scores = jnp.einsum(
        "rqhd,rkhd->rhqk", queries, key_heads, preferred_element_type=jnp.float32
    )
    query_pos = query_first + jnp.arange(queries.shape[1], dtype=jnp.int32)
    key_pos = key_first + jnp.arange(key_heads.shape[1], dtype=jnp.int32)
    same_doc = doc_index(offsets, query_pos)[:, :, None] == doc_index(offsets, key_pos)[:, None, :]
    allowed = jnp.logical_and(same_doc, key_pos[None, None, :] <= query_pos[None, :, None])
    return jnp.where(allowed[:, None], jnp.exp(raw_scores * score_scale), 0.0)


def gather_rows(values):
    return lax.all_gather(values, "tensor", axis=1, tiled=True)


def column_forward(input_rows, frozen_weight, down_adapter_matrix, up_adapter_matrix, magnitude):
    weight_heading = frozen_weight.astype(jnp.float32) + adapter_scale * jnp.einsum(
        "jdk,jkn->jdn",
        down_adapter_matrix.astype(jnp.float32),
        up_adapter_matrix.astype(jnp.float32),
        precision=maximal_precision,
    )
    lengths = jnp.sqrt(jnp.sum(weight_heading * weight_heading, axis=1))
    adapter_activation_rows = jnp.einsum(
        "rcd,jdk->jrck", input_rows, down_adapter_matrix, preferred_element_type=jnp.float32
    ).astype(jnp.bfloat16)
    frozen_output_rows = jnp.einsum(
        "rcd,jdn->jrcn", input_rows, frozen_weight, preferred_element_type=jnp.float32
    )
    plain_output_rows = frozen_output_rows + adapter_scale * jnp.einsum(
        "jrck,jkn->jrcn",
        adapter_activation_rows,
        up_adapter_matrix,
        preferred_element_type=jnp.float32,
    )
    outputs = plain_output_rows * (magnitude / lengths)[:, None, None, :]
    return (outputs, plain_output_rows, adapter_activation_rows, weight_heading, lengths)


def column_backward(
    grads,
    input_rows,
    plain_output_rows,
    adapter_activation_rows,
    weight_heading,
    lengths,
    frozen_weight,
    down_adapter_matrix,
    up_adapter_matrix,
    magnitude,
):
    scale_sum = jnp.sum(plain_output_rows * grads, axis=(1, 2))
    grad_plain = (grads * (magnitude / lengths)[:, None, None, :]).astype(jnp.bfloat16)
    magnitude_ratio = -scale_sum * magnitude / (lengths * lengths * lengths)
    grad_dir = weight_heading * magnitude_ratio[:, None, :]
    adapter_rank_part = adapter_scale * jnp.einsum(
        "jrcn,jkn->jrck", grad_plain, up_adapter_matrix, preferred_element_type=jnp.float32
    )
    column_norm_part = adapter_scale * jnp.einsum(
        "jdn,jkn->jdk", grad_dir, up_adapter_matrix.astype(jnp.float32), precision=maximal_precision
    )
    grad_rank, norm_part = (
        lax.psum(adapter_rank_part.astype(jnp.bfloat16), "tensor").astype(jnp.float32),
        lax.psum(column_norm_part.astype(jnp.bfloat16), "tensor").astype(jnp.float32),
    )
    grad_rank = grad_rank.astype(jnp.bfloat16)
    down_adapter_gradient = (
        jnp.einsum("rcd,jrck->jdk", input_rows, grad_rank, preferred_element_type=jnp.float32)
        + norm_part
    )
    up_adapter_gradient = adapter_scale * jnp.einsum(
        "jrck,jrcn->jkn", adapter_activation_rows, grad_plain, preferred_element_type=jnp.float32
    )
    up_adapter_gradient = up_adapter_gradient + adapter_scale * jnp.einsum(
        "jdk,jdn->jkn",
        down_adapter_matrix.astype(jnp.float32),
        grad_dir,
        precision=maximal_precision,
    )
    partial_in = jnp.einsum(
        "jrcn,jdn->rcd", grad_plain, frozen_weight, preferred_element_type=jnp.float32
    )
    grad_shard = lax.psum_scatter(
        partial_in.astype(jnp.bfloat16), "tensor", scatter_dimension=1, tiled=True
    ).astype(jnp.float32)
    quarter = grad_shard.shape[1]
    begin_row = lax.axis_index("tensor") * quarter
    local_rank = lax.dynamic_slice_in_dim(grad_rank, begin_row, quarter, 2)
    grad_shard = grad_shard + jnp.einsum(
        "jrck,jdk->rcd", local_rank, down_adapter_matrix, preferred_element_type=jnp.float32
    )
    return (grad_shard, down_adapter_gradient, up_adapter_gradient, scale_sum / lengths)


def row_forward(input_rows, frozen_weight, down_adapter_matrix, up_adapter_matrix):
    weight_heading = frozen_weight.astype(jnp.float32) + adapter_scale * jnp.dot(
        down_adapter_matrix.astype(jnp.float32),
        up_adapter_matrix.astype(jnp.float32),
        precision=maximal_precision,
    )
    rank_part = jnp.einsum(
        "rcn,nk->rck", input_rows, down_adapter_matrix, preferred_element_type=jnp.float32
    )
    square_part = jnp.sum(weight_heading * weight_heading, axis=0)
    cross_part = jnp.dot(
        down_adapter_matrix.astype(jnp.float32).T, weight_heading, precision=maximal_precision
    )
    adapter_activation_rows, squares, mixed_product_sum = (
        lax.psum(rank_part.astype(jnp.bfloat16), "tensor").astype(jnp.float32),
        lax.psum(square_part.astype(jnp.bfloat16), "tensor").astype(jnp.float32),
        lax.psum(cross_part.astype(jnp.bfloat16), "tensor").astype(jnp.float32),
    )
    adapter_activation_rows = adapter_activation_rows.astype(jnp.bfloat16)
    lengths = jnp.sqrt(squares)
    partial_out = jnp.einsum(
        "rcn,nd->rcd", input_rows, frozen_weight, preferred_element_type=jnp.float32
    )
    partial_output_rows = lax.psum_scatter(
        partial_out.astype(jnp.bfloat16), "tensor", scatter_dimension=1, tiled=True
    ).astype(jnp.float32)
    quarter = partial_output_rows.shape[1]
    begin_row = lax.axis_index("tensor") * quarter
    local_rank = lax.dynamic_slice_in_dim(adapter_activation_rows, begin_row, quarter, 1)
    plain_output_rows = partial_output_rows + adapter_scale * jnp.einsum(
        "rck,kd->rcd", local_rank, up_adapter_matrix, preferred_element_type=jnp.float32
    )
    return (plain_output_rows, adapter_activation_rows, weight_heading, lengths, mixed_product_sum)


def row_backward(
    grad_shard,
    input_rows,
    plain_output_rows,
    adapter_activation_rows,
    weight_heading,
    lengths,
    mixed_product_sum,
    frozen_weight,
    down_adapter_matrix,
    up_adapter_matrix,
    magnitude,
):
    scale_sum = lax.psum(jnp.sum(plain_output_rows * grad_shard, axis=(0, 1)), "tensor")
    grad_plain = (grad_shard * (magnitude / lengths)).astype(jnp.bfloat16)
    complete_weight_gradient = lax.all_gather(grad_plain, "tensor", axis=1, tiled=True)
    magnitude_ratio = -scale_sum * magnitude / (lengths * lengths * lengths)
    grad_rank = (
        adapter_scale
        * jnp.einsum(
            "fxe,ye->fxy",
            complete_weight_gradient,
            up_adapter_matrix,
            preferred_element_type=jnp.float32,
        )
    ).astype(jnp.bfloat16)
    down_adapter_gradient = jnp.einsum(
        "rcn,rck->nk", input_rows, grad_rank, preferred_element_type=jnp.float32
    )
    down_adapter_gradient = down_adapter_gradient + adapter_scale * jnp.dot(
        weight_heading * magnitude_ratio,
        up_adapter_matrix.astype(jnp.float32).T,
        precision=maximal_precision,
    )
    up_adapter_gradient = (
        adapter_scale
        * jnp.einsum(
            "rck,rcd->kd",
            adapter_activation_rows,
            complete_weight_gradient,
            preferred_element_type=jnp.float32,
        )
        + adapter_scale * mixed_product_sum * magnitude_ratio
    )
    grad_inner = jnp.einsum(
        "rcd,nd->rcn", complete_weight_gradient, frozen_weight, preferred_element_type=jnp.float32
    )
    grad_inner = grad_inner + jnp.einsum(
        "rck,nk->rcn", grad_rank, down_adapter_matrix, preferred_element_type=jnp.float32
    )
    return (grad_inner, down_adapter_gradient, up_adapter_gradient, scale_sum / lengths)


def attend_keys(queries, offsets, query_first):
    row_count, query_count, head_count, head_size = queries.shape

    def fold_keys(carried, pieces, first_key):
        key_part, value_part = pieces
        key_count = key_part.shape[1]
        block_len = math.gcd(key_count, score_block)

        def fold_advance(block_index, loop_state):
            offset_in = block_index * block_len
            key_first = first_key + offset_in
            key_block = lax.dynamic_slice_in_dim(key_part, offset_in, block_len, 1).reshape(
                row_count, block_len, head_count, head_size
            )
            value_block = lax.dynamic_slice_in_dim(value_part, offset_in, block_len, 1).reshape(
                row_count, block_len, head_count, head_size
            )

            def fold_compute(inner_state):
                totals, accumulated = inner_state
                weights = block_weights(queries, key_block, offsets, query_first, key_first)
                totals = totals + jnp.sum(weights, axis=-1)
                accumulated = accumulated + jnp.einsum(
                    "rhqk,rkhd->rqhd",
                    weights.astype(jnp.bfloat16),
                    value_block,
                    preferred_element_type=jnp.float32,
                )
                return (totals, accumulated)

            is_live = block_active(
                offsets,
                key_first,
                key_first + block_len - 1,
                query_first,
                query_first + query_count - 1,
            )
            return lax.cond(is_live, fold_compute, keep_state, loop_state)

        return lax.fori_loop(0, key_count // block_len, fold_advance, carried)

    return fold_keys


def query_grads(queries, douter, dlog_heads, key_all, value_all, offsets, query_first):
    row_count, query_count, head_count, head_size = queries.shape
    total_len = key_all.shape[1]
    feat_width = head_count * head_size
    block_len = math.gcd(total_len, score_block)
    score_scale = 1.0 / math.sqrt(head_size)

    def block_terms(block_index):
        offset_in = block_index * block_len
        key_block = lax.dynamic_slice_in_dim(key_all, offset_in, block_len, 1).reshape(
            row_count, block_len, head_count, head_size
        )
        value_block = lax.dynamic_slice_in_dim(value_all, offset_in, block_len, 1).reshape(
            row_count, block_len, head_count, head_size
        )
        weights = block_weights(queries, key_block, offsets, query_first, offset_in)
        dweights = jnp.einsum(
            "rqhd,rkhd->rhqk", douter, value_block, preferred_element_type=jnp.float32
        )
        dscores = (score_scale * weights * (dweights + dlog_heads[..., None])).astype(jnp.bfloat16)
        return (weights, dscores, key_block)

    def live_block(block_index):
        offset_in = block_index * block_len
        return block_active(
            offsets,
            offset_in,
            offset_in + block_len - 1,
            query_first,
            query_first + query_count - 1,
        )

    def query_advance(block_index, loop_state):
        dq_acc, buffer = loop_state

        def query_compute(dq_in):
            weights, dscores, key_block = block_terms(block_index)
            dq_out = dq_in + jnp.einsum(
                "rhqk,rkhd->rqhd", dscores, key_block, preferred_element_type=jnp.float32
            )
            dkey_rows = jnp.einsum(
                "rhqk,rqhd->rkhd", dscores, queries, preferred_element_type=jnp.float32
            ).reshape(row_count, block_len, feat_width)
            dvalues = jnp.einsum(
                "rhqk,rqhd->rkhd",
                weights.astype(jnp.bfloat16),
                douter,
                preferred_element_type=jnp.float32,
            ).reshape(row_count, block_len, feat_width)
            return (dq_out, jnp.concatenate([dkey_rows, dvalues], axis=-1))

        def skip_block(dq_in):
            return (dq_in, jnp.zeros((row_count, block_len, 2 * feat_width), jnp.float32))

        dq_acc, block_term = lax.cond(live_block(block_index), query_compute, skip_block, dq_acc)
        buffer = lax.dynamic_update_slice_in_dim(buffer, block_term, block_index * block_len, 1)
        return (dq_acc, buffer)

    start_state = (
        jnp.zeros(queries.shape, jnp.float32),
        jnp.zeros((row_count, total_len, 2 * feat_width), jnp.float32),
    )
    return lax.fori_loop(0, total_len // block_len, query_advance, start_state)


def local(
    layer_in,
    cotangent,
    doc_lengths,
    pad_counts,
    gain_attn,
    gain_ffn,
    w_qkv,
    a_qkv,
    b_qkv,
    m_qkv,
    w_out,
    a_out,
    b_out,
    m_out,
    w_gateup,
    a_gateup,
    b_gateup,
    m_gateup,
    w_down,
    a_down,
    b_down,
    m_down,
):
    row_count, quarter, model_width = layer_in.shape
    group_len = quarter * lax.axis_size("tensor")
    total_len = group_len * lax.axis_size("seq")
    group_first = lax.axis_index("seq") * group_len
    shard_first = group_first + lax.axis_index("tensor") * quarter
    feat_width = w_qkv.shape[2]
    head_count = feat_width // HEAD_DIM
    four_d = (row_count, group_len, head_count, HEAD_DIM)
    flat_shape = (row_count, group_len, feat_width)
    offsets = jnp.cumsum(doc_lengths, axis=1)
    cosine, sine_table = rotary_tables(
        group_first + jnp.arange(group_len, dtype=jnp.int32), HEAD_DIM
    )
    wide_in = layer_in.astype(jnp.float32)
    normed_a = gather_rows(rms_norm(wide_in, gain_attn).astype(jnp.bfloat16))
    qkv_out, qkv_plain, qkv_rank, qkv_dir, qkv_len = column_forward(
        normed_a, w_qkv, a_qkv, b_qkv, m_qkv
    )
    queries = rotate(qkv_out[0].reshape(four_d), cosine, sine_table).astype(jnp.bfloat16)
    key_heads = rotate(qkv_out[1].reshape(four_d), cosine, sine_table).astype(jnp.bfloat16)
    value_heads = qkv_out[2].reshape(four_d).astype(jnp.bfloat16)
    key_flat = key_heads.reshape(flat_shape)
    value_flat = value_heads.reshape(flat_shape)
    start_state = (
        jnp.zeros((row_count, head_count, group_len), jnp.float32),
        jnp.zeros(four_d, jnp.float32),
    )
    fold_keys = attend_keys(queries, offsets, group_first)
    totals, accumulated = fold_keys(
        start_state,
        (
            lax.all_gather(key_flat, "seq", axis=1, tiled=True),
            lax.all_gather(value_flat, "seq", axis=1, tiled=True),
        ),
        jnp.int32(0),
    )
    denominator = jnp.transpose(totals, (0, 2, 1))[..., None]
    attended = accumulated / denominator
    attended_b = attended.astype(jnp.bfloat16).reshape(flat_shape)
    out_plain, out_rank, out_dir, out_len, out_cross = row_forward(attended_b, w_out, a_out, b_out)
    middle = wide_in + out_plain * (m_out / out_len)
    normed_f = gather_rows(rms_norm(middle, gain_ffn).astype(jnp.bfloat16))
    gu_out, gu_plain, gu_rank, gu_dir, gu_len = column_forward(
        normed_f, w_gateup, a_gateup, b_gateup, m_gateup
    )
    gate_act = gu_out[0]
    up_act = gu_out[1]
    hidden = (jax.nn.silu(gate_act) * up_act).astype(jnp.bfloat16)
    down_plain, down_rank, down_dir, down_len, down_cross = row_forward(
        hidden, w_down, a_down, b_down
    )
    layer_sum = middle + down_plain * (m_down / down_len)
    positions = shard_first + jnp.arange(quarter, dtype=jnp.int32)
    valid_mask = (positions[None, :] < total_len - pad_counts[:, None]).astype(jnp.float32)
    cot_full = cotangent.astype(jnp.float32) * valid_mask[:, :, None]
    grad_hidden, grad_a_down, grad_b_down, grad_m_down = row_backward(
        cot_full,
        hidden,
        down_plain,
        down_rank,
        down_dir,
        down_len,
        down_cross,
        w_down,
        a_down,
        b_down,
        m_down,
    )
    sigmoid_gate = jax.nn.sigmoid(gate_act)
    grad_gate = grad_hidden * up_act * sigmoid_gate * (1.0 + gate_act * (1.0 - sigmoid_gate))
    grad_up = grad_hidden * gate_act * sigmoid_gate
    grad_norm_f, grad_a_gu, grad_b_gu, grad_m_gu = column_backward(
        jnp.stack([grad_gate, grad_up]),
        normed_f,
        gu_plain,
        gu_rank,
        gu_dir,
        gu_len,
        w_gateup,
        a_gateup,
        b_gateup,
        m_gateup,
    )
    norm_pull = jax.vjp(partial(rms_norm, gain=gain_ffn), middle)[1]
    grad_middle = cot_full + norm_pull(grad_norm_f)[0]
    grad_att, grad_a_out, grad_b_out, grad_m_out = row_backward(
        grad_middle,
        attended_b,
        out_plain,
        out_rank,
        out_dir,
        out_len,
        out_cross,
        w_out,
        a_out,
        b_out,
        m_out,
    )
    grad_att4 = grad_att.reshape(four_d)
    douter = (grad_att4 / denominator).astype(jnp.bfloat16)
    dlog_rows = -jnp.sum(grad_att4 * attended, axis=-1) / denominator[..., 0]
    dlog_heads = jnp.transpose(dlog_rows, (0, 2, 1))
    key_all, value_all = (
        lax.all_gather(key_flat, "seq", axis=1, tiled=True),
        lax.all_gather(value_flat, "seq", axis=1, tiled=True),
    )
    grad_q, buffer = query_grads(
        queries, douter, dlog_heads, key_all, value_all, offsets, group_first
    )
    grad_kv = lax.psum_scatter(
        buffer.astype(jnp.bfloat16), "seq", scatter_dimension=1, tiled=True
    ).astype(jnp.float32)
    grad_k = grad_kv[..., :feat_width].reshape(four_d)
    grad_v = grad_kv[..., feat_width:].reshape(four_d)
    stacked = jnp.stack(
        [
            rotate_back(grad_q, cosine, sine_table).reshape(flat_shape),
            rotate_back(grad_k, cosine, sine_table).reshape(flat_shape),
            grad_v.reshape(flat_shape),
        ]
    )
    grad_norm_a, grad_a_qkv, grad_b_qkv, grad_m_qkv = column_backward(
        stacked, normed_a, qkv_plain, qkv_rank, qkv_dir, qkv_len, w_qkv, a_qkv, b_qkv, m_qkv
    )
    attn_pull = jax.vjp(partial(rms_norm, gain=gain_attn), wide_in)[1]
    grad_in = grad_middle + attn_pull(grad_norm_a)[0]
    summed = (
        lax.psum(grad_a_qkv.astype(jnp.bfloat16), "seq").astype(jnp.float32),
        lax.psum(grad_b_qkv.astype(jnp.bfloat16), "seq").astype(jnp.float32),
        lax.psum(grad_m_qkv.astype(jnp.bfloat16), "seq").astype(jnp.float32),
        lax.psum(grad_a_out.astype(jnp.bfloat16), "seq").astype(jnp.float32),
        lax.psum(grad_b_out.astype(jnp.bfloat16), "seq").astype(jnp.float32),
        lax.psum(grad_m_out.astype(jnp.bfloat16), "seq").astype(jnp.float32),
        lax.psum(grad_a_gu.astype(jnp.bfloat16), "seq").astype(jnp.float32),
        lax.psum(grad_b_gu.astype(jnp.bfloat16), "seq").astype(jnp.float32),
        lax.psum(grad_m_gu.astype(jnp.bfloat16), "seq").astype(jnp.float32),
        lax.psum(grad_a_down.astype(jnp.bfloat16), "seq").astype(jnp.float32),
        lax.psum(grad_b_down.astype(jnp.bfloat16), "seq").astype(jnp.float32),
        lax.psum(grad_m_down.astype(jnp.bfloat16), "seq").astype(jnp.float32),
    )
    return (
        layer_sum.astype(jnp.bfloat16),
        grad_in,
        summed[0],
        summed[1],
        summed[2],
        summed[3],
        summed[4],
        summed[5],
        summed[6],
        summed[7],
        summed[8],
        summed[9],
        summed[10],
        summed[11],
    )


def solution(mesh):
    in_specs = (
        P(None, ("seq", "tensor"), None),
        P(None, ("seq", "tensor"), None),
        P(),
        P(),
        P(),
        P(),
        P(None, None, "tensor"),
        P(),
        P(None, None, "tensor"),
        P(None, "tensor"),
        P("tensor", None),
        P("tensor", None),
        P(),
        P(),
        P(None, None, "tensor"),
        P(),
        P(None, None, "tensor"),
        P(None, "tensor"),
        P("tensor", None),
        P("tensor", None),
        P(),
        P(),
    )
    out_specs = (
        P(None, ("seq", "tensor"), None),
        P(None, ("seq", "tensor"), None),
        P(),
        P(None, None, "tensor"),
        P(None, "tensor"),
        P("tensor", None),
        P(),
        P(),
        P(),
        P(None, None, "tensor"),
        P(None, "tensor"),
        P("tensor", None),
        P(),
        P(),
    )
    return jax.shard_map(local, mesh=mesh, in_specs=in_specs, out_specs=out_specs, check_vma=False)
```

profile of v0, /device:TPU:0, one launch (start us, length us, event | category | flops | bytes accessed | tf_op | source)
XLA Modules:
  0.0 1139.3 jit_solution(15481331795566915263)
XLA Ops:
  20.6 22.9 %all-gather.8.cloned.1.call-done = bf16[6,128,2048]{2,1,0:T(8,128)(2,1)} async-done(((bf16[6,32,2048]{2,1,0:T(8,128)(2,1)}), bf16[6,128,2048]{2,1,0:T(8,128)(2,1)}) %all-gather.8.cloned.1.call-update) | async-done | bytes 3145744 | tf_op jit(solution)/shard_map/all_gather | solution.py:72
  74.9 84.4 %all-gather.18.cloned.1.call-done = bf16[1,6,1024,512]{3,2,0,1:T(8,128)(2,1)} async-done(((bf16[1,6,128,512]{3,2,0,1:T(8,128)(2,1)}), bf16[1,6,1024,512]{3,2,0,1:T(8,128)(2,1)}) %all-gather.18.cloned.1.call-update) | async-done | bytes 6291472 | tf_op jit(solution)/shard_map/all_gather | solution.py:407
  159.2 8.7 copy.147
  168.0 91.3 %all-gather.10.cloned.1.call-done = bf16[6,1024,512]{2,1,0:T(8,128)(2,1)} async-done(((bf16[6,128,512]{2,1,0:T(8,128)(2,1)}), bf16[6,1024,512]{2,1,0:T(8,128)(2,1)}) %all-gather.10.cloned.1.call-update) | async-done | bytes 6291472 | tf_op jit(solution)/shard_map/all_gather | solution.py:406
  259.3 8.7 copy.145
  268.1 12.1 %while.43 = (s32[]{:T(128)}, f32[6,4,128]{2,1,0:T(4,128)S(1)}, f32[6,128,4,128]{3,1,2,0:T(8,128)S(1)}, s32[]{:T(128)}, s32[6,8]{1,0:T(8,128)S(1)}, /*index=5*/s3...) while((s32[]{:T(128)}, f32[6,4,128]{2,1,0:T(4,128)S(1)}, ...), condition=%wide.region_11.12_spmd, body=%wide.region_3.11_spmd.sunk | while | flops 816078016 | bytes 36788728 | solution.py:281
  298.8 10.7 all-reduce.4
  310.8 20.7 %reduce-scatter.6.cloned.1.call-done = bf16[6,32,2048]{2,1,0:T(8,128)(2,1)} async-done(((bf16[6,128,2048]{2,1,0:T(8,128)(2,1)}), bf16[6,32,2048]{2,1,0:T(8,128)(2,1)}) %reduce-scatter.6.cloned.1.call-update) | async-done | bytes 786448 | tf_op jit(solution)/shard_map/reduce_scatter | solution.py:177
  336.0 12.6 %multiply_reduce_fusion = (f32[2,1408]{1,0:T(2,128)S(1)}, f32[2,2048,1408]{2,1,0:T(8,128)}) fusion(bf16[2,2048,16]{1,2,0:T(8,128)(2,1)S(1)} %copy-done.35, bf16[2,16,1408]{2,1,0:T(8,128)(2,1)S(1)} %copy-done.49, bf16[2,2048,1408]{2,1,0:T(8,128)(2,1)} %param.44), kind=kOutput, calls=%fused_computation.49 | convolution fusion | flops 213382400 | bytes 34835456 | tf_op jit(solution)/shard_map/jdk,jkn->jdn/dot_general | solution.py:76
  348.7 13.1 %all-gather.14.cloned.1.call-done = bf16[6,128,2048]{2,1,0:T(8,128)(2,1)} async-done(((bf16[6,32,2048]{2,1,0:T(8,128)(2,1)}), bf16[6,128,2048]{2,1,0:T(8,128)(2,1)}) %all-gather.14.cloned.1.call-update) | async-done | bytes 3145744 | tf_op jit(solution)/shard_map/all_gather | solution.py:204
  364.8 9.3 fusion.46
  374.1 18.4 %all-gather.12.cloned.1.call-done = bf16[6,128,2048]{2,1,0:T(8,128)(2,1)} async-done(((bf16[6,32,2048]{2,1,0:T(8,128)(2,1)}), bf16[6,128,2048]{2,1,0:T(8,128)(2,1)}) %all-gather.12.cloned.1.call-update) | async-done | bytes 3145744 | tf_op jit(solution)/shard_map/all_gather | solution.py:72
  392.4 15.1 %fusion.34 = f32[6,128,2,1408]{3,1,2,0:T(8,128)S(1)} fusion(bf16[2,2048,1408]{2,1,0:T(8,128)(2,1)} %param.44, bf16[6,128,2048]{2,1,0:T(8,128)(2,1)} %all-gather.12.cloned.1.call-done), kind=kOutput, calls=%fused_computation.63 | convolution fusion | flops 8858370048 | bytes 23330816 | tf_op jit(solution)/shard_map/rcd,jdn->jrcn/dot_general | solution.py:86
  425.8 14.4 %bitcast_convert_fusion.1 = bf16[6,128,2048]{2,1,0:T(8,128)(2,1)} fusion(bf16[2,6,128,1408]{3,2,0,1:T(8,128)(2,1)} %copy-done.16, bf16[2,2048,1408]{2,1,0:T(8,128)(2,1)} %param.44), kind=kOutput, calls=%fused_computation.76 | convolution fusion | flops 8859942912 | bytes 19005440 | tf_op jit(solution)/shard_map/jrcn,jdn->rcd/dot_general | solution.py:139
  440.3 8.9 fusion.57
  455.4 42.4 %reduce-scatter.10.cloned.1.call-done = bf16[6,32,2048]{2,1,0:T(8,128)(2,1)} async-done(((bf16[6,128,2048]{2,1,0:T(8,128)(2,1)}), bf16[6,32,2048]{2,1,0:T(8,128)(2,1)}) %reduce-scatter.10.cloned.1.call-update) | async-done | bytes 786448 | tf_op jit(solution)/shard_map/reduce_scatter | solution.py:142
  500.2 38.2 %reduce-scatter.8.cloned.1.call-done = bf16[6,32,2048]{2,1,0:T(8,128)(2,1)} async-done(((bf16[6,128,2048]{2,1,0:T(8,128)(2,1)}), bf16[6,32,2048]{2,1,0:T(8,128)(2,1)}) %reduce-scatter.8.cloned.1.call-update) | async-done | bytes 786448 | tf_op jit(solution)/shard_map/reduce_scatter | solution.py:177
  545.2 28.7 %all-gather.16.cloned.1.call-done = bf16[6,128,2048]{2,1,0:T(8,128)(2,1)} async-done(((bf16[6,32,2048]{2,1,0:T(8,128)(2,1)}), bf16[6,128,2048]{2,1,0:T(8,128)(2,1)}) %all-gather.16.cloned.1.call-update) | async-done | bytes 3145744 | tf_op jit(solution)/shard_map/all_gather | solution.py:204
  589.9 55.6 %while.44 = (s32[]{:T(128)}, f32[6,128,4,128]{1,3,2,0:T(8,128)}, bf16[6,1024,1024]{2,1,0:T(8,128)(2,1)}, s32[]{:T(128)}, s32[6,8]{1,0:T(8,128)S(1)}, /*index=5*/...) while((s32[]{:T(128)}, f32[6,128,4,128]{1,3,2,0:T(8,128)}, ...), condition=%wide.region_33.34_spmd, body=%wide.region_26.33_spmd.sunk | while | flops 2041339008 | bytes 117754568 | solution.py:348
  591.8 17.6 %conditional.5 = (f32[6,128,4,128]{1,3,2,0:T(8,128)}, bf16[6,512,1024]{1,2,0:T(8,128)(2,1)}) conditional(s32[]{:T(128)} %convert_element_type.563, f32[6,128,4,128]{1,3,2,0:T(8,128)} %get-tuple-element.1213, (s32[]{:T(128)}, bf16[6,1024,512]{1,2,0:T(8,128)(2,1)}, s32[6,8]{1,0:T(8,128)S(1)}, s32[]{:T(128)}, bf16[6,128,4,128]{1,3,2,0:T(8,128)(2,1)S(1)}, ...), branch_computations={%region_29.29_spmd, %region_30.32_spmd} | conditional | flops 2041338752 | bytes 83150848 | solution.py:340
  609.4 8.7 copy.238
  629.9 8.7 copy.238
  659.3 12.4 %fusion.98 = f32[2,16,1408]{2,1,0:T(8,128)S(1)} fusion(bf16[2,2048,16]{1,2,0:T(8,128)(2,1)S(1)} %copy-done.36, f32[2,2048,1408]{2,1,0:T(8,128)} %get-tuple-element.1013, f32[2,1408]{1,0:T(2,128)S(1)} %get-tuple-element.994), kind=kOutput, calls=%fused_computation.144 | convolution fusion | flops 1113063424 | bytes 23391232 | tf_op jit(solution)/shard_map/jdk,jdn->jkn/dot_general | solution.py:133
  673.2 16.2 %fusion.109 = bf16[2,2048,16]{1,2,0:T(8,128)(2,1)} fusion(bf16[2,16,1408]{2,1,0:T(8,128)(2,1)S(1)} %copy-done.50, f32[2,2048,1408]{2,1,0:T(8,128)} %get-tuple-element.1013, f32[2,1408]{1,0:T(2,128)S(1)} %get-tuple-element.994), kind=kOutput, calls=%fused_computation.150 | convolution fusion | flops 1113194496 | bytes 23301120 | tf_op jit(solution)/shard_map/jdn,jkn->jdk/dot_general | solution.py:118
  689.4 11.5 %all-reduce = (f32[2048]{0:T(1024)S(1)}, f32[2048]{0:T(1024)S(1)}) all-reduce(f32[2048]{0:T(1024)S(1)} %copy-done.93, f32[2048]{0:T(1024)S(1)} %copy-done.92), channel_id=1, replica_groups=mesh['seq'=8,'tensor'=4] {'tensor'}, use_global_device_ids=true, to_apply=%region_44.45 | all-reduce | flops 4096 | bytes 32768 | tf_op jit(solution)/shard_map/psum | solution.py:202
  702.2 8.7 fusion.121
  715.0 153.0 %reduce-scatter.12.cloned.1.call-done = bf16[6,128,1024]{2,1,0:T(8,128)(2,1)} async-done(((bf16[6,1024,1024]{2,1,0:T(8,128)(2,1)}), bf16[6,128,1024]{2,1,0:T(8,128)(2,1)}) %reduce-scatter.12.cloned.1.call-update) | async-done | bytes 1572880 | tf_op jit(solution)/shard_map/reduce_scatter | solution.py:484
  903.6 29.6 %all-reduce.17.cloned.1.call-done = (bf16[3,6,128,16]{2,3,1,0:T(8,128)(2,1)}, bf16[3,2048,16]{1,2,0:T(8,128)(2,1)}, bf16[16,2048]{1,0:T(8,128)(2,1)}, bf16[2,2048,16]{1,2,0:T(8,128)(2,1)}, bf16[16,2048]{1,0:T(8,128)(2,1)}) async-done(((bf16[3,6,128,16]{2,3,1,0:T(8,128)(2,1)}, bf16[3,2048,16]{1,2,0:T(8,128)(2,1)}, bf16[16,2048]{1,0:T(8,128)(2,1)}, bf16[2,2048,16]{1,2,0:T(8,128)(2,1)}, ...) | async-done | bytes 532496 | tf_op jit(solution)/shard_map/psum | solution.py:122
  940.0 9.3 bitcast_convert_fusion
  949.4 61.2 %all-reduce.11.cloned.1.call-done = (bf16[3,16,512]{2,1,0:T(8,128)(2,1)}, bf16[3,512]{1,0:T(4,128)(2,1)}, bf16[512,16]{0,1:T(8,128)(2,1)}, bf16[2048]{0:T(1024)(...) async-done(((bf16[3,16,512]{2,1,0:T(8,128)(2,1)}, bf16[3,512]{1,0:T(4,128)(2,1)}, bf16[512,16]{0,1:T(8,128)(2,1)}, ...) | async-done | bytes 127504 | tf_op jit(solution)/shard_map/psum | solution.py:503
  1019.9 69.3 %all-reduce.13.cloned.1.call-done = (bf16[3,2048,16]{1,2,0:T(8,128)(2,1)}, bf16[16,2048]{1,0:T(8,128)(2,1)}, bf16[2,2048,16]{1,2,0:T(8,128)(2,1)}, bf16[2,16,1408]{2,1,0:T(8,128)(2,1)}, bf16[16,2048]{1,0:T(8,128)(2,1)}) async-done(((bf16[3,2048,16]{1,2,0:T(8,128)(2,1)}, bf16[16,2048]{1,0:T(8,128)(2,1)}, bf16[2,2048,16]{1,2,0:T(8,128)(2,1)}, bf16[2,16,1408]{2,1,0:T(8,128)(2,1)}, bf16[16,2048]{1,0:T(8,128)(2,1)}), ...) | async-done | bytes 548880 | tf_op jit(solution)/shard_map/psum | solution.py:502
  1097.1 32.1 %reduce-scatter.14.cloned.1.call-done = bf16[6,32,2048]{2,1,0:T(8,128)(2,1)} async-done(((bf16[6,128,2048]{2,1,0:T(8,128)(2,1)}), bf16[6,32,2048]{2,1,0:T(8,128)(2,1)}) %reduce-scatter.14.cloned.1.call-update) | async-done | bytes 786448 | tf_op jit(solution)/shard_map/reduce_scatter | solution.py:142
  (419 shorter events, 263.4 us)
Async XLA Ops:
  7.2 36.3 %all-gather.8.cloned.1.call-start = ((), (), s32[]{:S(2)}) async-start(), calls=%async_computation.5 | async-start | bytes 3932160 | tf_op jit(solution)/shard_map/all_gather | solution.py:72
  12.2 147.1 %all-gather.18.cloned.1.call-start = ((), (), s32[]{:S(2)}) async-start(), calls=%async_computation.15 | async-start | bytes 7077888 | tf_op jit(solution)/shard_map/all_gather | solution.py:407
  20.6 33.3 %copy-start.73 = (f32[3,512]{1,0:T(4,128)}, f32[3,512]{1,0:T(4,128)S(1)}, u32[]{:S(2)}) copy-start(f32[3,512]{1,0:T(4,128)S(1)} %sqrt_divide_fusion) | copy-start | bytes 18436
  60.1 199.2 %all-gather.10.cloned.1.call-start = ((), (), s32[]{:S(2)}) async-start(), calls=%async_computation.6 | async-start | bytes 7077888 | tf_op jit(solution)/shard_map/all_gather | solution.py:406
  71.8 259.8 %reduce-scatter.6.cloned.1.call-start = ((), (), s32[]{:S(2)}) async-start(), calls=%async_computation.7 | async-start | bytes 3932160 | tf_op jit(solution)/shard_map/reduce_scatter | solution.py:177
  74.5 93.5 %copy-start.1 = (bf16[6,128,4,128]{1,3,2,0:T(8,128)(2,1)}, bf16[6,128,4,128]{1,3,2,0:T(8,128)(2,1)S(1)}, u32[]{:S(2)}) copy-start(bf16[6,128,4,128]{1,3,2,0:T(8,128)(2,1)S(1)} %fusion.140) | copy-start | bytes 2359300
  286.7 75.1 %all-gather.14.cloned.1.call-start = ((), (), s32[]{:S(2)}) async-start(), calls=%async_computation.10 | async-start | bytes 3932160 | tf_op jit(solution)/shard_map/all_gather | solution.py:204
  298.5 33.0 %copy-start.14 = (bf16[6,32,2048]{2,1,0:T(8,128)(2,1)S(1)}, bf16[6,32,2048]{2,1,0:T(8,128)(2,1)}, u32[]{:S(2)}) copy-start(bf16[6,32,2048]{2,1,0:T(8,128)(2,1)} %param.30) | copy-start | bytes 2359300
  298.6 33.0 %copy-start.40 = (bf16[16,2048]{1,0:T(8,128)(2,1)S(1)}, bf16[16,2048]{1,0:T(8,128)(2,1)}, u32[]{:S(2)}) copy-start(bf16[16,2048]{1,0:T(8,128)(2,1)} %param.42) | copy-start | bytes 196612
  310.7 81.7 %all-gather.12.cloned.1.call-start = ((), (), s32[]{:S(2)}) async-start(), calls=%async_computation.8 | async-start | bytes 3932160 | tf_op jit(solution)/shard_map/all_gather | solution.py:72
  335.7 119.6 %all-reduce.15.cloned.1.call-start = ((), (), s32[]{:S(2)}) async-start(), calls=%async_computation.18 | async-start | bytes 147456 | tf_op jit(solution)/shard_map/psum | solution.py:168
  364.8 45.2 %copy-start.69 = (bf16[6,128,16]{1,2,0:T(8,128)(2,1)}, bf16[6,128,16]{1,2,0:T(8,128)(2,1)S(1)}, u32[]{:S(2)}) copy-start(bf16[6,128,16]{1,2,0:T(8,128)(2,1)S(1)} %fusion.173) | copy-start | bytes 73732
  425.8 72.0 %reduce-scatter.10.cloned.1.call-start = ((), (), s32[]{:S(2)}) async-start(), calls=%async_computation.11 | async-start | bytes 3932160 | tf_op jit(solution)/shard_map/reduce_scatter | solution.py:142
  440.3 98.2 %reduce-scatter.8.cloned.1.call-start = ((), (), s32[]{:S(2)}) async-start(), calls=%async_computation.9 | async-start | bytes 3932160 | tf_op jit(solution)/shard_map/reduce_scatter | solution.py:177
  449.3 124.6 %all-gather.16.cloned.1.call-start = ((), (), s32[]{:S(2)}) async-start(), calls=%async_computation.12 | async-start | bytes 3932160 | tf_op jit(solution)/shard_map/all_gather | solution.py:204
  542.9 30.9 %copy-start.41 = (bf16[16,2048]{1,0:T(8,128)(2,1)S(1)}, bf16[16,2048]{1,0:T(8,128)(2,1)}, u32[]{:S(2)}) copy-start(bf16[16,2048]{1,0:T(8,128)(2,1)} %param.42) | copy-start | bytes 196612
  544.0 32.7 %copy-start.31 = (bf16[512,2048]{1,0:T(8,128)(2,1)S(1)}, bf16[512,2048]{1,0:T(8,128)(2,1)}, u32[]{:S(2)}) copy-start(bf16[512,2048]{1,0:T(8,128)(2,1)} %param.40) | copy-start | bytes 6291460
  545.1 322.8 %reduce-scatter.12.cloned.1.call-start = ((), (), s32[]{:S(2)}) async-start(), calls=%async_computation.13 | async-start | bytes 14155776 | tf_op jit(solution)/shard_map/reduce_scatter | solution.py:484
  645.5 287.7 %all-reduce.17.cloned.1.call-start = ((), (), s32[]{:S(2)}) async-start(), calls=%async_computation.19 | async-start | bytes 1064960 | tf_op jit(solution)/shard_map/psum | solution.py:122
  673.1 28.4 %copy-start.97 = (f32[2048]{0:T(1024)S(1)}, f32[2048]{0:T(1024)}, u32[]{:S(2)}) copy-start(f32[2048]{0:T(1024)} %param.43) | copy-start | bytes 24580
  673.2 29.0 %copy-start.38 = (bf16[16,2048]{1,0:T(8,128)(2,1)S(1)}, bf16[16,2048]{1,0:T(8,128)(2,1)}, u32[]{:S(2)}) copy-start(bf16[16,2048]{1,0:T(8,128)(2,1)} %param.50) | copy-start | bytes 196612
  715.0 154.8 %copy-start.46 = (f32[128,128]{0,1:T(8,128)S(1)}, f32[128,128]{0,1:T(8,128)}, u32[]{:S(2)}) copy-start(f32[128,128]{0,1:T(8,128)} %copy-done.45) | copy-start | bytes 196612
  897.3 35.9 %copy-start.12 = (bf16[6,128,2048]{2,1,0:T(8,128)(2,1)S(1)}, bf16[6,128,2048]{2,1,0:T(8,128)(2,1)}, u32[]{:S(2)}) copy-start(bf16[6,128,2048]{2,1,0:T(8,128)(2,1)} %all-gather.12.cloned.1.call-done) | copy-start | bytes 9437188
  900.5 35.1 %copy-start.68 = (bf16[6,128,16]{1,2,0:T(8,128)(2,1)S(1)}, bf16[6,128,16]{1,2,0:T(8,128)(2,1)}, u32[]{:S(2)}) copy-start(bf16[6,128,16]{1,2,0:T(8,128)(2,1)} %get-tuple-element.944) | copy-start | bytes 73732
  900.5 110.0 %all-reduce.11.cloned.1.call-start = ((), (), s32[]{:S(2)}) async-start(), calls=%async_computation.16 | async-start | bytes 257024 | tf_op jit(solution)/shard_map/psum | solution.py:503
  903.3 185.9 %all-reduce.13.cloned.1.call-start = ((), (), s32[]{:S(2)}) async-start(), calls=%async_computation.17 | async-start | bytes 1097728 | tf_op jit(solution)/shard_map/psum | solution.py:502
  939.9 189.2 %reduce-scatter.14.cloned.1.call-start = ((), (), s32[]{:S(2)}) async-start(), calls=%async_computation.14 | async-start | bytes 3932160 | tf_op jit(solution)/shard_map/reduce_scatter | solution.py:142
  949.3 179.9 %copy-start.15 = (bf16[6,32,2048]{2,1,0:T(8,128)(2,1)S(1)}, bf16[6,32,2048]{2,1,0:T(8,128)(2,1)}, u32[]{:S(2)}) copy-start(bf16[6,32,2048]{2,1,0:T(8,128)(2,1)} %param.30) | copy-start | bytes 2359300
  949.3 179.9 %copy-start.91 = (f32[2048]{0:T(1024)S(1)}, f32[2048]{0:T(1024)}, u32[]{:S(2)}) copy-start(f32[2048]{0:T(1024)} %param.34) | copy-start | bytes 24580
  949.3 181.6 %copy-start.86 = (f32[6,32]{1,0:T(8,128)S(1)}, f32[6,32]{1,0:T(8,128)}, u32[]{:S(2)}) copy-start(f32[6,32]{1,0:T(8,128)} %copy-done.85) | copy-start | bytes 2308
  949.3 181.6 %copy-start.18 = (f32[6,32,2048]{2,1,0:T(8,128)S(1)}, f32[6,32,2048]{2,1,0:T(8,128)}, u32[]{:S(2)}) copy-start(f32[6,32,2048]{2,1,0:T(8,128)} %copy-done.17) | copy-start | bytes 4718596
  949.3 181.6 %copy-start.88 = (f32[6,32]{1,0:T(8,128)S(1)}, f32[6,32]{1,0:T(8,128)}, u32[]{:S(2)}) copy-start(f32[6,32]{1,0:T(8,128)} %copy-done.87) | copy-start | bytes 2308
  (99 other events, 808.2 us)
Sparse Core Ops, SparseCore 0:
  12.3 31.2 all-gather.7
  60.2 99.0 all-gather.17
  162.0 97.2 all-gather.9
  286.8 44.6 reduce-scatter.5
  333.0 28.7 all-gather.13
  363.9 28.5 all-gather.11
  425.9 29.4 all-reduce.14
  457.9 39.7 reduce-scatter.9
  500.5 37.9 reduce-scatter.7
  545.3 28.5 all-gather.15
  645.6 222.2 reduce-scatter.11
  900.6 32.5 all-reduce.16
  939.1 71.3 all-reduce.10
  1015.5 73.6 all-reduce.12
  1091.7 37.4 reduce-scatter.13
where the time goes:
time: 1150 us; the launch traced here: 1140 us
  waiting for transfers between devices  712 us (62%)
  matrix products  230 us (20%)
  local copies, waits for them, and re-layouts  94.3 us (8%)
  other arithmetic  61.8 us (5%)
  blocking collectives  22.2 us (2%)
  between operations  15.5 us (1%)
    reduce_scatter x1, waiting for transfers between devices, local(): lax.psum_scatter(buffer.astype(jnp.bfloat16), 'seq', scatter_dimension=1,...  153 us
    all_gather x1, waiting for transfers between devices, local(): lax.all_gather(key_flat, 'seq', axis=1, tiled=True)  91.3 us
    all_gather x1, waiting for transfers between devices, local(): lax.all_gather(value_flat, 'seq', axis=1, tiled=True)  84.4 us
    reduce_scatter x2, waiting for transfers between devices, column_backward(): lax.psum_scatter(partial_in.astype(jnp.bfloat16), 'tensor', scatter_dimen...  74.4 us
    psum x1, waiting for transfers between devices, local(): lax.psum(grad_a_qkv.astype(jnp.bfloat16), 'seq').astype(jnp.float32)  69.3 us
    psum x1, waiting for transfers between devices, local(): lax.psum(grad_b_qkv.astype(jnp.bfloat16), 'seq').astype(jnp.float32)  61.2 us
    reduce_scatter x2, waiting for transfers between devices, row_forward(): lax.psum_scatter(partial_out.astype(jnp.bfloat16), 'tensor', scatter_dime...  58.9 us
    all_gather x2, waiting for transfers between devices, row_backward(): lax.all_gather(grad_plain, 'tensor', axis=1, tiled=True)  41.8 us
  transfers between devices with their start and end apart: 15, of which 15 were waited for; matrix products, arithmetic and copies ran while one was open for 17% of the time, Pallas kernels for 0%

commit v1 on v0

v1 whole, which is shorter than its diff:
```python
from functools import partial
import math

import jax
import jax.numpy as jnp
from jax import lax
from jax.experimental import pallas as pl
from jax.experimental.pallas import tpu as pltpu
from jax.sharding import PartitionSpec as P

HEAD_DIM = 128
LANES = 128
epsilon = 1e-05
adapter_scale = 2.0
rope_base = 10000.0
f32 = jnp.float32
bf16 = jnp.bfloat16
PIECES = (0, 2, 1, 3)
score_block = 256
NT = (((1,), (1,)), ((), ()))
NN = (((1,), (0,)), ((), ()))
TN = (((0,), (0,)), ((), ()))


def mm(a, b, dims=NN):
    return lax.dot_general(a, b, dims, preferred_element_type=f32)


def swap(values, bit):
    size = lax.axis_size("tensor")
    return lax.ppermute(values, "tensor", [(i, i ^ bit) for i in range(size)])


def gather_pieces(shard):
    far = swap(shard, 2)
    near = swap(shard, 1)
    both = swap(far, 1)
    return jnp.stack([shard, far, near, both])


def scatter_pieces(partial_sums):
    got = swap(partial_sums[2:4], 1)
    keep = partial_sums[0:2].astype(f32) + got.astype(f32)
    return keep[0] + swap(keep[1].astype(bf16), 2).astype(f32)


def tensor_sum(values):
    return values + swap(values, 1) + swap(values, 2) + swap(values, 3)


def exchange(values):
    return lax.all_to_all(values, "seq", 0, 0, tiled=True)


def seq_gather(values):
    size = lax.axis_size("seq")
    return exchange(jnp.broadcast_to(values[None], (size,) + values.shape))


def column_prep_kernel(w_ref, a_ref, b_ref, m_ref, out_ref, stat_ref, cross_ref):
    w, a, b = w_ref[0], a_ref[0], b_ref[0]
    heading = w.astype(f32) + adapter_scale * mm(a, b)
    square = jnp.sum(heading * heading, axis=0, keepdims=True)
    norm = jnp.sqrt(square)
    scale = m_ref[0] / norm
    scaled = (heading * scale).astype(bf16)
    out_ref[0] = scaled
    stat_ref[0] = jnp.concatenate([norm, scale], axis=0)
    cross_ref[0] = mm(a, scaled, TN)


def column_prep(weight, down, up, magnitude, block, interleave):
    members, width, out = weight.shape
    rank = down.shape[2]
    if interleave:
        scaled_shape = (1, width, members * out)
        scaled_map = lambda i, j: (0, 0, i * members + j)
    else:
        scaled_shape = (members, width, out)
        scaled_map = lambda i, j: (j, 0, i)
    return pl.pallas_call(
        column_prep_kernel,
        grid=(out // block, members),
        in_specs=[
            pl.BlockSpec((1, width, block), lambda i, j: (j, 0, i)),
            pl.BlockSpec((1, width, rank), lambda i, j: (j, 0, 0)),
            pl.BlockSpec((1, rank, block), lambda i, j: (j, 0, i)),
            pl.BlockSpec((1, 1, block), lambda i, j: (j, 0, i)),
        ],
        out_specs=[
            pl.BlockSpec((1, width, block), scaled_map),
            pl.BlockSpec((1, 2, block), lambda i, j: (j, 0, i)),
            pl.BlockSpec((1, rank, block), lambda i, j: (j, 0, i)),
        ],
        out_shape=[
            jax.ShapeDtypeStruct(scaled_shape, bf16),
            jax.ShapeDtypeStruct((members, 2, out), f32),
            jax.ShapeDtypeStruct((members, rank, out), f32),
        ],
        cost_estimate=pl.CostEstimate(
            flops=2 * members * width * out * 256, bytes_accessed=4 * members * width * out, transcendentals=0
        ),
        name="column_prep",
    )(weight, down, up, magnitude[:, None, :])


def row_prep_kernel(w_ref, a_ref, b_ref, out_ref, stat_ref):
    w, a, b = w_ref[...], a_ref[...], b_ref[...]
    heading = w.astype(f32) + adapter_scale * mm(a, b)
    narrow = heading.astype(bf16)
    out_ref[...] = narrow
    square = jnp.sum(heading * heading, axis=0, keepdims=True)
    stat_ref[...] = jnp.concatenate([mm(a, narrow, TN), jnp.broadcast_to(square, (8, square.shape[1]))], axis=0)


def row_prep(weight, down, up, block):
    rows, out = weight.shape
    rank = down.shape[1]
    return pl.pallas_call(
        row_prep_kernel,
        grid=(out // block,),
        in_specs=[
            pl.BlockSpec((rows, block), lambda i: (0, i)),
            pl.BlockSpec((rows, rank), lambda i: (0, 0)),
            pl.BlockSpec((rank, block), lambda i: (0, i)),
        ],
        out_specs=[
            pl.BlockSpec((rows, block), lambda i: (0, i)),
            pl.BlockSpec((rank + 8, block), lambda i: (0, i)),
        ],
        out_shape=[
            jax.ShapeDtypeStruct((rows, out), bf16),
            jax.ShapeDtypeStruct((rank + 8, out), f32),
        ],
        cost_estimate=pl.CostEstimate(flops=2 * rows * out * 256, bytes_accessed=4 * rows * out, transcendentals=0),
        name="row_prep",
    )(weight, down, up)


def turn_forward(values, cosine, signed_sine):
    return values * cosine + pltpu.roll(values, values.shape[1] // 2, 1) * signed_sine


def turn_backward(values, cosine, signed_sine):
    return values * cosine + pltpu.roll(values * signed_sine, values.shape[1] // 2, 1)


def over_blocks(total, block, body):
    if total // block <= 4:
        for i in range(total // block):
            body(i * block, (i + 1) * block)
    else:

        def step(i, carry):
            body(pl.multiple_of(i * block, block), total)
            return carry

        lax.fori_loop(0, total // block, step, 0)


def weights_t(keys, queries, kpos, qpos, qstart, scale):
    scores = mm(keys, queries, NT)
    allowed = jnp.logical_and(kpos <= qpos, kpos >= qstart)
    return jnp.where(allowed, jnp.exp(scores * scale), 0.0)


def attend_kernel(x_ref, cos_ref, sin_ref, kpos_ref, qinfo_ref, o_ref, l_ref, qs, ks, vt, os, *, scale, block):
    blocks, _, _, group, size = x_ref.shape
    total = blocks * group
    cosine, signed_sine = cos_ref[...], sin_ref[...]
    qs[...] = turn_forward(x_ref[:, 0, 0].reshape(total, size).astype(f32), cosine, signed_sine).astype(bf16)
    ks[...] = turn_forward(x_ref[:, 0, 1].reshape(total, size).astype(f32), cosine, signed_sine).astype(bf16)
    vt[...] = x_ref[:, 0, 2].reshape(total, size).astype(f32).T.astype(bf16)

    def body(first, last):
        at = pl.ds(first, block)
        weights = weights_t(
            ks[:last], qs[at, :], kpos_ref[:last], qinfo_ref[0, 0:1, at], qinfo_ref[0, 1:2, at], scale
        )
        totals = jnp.sum(weights, axis=0, keepdims=True)
        outer = mm(vt[:, :last], weights.astype(bf16))
        l_ref[0, 0:1, at] = totals
        os[at, :] = (outer / totals).T.astype(bf16)

    over_blocks(total, block, body)
    o_ref[:, 0] = os[...].reshape(blocks, group, size)


def attend(pairs, tables, kpos, qinfo):
    blocks, slots, _, group, size = pairs.shape
    total = blocks * group
    block = math.gcd(total, score_block)
    return pl.pallas_call(
        partial(attend_kernel, scale=1.0 / math.sqrt(size), block=block),
        grid=(slots,),
        in_specs=[
            pl.BlockSpec((blocks, 1, 3, group, size), lambda n: (0, n, 0, 0, 0)),
            pl.BlockSpec((total, size), lambda n: (0, 0)),
            pl.BlockSpec((total, size), lambda n: (0, 0)),
            pl.BlockSpec((total, 1), lambda n: (0, 0)),
            pl.BlockSpec((1, 2, total), lambda n: (n, 0, 0)),
        ],
        out_specs=[
            pl.BlockSpec((blocks, 1, group, size), lambda n: (0, n, 0, 0)),
            pl.BlockSpec((1, 1, total), lambda n: (n, 0, 0)),
        ],
        out_shape=[
            jax.ShapeDtypeStruct((blocks, slots, group, size), bf16),
            jax.ShapeDtypeStruct((slots, 1, total), f32),
        ],
        scratch_shapes=[
            pltpu.VMEM((total, size), bf16),
            pltpu.VMEM((total, size), bf16),
            pltpu.VMEM((size, total), bf16),
            pltpu.VMEM((total, size), bf16),
        ],
        cost_estimate=pl.CostEstimate(
            flops=slots * 4 * total * total * size,
            bytes_accessed=slots * total * size * 8,
            transcendentals=slots * total * total // 2,
        ),
        name="attend",
    )(pairs, *tables, kpos, qinfo)


def attend_back_kernel(
    x_ref, o_ref, d_ref, l_ref, cos_ref, sin_ref, kpos_ref, qinfo_ref, g_ref, s_ref,
    qs, ks, kt, vs, dk, dv, dq, *, scale, block
):
    blocks, _, _, group, size = x_ref.shape
    total = blocks * group
    cosine, signed_sine = cos_ref[...], sin_ref[...]
    plain = [x_ref[:, 0, j].reshape(total, size).astype(f32) for j in range(3)]
    qs[...] = turn_forward(plain[0], cosine, signed_sine).astype(bf16)
    turned = turn_forward(plain[1], cosine, signed_sine)
    ks[...] = turned.astype(bf16)
    kt[...] = turned.T.astype(bf16)
    vs[...] = plain[2].astype(bf16)
    dk[...] = jnp.zeros_like(dk)
    dv[...] = jnp.zeros_like(dv)

    def body(first, last):
        at = pl.ds(first, block)
        span = block // group
        rows = pl.ds(first // group, span)
        weights = weights_t(
            ks[:last], qs[at, :], kpos_ref[:last], qinfo_ref[0, 0:1, at], qinfo_ref[0, 1:2, at], scale
        )
        totals = l_ref[0, 0:1, at]
        grad_t = d_ref[rows, 0].reshape(block, size).astype(f32).T
        out_t = o_ref[rows, 0].reshape(block, size).astype(f32).T
        dlog = -jnp.sum(grad_t * out_t, axis=0, keepdims=True) / totals
        outer_t = (grad_t / totals).astype(bf16)
        dweights = mm(vs[:last], outer_t)
        dscores = (weights * (dweights + dlog)).astype(bf16)
        dk[:last] += mm(dscores, qs[at, :])
        dv[:last] += mm(weights.astype(bf16), outer_t, NT)
        dq[at, :] = mm(kt[:, :last], dscores).T

    over_blocks(total, block, body)
    grads = (
        turn_backward(dq[...] * scale, cosine, signed_sine),
        turn_backward(dk[...] * scale, cosine, signed_sine),
        dv[...],
    )
    sums = []
    for j in range(3):
        g_ref[:, 0, j] = grads[j].astype(bf16).reshape(blocks, group, size)
        sums.append(jnp.sum(grads[j] * plain[j], axis=0, keepdims=True))
    s_ref[0] = jnp.concatenate(sums, axis=0)


def attend_back(pairs, outputs, grads, totals, tables, kpos, qinfo):
    blocks, slots, _, group, size = pairs.shape
    total = blocks * group
    block = math.gcd(total, score_block)
    half = pl.BlockSpec((blocks, 1, group, size), lambda n: (0, n, 0, 0))
    whole = pl.BlockSpec((blocks, 1, 3, group, size), lambda n: (0, n, 0, 0, 0))
    return pl.pallas_call(
        partial(attend_back_kernel, scale=1.0 / math.sqrt(size), block=block),
        grid=(slots,),
        in_specs=[
            whole,
            half,
            half,
            pl.BlockSpec((1, 1, total), lambda n: (n, 0, 0)),
            pl.BlockSpec((total, size), lambda n: (0, 0)),
            pl.BlockSpec((total, size), lambda n: (0, 0)),
            pl.BlockSpec((total, 1), lambda n: (0, 0)),
            pl.BlockSpec((1, 2, total), lambda n: (n, 0, 0)),
        ],
        out_specs=[whole, pl.BlockSpec((1, 3, size), lambda n: (n, 0, 0))],
        out_shape=[
            jax.ShapeDtypeStruct(pairs.shape, bf16),
            jax.ShapeDtypeStruct((slots, 3, size), f32),
        ],
        scratch_shapes=[
            pltpu.VMEM((total, size), bf16),
            pltpu.VMEM((total, size), bf16),
            pltpu.VMEM((size, total), bf16),
            pltpu.VMEM((total, size), bf16),
            pltpu.VMEM((total, size), f32),
            pltpu.VMEM((total, size), f32),
            pltpu.VMEM((total, size), f32),
        ],
        cost_estimate=pl.CostEstimate(
            flops=slots * 10 * total * total * size,
            bytes_accessed=slots * total * size * 16,
            transcendentals=slots * total * total // 2,
        ),
        name="attend_back",
    )(pairs, outputs, grads, totals, *tables, kpos, qinfo)


def gated_kernel(x_ref, w_ref, e_ref, hidden_ref, grads_ref, sums_ref):
    both = mm(x_ref[...], w_ref[0])
    width = both.shape[1] // 2
    gate, up = both[:, :width], both[:, width:]
    dhid = e_ref[...].astype(f32)
    sig = 1.0 / (1.0 + jnp.exp(-gate))
    act = gate * sig
    hidden_ref[...] = (act * up).astype(bf16)
    dgate = dhid * up * (sig * (1.0 + gate * (1.0 - sig)))
    dup = dhid * act
    grads_ref[:, :width] = dgate.astype(bf16)
    grads_ref[:, width:] = dup.astype(bf16)
    sums_ref[...] = jnp.concatenate(
        [jnp.sum(gate * dgate, axis=0, keepdims=True), jnp.sum(up * dup, axis=0, keepdims=True)], axis=1
    )


def gated(rows, weight, dhid, block):
    count, width = rows.shape
    out = dhid.shape[1]
    return pl.pallas_call(
        gated_kernel,
        grid=(out // block,),
        in_specs=[
            pl.BlockSpec((count, width), lambda i: (0, 0)),
            pl.BlockSpec((1, width, 2 * block), lambda i: (0, 0, i)),
            pl.BlockSpec((count, block), lambda i: (0, i)),
        ],
        out_specs=[
            pl.BlockSpec((count, block), lambda i: (0, i)),
            pl.BlockSpec((count, 2 * block), lambda i: (0, i)),
            pl.BlockSpec((1, 2 * block), lambda i: (0, i)),
        ],
        out_shape=[
            jax.ShapeDtypeStruct((count, out), bf16),
            jax.ShapeDtypeStruct((count, 2 * out), bf16),
            jax.ShapeDtypeStruct((1, 2 * out), f32),
        ],
        cost_estimate=pl.CostEstimate(
            flops=4 * count * width * out,
            bytes_accessed=4 * width * out + 2 * count * (width + 4 * out),
            transcendentals=count * out,
        ),
        name="gated",
    )(rows, weight, dhid)


def norm_scale(values):
    return lax.rsqrt(jnp.mean(values * values, axis=-1, keepdims=True) + epsilon)


def norm_back(values, gain, grad):
    r = norm_scale(values)
    weighted = gain * grad
    return r * weighted - values * (r * r * r) * jnp.mean(values * weighted, axis=-1, keepdims=True)


def rotary_tables(positions, head_size):
    half_size = head_size // 2
    frequency = rope_base ** (-(2.0 * jnp.arange(half_size, dtype=f32)) / head_size)
    angles = positions.astype(f32)[:, None] * frequency[None, :]
    cosine, sine = jnp.cos(angles), jnp.sin(angles)
    return (jnp.concatenate([cosine, cosine], axis=-1), jnp.concatenate([-sine, sine], axis=-1))


def interleaved(values, block):
    lead, out = values.shape[:-2], values.shape[-1]
    parts = values.reshape(lead + (2, out // block, block))
    return jnp.swapaxes(parts, -3, -2).reshape(lead + (2 * out,))


def separated(values, block):
    lead, both = values.shape[:-1], values.shape[-1]
    parts = values.reshape(lead + (both // (2 * block), 2, block))
    return jnp.swapaxes(parts, -3, -2).reshape(lead + (2, both // 2))


def block_diagonal(values):
    members, rank, out = values.shape
    eye = jnp.eye(members, dtype=values.dtype)
    return (eye[:, None, :, None] * values[:, :, None, :]).reshape(members * rank, members * out)


def local(
    layer_in, cotangent, doc_lengths, pad_counts, gain_attn, gain_ffn, w_qkv, a_qkv, b_qkv, m_qkv, w_out, a_out,
    b_out, m_out, w_gateup, a_gateup, b_gateup, m_gateup, w_down, a_down, b_down, m_down,
):
    rows, quarter, width = layer_in.shape
    tensor, seq = lax.axis_size("tensor"), lax.axis_size("seq")
    assert tensor == len(PIECES)
    me_t, me_s = lax.axis_index("tensor"), lax.axis_index("seq")
    group = quarter * tensor
    total = group * seq
    feat = w_qkv.shape[2]
    heads = feat // HEAD_DIM
    rank = a_qkv.shape[2]
    ff = w_down.shape[0]
    tokens = group * rows
    ff_block = LANES
    pair_count = rows * heads
    slots = -(-pair_count // seq)

    piece_of = jnp.bitwise_xor(me_t, jnp.array(PIECES, jnp.int32))
    in_block = (piece_of[:, None] * quarter + jnp.arange(quarter, dtype=jnp.int32)[None, :]).reshape(group)
    positions = (jnp.arange(seq, dtype=jnp.int32)[:, None] * group + in_block[None, :]).reshape(total)
    tables = rotary_tables(positions, HEAD_DIM)
    offsets = jnp.cumsum(doc_lengths, axis=1)
    starts = jnp.max(
        jnp.where(offsets[:, :, None] <= positions[None, None, :], offsets[:, :, None], 0), axis=1
    )
    my_rows = jnp.minimum((me_s * slots + jnp.arange(slots)) // heads, rows - 1)
    row_choice = (my_rows[:, None] == jnp.arange(rows)[None, :])[:, :, None]
    my_starts = jnp.sum(jnp.where(row_choice, starts[None], 0), axis=1)
    qinfo = jnp.stack([jnp.broadcast_to(positions[None], (slots, total)), my_starts], axis=1)
    kpos = positions[:, None]

    def to_pairs(values, parts):
        laid = values.reshape(tensor, rows, quarter, parts, heads, HEAD_DIM).transpose(1, 4, 3, 0, 2, 5)
        laid = laid.reshape(pair_count, parts, group, HEAD_DIM)
        if slots * seq > pair_count:
            laid = jnp.pad(laid, ((0, slots * seq - pair_count), (0, 0), (0, 0), (0, 0)))
        return exchange(laid.reshape(seq, slots, parts, group, HEAD_DIM))

    def from_pairs(values, parts):
        laid = exchange(values).reshape(seq * slots, parts, group, HEAD_DIM)[:pair_count]
        laid = laid.reshape(rows, heads, parts, tensor, quarter, HEAD_DIM).transpose(3, 0, 4, 2, 1, 5)
        return laid.reshape(tokens, parts * heads * HEAD_DIM)

    def gathered(shard):
        return gather_pieces(shard).reshape(tokens, width)

    def scattered(partial_sums):
        return scatter_pieces(partial_sums.astype(bf16).reshape(tensor, rows, quarter, -1))

    wide_in = layer_in.astype(f32)
    normed_a = gathered((wide_in * norm_scale(wide_in) * gain_attn).astype(bf16))

    down_w, down_stat = row_prep(w_down, a_down, b_down, 256)
    qkv_w, qkv_stat, qkv_cross = column_prep(w_qkv, a_qkv, b_qkv, m_qkv, 256, False)
    out_w, out_stat = row_prep(w_out, a_out, b_out, 512)
    gu_w, gu_stat, gu_cross = column_prep(w_gateup, a_gateup, b_gateup, m_gateup, ff_block, True)
    squares = tensor_sum(jnp.stack([down_stat[rank], out_stat[rank]]))
    down_scale, out_scale = m_down / jnp.sqrt(squares[0]), m_out / jnp.sqrt(squares[1])

    owned = me_s * group + me_t * quarter + jnp.arange(quarter, dtype=jnp.int32)
    valid = (owned[None, :] < total - pad_counts[:, None]).astype(f32)
    cot = cotangent.astype(f32) * valid[:, :, None]
    du_down = gathered((cot * down_scale).astype(bf16))
    dhid = mm(du_down, down_w, NT).astype(bf16)
    dt_down = (adapter_scale * mm(du_down, b_down, NT)).astype(bf16)

    qkv_rows = jnp.concatenate([mm(normed_a, qkv_w[j]).astype(bf16) for j in range(3)], axis=1)
    pairs = to_pairs(qkv_rows, 3)
    outputs, totals = attend(pairs, tables, kpos, qinfo)
    att = from_pairs(outputs[:, :, None], 1)
    u_out = scattered(mm(att, out_w)) * out_scale
    middle = wide_in + u_out

    normed_f = gathered((middle * norm_scale(middle) * gain_ffn).astype(bf16))
    hidden, d_gu, gu_sum = gated(normed_f, gu_w, dhid, ff_block)
    grad_norm_f = scattered(mm(d_gu, gu_w[0], NT))
    d_mid = cot + norm_back(middle, gain_ffn, grad_norm_f)
    du_out = gathered((d_mid * out_scale).astype(bf16))
    d_att = mm(du_out, out_w, NT).astype(bf16)

    d_pairs, pair_sums = attend_back(
        pairs, outputs, to_pairs(d_att, 1)[:, :, 0], totals, tables, kpos, qinfo
    )
    d_qkv = from_pairs(d_pairs, 3)
    grad_norm_a = scattered(sum(mm(d_qkv[:, j * feat:(j + 1) * feat], qkv_w[j], NT) for j in range(3)))
    grad_in = d_mid + norm_back(wide_in, gain_attn, grad_norm_a)

    u_down = scattered(mm(hidden, down_w)) * down_scale
    layer_out = (middle + u_down).astype(bf16)

    row_sums = tensor_sum(
        jnp.stack([jnp.sum(u_down * cot, axis=(0, 1)), jnp.sum(u_out * d_mid, axis=(0, 1))])
    )
    down_sum, out_sum = row_sums[0], row_sums[1]
    gu_sums = separated(gu_sum[0], ff_block)
    my_heads = (me_s * slots + jnp.arange(slots)) % heads
    live = me_s * slots + jnp.arange(slots) < pair_count
    head_choice = jnp.logical_and(my_heads[:, None] == jnp.arange(heads)[None, :], live[:, None])
    qkv_sums = jnp.sum(
        jnp.where(head_choice[:, None, :, None], pair_sums[:, :, None, :], 0.0), axis=0
    ).reshape(3, feat)

    def column_grads(rows_in, grads, weight, down, up_cat, scale_cat, coef_cat, cross_cat, members):
        t = mm(rows_in, down.transpose(1, 0, 2).reshape(width, members * rank)).astype(bf16)
        grad_b = adapter_scale * (mm(t, grads, TN) * scale_cat + coef_cat * cross_cat)
        dt = mm(grads, (adapter_scale * up_cat * scale_cat).astype(bf16), NT).astype(bf16)
        grad_a = mm(dt, rows_in, TN) + adapter_scale * mm((coef_cat * up_cat).astype(bf16), weight, NT)
        return grad_a, grad_b

    qkv_cat = lambda v: block_diagonal(v)
    gu_cat = lambda v: interleaved(
        block_diagonal(v).reshape(2 * rank, 2, ff), ff_block
    )
    qkv_coef = -qkv_sums / (m_qkv * qkv_stat[:, 0])
    gu_coef = -gu_sums / (m_gateup * gu_stat[:, 0])
    qkv_flat = qkv_w.transpose(1, 0, 2).reshape(width, 3 * feat)
    grad_a_qkv, grad_b_qkv = column_grads(
        normed_a, d_qkv, qkv_flat, a_qkv, qkv_cat(b_qkv.astype(f32)), qkv_stat[:, 1].reshape(-1),
        qkv_coef.reshape(-1), qkv_cat(qkv_cross), 3,
    )
    grad_b_qkv = jnp.stack(
        [grad_b_qkv[j * rank:(j + 1) * rank, j * feat:(j + 1) * feat] for j in range(3)]
    )
    grad_a_gu, grad_b_gu = column_grads(
        normed_f, d_gu, gu_w[0], a_gateup, gu_cat(b_gateup.astype(f32)), interleaved(gu_stat[:, 1], ff_block),
        interleaved(gu_coef, ff_block), gu_cat(gu_cross), 2,
    )
    grad_b_gu = separated(grad_b_gu, ff_block)
    grad_b_gu = jnp.stack([grad_b_gu[j * rank:(j + 1) * rank, j] for j in range(2)])

    def row_grads(rows_in, grads, dt, weight, down, up, square, stat, sums):
        coef = -sums / square
        t = mm(rows_in, down).astype(bf16)
        grad_b = adapter_scale * (mm(t, grads, TN) + coef * stat[:rank])
        grad_a = mm(dt, rows_in, TN) + adapter_scale * mm((coef * up.astype(f32)).astype(bf16), weight, NT)
        return grad_a, grad_b

    grad_a_out, grad_b_out = row_grads(
        att, du_out, (adapter_scale * mm(du_out, b_out, NT)).astype(bf16), out_w, a_out, b_out, squares[1], out_stat,
        out_sum,
    )
    grad_a_down, grad_b_down = row_grads(
        hidden, du_down, dt_down, down_w, a_down, b_down, squares[0], down_stat, down_sum
    )

    def reduce_all(over_all, over_seq):
        def packed(parts):
            flat = jnp.concatenate([p.astype(bf16).reshape(-1, LANES) for p in parts])
            return flat

        everything, lone = packed(over_all), packed(over_seq)
        unit = seq * 8
        pads = [(-len(v)) % unit for v in (everything, lone)]
        everything, lone = [
            jnp.pad(v, ((0, p), (0, 0))).reshape(seq, -1, LANES) for v, p in zip((everything, lone), pads)
        ]
        cut = everything.shape[1]
        mine = jnp.sum(exchange(jnp.concatenate([everything, lone], axis=1)).astype(f32), axis=0)
        shared = tensor_sum(mine[:cut].astype(bf16).astype(f32))
        back = seq_gather(jnp.concatenate([shared.astype(bf16), mine[cut:].astype(bf16)]))
        found = []
        for parts, values in ((over_all, back[:, :cut]), (over_seq, back[:, cut:])):
            flat, at = values.reshape(-1, LANES).astype(f32), 0
            for p in parts:
                count = p.size // LANES
                found.append(flat[at:at + count].reshape(p.shape))
                at += count
        return found

    (g_a_gu, g_b_out, g_b_down, g_b_gu, g_a_out, g_a_down, s_gu, s_out, s_down) = reduce_all(
        [grad_a_gu, grad_b_out, grad_b_down], [grad_b_gu, grad_a_out, grad_a_down, gu_sums, out_sum, down_sum]
    )
    g_a_qkv, g_b_qkv, s_qkv = reduce_all([grad_a_qkv], [grad_b_qkv, qkv_sums])
    return (
        layer_out,
        grad_in,
        g_a_qkv.reshape(3, rank, width).transpose(0, 2, 1),
        g_b_qkv,
        s_qkv / m_qkv,
        g_a_out.T,
        g_b_out,
        s_out / m_out,
        g_a_gu.reshape(2, rank, width).transpose(0, 2, 1),
        g_b_gu,
        s_gu / m_gateup,
        g_a_down.T,
        g_b_down,
        s_down / m_down,
    )


def solution(mesh):
    split = P(None, ("seq", "tensor"), None)
    in_specs = (
        split, split, P(), P(), P(), P(),
        P(None, None, "tensor"), P(), P(None, None, "tensor"), P(None, "tensor"),
        P("tensor", None), P("tensor", None), P(), P(),
        P(None, None, "tensor"), P(), P(None, None, "tensor"), P(None, "tensor"),
        P("tensor", None), P("tensor", None), P(), P(),
    )
    out_specs = (
        split, split,
        P(), P(None, None, "tensor"), P(None, "tensor"),
        P("tensor", None), P(), P(),
        P(), P(None, None, "tensor"), P(None, "tensor"),
        P("tensor", None), P(), P(),
    )
    return jax.shard_map(local, mesh=mesh, in_specs=in_specs, out_specs=out_specs, check_vma=False)
```

time: 1150 us -> 596 us (0.52)
  waiting for transfers between devices: 712 us -> 191 us
  matrix products: 230 us -> 110 us
  Pallas kernels: 0 us -> 83.8 us
  starting transfers between devices: 1.22 us -> 57.6 us
  blocking collectives: 22.2 us -> 0 us
  between operations: 15.5 us -> 2.5 us
    reduce_scatter x5 -> x0, waiting for transfers between devices: 286 us -> none  [the longest x1 153 us: local(): lax.psum_scatter(buffer.astype(jnp.bfloat16), 'seq', scatter_dimension=1,...]
    all_gather x6 -> x0, waiting for transfers between devices: 259 us -> none  [the longest x1 91.3 us: local(): lax.all_gather(key_flat, 'seq', axis=1, tiled=True)]
    psum x4 -> x0, waiting for transfers between devices: 166 us -> none  [the longest x1 69.3 us: local(): lax.psum(grad_a_qkv.astype(jnp.bfloat16), 'seq').astype(jnp.float32)]
    dot_general x51 -> x23, matrix products: 230 us -> 110 us  [mm(): return lax.dot_general(a, b, dims, preferred_element_type=f32)]
    all_to_all x0 -> x8, waiting for transfers between devices: none -> 97.5 us  [exchange(): return lax.all_to_all(values, 'seq', 0, 0, tiled=True)]
    ppermute x0 -> x32, waiting for transfers between devices: none -> 93.6 us  [swap(): return lax.ppermute(values, 'tensor', [(i, i ^ bit) for i in range(size)])]
    pallas_call x0 -> x7, Pallas kernels: none -> 83.8 us  [the longest x2 33.7 us: column_prep(): pl.pallas_call(column_prep_kernel, grid=(out // block, members), in_specs...]
    all_to_all x0 -> x8, starting transfers between devices: none -> 36 us  [exchange(): return lax.all_to_all(values, 'seq', 0, 0, tiled=True)]
  transfers between devices with their start and end apart: 15 -> 40, of which waited for: 15 -> 18; matrix products, arithmetic and copies ran while one was open for 17% -> 29% of each run, Pallas kernels for 0% -> 10%
where the time goes in v1:
time: 596 us; the launch traced here: 585 us
  waiting for transfers between devices  191 us (32%)
  matrix products  110 us (18%)
  local copies, waits for them, and re-layouts  87.9 us (15%)
  Pallas kernels  83.8 us (14%)
  starting transfers between devices  57.6 us (10%)
  other arithmetic  51.6 us (9%)
    dot_general x23, matrix products, mm(): return lax.dot_general(a, b, dims, preferred_element_type=f32)  110 us
    all_to_all x8, waiting for transfers between devices, exchange(): return lax.all_to_all(values, 'seq', 0, 0, tiled=True)  97.5 us
    ppermute x32, waiting for transfers between devices, swap(): return lax.ppermute(values, 'tensor', [(i, i ^ bit) for i in range(size)])  93.6 us
    all_to_all x8, starting transfers between devices, exchange(): return lax.all_to_all(values, 'seq', 0, 0, tiled=True)  36 us
    pallas_call x2, Pallas kernels, column_prep(): pl.pallas_call(column_prep_kernel, grid=(out // block, members), in_specs...  33.7 us
    ppermute x32, starting transfers between devices, swap(): return lax.ppermute(values, 'tensor', [(i, i ^ bit) for i in range(size)])  21.5 us
    pallas_call x1, Pallas kernels, gated(): pl.pallas_call(gated_kernel, grid=(out // block,), in_specs=[pl.BlockSpec...  18.3 us
    unnamed x149, local copies, waits for them, and re-layouts  14.4 us
  transfers between devices with their start and end apart: 40, of which 18 were waited for; matrix products, arithmetic and copies ran while one was open for 29% of the time, Pallas kernels for 10%

profile of v1, /device:TPU:0, one launch (start us, length us, event | category | flops | bytes accessed | tf_op | source)
XLA Modules:
  0.0 585.0 jit_solution(10422314395680215098)
XLA Ops:
  7.9 17.7 %collective-permute-done = bf16[6,32,2048]{2,1,0:T(8,128)(2,1)S(1)} collective-permute-done((bf16[6,32,2048]{2,1,0:T(8,128)(2,1)}, bf16[6,32,2048]{2,1,0:T(8,128)(2,1)S(1)}, u32[]{:S(2)}, u32[]{:S(2)}) %collective-permute-start) | collective-permute-done | bytes 786464 | tf_op jit(solution)/shard_map/ppermute | solution.py:31
  27.7 9.8 %column_prep.2 = (bf16[3,2048,512]{2,1,0:T(8,128)(2,1)}, f32[3,2,512]{2,1,0:T(2,128)}, f32[3,16,512]{2,1,0:T(8,128)}) custom-call(bf16[3,2048,512]{2,1,0:T(8,128)(2,1)} %w_ref.4, bf16[3,2048,16]{2,1,0:T(8,128)(2,1)} %copy.82.a_ref, bf16[3,16,512]{2,1,0:T(8,128)(2,1)} %b_ref.4, f32[3,1,512]{2,1,0:T(1,128)} %broadcast_in_dim.53.m_ref), custom_call_target="tpu_custom_call" | custom-call | flops 1610612736 | bytes 12582912 | tf_op jit(solution)/shard_map/column_prep/pallas_call | solution.py:81
  53.4 5.2 reshape.609
  62.3 6.5 %all-to-all-start = ((bf16[8,3,3,128,128]{4,3,2,1,0:T(8,128)(2,1)}), bf16[8,3,3,128,128]{4,3,2,1,0:T(8,128)(2,1)}, u32[]{:S(2)}, u32[]{:S(2)}) async-start(bf16[8,3,3,128,128]{4,3,2,1,0:T(8,128)(2,1)} %bitcast.287), calls=%async_computation | async-start | bytes 4718592 | tf_op jit(solution)/shard_map/all_to_all | solution.py:52
  74.5 48.8 %all-to-all-done.x_ref = bf16[8,3,3,128,128]{4,3,2,1,0:T(8,128)(2,1)} async-done(((bf16[8,3,3,128,128]{4,3,2,1,0:T(8,128)(2,1)}), bf16[8,3,3,128,128]{4,3,2,1,0:T(8,128)(2,1)}, u32[]{:S(2)}, u32[]{:S(2)}) %all-to-all-start) | async-done | bytes 2359328 | tf_op jit(solution)/shard_map/all_to_all | solution.py:52
  123.3 7.4 %attend.1 = (bf16[8,3,128,128]{3,2,1,0:T(8,128)(2,1)}, f32[3,1,1024]{2,1,0:T(1,128)}) custom-call(bf16[8,3,3,128,128]{4,3,2,1,0:T(8,128)(2,1)} %all-to-all-done.x_ref, f32[1024,128]{1,0:T(8,128)} %get-tuple-element.102.cos_ref, f32[1024,128]{1,0:T(8,128)} %get-tuple-element.103.sin_ref, s32[1024,1]{1,0:T(8,128)} %copy.85.kpos_ref, ...), custom_call_target="tpu_custom_call" | custom-call | flops 1610612736 | bytes 3145728 | tf_op jit(solution)/shard_map/attend/pallas_call | solution.py:193
  136.1 8.8 %row_prep.3 = (bf16[1408,2048]{1,0:T(8,128)(2,1)}, f32[24,2048]{1,0:T(8,128)}) custom-call(bf16[1408,2048]{1,0:T(8,128)(2,1)} %w_ref.6, bf16[1408,16]{1,0:T(8,128)(2,1)} %copy.89.a_ref, bf16[16,2048]{1,0:T(8,128)(2,1)} %b_ref.6), custom_call_target="tpu_custom_call" | custom-call | flops 1476395008 | bytes 11534336 | tf_op jit(solution)/shard_map/row_prep/pallas_call | solution.py:119
  145.8 4.6 row_prep.2
  171.2 23.9 %column_prep.3 = (bf16[1,2048,2816]{2,1,0:T(8,128)(2,1)}, f32[2,2,1408]{2,1,0:T(2,128)}, f32[2,16,1408]{2,1,0:T(8,128)}) custom-call(bf16[2,2048,1408]{2,1,0:T(8,128)(2,1)} %w_ref.7, bf16[2,2048,16]{2,1,0:T(8,128)(2,1)} %copy.90.a_ref, bf16[2,16,1408]{2,1,0:T(8,128)(2,1)} %b_ref.7, f32[2,1,1408]{2,1,0:T(1,128)} %broadcast_in_dim.59.m_ref), custom_call_target="tpu_custom_call" | custom-call | flops 2952790016 | bytes 23068672 | tf_op jit(solution)/shard_map/column_prep/pallas_call | solution.py:81
  208.8 15.9 %collective-permute-done.8 = bf16[6,32,2048]{2,1,0:T(8,128)(2,1)S(1)} collective-permute-done((bf16[6,32,2048]{2,1,0:T(8,128)(2,1)S(1)}, bf16[6,32,2048]{2,1,0:T(8,128)(2,1)S(1)}, u32[]{:S(2)}, u32[]{:S(2)}) %collective-permute-start.8) | collective-permute-done | bytes 786464 | tf_op jit(solution)/shard_map/ppermute | solution.py:31
  224.7 6.3 %convolution_convert_fusion.2.e_ref = bf16[768,1408]{1,0:T(8,128)(2,1)} fusion(bf16[768,2048]{1,0:T(8,128)(2,1)S(1)} %bitcast.278, bf16[1408,2048]{1,0:T(8,128)(2,1)S(1)} %bitcast.298), kind=kOutput, calls=%fused_computation.11 | convolution fusion | flops 4430266368 | bytes 11075584 | tf_op jit(solution)/shard_map/dot_general | solution.py:26
  233.1 18.3 %gated.1 = (bf16[768,1408]{1,0:T(8,128)(2,1)}, bf16[768,2816]{1,0:T(8,128)(2,1)}, f32[1,2816]{1,0:T(1,128)}) custom-call(bf16[768,2048]{1,0:T(8,128)(2,1)} %bitcast.275, bf16[1,2048,2816]{2,1,0:T(8,128)(2,1)} %get-tuple-element.36.w_ref, bf16[768,1408]{1,0:T(8,128)(2,1)} %convolution_convert_fusion.2.e_ref), custom_call_target="tpu_custom_call" | custom-call | flops 8858370048 | bytes 23330816 | tf_op jit(solution)/shard_map/gated/pallas_call | solution.py:335
  255.2 8.4 %fusion.14 = f32[32,2048]{1,0:T(8,128)} fusion(bf16[32,2816]{1,0:T(8,128)(2,1)S(1)} %convert_element_type.394, bf16[1,2048,2816]{2,1,0:T(8,128)(2,1)} %get-tuple-element.36.w_ref), kind=kOutput, calls=%fused_computation.36 | convolution fusion | flops 369164288 | bytes 11976704 | tf_op jit(solution)/shard_map/dot_general | solution.py:26
  263.9 13.3 %fusion.6 = bf16[768,2048]{1,0:T(8,128)(2,1)S(1)} fusion(bf16[768,2816]{1,0:T(8,128)(2,1)} %get-tuple-element.39, bf16[1,2048,2816]{2,1,0:T(8,128)(2,1)} %get-tuple-element.36.w_ref), kind=kOutput, calls=%fused_computation.9 | convolution fusion | flops 8859942912 | bytes 19005440 | tf_op jit(solution)/shard_map/dot_general | solution.py:26
  279.9 8.2 %convolution_convert_fusion.1 = bf16[768,2048]{1,0:T(8,128)(2,1)S(1)} fusion(bf16[768,1408]{1,0:T(8,128)(2,1)S(1)} %copy-done.15, bf16[1408,2048]{1,0:T(8,128)(2,1)} %get-tuple-element.37), kind=kOutput, calls=%fused_computation.10 | convolution fusion | flops 4430757888 | bytes 11075584 | tf_op jit(solution)/shard_map/dot_general | solution.py:26
  291.0 6.2 %fusion.9 = bf16[32,2816]{1,0:T(8,128)(2,1)} fusion(bf16[768,2816]{1,0:T(8,128)(2,1)} %get-tuple-element.39, bf16[768,2048]{1,0:T(8,128)(2,1)} %bitcast.276, bf16[2048,32]{0,1:T(8,128)(2,1)} %bitcast.329, f32[32,2816]{1,0:T(8,128)S(1)} %mul.614, f32[2816]{0:T(1024)S(1)} %mul.609, f32[2816]{0:T(1024)S(1)} %mul.587), kind=kOutput, calls=%fused_computation.12 | convolution fusion | flops 239550464 | bytes 8165376 | tf_op jit(solution)/shard_map/dot_general | solution.py:26
  300.5 5.7 fusion.17
  322.1 9.3 %collective-permute-done.17 = bf16[6,32,2048]{2,1,0:T(8,128)(2,1)S(1)} collective-permute-done((bf16[6,32,2048]{2,1,0:T(8,128)(2,1)}, bf16[6,32,2048]{2,1,0:T(8,128)(2,1)S(1)}, u32[]{:S(2)}, u32[]{:S(2)}) %collective-permute-start.17) | collective-permute-done | bytes 786464 | tf_op jit(solution)/shard_map/ppermute | solution.py:31
  333.2 14.1 %collective-permute-done.15 = bf16[6,32,2048]{2,1,0:T(8,128)(2,1)} collective-permute-done((bf16[6,32,2048]{2,1,0:T(8,128)(2,1)}, bf16[6,32,2048]{2,1,0:T(8,128)(2,1)}, u32[]{:S(2)}, u32[]{:S(2)}) %collective-permute-start.15) | collective-permute-done | bytes 786464 | tf_op jit(solution)/shard_map/ppermute | solution.py:31
  347.4 4.7 multiply_reduce_fusion.1
  357.0 17.2 %collective-permute-done.18 = bf16[6,32,2048]{2,1,0:T(8,128)(2,1)S(1)} collective-permute-done((bf16[6,32,2048]{2,1,0:T(8,128)(2,1)S(1)}, bf16[6,32,2048]{2,1,0:T(8,128)(2,1)S(1)}, u32[]{:S(2)}, u32[]{:S(2)}) %collective-permute-start.18) | collective-permute-done | bytes 786464 | tf_op jit(solution)/shard_map/ppermute | solution.py:31
  416.0 10.9 %attend_back.1 = (bf16[8,3,3,128,128]{4,3,2,1,0:T(8,128)(2,1)}, f32[3,3,128]{2,1,0:T(4,128)}) custom-call(bf16[8,3,3,128,128]{4,3,2,1,0:T(8,128)(2,1)} %all-to-all-done.x_ref, bf16[8,3,128,128]{3,2,1,0:T(8,128)(2,1)} %get-tuple-element.32.o_ref, bf16[8,3,128,128]{3,2,1,0:T(8,128)(2,1)} %bitcast.48.d_ref, f32[3,1,1024]{2,1,0:T(1,128)} %get-tuple-element.40.l_ref, ...), custom_call_target="tpu_custom_call" | custom-call | flops 4026531840 | bytes 6291456 | tf_op jit(solution)/shard_map/attend_back/pallas_call | solution.py:279
  433.1 8.9 %copy.94 = bf16[2048,3,512]{0,2,1:T(8,128)(2,1)} copy(bf16[2048,3,512]{2,0,1:T(8,128)(2,1)} %bitcast.285) | data formatting | bytes 12582912 | tf_op jit(solution)/shard_map/transpose | solution.py:515
  453.2 33.7 %all-to-all-done.3 = bf16[8,3,3,128,128]{4,3,2,1,0:T(8,128)(2,1)S(1)} async-done(((bf16[8,3,3,128,128]{4,3,2,1,0:T(8,128)(2,1)}), bf16[8,3,3,128,128]{4,3,2,1,0:T(8,128)(2,1)S(1)}, u32[]{:S(2)}, u32[]{:S(2)}) %all-to-all-start.3) | async-done | bytes 2359328 | tf_op jit(solution)/shard_map/all_to_all | solution.py:52
  499.0 6.1 %fusion.27 = f32[768,2048]{1,0:T(8,128)} fusion(bf16[3,2048,512]{2,1,0:T(8,128)(2,1)} %get-tuple-element.31, bf16[768,1536]{1,0:T(8,128)(2,1)S(1)} %reshape.615), kind=kOutput, calls=%fused_computation.50 | convolution fusion | flops 1610612736 | bytes 9175040 | tf_op jit(solution)/shard_map/dot_general | solution.py:26
  505.0 6.0 %fusion.31 = f32[768,2048]{1,0:T(8,128)} fusion(bf16[3,2048,512]{2,1,0:T(8,128)(2,1)} %get-tuple-element.31, bf16[768,1536]{1,0:T(8,128)(2,1)S(1)} %reshape.615), kind=kOutput, calls=%fused_computation.54 | convolution fusion | flops 1610612736 | bytes 9175040 | tf_op jit(solution)/shard_map/dot_general | solution.py:26
  511.0 4.3 fusion.12
  516.4 7.0 %add_convert_fusion = bf16[768,2048]{1,0:T(8,128)(2,1)S(1)} fusion(f32[768,2048]{1,0:T(8,128)} %fusion.31, f32[768,2048]{1,0:T(8,128)} %fusion.27, bf16[3,2048,512]{2,1,0:T(8,128)(2,1)} %get-tuple-element.31, bf16[768,1536]{1,0:T(8,128)(2,1)S(1)} %reshape.615), kind=kOutput, calls=%fused_computation.4 | convolution fusion | flops 1615331328 | bytes 18612224 | tf_op jit(solution)/shard_map/dot_general | solution.py:26
  525.5 4.5 fusion.13
  531.6 6.0 %all-to-all-start.4 = ((bf16[8,128,128]{2,1,0:T(8,128)(2,1)}), bf16[8,128,128]{2,1,0:T(8,128)(2,1)S(1)}, u32[]{:S(2)}, u32[]{:S(2)}) async-start(bf16[8,128,128]{2,1,0:T(8,128)(2,1)} %pad_maximum_fusion.8), calls=%async_computation.4 | async-start | bytes 524288 | tf_op jit(solution)/shard_map/all_to_all | solution.py:52
  537.7 9.5 %all-to-all-done.4 = bf16[8,128,128]{2,1,0:T(8,128)(2,1)S(1)} async-done(((bf16[8,128,128]{2,1,0:T(8,128)(2,1)}), bf16[8,128,128]{2,1,0:T(8,128)(2,1)S(1)}, u32[]{:S(2)}, u32[]{:S(2)}) %all-to-all-start.4) | async-done | bytes 262176 | tf_op jit(solution)/shard_map/all_to_all | solution.py:52
  571.6 8.1 %collective-permute-done.22 = bf16[6,32,2048]{2,1,0:T(8,128)(2,1)S(1)} collective-permute-done((bf16[6,32,2048]{2,1,0:T(8,128)(2,1)}, bf16[6,32,2048]{2,1,0:T(8,128)(2,1)S(1)}, u32[]{:S(2)}, u32[]{:S(2)}) %collective-permute-start.22) | collective-permute-done | bytes 786464 | tf_op jit(solution)/shard_map/ppermute | solution.py:31
  (399 shorter events, 217.0 us)
Async XLA Ops:
  4.9 20.7 %collective-permute-start = (bf16[6,32,2048]{2,1,0:T(8,128)(2,1)}, bf16[6,32,2048]{2,1,0:T(8,128)(2,1)S(1)}, u32[]{:S(2)}, u32[]{:S(2)}) collective-permute-start(bf16[6,32,2048]{2,1,0:T(8,128)(2,1)} %fusion.43), channel_id=1, source_target_pairs={{0,2},{1,3},{2,0},{3,1},{4,6},{5,7},{6,4},{7,5},{8,10},{9,11},{10,... | collective-permute-start | bytes 2359304 | tf_op jit(solution)/shard_map/ppermute | solution.py:31
  7.9 30.0 %collective-permute-start.1 = (bf16[6,32,2048]{2,1,0:T(8,128)(2,1)}, bf16[6,32,2048]{2,1,0:T(8,128)(2,1)S(1)}, u32[]{:S(2)}, u32[]{:S(2)}) collective-permute-start(bf16[6,32,2048]{2,1,0:T(8,128)(2,1)} %fusion.43), channel_id=1, source_target_pairs={{0,1},{1,0},{2,3},{3,2},{4,5},{5,4},{6,7},{7,6},{8,9},{9,8},{10,11... | collective-permute-start | bytes 2359304 | tf_op jit(solution)/shard_map/ppermute | solution.py:31
  25.6 12.2 %collective-permute-start.2 = (bf16[6,32,2048]{2,1,0:T(8,128)(2,1)S(1)}, bf16[6,32,2048]{2,1,0:T(8,128)(2,1)}, u32[]{:S(2)}, u32[]{:S(2)}) collective-permute-start(bf16[6,32,2048]{2,1,0:T(8,128)(2,1)S(1)} %collective-permute-done), channel_id=1, source_target_pairs={{0,1},{1,0},{2,3},{3,2},{4,5},{5,4},{6,7},{7,6},{8,9},{9,8},{10,11... | collective-permute-start | bytes 2359304 | tf_op jit(solution)/shard_map/ppermute | solution.py:31
  62.3 61.0 %all-to-all-start = ((bf16[8,3,3,128,128]{4,3,2,1,0:T(8,128)(2,1)}), bf16[8,3,3,128,128]{4,3,2,1,0:T(8,128)(2,1)}, u32[]{:S(2)}, u32[]{:S(2)}) async-start(bf16[8,3,3,128,128]{4,3,2,1,0:T(8,128)(2,1)} %bitcast.287), calls=%async_computation | async-start | bytes 4718592 | tf_op jit(solution)/shard_map/all_to_all | solution.py:52
  130.7 24.0 %all-to-all-start.1 = ((bf16[8,3,1,128,128]{4,3,1,2,0:T(8,128)(2,1)}), bf16[8,3,1,128,128]{4,3,1,2,0:T(8,128)(2,1)S(1)}, u32[]{:S(2)}, u32[]{:S(2)}) async-start(bf16[8,3,1,128,128]{4,3,1,2,0:T(8,128)(2,1)} %bitcast.323), calls=%async_computation.1 | async-start | bytes 1572864 | tf_op jit(solution)/shard_map/all_to_all | solution.py:52
  151.3 12.7 %collective-permute-start.5 = (f32[2,2048]{1,0:T(2,128)S(1)}, f32[2,2048]{1,0:T(2,128)S(1)}, u32[]{:S(2)}, u32[]{:S(2)}) collective-permute-start(f32[2,2048]{1,0:T(2,128)S(1)} %pad_maximum_fusion.14), channel_id=1, source_target_pairs={{0,1},{1,0},{2,3},{3,2},{4,5},{5,4},{6,7},{7,6},{8,9},{9,8},{10,11... | collective-permute-start | bytes 49160 | tf_op jit(solution)/shard_map/ppermute | solution.py:31
  151.3 12.7 %collective-permute-start.6 = (f32[2,2048]{1,0:T(2,128)S(1)}, f32[2,2048]{1,0:T(2,128)S(1)}, u32[]{:S(2)}, u32[]{:S(2)}) collective-permute-start(f32[2,2048]{1,0:T(2,128)S(1)} %pad_maximum_fusion.14), channel_id=1, source_target_pairs={{0,2},{1,3},{2,0},{3,1},{4,6},{5,7},{6,4},{7,5},{8,10},{9,11},{10,... | collective-permute-start | bytes 49160 | tf_op jit(solution)/shard_map/ppermute | solution.py:31
  152.9 11.1 %collective-permute-start.7 = (f32[2,2048]{1,0:T(2,128)S(1)}, f32[2,2048]{1,0:T(2,128)S(1)}, u32[]{:S(2)}, u32[]{:S(2)}) collective-permute-start(f32[2,2048]{1,0:T(2,128)S(1)} %pad_maximum_fusion.14), channel_id=1, source_target_pairs={{0,3},{1,2},{2,1},{3,0},{4,7},{5,6},{6,5},{7,4},{8,11},{9,10},{10,... | collective-permute-start | bytes 49160 | tf_op jit(solution)/shard_map/ppermute | solution.py:31
  161.2 5.5 collective-permute-start.3
  165.3 33.1 %collective-permute-start.11 = (bf16[6,32,2048]{2,1,0:T(8,128)(2,1)}, bf16[6,32,2048]{2,1,0:T(8,128)(2,1)}, u32[]{:S(2)}, u32[]{:S(2)}) collective-permute-start(bf16[6,32,2048]{2,1,0:T(8,128)(2,1)} %multiply_convert_fusion.1), channel_id=1, source_target_pairs={{0,2},{1,3},{2,0},{3,1},{4,6},{5,7},{6,4},{7,5},{8,10},{9,11},{10,... | collective-permute-start | bytes 2359304 | tf_op jit(solution)/shard_map/ppermute | solution.py:31
  170.6 31.8 %collective-permute-start.4 = (bf16[6,32,2048]{2,1,0:T(8,128)(2,1)S(1)}, bf16[6,32,2048]{2,1,0:T(8,128)(2,1)}, u32[]{:S(2)}, u32[]{:S(2)}) collective-permute-start(bf16[6,32,2048]{2,1,0:T(8,128)(2,1)S(1)} %fusion.69), channel_id=1, source_target_pairs={{0,2},{1,3},{2,0},{3,1},{4,6},{5,7},{6,4},{7,5},{8,10},{9,11},{10,... | collective-permute-start | bytes 2359304 | tf_op jit(solution)/shard_map/ppermute | solution.py:31
  198.3 8.9 %collective-permute-start.12 = (bf16[6,32,2048]{2,1,0:T(8,128)(2,1)}, bf16[6,32,2048]{2,1,0:T(8,128)(2,1)S(1)}, u32[]{:S(2)}, u32[]{:S(2)}) collective-permute-start(bf16[6,32,2048]{2,1,0:T(8,128)(2,1)} %multiply_convert_fusion.1), channel_id=1, source_target_pairs={{0,1},{1,0},{2,3},{3,2},{4,5},{5,4},{6,7},{7,6},{8,9},{9,8},{10,11... | collective-permute-start | bytes 2359304 | tf_op jit(solution)/shard_map/ppermute | solution.py:31
  198.4 8.9 %collective-permute-start.13 = (bf16[6,32,2048]{2,1,0:T(8,128)(2,1)}, bf16[6,32,2048]{2,1,0:T(8,128)(2,1)S(1)}, u32[]{:S(2)}, u32[]{:S(2)}) collective-permute-start(bf16[6,32,2048]{2,1,0:T(8,128)(2,1)} %collective-permute-done.11), channel_id=1, source_target_pairs={{0,1},{1,0},{2,3},{3,2},{4,5},{5,4},{6,7},{7,6},{8,9},{9,8},{10,11... | collective-permute-start | bytes 2359304 | tf_op jit(solution)/shard_map/ppermute | solution.py:31
  205.4 19.2 %collective-permute-start.8 = (bf16[6,32,2048]{2,1,0:T(8,128)(2,1)S(1)}, bf16[6,32,2048]{2,1,0:T(8,128)(2,1)S(1)}, u32[]{:S(2)}, u32[]{:S(2)}) collective-permute-start(bf16[6,32,2048]{2,1,0:T(8,128)(2,1)S(1)} %multiply_convert_fusion.2), channel_id=1, source_target_pairs={{0,2},{1,3},{2,0},{3,1},{4,6},{5,7},{6,4},{7,5},{8,10},{9,11},{10,... | collective-permute-start | bytes 2359304 | tf_op jit(solution)/shard_map/ppermute | solution.py:31
  208.7 22.5 %collective-permute-start.9 = (bf16[6,32,2048]{2,1,0:T(8,128)(2,1)S(1)}, bf16[6,32,2048]{2,1,0:T(8,128)(2,1)S(1)}, u32[]{:S(2)}, u32[]{:S(2)}) collective-permute-start(bf16[6,32,2048]{2,1,0:T(8,128)(2,1)S(1)} %multiply_convert_fusion.2), channel_id=1, source_target_pairs={{0,1},{1,0},{2,3},{3,2},{4,5},{5,4},{6,7},{7,6},{8,9},{9,8},{10,11... | collective-permute-start | bytes 2359304 | tf_op jit(solution)/shard_map/ppermute | solution.py:31
  224.7 6.5 %collective-permute-start.10 = (bf16[6,32,2048]{2,1,0:T(8,128)(2,1)S(1)}, bf16[6,32,2048]{2,1,0:T(8,128)(2,1)S(1)}, u32[]{:S(2)}, u32[]{:S(2)}) collective-permute-start(bf16[6,32,2048]{2,1,0:T(8,128)(2,1)S(1)} %collective-permute-done.8), channel_id=1, source_target_pairs={{0,1},{1,0},{2,3},{3,2},{4,5},{5,4},{6,7},{7,6},{8,9},{9,8},{10,11... | collective-permute-start | bytes 2359304 | tf_op jit(solution)/shard_map/ppermute | solution.py:31
  279.1 28.1 %collective-permute-start.16 = (bf16[2,6,32,2048]{3,2,1,0:T(8,128)(2,1)}, bf16[2,6,32,2048]{3,2,1,0:T(8,128)(2,1)}, u32[]{:S(2)}, u32[]{:S(2)}) collective-permute-start(bf16[2,6,32,2048]{3,2,1,0:T(8,128)(2,1)} %bitcast.38), channel_id=1, source_target_pairs={{0,1},{1,0},{2,3},{3,2},{4,5},{5,4},{6,7},{7,6},{8,9},{9,8},{10,11... | collective-permute-start | bytes 4718600 | tf_op jit(solution)/shard_map/ppermute | solution.py:31
  290.2 22.0 %collective-permute-start.14 = (bf16[2,6,32,2048]{3,2,1,0:T(8,128)(2,1)}, bf16[2,6,32,2048]{3,2,1,0:T(8,128)(2,1)}, u32[]{:S(2)}, u32[]{:S(2)}) collective-permute-start(bf16[2,6,32,2048]{3,2,1,0:T(8,128)(2,1)} %bitcast.33), channel_id=1, source_target_pairs={{0,1},{1,0},{2,3},{3,2},{4,5},{5,4},{6,7},{7,6},{8,9},{9,8},{10,11... | collective-permute-start | bytes 4718600 | tf_op jit(solution)/shard_map/ppermute | solution.py:31
  310.7 20.6 %collective-permute-start.17 = (bf16[6,32,2048]{2,1,0:T(8,128)(2,1)}, bf16[6,32,2048]{2,1,0:T(8,128)(2,1)S(1)}, u32[]{:S(2)}, u32[]{:S(2)}) collective-permute-start(bf16[6,32,2048]{2,1,0:T(8,128)(2,1)} %fusion.71), channel_id=1, source_target_pairs={{0,2},{1,3},{2,0},{3,1},{4,6},{5,7},{6,4},{7,5},{8,10},{9,11},{10,... | collective-permute-start | bytes 2359304 | tf_op jit(solution)/shard_map/ppermute | solution.py:31
  316.2 31.1 %collective-permute-start.15 = (bf16[6,32,2048]{2,1,0:T(8,128)(2,1)}, bf16[6,32,2048]{2,1,0:T(8,128)(2,1)}, u32[]{:S(2)}, u32[]{:S(2)}) collective-permute-start(bf16[6,32,2048]{2,1,0:T(8,128)(2,1)} %fusion.70), channel_id=1, source_target_pairs={{0,2},{1,3},{2,0},{3,1},{4,6},{5,7},{6,4},{7,5},{8,10},{9,11},{10,... | collective-permute-start | bytes 2359304 | tf_op jit(solution)/shard_map/ppermute | solution.py:31
  354.2 19.9 %collective-permute-start.18 = (bf16[6,32,2048]{2,1,0:T(8,128)(2,1)S(1)}, bf16[6,32,2048]{2,1,0:T(8,128)(2,1)S(1)}, u32[]{:S(2)}, u32[]{:S(2)}) collective-permute-start(bf16[6,32,2048]{2,1,0:T(8,128)(2,1)S(1)} %multiply_convert_fusion), channel_id=1, source_target_pairs={{0,2},{1,3},{2,0},{3,1},{4,6},{5,7},{6,4},{7,5},{8,10},{9,11},{10,... | collective-permute-start | bytes 2359304 | tf_op jit(solution)/shard_map/ppermute | solution.py:31
  355.9 20.5 %collective-permute-start.19 = (bf16[6,32,2048]{2,1,0:T(8,128)(2,1)S(1)}, bf16[6,32,2048]{2,1,0:T(8,128)(2,1)S(1)}, u32[]{:S(2)}, u32[]{:S(2)}) collective-permute-start(bf16[6,32,2048]{2,1,0:T(8,128)(2,1)S(1)} %multiply_convert_fusion), channel_id=1, source_target_pairs={{0,1},{1,0},{2,3},{3,2},{4,5},{5,4},{6,7},{7,6},{8,9},{9,8},{10,11... | collective-permute-start | bytes 2359304 | tf_op jit(solution)/shard_map/ppermute | solution.py:31
  386.4 25.3 %all-to-all-start.2 = ((bf16[8,3,1,128,128]{4,3,1,2,0:T(8,128)(2,1)}), bf16[8,3,1,128,128]{4,3,1,2,0:T(8,128)(2,1)}, u32[]{:S(2)}, u32[]{:S(2)}) async-start(bf16[8,3,1,128,128]{4,3,1,2,0:T(8,128)(2,1)} %bitcast.301), calls=%async_computation.2 | async-start | bytes 1572864 | tf_op jit(solution)/shard_map/all_to_all | solution.py:52
  411.7 17.4 %all-to-all-start.6 = ((bf16[8,216,128]{2,1,0:T(8,128)(2,1)}), bf16[8,216,128]{2,1,0:T(8,128)(2,1)S(1)}, u32[]{:S(2)}, u32[]{:S(2)}) async-start(bf16[8,216,128]{2,1,0:T(8,128)(2,1)} %pad_maximum_fusion.7), calls=%async_computation.6 | async-start | bytes 884736 | tf_op jit(solution)/shard_map/all_to_all | solution.py:52
  429.1 57.8 %all-to-all-start.3 = ((bf16[8,3,3,128,128]{4,3,2,1,0:T(8,128)(2,1)}), bf16[8,3,3,128,128]{4,3,2,1,0:T(8,128)(2,1)S(1)}, u32[]{:S(2)}, u32[]{:S(2)}) async-start(bf16[8,3,3,128,128]{4,3,2,1,0:T(8,128)(2,1)} %get-tuple-element.41), calls=%async_computation.3 | async-start | bytes 4718592 | tf_op jit(solution)/shard_map/all_to_all | solution.py:52
  442.3 4.6 collective-permute-start.30
  487.8 43.9 %all-to-all-start.7 = ((bf16[8,216,128]{2,1,0:T(8,128)(2,1)}), bf16[8,216,128]{2,1,0:T(8,128)(2,1)S(1)}, u32[]{:S(2)}, u32[]{:S(2)}) async-start(bf16[8,216,128]{2,1,0:T(8,128)(2,1)} %broadcast_in_dim.64), calls=%async_computation.7 | async-start | bytes 884736 | tf_op jit(solution)/shard_map/all_to_all | solution.py:52
  525.5 31.4 %collective-permute-start.21 = (bf16[2,6,32,2048]{3,2,1,0:T(8,128)(2,1)}, bf16[2,6,32,2048]{3,2,1,0:T(8,128)(2,1)}, u32[]{:S(2)}, u32[]{:S(2)}) collective-permute-start(bf16[2,6,32,2048]{3,2,1,0:T(8,128)(2,1)} %bitcast.52), channel_id=1, source_target_pairs={{0,1},{1,0},{2,3},{3,2},{4,5},{5,4},{6,7},{7,6},{8,9},{9,8},{10,11... | collective-permute-start | bytes 4718600 | tf_op jit(solution)/shard_map/ppermute | solution.py:31
  531.6 15.6 %all-to-all-start.4 = ((bf16[8,128,128]{2,1,0:T(8,128)(2,1)}), bf16[8,128,128]{2,1,0:T(8,128)(2,1)S(1)}, u32[]{:S(2)}, u32[]{:S(2)}) async-start(bf16[8,128,128]{2,1,0:T(8,128)(2,1)} %pad_maximum_fusion.8), calls=%async_computation.4 | async-start | bytes 524288 | tf_op jit(solution)/shard_map/all_to_all | solution.py:52
  547.4 4.2 collective-permute-start.24
  553.3 14.5 %all-to-all-start.5 = ((bf16[8,128,128]{2,1,0:T(8,128)(2,1)}), bf16[8,128,128]{2,1,0:T(8,128)(2,1)S(1)}, u32[]{:S(2)}, u32[]{:S(2)}) async-start(bf16[8,128,128]{2,1,0:T(8,128)(2,1)} %broadcast_in_dim.63), calls=%async_computation.5 | async-start | bytes 524288 | tf_op jit(solution)/shard_map/all_to_all | solution.py:52
  560.0 19.7 %collective-permute-start.22 = (bf16[6,32,2048]{2,1,0:T(8,128)(2,1)}, bf16[6,32,2048]{2,1,0:T(8,128)(2,1)S(1)}, u32[]{:S(2)}, u32[]{:S(2)}) collective-permute-start(bf16[6,32,2048]{2,1,0:T(8,128)(2,1)} %fusion.72), channel_id=1, source_target_pairs={{0,2},{1,3},{2,0},{3,1},{4,6},{5,7},{6,4},{7,5},{8,10},{9,11},{10,... | collective-permute-start | bytes 2359304 | tf_op jit(solution)/shard_map/ppermute | solution.py:31
  (78 other events, 912.0 us)

commit v2 on v1

v2 whole, which is shorter than its diff:
```python
from functools import partial
import math

import jax
import jax.numpy as jnp
from jax import lax
from jax.experimental import pallas as pl
from jax.experimental.pallas import tpu as pltpu
from jax.sharding import PartitionSpec as P

HEAD_DIM = 128
LANES = 128
epsilon = 1e-05
adapter_scale = 2.0
rope_base = 10000.0
f32 = jnp.float32
bf16 = jnp.bfloat16
PIECES = (0, 2, 1, 3)
score_block = 256
GATED_BLOCKS = 2
NT = (((1,), (1,)), ((), ()))
NN = (((1,), (0,)), ((), ()))
TN = (((0,), (0,)), ((), ()))


def cost(flops, bytes_accessed, transcendentals):
    return pl.CostEstimate(flops=flops // 64, bytes_accessed=bytes_accessed // 64, transcendentals=0)


def mm(a, b, dims=NN):
    return lax.dot_general(a, b, dims, preferred_element_type=f32)


def swap(values, bit):
    size = lax.axis_size("tensor")
    return lax.ppermute(values, "tensor", [(i, i ^ bit) for i in range(size)])


def gather_start(shard):
    return shard, swap(shard, 2), swap(shard, 1)


def gather_end(shard, far, near):
    return [shard, far, near, swap(far, 1)]


def scatter_start(kept, near, send):
    got = swap(send, 1)
    return kept, got, (near.astype(f32) + got[1].astype(f32)).astype(bf16)


def scatter_end(kept, got, passed):
    return kept.astype(f32) + got[0].astype(f32) + swap(passed, 2).astype(f32)


def after(value, *others):
    return lax.optimization_barrier((value, *others))


def tensor_sum(values):
    return values + swap(values, 1) + swap(values, 2) + swap(values, 3)


def exchange(values):
    return lax.all_to_all(values, "seq", 0, 0, tiled=True)


def seq_gather(values):
    size = lax.axis_size("seq")
    return exchange(jnp.broadcast_to(values[None], (size,) + values.shape))


def column_prep_kernel(w_ref, a_ref, b_ref, m_ref, out_ref, stat_ref, cross_ref):
    members, width, block = w_ref.shape
    rank = cross_ref.shape[1]
    product = mm(a_ref[...], b_ref[0], TN)
    i = pl.program_id(0)
    for j in range(members):
        heading = w_ref[j].astype(f32) + adapter_scale * product[:, j * block:(j + 1) * block]
        norm = jnp.sqrt(jnp.sum(heading * heading, axis=0, keepdims=True))
        scale = m_ref[j] / norm
        scaled = (heading * scale).astype(bf16)
        if out_ref.shape[1] == members * block:
            out_ref[:, j * block:(j + 1) * block] = scaled
        else:
            out_ref[:, pl.ds(pl.multiple_of(j * (out_ref.shape[1] // members) + i * block, block), block)] = scaled
        stat_ref[j] = jnp.concatenate([norm, scale], axis=0)
        cross_ref[j] = mm(a_ref[j * rank:(j + 1) * rank, :], scaled)


def column_prep(weight, down, up, magnitude, block, alternate):
    members, width, out = weight.shape
    rank = down.shape[2]
    wide = members * block
    eye = jnp.eye(members, dtype=bf16)[:, None, None, :, None]
    blocks = up.reshape(members, rank, out // block, 1, block) * eye
    blocks = blocks.transpose(2, 0, 1, 3, 4).reshape(out // block, members * rank, wide)
    flat = down.transpose(0, 2, 1).reshape(members * rank, width)
    if alternate:
        scaled_spec = pl.BlockSpec((width, wide), lambda i: (0, i))
    else:
        scaled_spec = pl.BlockSpec((width, members * out), lambda i: (0, 0))
    return pl.pallas_call(
        column_prep_kernel,
        grid=(out // block,),
        in_specs=[
            pl.BlockSpec((members, width, block), lambda i: (0, 0, i)),
            pl.BlockSpec((members * rank, width), lambda i: (0, 0)),
            pl.BlockSpec((1, members * rank, wide), lambda i: (i, 0, 0)),
            pl.BlockSpec((members, 1, block), lambda i: (0, 0, i)),
        ],
        out_specs=[
            scaled_spec,
            pl.BlockSpec((members, 2, block), lambda i: (0, 0, i)),
            pl.BlockSpec((members, rank, block), lambda i: (0, 0, i)),
        ],
        out_shape=[
            jax.ShapeDtypeStruct((width, members * out), bf16),
            jax.ShapeDtypeStruct((members, 2, out), f32),
            jax.ShapeDtypeStruct((members, rank, out), f32),
        ],
        cost_estimate=cost(
            flops=4 * members * width * out * 256, bytes_accessed=4 * members * width * out, transcendentals=0
        ),
        name="column_prep",
    )(weight, flat, blocks, magnitude[:, None, :])


def row_prep_kernel(w_ref, a_ref, b_ref, out_ref, cross_ref, square_ref):
    heading = w_ref[...].astype(f32) + adapter_scale * mm(a_ref[...], b_ref[...], TN)
    narrow = heading.astype(bf16)
    out_ref[...] = narrow
    cross_ref[...] = mm(a_ref[...], narrow)
    square_ref[...] = jnp.sum(heading * heading, axis=0, keepdims=True)


def row_prep(weight, down, up, block):
    rows, out = weight.shape
    rank = down.shape[1]
    along = lambda n: pl.BlockSpec((n, block), lambda i: (0, i))
    return pl.pallas_call(
        row_prep_kernel,
        grid=(out // block,),
        in_specs=[along(rows), pl.BlockSpec((rank, rows), lambda i: (0, 0)), along(rank)],
        out_specs=[along(rows), along(rank), along(1)],
        out_shape=[
            jax.ShapeDtypeStruct((rows, out), bf16),
            jax.ShapeDtypeStruct((rank, out), f32),
            jax.ShapeDtypeStruct((1, out), f32),
        ],
        cost_estimate=cost(flops=2 * rows * out * 256, bytes_accessed=4 * rows * out, transcendentals=0),
        name="row_prep",
    )(weight, down.T, up)


def turn_forward(values, cosine, signed_sine):
    return values * cosine + pltpu.roll(values, values.shape[1] // 2, 1) * signed_sine


def turn_backward(values, cosine, signed_sine):
    return values * cosine + pltpu.roll(values * signed_sine, values.shape[1] // 2, 1)


def over_blocks(total, block, body):
    if total // block <= 4:
        for i in range(total // block):
            body(i * block, (i + 1) * block)
    else:

        def step(i, carry):
            body(pl.multiple_of(i * block, block), total)
            return carry

        lax.fori_loop(0, total // block, step, 0)


def weights_t(keys, queries, kpos, qpos, qstart, scale):
    scores = mm(keys, queries, NT)
    allowed = jnp.logical_and(kpos <= qpos, kpos >= qstart)
    return jnp.where(allowed, jnp.exp(scores * scale), 0.0)


def attend_kernel(x_ref, cos_ref, sin_ref, kpos_ref, qinfo_ref, o_ref, l_ref, qs, ks, vt, os, *, scale, block):
    blocks, _, _, group, size = x_ref.shape
    total = blocks * group
    cosine, signed_sine = cos_ref[...], sin_ref[...]
    qs[...] = turn_forward(x_ref[:, 0, 0].reshape(total, size).astype(f32), cosine, signed_sine).astype(bf16)
    ks[...] = turn_forward(x_ref[:, 0, 1].reshape(total, size).astype(f32), cosine, signed_sine).astype(bf16)
    vt[...] = x_ref[:, 0, 2].reshape(total, size).astype(f32).T.astype(bf16)

    def body(first, last):
        at = pl.ds(first, block)
        weights = weights_t(
            ks[:last], qs[at, :], kpos_ref[:last], qinfo_ref[0, 0:1, at], qinfo_ref[0, 1:2, at], scale
        )
        totals = jnp.sum(weights, axis=0, keepdims=True)
        outer = mm(vt[:, :last], weights.astype(bf16))
        l_ref[0, 0:1, at] = totals
        os[at, :] = (outer / totals).T.astype(bf16)

    over_blocks(total, block, body)
    o_ref[:, 0] = os[...].reshape(blocks, group, size)


def attend(pairs, tables, kpos, qinfo):
    blocks, slots, _, group, size = pairs.shape
    total = blocks * group
    block = math.gcd(total, score_block)
    return pl.pallas_call(
        partial(attend_kernel, scale=1.0 / math.sqrt(size), block=block),
        grid=(slots,),
        in_specs=[
            pl.BlockSpec((blocks, 1, 3, group, size), lambda n: (0, n, 0, 0, 0)),
            pl.BlockSpec((total, size), lambda n: (0, 0)),
            pl.BlockSpec((total, size), lambda n: (0, 0)),
            pl.BlockSpec((total, 1), lambda n: (0, 0)),
            pl.BlockSpec((1, 2, total), lambda n: (n, 0, 0)),
        ],
        out_specs=[
            pl.BlockSpec((blocks, 1, group, size), lambda n: (0, n, 0, 0)),
            pl.BlockSpec((1, 1, total), lambda n: (n, 0, 0)),
        ],
        out_shape=[
            jax.ShapeDtypeStruct((blocks, slots, group, size), bf16),
            jax.ShapeDtypeStruct((slots, 1, total), f32),
        ],
        scratch_shapes=[
            pltpu.VMEM((total, size), bf16),
            pltpu.VMEM((total, size), bf16),
            pltpu.VMEM((size, total), bf16),
            pltpu.VMEM((total, size), bf16),
        ],
        cost_estimate=cost(
            flops=slots * 4 * total * total * size,
            bytes_accessed=slots * total * size * 8,
            transcendentals=slots * total * total // 2,
        ),
        name="attend",
    )(pairs, *tables, kpos, qinfo)


def attend_back_kernel(
    x_ref, o_ref, d_ref, l_ref, cos_ref, sin_ref, kpos_ref, qinfo_ref, g_ref, s_ref,
    qs, ks, kt, vs, dk, dv, dq, *, scale, block
):
    blocks, _, _, group, size = x_ref.shape
    total = blocks * group
    cosine, signed_sine = cos_ref[...], sin_ref[...]
    plain = [x_ref[:, 0, j].reshape(total, size).astype(f32) for j in range(3)]
    qs[...] = turn_forward(plain[0], cosine, signed_sine).astype(bf16)
    turned = turn_forward(plain[1], cosine, signed_sine)
    ks[...] = turned.astype(bf16)
    kt[...] = turned.T.astype(bf16)
    vs[...] = plain[2].astype(bf16)
    dk[...] = jnp.zeros_like(dk)
    dv[...] = jnp.zeros_like(dv)

    def body(first, last):
        at = pl.ds(first, block)
        span = block // group
        rows = pl.ds(first // group, span)
        weights = weights_t(
            ks[:last], qs[at, :], kpos_ref[:last], qinfo_ref[0, 0:1, at], qinfo_ref[0, 1:2, at], scale
        )
        totals = l_ref[0, 0:1, at]
        grad_t = d_ref[rows, 0].reshape(block, size).astype(f32).T
        out_t = o_ref[rows, 0].reshape(block, size).astype(f32).T
        dlog = -jnp.sum(grad_t * out_t, axis=0, keepdims=True) / totals
        outer_t = (grad_t / totals).astype(bf16)
        dweights = mm(vs[:last], outer_t)
        dscores = (weights * (dweights + dlog)).astype(bf16)
        dk[:last] += mm(dscores, qs[at, :])
        dv[:last] += mm(weights.astype(bf16), outer_t, NT)
        dq[at, :] = mm(kt[:, :last], dscores).T

    over_blocks(total, block, body)
    grads = (
        turn_backward(dq[...] * scale, cosine, signed_sine),
        turn_backward(dk[...] * scale, cosine, signed_sine),
        dv[...],
    )
    sums = []
    for j in range(3):
        g_ref[:, 0, j] = grads[j].astype(bf16).reshape(blocks, group, size)
        sums.append(jnp.sum(grads[j] * plain[j], axis=0, keepdims=True))
    s_ref[0] = jnp.concatenate(sums, axis=0)


def attend_back(pairs, outputs, grads, totals, tables, kpos, qinfo):
    blocks, slots, _, group, size = pairs.shape
    total = blocks * group
    block = math.gcd(total, score_block)
    half = pl.BlockSpec((blocks, 1, group, size), lambda n: (0, n, 0, 0))
    whole = pl.BlockSpec((blocks, 1, 3, group, size), lambda n: (0, n, 0, 0, 0))
    return pl.pallas_call(
        partial(attend_back_kernel, scale=1.0 / math.sqrt(size), block=block),
        grid=(slots,),
        in_specs=[
            whole,
            half,
            half,
            pl.BlockSpec((1, 1, total), lambda n: (n, 0, 0)),
            pl.BlockSpec((total, size), lambda n: (0, 0)),
            pl.BlockSpec((total, size), lambda n: (0, 0)),
            pl.BlockSpec((total, 1), lambda n: (0, 0)),
            pl.BlockSpec((1, 2, total), lambda n: (n, 0, 0)),
        ],
        out_specs=[whole, pl.BlockSpec((1, 3, size), lambda n: (n, 0, 0))],
        out_shape=[
            jax.ShapeDtypeStruct(pairs.shape, bf16),
            jax.ShapeDtypeStruct((slots, 3, size), f32),
        ],
        scratch_shapes=[
            pltpu.VMEM((total, size), bf16),
            pltpu.VMEM((total, size), bf16),
            pltpu.VMEM((size, total), bf16),
            pltpu.VMEM((total, size), bf16),
            pltpu.VMEM((total, size), f32),
            pltpu.VMEM((total, size), f32),
            pltpu.VMEM((total, size), f32),
        ],
        cost_estimate=cost(
            flops=slots * 10 * total * total * size,
            bytes_accessed=slots * total * size * 16,
            transcendentals=slots * total * total // 2,
        ),
        name="attend_back",
    )(pairs, outputs, grads, totals, *tables, kpos, qinfo)


def to_pairs_kernel(*refs, dims):
    x_refs, w_ref, out_ref, xs = refs[:4], refs[4], refs[5], refs[6]
    count = x_refs[0].shape[0]

    @pl.when(jnp.logical_and(pl.program_id(0) == 0, pl.program_id(1) == 0))
    def _():
        for i in range(4):
            xs[i * count:(i + 1) * count] = x_refs[i][...]

    rows, heads, _, pieces, quarter, size = out_ref.shape
    product = mm(xs[...], w_ref[...], dims).astype(bf16)
    for i in range(pieces):
        for r in range(rows):
            at = (i * rows + r) * quarter
            for h in range(heads):
                out_ref[r, h, 0, i] = product[at:at + quarter, h * size:(h + 1) * size]


def project_to_pairs(pieces, weight, dims, parts, heads, size, span):
    rows, quarter, width = pieces[0].shape
    count = rows * quarter
    wide = span * size
    steps = heads // span
    if dims == NN:
        w_spec = pl.BlockSpec((width, wide), lambda j, h: (0, j * steps + h))
    else:
        w_spec = pl.BlockSpec((wide, width), lambda j, h: (j * steps + h, 0))
    return pl.pallas_call(
        partial(to_pairs_kernel, dims=dims),
        grid=(parts, steps),
        in_specs=[pl.BlockSpec(memory_space=pltpu.VMEM)] * 4 + [w_spec],
        out_specs=[
            pl.BlockSpec((rows, span, 1, 4, quarter, size), lambda j, h: (0, h, j, 0, 0, 0)),
            pl.BlockSpec((4 * count, width), lambda j, h: (0, 0)),
        ],
        out_shape=[
            jax.ShapeDtypeStruct((rows, heads, parts, 4, quarter, size), bf16),
            jax.ShapeDtypeStruct((4 * count, width), bf16),
        ],
        cost_estimate=cost(
            flops=8 * count * width * parts * heads * size,
            bytes_accessed=2 * width * (8 * count + parts * heads * size),
            transcendentals=0,
        ),
        name="project_to_pairs",
    )(*[p.reshape(count, width) for p in pieces], weight)


def split_out(product, out_refs, at):
    kept_ref, near_ref, send_ref = out_refs
    half = product.shape[0] // 4
    kept_ref[at:at + half] = product[:half]
    near_ref[at:at + half] = product[half:2 * half]
    for i in range(2):
        send_ref[i, at:at + half] = product[(i + 2) * half:(i + 3) * half]


def split_specs(count, out, block):
    one, two = pl.BlockSpec((count, block), lambda n: (0, n)), pl.BlockSpec((2, count, block), lambda n: (0, 0, n))
    shapes = [(count, out), (count, out), (2, count, out)]
    return [one, one, two], [jax.ShapeDtypeStruct(v, bf16) for v in shapes]


def by_rows(kept, near, send, quarter):
    shape = (kept.shape[0] // quarter, quarter, kept.shape[1])
    return kept.reshape(shape), near.reshape(shape), send.reshape((2,) + shape)


def join_pairs(x_ref, flat_ref):
    rows, heads, parts, pieces, quarter, size = x_ref.shape
    for i in range(pieces):
        for r in range(rows):
            at = (i * rows + r) * quarter
            for j in range(parts):
                for h in range(heads):
                    col = (j * heads + h) * size
                    flat_ref[at:at + quarter, col:col + size] = x_ref[r, h, j, i]


def from_pairs_kernel(x_ref, w_ref, flat_ref, *out_refs):
    @pl.when(pl.program_id(0) == 0)
    def _():
        join_pairs(x_ref, flat_ref)

    split_out(mm(flat_ref[...], w_ref[...]).astype(bf16), out_refs, 0)


def project_from_pairs(pairs, weight, block):
    rows, heads, parts, pieces, quarter, size = pairs.shape
    count, width = rows * quarter, parts * heads * size
    out = weight.shape[1]
    specs, shapes = split_specs(count, out, block)
    flat, *split = pl.pallas_call(
        from_pairs_kernel,
        grid=(out // block,),
        in_specs=[pl.BlockSpec(pairs.shape, lambda n: (0,) * 6), pl.BlockSpec((width, block), lambda n: (0, n))],
        out_specs=[pl.BlockSpec((4 * count, width), lambda n: (0, 0))] + specs,
        out_shape=[jax.ShapeDtypeStruct((4 * count, width), bf16)] + shapes,
        cost_estimate=cost(
            flops=8 * count * width * out, bytes_accessed=2 * (out * width + 4 * count * (2 * width + out)),
            transcendentals=0,
        ),
        name="project_from_pairs",
    )(pairs, weight)
    return flat, by_rows(*split, quarter)


def project_split_kernel(*refs, dims):
    x_refs, w_ref, out_refs = refs[:-4], refs[-4], refs[-3:]
    at = 0
    for x_ref in x_refs:
        split_out(mm(x_ref[...], w_ref[...], dims).astype(bf16), out_refs, at)
        at += x_ref.shape[0] // 4


def project_split(flats, weight, dims, block, quarter):
    width = flats[0].shape[1]
    count = sum(v.shape[0] for v in flats) // 4
    if dims == NN:
        out = weight.shape[1]
        w_spec = pl.BlockSpec((width, block), lambda n: (0, n))
    else:
        out = weight.shape[0]
        w_spec = pl.BlockSpec((block, width), lambda n: (n, 0))
    specs, shapes = split_specs(count, out, block)
    split = pl.pallas_call(
        partial(project_split_kernel, dims=dims),
        grid=(out // block,),
        in_specs=[pl.BlockSpec(v.shape, lambda n: (0, 0)) for v in flats] + [w_spec],
        out_specs=specs,
        out_shape=shapes,
        cost_estimate=cost(
            flops=8 * count * width * out, bytes_accessed=2 * (out * width + 4 * count * (width + out)), transcendentals=0
        ),
        name="project_split",
    )(*flats, weight)
    return by_rows(*split, quarter)


def cotangent_kernel(*refs):
    x_refs, w_ref, out_ref, flat_ref = refs[:4], refs[4], refs[5], refs[6]
    part = x_refs[0].shape[0]
    for i in range(4):
        flat_ref[i * part:(i + 1) * part] = x_refs[i][...]
    out_ref[...] = mm(flat_ref[...], w_ref[...], NT).astype(bf16)


def project_cotangent(pieces, weight, rows, first):
    total, quarter, width = pieces[0].shape
    part = rows * quarter
    at = first // rows
    out = weight.shape[0]
    return pl.pallas_call(
        cotangent_kernel,
        grid=(1,),
        in_specs=[pl.BlockSpec((part, width), lambda c: (at, 0))] * 4 + [pl.BlockSpec((out, width), lambda c: (0, 0))],
        out_specs=[pl.BlockSpec((4 * part, out), lambda c: (0, 0)), pl.BlockSpec((4 * part, width), lambda c: (0, 0))],
        out_shape=[jax.ShapeDtypeStruct((4 * part, out), bf16), jax.ShapeDtypeStruct((4 * part, width), bf16)],
        cost_estimate=cost(
            flops=8 * part * width * out, bytes_accessed=2 * width * (out + 8 * part), transcendentals=0
        ),
        name="project_cotangent",
    )(*[p.reshape(total * quarter, width) for p in pieces], weight)


def assemble(pairs):
    rows, heads, parts, pieces, quarter, size = pairs.shape
    tokens, width = 4 * rows * quarter, parts * heads * size
    return pl.pallas_call(
        join_pairs,
        out_shape=jax.ShapeDtypeStruct((tokens, width), bf16),
        cost_estimate=cost(flops=0, bytes_accessed=4 * tokens * width, transcendentals=0),
        name="assemble",
    )(pairs)


def runs(lengths, cut):
    at = 0
    for k, n in enumerate(lengths):
        start = 0
        while start < n:
            step = min(n - start, cut - at % cut)
            yield k, start, at, step
            start += step
            at += step


def width_of(sizes, pieces):
    return -(-sum(sizes) // (pieces * LANES)) * LANES


def part_of(ref, j, rank, lanes):
    return ref.at[j, :, lanes] if len(ref.shape) == 3 else ref.at[j * rank:(j + 1) * rank, lanes]


def pack_kernel(*refs, plan, counts, vectors):
    total = sum(counts)
    in_refs, sum_refs, out_ref, sums = refs[:total], refs[total:-2], refs[-2], refs[-1]
    rank = out_ref.shape[1]
    sums[...] = jnp.zeros_like(sums)
    row = 0
    for ref in sum_refs:
        for j in range(ref.shape[0]):
            sums[row:row + 1, :ref.shape[2]] = ref[j]
            row += 1
    base = 0
    for entries, cut in plan:
        sizes = [n for _, _, n in entries]
        for k, start, at, n in runs(sizes, cut):
            which, j, _ = entries[k]
            lanes = slice(start, start + n)
            values = sums[:, lanes] if which is None else part_of(in_refs[which], j, rank, lanes)[...]
            out_ref[at // cut, :, base + at % cut:base + at % cut + n] = values.astype(bf16)
        end = sum(sizes)
        while end < out_ref.shape[0] * cut:
            n = cut - end % cut
            out_ref[end // cut, :, base + end % cut:base + end % cut + n] = jnp.zeros((rank, n), bf16)
            end += n
        base += cut


def unpack_kernel(*refs, plan, count):
    x_ref, m_refs, out_refs = refs[0], refs[1:1 + count], refs[1 + count:]
    rank = x_ref.shape[1]
    base = 0
    for entries, cut in plan:
        for k, start, at, n in runs([n for _, _, n in entries], cut):
            values = x_ref[at // cut, :, base + at % cut:base + at % cut + n].astype(f32)
            which, j, _ = entries[k]
            if which is not None:
                part_of(out_refs[which], j, rank, slice(start, start + n))[...] = values
                continue
            row = 0
            for m_ref, out_ref in zip(m_refs, out_refs[-count:]):
                members, size = m_ref.shape
                stop = min(start + n, size)
                if start < stop:
                    out_ref[:, start:stop] = values[row:row + members, :stop - start] / m_ref[:, start:stop]
                row += members
        base += cut


def packing(over_all, over_seq, width, pieces, rank):
    plan, at = [], 0
    for arrays in (over_all, over_seq):
        entries = []
        for v in arrays:
            members = v.shape[0] if len(v.shape) == 3 else v.shape[0] // rank
            entries += [(at, j, v.shape[-1]) for j in range(members)]
            at += 1
        plan.append(entries)
    plan[1].append((None, 0, width))
    return [(entries, width_of([n for _, _, n in entries], pieces)) for entries in plan]


def pack(plan, arrays, vectors, pieces, rank, width):
    return pl.pallas_call(
        partial(pack_kernel, plan=plan, counts=[len(arrays)], vectors=len(vectors)),
        out_shape=jax.ShapeDtypeStruct((pieces, rank, sum(cut for _, cut in plan)), bf16),
        scratch_shapes=[pltpu.VMEM((rank, width), f32)],
        cost_estimate=cost(flops=0, bytes_accessed=4 * sum(v.size for v in arrays), transcendentals=0),
        name="pack",
    )(*arrays, *vectors)


def unpack(plan, values, arrays, magnitudes):
    return pl.pallas_call(
        partial(unpack_kernel, plan=plan, count=len(magnitudes)),
        out_shape=[jax.ShapeDtypeStruct(v.shape, f32) for v in (*arrays, *magnitudes)],
        cost_estimate=cost(flops=0, bytes_accessed=6 * values.size, transcendentals=0),
        name="unpack",
    )(values, *magnitudes)


def gated_kernel(*refs):
    x_refs, w_ref, e_ref, hidden_ref, grads_ref, sums_ref, xs = refs[:4], *refs[4:]
    count = x_refs[0].shape[0]

    @pl.when(pl.program_id(0) == 0)
    def _():
        for i in range(4):
            xs[i * count:(i + 1) * count] = x_refs[i][...]

    product = mm(xs[...], w_ref[...])
    block = LANES
    for k in range(product.shape[1] // (2 * block)):
        at, mine = k * 2 * block, slice(k * block, (k + 1) * block)
        gate, up = product[:, at:at + block], product[:, at + block:at + 2 * block]
        dhid = e_ref[:, mine].astype(f32)
        sig = 1.0 / (1.0 + jnp.exp(-gate))
        act = gate * sig
        hidden_ref[:, mine] = (act * up).astype(bf16)
        dgate = dhid * up * (sig * (1.0 + gate * (1.0 - sig)))
        dup = dhid * act
        grads_ref[:, at:at + block] = dgate.astype(bf16)
        grads_ref[:, at + block:at + 2 * block] = dup.astype(bf16)
        sums_ref[0, :, mine] = jnp.sum(gate * dgate, axis=0, keepdims=True)
        sums_ref[1, :, mine] = jnp.sum(up * dup, axis=0, keepdims=True)


def gated(pieces, weight, dhid):
    rows, quarter, width = pieces[0].shape
    count = rows * quarter
    out = dhid.shape[1]
    block = GATED_BLOCKS * LANES
    return pl.pallas_call(
        gated_kernel,
        grid=(-(-out // block),),
        in_specs=[pl.BlockSpec(memory_space=pltpu.VMEM)] * 4
        + [
            pl.BlockSpec((width, 2 * block), lambda i: (0, i)),
            pl.BlockSpec((4 * count, block), lambda i: (0, i)),
        ],
        out_specs=[
            pl.BlockSpec((4 * count, block), lambda i: (0, i)),
            pl.BlockSpec((4 * count, 2 * block), lambda i: (0, i)),
            pl.BlockSpec((2, 1, block), lambda i: (0, 0, i)),
            pl.BlockSpec((4 * count, width), lambda i: (0, 0)),
        ],
        out_shape=[
            jax.ShapeDtypeStruct((4 * count, out), bf16),
            jax.ShapeDtypeStruct((4 * count, 2 * out), bf16),
            jax.ShapeDtypeStruct((2, 1, out), f32),
            jax.ShapeDtypeStruct((4 * count, width), bf16),
        ],
        cost_estimate=cost(
            flops=16 * count * width * out,
            bytes_accessed=4 * width * out + 8 * count * (2 * width + 4 * out),
            transcendentals=4 * count * out,
        ),
        name="gated",
    )(*[p.reshape(count, width) for p in pieces], weight, dhid)


def chunk_lanes(refs):
    ends = [0]
    for ref in refs:
        ends.append(ends[-1] + ref.shape[0])
    return [slice(a, b) for a, b in zip(ends, ends[1:])]


def column_grads_kernel(*refs, chunks, steps):
    x_refs, d_refs, refs = refs[:chunks], refs[chunks:2 * chunks], refs[2 * chunks:]
    w_ref, a_ref, b_ref, stat_ref, m_ref, sum_ref, cross_ref, gb_ref, ga_ref, ts, dts, es = refs
    members, rank, block = b_ref.shape
    lanes = chunk_lanes(x_refs)
    i = pl.program_id(0)

    @pl.when(i == 0)
    def _():
        for c in range(chunks):
            ts[:, lanes[c]] = mm(a_ref[...], x_refs[c][...], NT).astype(bf16)
        dts[...] = jnp.zeros_like(dts)

    @pl.when(i < steps)
    def _():
        found = sum(mm(ts[:, lanes[c]], d_refs[c][...]) for c in range(chunks))
        spread, along = [], []
        for j in range(members):
            b = b_ref[j].astype(f32)
            scale = stat_ref[j, 1:2]
            coef = -sum_ref[j] / (m_ref[j] * stat_ref[j, 0:1])
            mine = found[j * rank:(j + 1) * rank, j * block:(j + 1) * block]
            gb_ref[j] = (adapter_scale * (mine * scale + coef * cross_ref[j])).astype(bf16)
            empty = jnp.zeros((rank, block), f32)
            row = lambda v: jnp.concatenate([v if k == j else empty for k in range(members)], axis=1)
            spread.append(row(adapter_scale * coef * b))
            along.append(row(adapter_scale * scale * b))
        wide = members * block
        es[:, pl.ds(pl.multiple_of(i * wide, wide), wide)] = jnp.concatenate(spread, axis=0).astype(bf16)
        up = jnp.concatenate(along, axis=0).astype(bf16)
        for c in range(chunks):
            dts[:, lanes[c]] += mm(up, d_refs[c][...], NT)

    @pl.when(i >= steps)
    def _():
        span = w_ref.shape[0]
        at = pl.ds(pl.multiple_of((i - steps) * span, span), span)
        total = mm(es[...], w_ref[...], NT)
        for c in range(chunks):
            total = total + mm(dts[:, lanes[c]].astype(bf16), x_refs[c][:, at])
        ga_ref[...] = total.astype(bf16)


def column_grads(rows, grads, weight, down, up, stat, magnitude, sums, cross, block):
    tokens, width = sum(v.shape[0] for v in rows), rows[0].shape[1]
    members, rank, out = up.shape
    chunks, steps, span = len(rows), out // block, 512
    first = lambda i: jnp.minimum(i, steps - 1)
    then = lambda i: jnp.maximum(i - steps, 0)
    part = lambda n: pl.BlockSpec((members, n, block), lambda i: (0, 0, first(i)))
    wide = members * block
    ranks = members * rank
    grad_b, grad_a = pl.pallas_call(
        partial(column_grads_kernel, chunks=chunks, steps=steps),
        grid=(steps + width // span,),
        in_specs=[pl.BlockSpec(v.shape, lambda i: (0, 0)) for v in rows]
        + [pl.BlockSpec((v.shape[0], wide), lambda i: (0, first(i))) for v in grads]
        + [
            pl.BlockSpec((span, members * out), lambda i: (then(i), 0)),
            pl.BlockSpec((ranks, width), lambda i: (0, 0)),
            part(rank), part(2), part(1), part(1), part(rank),
        ],
        out_specs=[part(rank), pl.BlockSpec((ranks, span), lambda i: (0, then(i)))],
        out_shape=[
            jax.ShapeDtypeStruct((members, rank, out), bf16),
            jax.ShapeDtypeStruct((ranks, width), bf16),
        ],
        scratch_shapes=[
            pltpu.VMEM((ranks, tokens), bf16),
            pltpu.VMEM((ranks, tokens), f32),
            pltpu.VMEM((ranks, members * out), bf16),
        ],
        cost_estimate=cost(
            flops=4 * 256 * width * members * out // 4,
            bytes_accessed=2 * (width * members * out + tokens * (width + members * out)),
            transcendentals=0,
        ),
        name="column_grads",
    )(*rows, *grads, weight, down.transpose(0, 2, 1).reshape(ranks, width), up, stat, magnitude[:, None, :], sums, cross)
    return grad_a, grad_b


def row_grads_kernel(*refs, chunks):
    h_refs, d_refs, refs = refs[:chunks], refs[chunks:2 * chunks], refs[2 * chunks:]
    w_ref, a_ref, b_ref, stat_ref, coef_ref, ga_ref, gb_ref, ts, dts, acc = refs
    lanes = chunk_lanes(h_refs)
    i = pl.program_id(0)

    @pl.when(i == 0)
    def _():
        for c in range(chunks):
            ts[:, lanes[c]] = mm(a_ref[...], h_refs[c][...], NT).astype(bf16)
        dts[...] = jnp.zeros_like(dts)
        acc[...] = jnp.zeros_like(acc)

    b = b_ref[...].astype(f32)
    coef = coef_ref[...]
    found = sum(mm(ts[:, lanes[c]], d_refs[c][...]) for c in range(chunks))
    gb_ref[...] = (adapter_scale * (found + coef * stat_ref[...])).astype(bf16)
    up = (adapter_scale * b).astype(bf16)
    for c in range(chunks):
        dts[:, lanes[c]] += mm(up, d_refs[c][...], NT)
    acc[...] += mm((adapter_scale * coef * b).astype(bf16), w_ref[...], NT)

    @pl.when(i == pl.num_programs(0) - 1)
    def _():
        total = acc[...]
        for c in range(chunks):
            total = total + mm(dts[:, lanes[c]].astype(bf16), h_refs[c][...])
        ga_ref[...] = total.astype(bf16)


def row_grads(rows, grads, weight, down, up, stat, coef, block):
    tokens, count = sum(v.shape[0] for v in rows), rows[0].shape[1]
    rank, out = up.shape
    chunks = len(rows)
    along = lambda n: pl.BlockSpec((n, block), lambda i: (0, i))
    return pl.pallas_call(
        partial(row_grads_kernel, chunks=chunks),
        grid=(out // block,),
        in_specs=[pl.BlockSpec(v.shape, lambda i: (0, 0)) for v in rows]
        + [pl.BlockSpec((v.shape[0], block), lambda i: (0, i)) for v in grads]
        + [along(count), pl.BlockSpec((rank, count), lambda i: (0, 0)), along(rank), along(rank), along(1)],
        out_specs=[pl.BlockSpec((rank, count), lambda i: (0, 0)), along(rank)],
        out_shape=[jax.ShapeDtypeStruct((rank, count), bf16), jax.ShapeDtypeStruct((rank, out), bf16)],
        scratch_shapes=[
            pltpu.VMEM((rank, tokens), bf16),
            pltpu.VMEM((rank, tokens), f32),
            pltpu.VMEM((rank, count), f32),
        ],
        cost_estimate=cost(
            flops=256 * count * out, bytes_accessed=2 * (count * out + tokens * (count + out)), transcendentals=0
        ),
        name="row_grads",
    )(*rows, *grads, weight, down.T, up, stat, coef)


def norm_scale(values):
    return lax.rsqrt(jnp.mean(values * values, axis=-1, keepdims=True) + epsilon)


def norm_back(values, gain, grad):
    r = norm_scale(values)
    weighted = gain * grad
    return r * weighted - values * (r * r * r) * jnp.mean(values * weighted, axis=-1, keepdims=True)


def rotary_tables(positions, head_size):
    half_size = head_size // 2
    frequency = rope_base ** (-(2.0 * jnp.arange(half_size, dtype=f32)) / head_size)
    angles = positions.astype(f32)[:, None] * frequency[None, :]
    cosine, sine = jnp.cos(angles), jnp.sin(angles)
    return (jnp.concatenate([cosine, cosine], axis=-1), jnp.concatenate([-sine, sine], axis=-1))


def local(
    layer_in, cotangent, doc_lengths, pad_counts, gain_attn, gain_ffn, w_qkv, a_qkv, b_qkv, m_qkv, w_out, a_out,
    b_out, m_out, w_gateup, a_gateup, b_gateup, m_gateup, w_down, a_down, b_down, m_down,
):
    rows, quarter, width = layer_in.shape
    tensor, seq = lax.axis_size("tensor"), lax.axis_size("seq")
    assert tensor == len(PIECES)
    me_t, me_s = lax.axis_index("tensor"), lax.axis_index("seq")
    group = quarter * tensor
    total = group * seq
    feat = w_qkv.shape[2]
    heads = feat // HEAD_DIM
    rank = a_qkv.shape[2]
    ff = w_down.shape[0]
    piece_of = jnp.bitwise_xor(me_t, jnp.array(PIECES, jnp.int32))
    in_block = (piece_of[:, None] * quarter + jnp.arange(quarter, dtype=jnp.int32)[None, :]).reshape(group)
    positions = (jnp.arange(seq, dtype=jnp.int32)[:, None] * group + in_block[None, :]).reshape(total)
    tables = rotary_tables(positions, HEAD_DIM)
    offsets = jnp.cumsum(doc_lengths, axis=1)
    starts = jnp.max(
        jnp.where(offsets[:, :, None] <= positions[None, None, :], offsets[:, :, None], 0), axis=1
    )
    kpos = positions[:, None]
    few = rows // 3
    cuts = [slice(rows - few, rows), slice(0, rows - few)]
    span = range(2)
    pair_counts = [(at.stop - at.start) * heads for at in cuts]
    slots = [-(-count // seq) for count in pair_counts]
    mine = [me_s * slots[c] + jnp.arange(slots[c]) for c in span]
    live = [mine[c] < pair_counts[c] for c in span]

    def pair_info(c):
        row = jnp.minimum(mine[c] // heads + cuts[c].start, cuts[c].stop - 1)
        chosen = (row[:, None] == jnp.arange(rows)[None, :])[:, :, None]
        return jnp.stack(
            [jnp.broadcast_to(positions[None], (slots[c], total)), jnp.sum(jnp.where(chosen, starts[None], 0), axis=1)],
            axis=1,
        )

    qinfo = [pair_info(c) for c in span]

    def send_pairs(values, c):
        parts = values.shape[2]
        laid = values.reshape(pair_counts[c], parts, group, HEAD_DIM)
        if slots[c] * seq > pair_counts[c]:
            laid = jnp.pad(laid, ((0, slots[c] * seq - pair_counts[c]), (0, 0), (0, 0), (0, 0)))
        return exchange(laid.reshape(seq, slots[c], parts, group, HEAD_DIM))

    def fetch_pairs(values, c):
        parts = values.shape[2]
        laid = exchange(values).reshape(seq * slots[c], parts, group, HEAD_DIM)[:pair_counts[c]]
        return laid.reshape(pair_counts[c] // heads, heads, parts, tensor, quarter, HEAD_DIM)

    def to_heads(pieces, weight):
        return project_to_pairs(pieces, weight, NN, 3, heads, HEAD_DIM, heads)

    def back_to_heads(pieces, weight):
        return project_to_pairs(pieces, weight, NT, 1, heads, HEAD_DIM, 2)

    owned = me_s * group + me_t * quarter + jnp.arange(quarter, dtype=jnp.int32)
    valid = (owned[None, :] < total - pad_counts[:, None]).astype(f32)
    cot = cotangent.astype(f32) * valid[:, :, None]
    wide_in = [layer_in[at].astype(f32) for at in cuts]

    def normed(values, gain):
        return (values * norm_scale(values) * gain).astype(bf16)

    started = [gather_start(normed(wide_in[c], gain_attn)) for c in span]
    qkv_w, qkv_stat, qkv_cross = column_prep(w_qkv, a_qkv, b_qkv, m_qkv, 256, False)
    started[0], qkv_w = after(started[0], qkv_w)
    normed_a, d_qkv, pairs, outputs, totals, att = [[None] * 2 for _ in range(6)]
    laid, normed_a[0] = to_heads(gather_end(*started[0]), qkv_w)

    laid, started[1], w_out = after(laid, started[1], w_out)
    pairs[0] = send_pairs(laid, 0)
    laid, normed_a[1] = to_heads(gather_end(*started[1]), qkv_w)
    out_w, out_cross, out_square = row_prep(w_out, a_out, b_out, 512)
    pairs[0], laid, out_square, w_down = after(pairs[0], laid, out_square, w_down)

    outputs[0], totals[0] = attend(pairs[0], tables, kpos, qinfo[0])
    outputs[0], w_down = after(outputs[0], w_down)
    fetched = fetch_pairs(outputs[0][:, :, None], 0)
    down_w, down_cross, down_square = row_prep(w_down, a_down, b_down, 256)
    fetched, laid, down_square = after(fetched, laid, down_square)

    u_out, middle, hidden, d_gu, gu_sum, normed_f, d_mid, du_out, dhid, du_down = [[None] * 2 for _ in range(10)]

    def of_cotangent(whole, c):
        return project_cotangent(whole, down_w, cuts[c].stop - cuts[c].start, cuts[c].start)

    pairs[1] = send_pairs(laid, 1)
    squares = tensor_sum(jnp.concatenate([down_square, out_square]))
    fetched, squares = after(fetched, squares)
    down_square, out_square = squares[0:1], squares[1:2]
    down_scale, out_scale = m_down / jnp.sqrt(squares[0]), m_out / jnp.sqrt(squares[1])
    att[0], split = project_from_pairs(fetched, out_w, 512)
    moving, scaled, w_gateup = after(scatter_start(*split), (cot * down_scale).astype(bf16), w_gateup)
    tail, started = scatter_end(*moving), gather_start(scaled)
    gu_w, gu_stat, gu_cross = column_prep(w_gateup, a_gateup, b_gateup, m_gateup, LANES, True)
    tail, started, gu_w = after(tail, started, gu_w)
    u_out[0] = tail * out_scale
    middle[0] = wide_in[0] + u_out[0]
    h_f, whole_cot = after(normed(middle[0], gain_ffn), gather_end(*started))
    pairs[1], h_f = after(pairs[1], h_f)
    outputs[1], totals[1] = attend(pairs[1], tables, kpos, qinfo[1])
    started, outputs[1] = after(gather_start(h_f), outputs[1])

    fetched = fetch_pairs(outputs[1][:, :, None], 1)
    dhid[0], du_down[0] = of_cotangent(whole_cot, 0)
    hidden[0], d_gu[0], gu_sum[0], normed_f[0] = gated(gather_end(*started), gu_w, dhid[0])
    d_gu[0], fetched = after(d_gu[0], fetched)

    att[1], split = project_from_pairs(fetched, out_w, 512)
    moving, d_gu[0], whole_cot = after(scatter_start(*split), d_gu[0], whole_cot)
    split = project_split([d_gu[0]], gu_w, NT, 512, quarter)
    dhid[1], du_down[1] = of_cotangent(whole_cot, 1)
    tail, split, dhid[1] = after(scatter_end(*moving), split, dhid[1])
    u_out[1] = tail * out_scale
    middle[1] = wide_in[1] + u_out[1]
    h_f, split = after(normed(middle[1], gain_ffn), split)
    shard, far, near = gather_start(h_f)
    near, split = after(near, split)
    started = (shard, far, near)
    d_mid[0] = cot[cuts[0]] + norm_back(middle[0], gain_ffn, scatter_end(*scatter_start(*split)))
    behind = gather_start((d_mid[0] * out_scale).astype(bf16))
    d_att, du_out[0] = back_to_heads(gather_end(*behind), out_w)
    whole, d_att = after(gather_end(*started), d_att)

    d_outputs = send_pairs(d_att, 0)[:, :, 0]
    hidden[1], d_gu[1], gu_sum[1], normed_f[1] = gated(whole, gu_w, dhid[1])
    d_gu[1], d_outputs = after(d_gu[1], d_outputs)
    moving, d_outputs = after(scatter_start(*project_split([d_gu[1]], gu_w, NT, 512, quarter)), d_outputs)
    d_pairs, pair_sums = [None] * 2, [None] * 2
    d_pairs[0], pair_sums[0] = attend_back(pairs[0], outputs[0], d_outputs, totals[0], tables, kpos, qinfo[0])
    fetched = fetch_pairs(d_pairs[0], 0)
    d_mid[1] = cot[cuts[1]] + norm_back(middle[1], gain_ffn, scatter_end(*moving))
    scaled, hidden = after((d_mid[1] * out_scale).astype(bf16), hidden)
    split = project_split(hidden[::-1], down_w, NN, 512, quarter)
    started, split, fetched = after(gather_start(scaled), split, fetched)
    d_att, du_out[1] = back_to_heads(gather_end(*started), out_w)

    d_att, fetched, out_sum = after(d_att, fetched, sum(jnp.sum(u_out[c] * d_mid[c], axis=(0, 1)) for c in span)[None])
    d_outputs = send_pairs(d_att, 1)[:, :, 0]
    out_sum, fetched = after(tensor_sum(out_sum), fetched)
    d_qkv[0] = assemble(fetched)
    split_in = [project_split([d_qkv[0]], qkv_w, NT, 512, quarter), None]
    d_outputs, split_in[0], out_sum, d_gu = after(d_outputs, split_in[0], out_sum, d_gu)
    d_pairs[1], pair_sums[1] = attend_back(pairs[1], outputs[1], d_outputs, totals[1], tables, kpos, qinfo[1])

    d_pairs[1], split, att, d_gu, split_in[0] = after(d_pairs[1], split, att, d_gu, split_in[0])
    fetched = fetch_pairs(d_pairs[1], 1)
    moving, d_gu = after(scatter_start(*split), d_gu)
    gu_sums = sum(gu_sum)
    grad_a_gu, grad_b_gu = column_grads(
        normed_f, d_gu, gu_w, a_gateup, b_gateup, gu_stat, m_gateup, gu_sums, gu_cross, LANES
    )
    tail, grad_a_gu, att = after(scatter_end(*moving), grad_a_gu, att)
    u_down = tail * down_scale
    layer_out = (jnp.concatenate(middle[::-1]) + u_down).astype(bf16)
    down_sum = tensor_sum(jnp.sum(u_down * cot, axis=(0, 1))[None])
    grad_a_out, grad_b_out = row_grads(att, du_out, out_w, a_out, b_out, out_cross, -out_sum / out_square, 512)
    grad_a_down, grad_b_down = row_grads(
        hidden, du_down, down_w, a_down, b_down, down_cross, -down_sum / down_square, 512
    )
    grad_norm_a = [scatter_end(*scatter_start(*split_in[0])), None]
    fetched, grad_a_out, grad_a_down, layer_out, grad_norm_a[0] = after(
        fetched, grad_a_out, grad_a_down, layer_out, grad_norm_a[0]
    )
    d_qkv[1] = assemble(fetched)

    qkv_sums = 0.0
    for c in span:
        choice = jnp.logical_and((mine[c] % heads)[:, None] == jnp.arange(heads)[None, :], live[c][:, None])
        qkv_sums = qkv_sums + jnp.sum(jnp.where(choice[:, None, :, None], pair_sums[c][:, :, None, :], 0.0), axis=0)
    qkv_sums = qkv_sums.reshape(3, 1, feat)
    grad_a_qkv, grad_b_qkv = column_grads(
        normed_a, d_qkv, qkv_w, a_qkv, b_qkv, qkv_stat, m_qkv, qkv_sums, qkv_cross, feat
    )

    over_all = [grad_a_gu, grad_b_out, grad_b_down, grad_a_qkv]
    over_seq = [grad_b_gu, grad_a_out, grad_a_down, grad_b_qkv]
    vectors = [gu_sums, out_sum[None], down_sum[None], qkv_sums]
    plan = packing(over_all, over_seq, width, seq, rank)
    cut = plan[0][1]
    packed, d_qkv[1] = after(pack(plan, over_all + over_seq, vectors, seq, rank, width), d_qkv[1])
    added = exchange(packed)
    split_in[1] = project_split([d_qkv[1]], qkv_w, NT, 512, quarter)
    grad_norm_a[1] = scatter_end(*scatter_start(*split_in[1]))
    grad_in = jnp.concatenate(
        [d_mid[c] + norm_back(wide_in[c], gain_attn, grad_norm_a[c]) for c in reversed(span)]
    )
    added = jnp.sum(added.astype(f32), axis=0).astype(bf16)
    shared = added[:, :cut]
    shared = shared.astype(f32) + swap(shared, 1).astype(f32) + swap(shared, 2).astype(f32) + swap(shared, 3).astype(f32)
    back = seq_gather(jnp.concatenate([shared.astype(bf16), added[:, cut:]], axis=1))
    g_a_gu, g_b_out, g_b_down, g_a_qkv, g_b_gu, g_a_out, g_a_down, g_b_qkv, s_gu, s_out, s_down, s_qkv = unpack(
        plan, back, over_all + over_seq, [m_gateup, m_out[None], m_down[None], m_qkv]
    )
    return (
        layer_out,
        grad_in,
        g_a_qkv.reshape(3, rank, width).transpose(0, 2, 1),
        g_b_qkv,
        s_qkv,
        g_a_out.T,
        g_b_out,
        s_out[0],
        g_a_gu.reshape(2, rank, width).transpose(0, 2, 1),
        g_b_gu,
        s_gu,
        g_a_down.T,
        g_b_down,
        s_down[0],
    )


def solution(mesh):
    split = P(None, ("seq", "tensor"), None)
    in_specs = (
        split, split, P(), P(), P(), P(),
        P(None, None, "tensor"), P(), P(None, None, "tensor"), P(None, "tensor"),
        P("tensor", None), P("tensor", None), P(), P(),
        P(None, None, "tensor"), P(), P(None, None, "tensor"), P(None, "tensor"),
        P("tensor", None), P("tensor", None), P(), P(),
    )
    out_specs = (
        split, split,
        P(), P(None, None, "tensor"), P(None, "tensor"),
        P("tensor", None), P(), P(),
        P(), P(None, None, "tensor"), P(None, "tensor"),
        P("tensor", None), P(), P(),
    )
    return jax.shard_map(local, mesh=mesh, in_specs=in_specs, out_specs=out_specs, check_vma=False)
```

time: 596 us -> 466 us (0.78)
  Pallas kernels: 83.8 us -> 223 us
  matrix products: 110 us -> 0 us
  waiting for transfers between devices: 191 us -> 81.6 us
  local copies, waits for them, and re-layouts: 87.9 us -> 14.6 us
  starting transfers between devices: 57.6 us -> 90.5 us
    pallas_call x5 -> x27, Pallas kernels: 65.5 us -> 200 us  [the longest x5 40.1 us: project_split(): pl.pallas_call(partial(project_split_kernel, dims=dims), grid=(out // blo...]
    dot_general x23 -> x0, matrix products: 110 us -> none  [mm(): return lax.dot_general(a, b, dims, preferred_element_type=f32)]
    all_to_all x8 -> x10, waiting for transfers between devices: 97.5 us -> 25.1 us  [exchange(): return lax.all_to_all(values, 'seq', 0, 0, tiled=True)]
    ppermute x32 -> x47, waiting for transfers between devices: 93.6 us -> 56.5 us  [swap(): return lax.ppermute(values, 'tensor', [(i, i ^ bit) for i in range(size)])]
    all_to_all x8 -> x10, starting transfers between devices: 36 us -> 63.7 us  [exchange(): return lax.all_to_all(values, 'seq', 0, 0, tiled=True)]
    reshape x18 -> x0, local copies, waits for them, and re-layouts: 20 us -> none  [the longest x2 7.98 us: to_pairs(): values.reshape(tensor, rows, quarter, parts, heads, HEAD_DIM)]
    transpose x6 -> x0, local copies, waits for them, and re-layouts: 15.6 us -> none  [the longest x1 8.89 us: local(): qkv_flat = qkv_w.transpose(1, 0, 2).reshape(width, 3 * feat)]
    slice x17 -> x2, local copies, waits for them, and re-layouts: 10.1 us -> 0.01 us  [the longest x1 0.01 us: local(): shared = added[:, :cut]]
  transfers between devices with their start and end apart: 40 -> 57, of which waited for: 18 -> 25; matrix products, arithmetic and copies ran while one was open for 29% -> 10% of each run, Pallas kernels for 10% -> 38%
where the time goes in v2:
time: 466 us; the launch traced here: 459 us
  Pallas kernels  223 us (48%)
  starting transfers between devices  90.5 us (19%)
  waiting for transfers between devices  81.6 us (18%)
  other arithmetic  47.1 us (10%)
  local copies, waits for them, and re-layouts  14.6 us (3%)
    all_to_all x10, starting transfers between devices, exchange(): return lax.all_to_all(values, 'seq', 0, 0, tiled=True)  63.7 us
    ppermute x47, waiting for transfers between devices, swap(): return lax.ppermute(values, 'tensor', [(i, i ^ bit) for i in range(size)])  56.5 us
    pallas_call x5, Pallas kernels, project_split(): pl.pallas_call(partial(project_split_kernel, dims=dims), grid=(out // blo...  40.1 us
    pallas_call x2, Pallas kernels, column_grads(): pl.pallas_call(partial(column_grads_kernel, chunks=chunks, steps=steps),...  28.2 us
    ppermute x47, starting transfers between devices, swap(): return lax.ppermute(values, 'tensor', [(i, i ^ bit) for i in range(size)])  26.8 us
    pallas_call x2, Pallas kernels, column_prep(): pl.pallas_call(column_prep_kernel, grid=(out // block,), in_specs=[pl.Blo...  25.5 us
    all_to_all x10, waiting for transfers between devices, exchange(): return lax.all_to_all(values, 'seq', 0, 0, tiled=True)  25.1 us
    pallas_call x2, Pallas kernels, gated(): pl.pallas_call(gated_kernel, grid=(-(-out // block),), in_specs=[pl.Block...  23.9 us
  transfers between devices with their start and end apart: 57, of which 25 were waited for; matrix products, arithmetic and copies ran while one was open for 10% of the time, Pallas kernels for 38%

profile of v2, /device:TPU:0, one launch (start us, length us, event | category | flops | bytes accessed | tf_op | source)
XLA Modules:
  0.0 459.2 jit_solution(8930662490661877207)
XLA Ops:
  11.5 8.9 %column_prep.2 = (bf16[2048,1536]{1,0:T(8,128)(2,1)}, f32[3,2,512]{2,1,0:T(2,128)}, f32[3,16,512]{2,1,0:T(8,128)}) custom-call(bf16[3,2048,512]{2,1,0:T(8,128)(2,1)} %w_ref.1, bf16[48,2048]{1,0:T(8,128)(2,1)} %bitcast.227, bf16[2,48,768]{2,1,0:T(8,128)(2,1)} %broadcast_multiply_fusion.1.b_ref, f32[3,1,512]{2,1,0:T(1,128)} %broadcast_in_dim.103.m_ref.refs_8_), custom_call_target="tpu_custom_call" | custom-call | flops 50331648 | bytes 196608 | tf_op jit(solution)/shard_map/column_prep/pallas_call | solution.py:103
  23.0 6.2 %project_to_pairs.4 = (bf16[2,4,3,4,32,128]{5,4,3,2,1,0:T(8,128)(2,1)}, bf16[256,2048]{1,0:T(8,128)(2,1)}) custom-call(bf16[64,2048]{1,0:T(8,128)(2,1)} %bitcast.217, bf16[64,2048]{1,0:T(8,128)(2,1)} %bitcast.4.refs_1_, bf16[64,2048]{1,0:T(8,128)(2,1)} %bitcast.246, bf16[64,2048]{1,0:T(8,128)(2,1)} %bitcast.252, ...), custom_call_target="tpu_custom_call" | custom-call | flops 25165824 | bytes 131072 | tf_op jit(solution)/shard_map/project_to_pairs/pallas_call | solution.py:358
  29.2 6.1 %all-to-all-start = ((bf16[8,1,3,128,128]{4,3,2,1,0:T(8,128)(2,1)}), bf16[8,1,3,128,128]{4,3,2,1,0:T(8,128)(2,1)S(1)}, u32[]{:S(2)}, u32[]{:S(2)}) async-start(bf16[8,1,3,128,128]{4,3,2,1,0:T(8,128)(2,1)} %bitcast.224), calls=%async_computation | async-start | bytes 1572864 | tf_op jit(solution)/shard_map/all_to_all | solution.py:65
  46.4 8.1 %project_to_pairs.5 = (bf16[4,4,3,4,32,128]{5,4,3,2,1,0:T(8,128)(2,1)}, bf16[512,2048]{1,0:T(8,128)(2,1)}) custom-call(bf16[128,2048]{1,0:T(8,128)(2,1)} %bitcast.209, bf16[128,2048]{1,0:T(8,128)(2,1)} %bitcast.232, bf16[128,2048]{1,0:T(8,128)(2,1)} %bitcast.231, bf16[128,2048]{1,0:T(8,128)(2,1)} %bitcast.235, ...), custom_call_target="tpu_custom_call" | custom-call | flops 50331648 | bytes 163840 | tf_op jit(solution)/shard_map/project_to_pairs/pallas_call | solution.py:358
  65.4 8.9 %row_prep.3 = (bf16[1408,2048]{1,0:T(8,128)(2,1)}, f32[16,2048]{1,0:T(8,128)}, f32[1,2048]{1,0:T(1,128)}) custom-call(bf16[1408,2048]{1,0:T(8,128)(2,1)} %w_ref.3, bf16[16,1408]{1,0:T(8,128)(2,1)} %bitcast.257, bf16[16,2048]{1,0:T(8,128)(2,1)} %refs_6_.6), custom_call_target="tpu_custom_call" | custom-call | flops 23068672 | bytes 180224 | tf_op jit(solution)/shard_map/row_prep/pallas_call | solution.py:141
  78.4 5.9 %all-to-all-start.2 = ((bf16[8,2,3,128,128]{4,3,2,1,0:T(8,128)(2,1)}), bf16[8,2,3,128,128]{4,3,2,1,0:T(8,128)(2,1)S(1)}, u32[]{:S(2)}, u32[]{:S(2)}) async-start(bf16[8,2,3,128,128]{4,3,2,1,0:T(8,128)(2,1)} %bitcast.215), calls=%async_computation.2 | async-start | bytes 3145728 | tf_op jit(solution)/shard_map/all_to_all | solution.py:65
  99.3 16.6 %column_prep.3 = (bf16[2048,2816]{1,0:T(8,128)(2,1)}, f32[2,2,1408]{2,1,0:T(2,128)}, f32[2,16,1408]{2,1,0:T(8,128)}) custom-call(bf16[2,2048,1408]{2,1,0:T(8,128)(2,1)} %w_ref.4, bf16[32,2048]{1,0:T(8,128)(2,1)} %bitcast.229, bf16[11,32,256]{2,1,0:T(8,128)(2,1)} %broadcast_multiply_fusion.b_ref, f32[2,1,1408]{2,1,0:T(1,128)} %broadcast_in_dim.115.m_ref.refs_8_), custom_call_target="tpu_custom_call" | custom-call | flops 92274688 | bytes 360448 | tf_op jit(solution)/shard_map/column_prep/pallas_call | solution.py:103
  124.7 5.7 %attend.3 = (bf16[8,2,128,128]{3,2,1,0:T(8,128)(2,1)}, f32[2,1,1024]{2,1,0:T(1,128)}) custom-call(bf16[8,2,3,128,128]{4,3,2,1,0:T(8,128)(2,1)} %copy-done.1, f32[1024,128]{1,0:T(8,128)} %get-tuple-element.459.cos_ref, f32[1024,128]{1,0:T(8,128)} %get-tuple-element.460.sin_ref, s32[1024,1]{1,0:T(8,128)} %copy.57.kpos_ref, s32[2,2,1024]{2,1,0:T(2,128)} %pad_add_fusion.qinfo_ref), custom_call_target="tpu_custom_call" | custom-call | flops 16777216 | bytes 32768 | tf_op jit(solution)/shard_map/attend/pallas_call | solution.py:209
  131.2 6.0 %all-to-all-start.3 = ((bf16[8,2,1,128,128]{4,3,1,2,0:T(8,128)(2,1)}), bf16[8,2,1,128,128]{4,3,1,2,0:T(8,128)(2,1)S(1)}, u32[]{:S(2)}, u32[]{:S(2)}) async-start(bf16[8,2,1,128,128]{4,3,1,2,0:T(8,128)(2,1)} %bitcast.214), calls=%async_computation.3 | async-start | bytes 1048576 | tf_op jit(solution)/shard_map/all_to_all | solution.py:65
  137.3 5.7 %project_cotangent.2 = (bf16[256,1408]{1,0:T(8,128)(2,1)}, bf16[256,2048]{1,0:T(8,128)(2,1)}) custom-call(bf16[192,2048]{1,0:T(8,128)(2,1)} %bitcast.204, bf16[192,2048]{1,0:T(8,128)(2,1)} %bitcast.40.refs_1_, bf16[192,2048]{1,0:T(8,128)(2,1)} %bitcast.41.refs_2_, bf16[192,2048]{1,0:T(8,128)(2,1)} %bitcast.206, ...), custom_call_target="tpu_custom_call" | custom-call | flops 23068672 | bytes 122880 | tf_op jit(solution)/shard_map/project_cotangent/pallas_call | solution.py:483
  143.7 10.0 %gated.2 = (bf16[256,1408]{1,0:T(8,128)(2,1)}, bf16[256,2816]{1,0:T(8,128)(2,1)}, f32[2,1,1408]{2,1,0:T(1,128)}, bf16[256,2048]{1,0:T(8,128)(2,1)}) custom-call(bf16[64,2048]{1,0:T(8,128)(2,1)} %bitcast.219, bf16[64,2048]{1,0:T(8,128)(2,1)} %bitcast.36.refs_1_, bf16[64,2048]{1,0:T(8,128)(2,1)} %bitcast.37.refs_2_, bf16[64,2048]{1,0:T(8,128)(2,1)} %bitcast.253, ...), custom_call_target="tpu_custom_call" | custom-call | flops 46137344 | bytes 258048 | tf_op jit(solution)/shard_map/gated/pallas_call | solution.py:636
  165.0 7.8 %project_split.5 = (bf16[64,2048]{1,0:T(8,128)(2,1)}, bf16[64,2048]{1,0:T(8,128)(2,1)}, bf16[2,64,2048]{2,1,0:T(8,128)(2,1)}) custom-call(bf16[256,2816]{1,0:T(8,128)(2,1)} %get-tuple-element.370.refs_0_.refs_2_, bf16[2048,2816]{1,0:T(8,128)(2,1)} %get-tuple-element.269.refs_4_.refs_1_), custom_call_target="tpu_custom_call" | custom-call | flops 46137344 | bytes 219136 | tf_op jit(solution)/shard_map/project_split/pallas_call | solution.py:456
  172.8 7.9 %project_cotangent.3 = (bf16[512,1408]{1,0:T(8,128)(2,1)}, bf16[512,2048]{1,0:T(8,128)(2,1)}) custom-call(bf16[192,2048]{1,0:T(8,128)(2,1)} %bitcast.205, bf16[192,2048]{1,0:T(8,128)(2,1)} %bitcast.55.refs_1_, bf16[192,2048]{1,0:T(8,128)(2,1)} %bitcast.56.refs_2_, bf16[192,2048]{1,0:T(8,128)(2,1)} %bitcast.207, ...), custom_call_target="tpu_custom_call" | custom-call | flops 46137344 | bytes 155648 | tf_op jit(solution)/shard_map/project_cotangent/pallas_call | solution.py:483
  188.8 7.1 %collective-permute-done.23 = bf16[2,32,2048]{2,1,0:T(8,128)(2,1)S(1)} collective-permute-done((bf16[2,32,2048]{2,1,0:T(8,128)(2,1)S(1)}, bf16[2,32,2048]{2,1,0:T(8,128)(2,1)S(1)}, u32[]{:S(2)}, u32[]{:S(2)}) %collective-permute-start.23) | collective-permute-done | bytes 262176 | tf_op jit(solution)/shard_map/ppermute | solution.py:36
  198.9 8.3 %collective-permute-done.19 = bf16[4,32,2048]{2,1,0:T(8,128)(2,1)} collective-permute-done((bf16[4,32,2048]{2,1,0:T(8,128)(2,1)S(1)}, bf16[4,32,2048]{2,1,0:T(8,128)(2,1)}, u32[]{:S(2)}, u32[]{:S(2)}) %collective-permute-start.19) | collective-permute-done | bytes 524320 | tf_op jit(solution)/shard_map/ppermute | solution.py:36
  218.6 14.5 %all-to-all-start.4 = ((bf16[8,1,1,128,128]{4,3,2,1,0:T(8,128)(2,1)}), bf16[8,1,1,128,128]{4,3,2,1,0:T(8,128)(2,1)S(1)}, u32[]{:S(2)}, u32[]{:S(2)}) async-start(bf16[8,1,1,128,128]{4,3,2,1,0:T(8,128)(2,1)} %bitcast.255), calls=%async_computation.4 | async-start | bytes 524288 | tf_op jit(solution)/shard_map/all_to_all | solution.py:65
  233.1 13.9 %gated.3 = (bf16[512,1408]{1,0:T(8,128)(2,1)}, bf16[512,2816]{1,0:T(8,128)(2,1)}, f32[2,1,1408]{2,1,0:T(1,128)}, bf16[512,2048]{1,0:T(8,128)(2,1)}) custom-call(bf16[128,2048]{1,0:T(8,128)(2,1)} %bitcast.210, bf16[128,2048]{1,0:T(8,128)(2,1)} %bitcast.65.refs_1_, bf16[128,2048]{1,0:T(8,128)(2,1)} %bitcast.233, bf16[128,2048]{1,0:T(8,128)(2,1)} %bitcast.234, ...), custom_call_target="tpu_custom_call" | custom-call | flops 92274688 | bytes 335872 | tf_op jit(solution)/shard_map/gated/pallas_call | solution.py:636
  246.9 10.6 %project_split.6 = (bf16[128,2048]{1,0:T(8,128)(2,1)}, bf16[128,2048]{1,0:T(8,128)(2,1)}, bf16[2,128,2048]{2,1,0:T(8,128)(2,1)}) custom-call(bf16[512,2816]{1,0:T(8,128)(2,1)} %get-tuple-element.371.refs_0_.refs_3_, bf16[2048,2816]{1,0:T(8,128)(2,1)} %get-tuple-element.269.refs_4_.refs_1_), custom_call_target="tpu_custom_call" | custom-call | flops 92274688 | bytes 258048 | tf_op jit(solution)/shard_map/project_split/pallas_call | solution.py:456
  268.6 6.0 %all-to-all-start.5 = ((bf16[8,1,3,128,128]{4,3,2,1,0:T(8,128)(2,1)}), bf16[8,1,3,128,128]{4,3,2,1,0:T(8,128)(2,1)}, u32[]{:S(2)}, u32[]{:S(2)}) async-start(bf16[8,1,3,128,128]{4,3,2,1,0:T(8,128)(2,1)} %get-tuple-element.332), calls=%async_computation.5 | async-start | bytes 1572864 | tf_op jit(solution)/shard_map/all_to_all | solution.py:65
  282.0 8.7 %project_split.7 = (bf16[192,2048]{1,0:T(8,128)(2,1)}, bf16[192,2048]{1,0:T(8,128)(2,1)}, bf16[2,192,2048]{2,1,0:T(8,128)(2,1)}) custom-call(bf16[512,1408]{1,0:T(8,128)(2,1)} %get-tuple-element.325.refs_0_.refs_1_, bf16[256,1408]{1,0:T(8,128)(2,1)} %get-tuple-element.326.refs_1_.refs_0_, bf16[1408,2048]{1,0:T(8,128)(2,1)} %get-tuple-element.274.refs_4_.refs_2_), custom_call_target="tpu_custom_call" | custom-call | flops 69206016 | bytes 173056 | tf_op jit(solution)/shard_map/project_split/pallas_call | solution.py:456
  303.3 6.0 %all-to-all-start.6 = ((bf16[8,2,1,128,128]{4,3,1,2,0:T(8,128)(2,1)}), bf16[8,2,1,128,128]{4,3,1,2,0:T(8,128)(2,1)}, u32[]{:S(2)}, u32[]{:S(2)}) async-start(bf16[8,2,1,128,128]{4,3,1,2,0:T(8,128)(2,1)} %bitcast.241), calls=%async_computation.6 | async-start | bytes 1048576 | tf_op jit(solution)/shard_map/all_to_all | solution.py:65
  315.2 5.7 %project_split.8 = (bf16[64,2048]{1,0:T(8,128)(2,1)}, bf16[64,2048]{1,0:T(8,128)(2,1)}, bf16[2,64,2048]{2,1,0:T(8,128)(2,1)}) custom-call(bf16[256,1536]{1,0:T(8,128)(2,1)} %assemble.2.refs_0_.refs_2_, bf16[2048,1536]{1,0:T(8,128)(2,1)} %get-tuple-element.225.refs_4_.refs_1_), custom_call_target="tpu_custom_call" | custom-call | flops 25165824 | bytes 126976 | tf_op jit(solution)/shard_map/project_split/pallas_call | solution.py:456
  324.2 8.1 %attend_back.3 = (bf16[8,2,3,128,128]{4,3,2,1,0:T(8,128)(2,1)}, f32[2,3,128]{2,1,0:T(4,128)}) custom-call(bf16[8,2,3,128,128]{4,3,2,1,0:T(8,128)(2,1)} %copy-done.1, bf16[8,2,128,128]{3,2,1,0:T(8,128)(2,1)} %get-tuple-element.265.o_ref, bf16[8,2,128,128]{3,2,1,0:T(8,128)(2,1)} %bitcast.87.d_ref, f32[2,1,1024]{2,1,0:T(1,128)} %get-tuple-element.347.l_ref, ...), custom_call_target="tpu_custom_call" | custom-call | flops 41943040 | bytes 65536 | tf_op jit(solution)/shard_map/attend_back/pallas_call | solution.py:295
  345.0 17.8 %column_grads.2 = (bf16[2,16,1408]{2,1,0:T(8,128)(2,1)}, bf16[32,2048]{1,0:T(8,128)(2,1)}) custom-call(bf16[256,2048]{1,0:T(8,128)(2,1)} %get-tuple-element.368.refs_0_, bf16[512,2048]{1,0:T(8,128)(2,1)} %get-tuple-element.369.refs_1_, bf16[256,2816]{1,0:T(8,128)(2,1)} %get-tuple-element.370.refs_0_.refs_2_, ...), custom_call_target="tpu_custom_call" | custom-call | flops 23068672 | bytes 296960 | tf_op jit(solution)/shard_map/column_grads/pallas_call | solution.py:724
  370.7 6.0 %row_grads.2 = (bf16[16,512]{1,0:T(8,128)(2,1)}, bf16[16,2048]{1,0:T(8,128)(2,1)}) custom-call(bf16[256,512]{1,0:T(8,128)(2,1)} %get-tuple-element.379.refs_0_, bf16[512,512]{1,0:T(8,128)(2,1)} %get-tuple-element.380.refs_1_, bf16[256,2048]{1,0:T(8,128)(2,1)} %get-tuple-element.381.refs_2_, bf16[512,2048]{1,0:T(8,128)(2,1)} %get-tuple-element.382.refs_3_, ...), custom_call_target="tpu_custom_call" | custom-call | flops 4194304 | bytes 94208 | tf_op jit(solution)/shard_map/row_grads/pallas_call | solution.py:789
  376.7 8.4 %row_grads.3 = (bf16[16,1408]{1,0:T(8,128)(2,1)}, bf16[16,2048]{1,0:T(8,128)(2,1)}) custom-call(bf16[256,1408]{1,0:T(8,128)(2,1)} %get-tuple-element.326.refs_1_.refs_0_, bf16[512,1408]{1,0:T(8,128)(2,1)} %get-tuple-element.325.refs_0_.refs_1_, bf16[256,2048]{1,0:T(8,128)(2,1)} %get-tuple-element.386.refs_2_, bf16[512,2048]{1,0:T(8,128)(2,1)} %get-tuple-element.387.refs_3_, ...), custom_call_target="tpu_custom_call" | custom-call | flops 11534336 | bytes 173056 | tf_op jit(solution)/shard_map/row_grads/pallas_call | solution.py:789
  387.9 10.4 %column_grads.3 = (bf16[3,16,512]{2,1,0:T(8,128)(2,1)}, bf16[48,2048]{1,0:T(8,128)(2,1)}) custom-call(bf16[256,2048]{1,0:T(8,128)(2,1)} %get-tuple-element.398.refs_0_, bf16[512,2048]{1,0:T(8,128)(2,1)} %get-tuple-element.399.refs_1_, bf16[256,1536]{1,0:T(8,128)(2,1)} %assemble.2.refs_0_.refs_2_, bf16[512,1536]{1,0:T(8,128)(2,1)} %assemble.3.refs_3_.refs_0_, ...), custom_call_target="tpu_custom_call" | custom-call | flops 12582912 | bytes 184320 | tf_op jit(solution)/shard_map/column_grads/pallas_call | solution.py:724
  400.5 5.7 %all-to-all-start.8 = ((bf16[8,16,2944]{2,1,0:T(8,128)(2,1)}), bf16[8,16,2944]{2,1,0:T(8,128)(2,1)S(1)}, u32[]{:S(2)}, u32[]{:S(2)}) async-start(bf16[8,16,2944]{2,1,0:T(8,128)(2,1)} %pack.1), calls=%async_computation.8 | async-start | bytes 1507328 | tf_op jit(solution)/shard_map/all_to_all | solution.py:65
  406.2 7.3 %project_split.9 = (bf16[128,2048]{1,0:T(8,128)(2,1)}, bf16[128,2048]{1,0:T(8,128)(2,1)}, bf16[2,128,2048]{2,1,0:T(8,128)(2,1)}) custom-call(bf16[512,1536]{1,0:T(8,128)(2,1)} %assemble.3.refs_3_.refs_0_, bf16[2048,1536]{1,0:T(8,128)(2,1)} %get-tuple-element.225.refs_4_.refs_1_), custom_call_target="tpu_custom_call" | custom-call | flops 50331648 | bytes 155648 | tf_op jit(solution)/shard_map/project_split/pallas_call | solution.py:456
  413.7 12.0 %all-to-all-done.8 = bf16[8,16,2944]{2,1,0:T(8,128)(2,1)S(1)} async-done(((bf16[8,16,2944]{2,1,0:T(8,128)(2,1)}), bf16[8,16,2944]{2,1,0:T(8,128)(2,1)S(1)}, u32[]{:S(2)}, u32[]{:S(2)}) %all-to-all-start.8) | async-done | bytes 753696 | tf_op jit(solution)/shard_map/all_to_all | solution.py:65
  437.3 7.0 %collective-permute-done.43 = bf16[4,32,2048]{2,1,0:T(8,128)(2,1)} collective-permute-done((bf16[4,32,2048]{2,1,0:T(8,128)(2,1)}, bf16[4,32,2048]{2,1,0:T(8,128)(2,1)}, u32[]{:S(2)}, u32[]{:S(2)}) %collective-permute-start.43) | collective-permute-done | bytes 524320 | tf_op jit(solution)/shard_map/ppermute | solution.py:36
  448.7 8.0 %all-to-all-done.9.refs_0_ = bf16[8,16,2944]{2,1,0:T(8,128)(2,1)} async-done(((bf16[8,16,2944]{2,1,0:T(8,128)(2,1)}), bf16[8,16,2944]{2,1,0:T(8,128)(2,1)}, u32[]{:S(2)}, u32[]{:S(2)}) %all-to-all-start.9) | async-done | bytes 753696 | tf_op jit(solution)/shard_map/all_to_all | solution.py:65
  (372 shorter events, 181.9 us)
Async XLA Ops:
  3.5 16.9 %collective-permute-start.1 = (bf16[2,32,2048]{2,1,0:T(8,128)(2,1)S(1)}, bf16[2,32,2048]{2,1,0:T(8,128)(2,1)S(1)}, u32[]{:S(2)}, u32[]{:S(2)}) collective-permute-start(bf16[2,32,2048]{2,1,0:T(8,128)(2,1)S(1)} %fusion.20), channel_id=1, source_target_pairs={{0,1},{1,0},{2,3},{3,2},{4,5},{5,4},{6,7},{7,6},{8,9},{9,8},{10,11... | collective-permute-start | bytes 786440 | tf_op jit(solution)/shard_map/ppermute | solution.py:36
  4.1 16.4 %collective-permute-start = (bf16[2,32,2048]{2,1,0:T(8,128)(2,1)S(1)}, bf16[2,32,2048]{2,1,0:T(8,128)(2,1)}, u32[]{:S(2)}, u32[]{:S(2)}) collective-permute-start(bf16[2,32,2048]{2,1,0:T(8,128)(2,1)S(1)} %fusion.20), channel_id=1, source_target_pairs={{0,2},{1,3},{2,0},{3,1},{4,6},{5,7},{6,4},{7,5},{8,10},{9,11},{10,... | collective-permute-start | bytes 786440 | tf_op jit(solution)/shard_map/ppermute | solution.py:36
  9.4 19.8 %collective-permute-start.4 = (bf16[4,32,2048]{2,1,0:T(8,128)(2,1)S(1)}, bf16[4,32,2048]{2,1,0:T(8,128)(2,1)S(1)}, u32[]{:S(2)}, u32[]{:S(2)}) collective-permute-start(bf16[4,32,2048]{2,1,0:T(8,128)(2,1)S(1)} %fusion.5), channel_id=1, source_target_pairs={{0,1},{1,0},{2,3},{3,2},{4,5},{5,4},{6,7},{7,6},{8,9},{9,8},{10,11... | collective-permute-start | bytes 1572872 | tf_op jit(solution)/shard_map/ppermute | solution.py:36
  9.6 19.6 %collective-permute-start.3 = (bf16[4,32,2048]{2,1,0:T(8,128)(2,1)S(1)}, bf16[4,32,2048]{2,1,0:T(8,128)(2,1)S(1)}, u32[]{:S(2)}, u32[]{:S(2)}) collective-permute-start(bf16[4,32,2048]{2,1,0:T(8,128)(2,1)S(1)} %fusion.5), channel_id=1, source_target_pairs={{0,2},{1,3},{2,0},{3,1},{4,6},{5,7},{6,4},{7,5},{8,10},{9,11},{10,... | collective-permute-start | bytes 1572872 | tf_op jit(solution)/shard_map/ppermute | solution.py:36
  29.2 26.6 %all-to-all-start = ((bf16[8,1,3,128,128]{4,3,2,1,0:T(8,128)(2,1)}), bf16[8,1,3,128,128]{4,3,2,1,0:T(8,128)(2,1)S(1)}, u32[]{:S(2)}, u32[]{:S(2)}) async-start(bf16[8,1,3,128,128]{4,3,2,1,0:T(8,128)(2,1)} %bitcast.224), calls=%async_computation | async-start | bytes 1572864 | tf_op jit(solution)/shard_map/all_to_all | solution.py:65
  36.0 9.6 %collective-permute-start.5 = (bf16[4,32,2048]{2,1,0:T(8,128)(2,1)S(1)}, bf16[4,32,2048]{2,1,0:T(8,128)(2,1)S(1)}, u32[]{:S(2)}, u32[]{:S(2)}) collective-permute-start(bf16[4,32,2048]{2,1,0:T(8,128)(2,1)S(1)} %collective-permute-done.3), channel_id=1, source_target_pairs={{0,1},{1,0},{2,3},{3,2},{4,5},{5,4},{6,7},{7,6},{8,9},{9,8},{10,11... | collective-permute-start | bytes 1572872 | tf_op jit(solution)/shard_map/ppermute | solution.py:36
  60.6 14.3 %all-to-all-start.1 = ((bf16[8,1,1,128,128]{4,3,2,1,0:T(8,128)(2,1)}), bf16[8,1,1,128,128]{4,3,2,1,0:T(8,128)(2,1)S(1)}, u32[]{:S(2)}, u32[]{:S(2)}) async-start(bf16[8,1,1,128,128]{4,3,2,1,0:T(8,128)(2,1)} %bitcast.222), calls=%async_computation.1 | async-start | bytes 524288 | tf_op jit(solution)/shard_map/all_to_all | solution.py:65
  75.6 8.7 %collective-permute-start.7 = (f32[2,2048]{1,0:T(2,128)S(1)}, f32[2,2048]{1,0:T(2,128)S(1)}, u32[]{:S(2)}, u32[]{:S(2)}) collective-permute-start(f32[2,2048]{1,0:T(2,128)S(1)} %pad_maximum_fusion.4), channel_id=1, source_target_pairs={{0,2},{1,3},{2,0},{3,1},{4,6},{5,7},{6,4},{7,5},{8,10},{9,11},{10,... | collective-permute-start | bytes 49160 | tf_op jit(solution)/shard_map/ppermute | solution.py:36
  78.4 43.9 %all-to-all-start.2 = ((bf16[8,2,3,128,128]{4,3,2,1,0:T(8,128)(2,1)}), bf16[8,2,3,128,128]{4,3,2,1,0:T(8,128)(2,1)S(1)}, u32[]{:S(2)}, u32[]{:S(2)}) async-start(bf16[8,2,3,128,128]{4,3,2,1,0:T(8,128)(2,1)} %bitcast.215), calls=%async_computation.2 | async-start | bytes 3145728 | tf_op jit(solution)/shard_map/all_to_all | solution.py:65
  92.9 26.8 %collective-permute-start.12 = (bf16[6,32,2048]{2,1,0:T(8,128)(2,1)S(1)}, bf16[6,32,2048]{2,1,0:T(8,128)(2,1)}, u32[]{:S(2)}, u32[]{:S(2)}) collective-permute-start(bf16[6,32,2048]{2,1,0:T(8,128)(2,1)S(1)} %get-tuple-element.289), channel_id=1, source_target_pairs={{0,1},{1,0},{2,3},{3,2},{4,5},{5,4},{6,7},{7,6},{8,9},{9,8},{10,11... | collective-permute-start | bytes 2359304 | tf_op jit(solution)/shard_map/ppermute | solution.py:36
  93.4 26.3 %collective-permute-start.11 = (bf16[6,32,2048]{2,1,0:T(8,128)(2,1)S(1)}, bf16[6,32,2048]{2,1,0:T(8,128)(2,1)}, u32[]{:S(2)}, u32[]{:S(2)}) collective-permute-start(bf16[6,32,2048]{2,1,0:T(8,128)(2,1)S(1)} %get-tuple-element.289), channel_id=1, source_target_pairs={{0,2},{1,3},{2,0},{3,1},{4,6},{5,7},{6,4},{7,5},{8,10},{9,11},{10,... | collective-permute-start | bytes 2359304 | tf_op jit(solution)/shard_map/ppermute | solution.py:36
  94.9 23.7 %collective-permute-start.10 = (bf16[2,32,2048]{2,1,0:T(8,128)(2,1)}, bf16[2,32,2048]{2,1,0:T(8,128)(2,1)}, u32[]{:S(2)}, u32[]{:S(2)}) collective-permute-start(bf16[2,32,2048]{2,1,0:T(8,128)(2,1)} %fusion.31), channel_id=1, source_target_pairs={{0,2},{1,3},{2,0},{3,1},{4,6},{5,7},{6,4},{7,5},{8,10},{9,11},{10,... | collective-permute-start | bytes 786440 | tf_op jit(solution)/shard_map/ppermute | solution.py:36
  122.5 8.8 %collective-permute-start.14 = (bf16[2,32,2048]{2,1,0:T(8,128)(2,1)S(1)}, bf16[2,32,2048]{2,1,0:T(8,128)(2,1)}, u32[]{:S(2)}, u32[]{:S(2)}) collective-permute-start(bf16[2,32,2048]{2,1,0:T(8,128)(2,1)S(1)} %multiply_convert_fusion.4), channel_id=1, source_target_pairs={{0,2},{1,3},{2,0},{3,1},{4,6},{5,7},{6,4},{7,5},{8,10},{9,11},{10,... | collective-permute-start | bytes 786440 | tf_op jit(solution)/shard_map/ppermute | solution.py:36
  131.2 22.4 %all-to-all-start.3 = ((bf16[8,2,1,128,128]{4,3,1,2,0:T(8,128)(2,1)}), bf16[8,2,1,128,128]{4,3,1,2,0:T(8,128)(2,1)S(1)}, u32[]{:S(2)}, u32[]{:S(2)}) async-start(bf16[8,2,1,128,128]{4,3,1,2,0:T(8,128)(2,1)} %bitcast.214), calls=%async_computation.3 | async-start | bytes 1048576 | tf_op jit(solution)/shard_map/all_to_all | solution.py:65
  163.4 17.3 %collective-permute-start.18 = (bf16[4,32,2048]{2,1,0:T(8,128)(2,1)S(1)}, bf16[4,32,2048]{2,1,0:T(8,128)(2,1)S(1)}, u32[]{:S(2)}, u32[]{:S(2)}) collective-permute-start(bf16[4,32,2048]{2,1,0:T(8,128)(2,1)S(1)} %fusion.17), channel_id=1, source_target_pairs={{0,2},{1,3},{2,0},{3,1},{4,6},{5,7},{6,4},{7,5},{8,10},{9,11},{10,... | collective-permute-start | bytes 1572872 | tf_op jit(solution)/shard_map/ppermute | solution.py:36
  186.6 9.2 %collective-permute-start.23 = (bf16[2,32,2048]{2,1,0:T(8,128)(2,1)S(1)}, bf16[2,32,2048]{2,1,0:T(8,128)(2,1)S(1)}, u32[]{:S(2)}, u32[]{:S(2)}) collective-permute-start(bf16[2,32,2048]{2,1,0:T(8,128)(2,1)S(1)} %fusion.27), channel_id=1, source_target_pairs={{0,2},{1,3},{2,0},{3,1},{4,6},{5,7},{6,4},{7,5},{8,10},{9,11},{10,... | collective-permute-start | bytes 786440 | tf_op jit(solution)/shard_map/ppermute | solution.py:36
  187.2 20.0 %collective-permute-start.19 = (bf16[4,32,2048]{2,1,0:T(8,128)(2,1)S(1)}, bf16[4,32,2048]{2,1,0:T(8,128)(2,1)}, u32[]{:S(2)}, u32[]{:S(2)}) collective-permute-start(bf16[4,32,2048]{2,1,0:T(8,128)(2,1)S(1)} %multiply_convert_fusion.2), channel_id=1, source_target_pairs={{0,2},{1,3},{2,0},{3,1},{4,6},{5,7},{6,4},{7,5},{8,10},{9,11},{10,... | collective-permute-start | bytes 1572872 | tf_op jit(solution)/shard_map/ppermute | solution.py:36
  198.3 13.6 %collective-permute-start.24 = (bf16[2,32,2048]{2,1,0:T(8,128)(2,1)S(1)}, bf16[2,32,2048]{2,1,0:T(8,128)(2,1)S(1)}, u32[]{:S(2)}, u32[]{:S(2)}) collective-permute-start(bf16[2,32,2048]{2,1,0:T(8,128)(2,1)S(1)} %multiply_convert_fusion.3), channel_id=1, source_target_pairs={{0,2},{1,3},{2,0},{3,1},{4,6},{5,7},{6,4},{7,5},{8,10},{9,11},{10,... | collective-permute-start | bytes 786440 | tf_op jit(solution)/shard_map/ppermute | solution.py:36
  207.2 10.5 %collective-permute-start.21 = (bf16[4,32,2048]{2,1,0:T(8,128)(2,1)}, bf16[4,32,2048]{2,1,0:T(8,128)(2,1)S(1)}, u32[]{:S(2)}, u32[]{:S(2)}) collective-permute-start(bf16[4,32,2048]{2,1,0:T(8,128)(2,1)} %collective-permute-done.19), channel_id=1, source_target_pairs={{0,1},{1,0},{2,3},{3,2},{4,5},{5,4},{6,7},{7,6},{8,9},{9,8},{10,11... | collective-permute-start | bytes 1572872 | tf_op jit(solution)/shard_map/ppermute | solution.py:36
  218.6 28.4 %all-to-all-start.4 = ((bf16[8,1,1,128,128]{4,3,2,1,0:T(8,128)(2,1)}), bf16[8,1,1,128,128]{4,3,2,1,0:T(8,128)(2,1)S(1)}, u32[]{:S(2)}, u32[]{:S(2)}) async-start(bf16[8,1,1,128,128]{4,3,2,1,0:T(8,128)(2,1)} %bitcast.255), calls=%async_computation.4 | async-start | bytes 524288 | tf_op jit(solution)/shard_map/all_to_all | solution.py:65
  262.7 14.3 %collective-permute-start.28 = (bf16[4,32,2048]{2,1,0:T(8,128)(2,1)}, bf16[4,32,2048]{2,1,0:T(8,128)(2,1)}, u32[]{:S(2)}, u32[]{:S(2)}) collective-permute-start(bf16[4,32,2048]{2,1,0:T(8,128)(2,1)} %fusion.15), channel_id=1, source_target_pairs={{0,2},{1,3},{2,0},{3,1},{4,6},{5,7},{6,4},{7,5},{8,10},{9,11},{10,... | collective-permute-start | bytes 1572872 | tf_op jit(solution)/shard_map/ppermute | solution.py:36
  268.6 27.5 %all-to-all-start.5 = ((bf16[8,1,3,128,128]{4,3,2,1,0:T(8,128)(2,1)}), bf16[8,1,3,128,128]{4,3,2,1,0:T(8,128)(2,1)}, u32[]{:S(2)}, u32[]{:S(2)}) async-start(bf16[8,1,3,128,128]{4,3,2,1,0:T(8,128)(2,1)} %get-tuple-element.332), calls=%async_computation.5 | async-start | bytes 1572864 | tf_op jit(solution)/shard_map/all_to_all | solution.py:65
  281.5 9.2 %collective-permute-start.30 = (bf16[4,32,2048]{2,1,0:T(8,128)(2,1)}, bf16[4,32,2048]{2,1,0:T(8,128)(2,1)}, u32[]{:S(2)}, u32[]{:S(2)}) collective-permute-start(bf16[4,32,2048]{2,1,0:T(8,128)(2,1)} %multiply_convert_fusion.1), channel_id=1, source_target_pairs={{0,1},{1,0},{2,3},{3,2},{4,5},{5,4},{6,7},{7,6},{8,9},{9,8},{10,11... | collective-permute-start | bytes 1572872 | tf_op jit(solution)/shard_map/ppermute | solution.py:36
  281.5 14.7 %collective-permute-start.29 = (bf16[4,32,2048]{2,1,0:T(8,128)(2,1)}, bf16[4,32,2048]{2,1,0:T(8,128)(2,1)}, u32[]{:S(2)}, u32[]{:S(2)}) collective-permute-start(bf16[4,32,2048]{2,1,0:T(8,128)(2,1)} %multiply_convert_fusion.1), channel_id=1, source_target_pairs={{0,2},{1,3},{2,0},{3,1},{4,6},{5,7},{6,4},{7,5},{8,10},{9,11},{10,... | collective-permute-start | bytes 1572872 | tf_op jit(solution)/shard_map/ppermute | solution.py:36
  303.3 20.9 %all-to-all-start.6 = ((bf16[8,2,1,128,128]{4,3,1,2,0:T(8,128)(2,1)}), bf16[8,2,1,128,128]{4,3,1,2,0:T(8,128)(2,1)}, u32[]{:S(2)}, u32[]{:S(2)}) async-start(bf16[8,2,1,128,128]{4,3,1,2,0:T(8,128)(2,1)} %bitcast.241), calls=%async_computation.6 | async-start | bytes 1048576 | tf_op jit(solution)/shard_map/all_to_all | solution.py:65
  333.1 52.0 %all-to-all-start.7 = ((bf16[8,2,3,128,128]{4,3,2,1,0:T(8,128)(2,1)}), bf16[8,2,3,128,128]{4,3,2,1,0:T(8,128)(2,1)}, u32[]{:S(2)}, u32[]{:S(2)}) async-start(bf16[8,2,3,128,128]{4,3,2,1,0:T(8,128)(2,1)} %get-tuple-element.359), calls=%async_computation.7 | async-start | bytes 3145728 | tf_op jit(solution)/shard_map/all_to_all | solution.py:65
  340.7 22.1 %collective-permute-start.36 = (bf16[6,32,2048]{2,1,0:T(8,128)(2,1)}, bf16[6,32,2048]{2,1,0:T(8,128)(2,1)}, u32[]{:S(2)}, u32[]{:S(2)}) collective-permute-start(bf16[6,32,2048]{2,1,0:T(8,128)(2,1)} %fusion.2), channel_id=1, source_target_pairs={{0,2},{1,3},{2,0},{3,1},{4,6},{5,7},{6,4},{7,5},{8,10},{9,11},{10,... | collective-permute-start | bytes 2359304 | tf_op jit(solution)/shard_map/ppermute | solution.py:36
  343.5 24.7 %collective-permute-start.41 = (bf16[2,32,2048]{2,1,0:T(8,128)(2,1)}, bf16[2,32,2048]{2,1,0:T(8,128)(2,1)}, u32[]{:S(2)}, u32[]{:S(2)}) collective-permute-start(bf16[2,32,2048]{2,1,0:T(8,128)(2,1)} %fusion.25), channel_id=1, source_target_pairs={{0,2},{1,3},{2,0},{3,1},{4,6},{5,7},{6,4},{7,5},{8,10},{9,11},{10,... | collective-permute-start | bytes 786440 | tf_op jit(solution)/shard_map/ppermute | solution.py:36
  400.5 25.2 %all-to-all-start.8 = ((bf16[8,16,2944]{2,1,0:T(8,128)(2,1)}), bf16[8,16,2944]{2,1,0:T(8,128)(2,1)S(1)}, u32[]{:S(2)}, u32[]{:S(2)}) async-start(bf16[8,16,2944]{2,1,0:T(8,128)(2,1)} %pack.1), calls=%async_computation.8 | async-start | bytes 1507328 | tf_op jit(solution)/shard_map/all_to_all | solution.py:65
  413.5 14.5 %collective-permute-start.42 = (bf16[2,4,32,2048]{3,2,1,0:T(8,128)(2,1)}, bf16[2,4,32,2048]{3,2,1,0:T(8,128)(2,1)}, u32[]{:S(2)}, u32[]{:S(2)}) collective-permute-start(bf16[2,4,32,2048]{3,2,1,0:T(8,128)(2,1)} %bitcast.284), channel_id=1, source_target_pairs={{0,1},{1,0},{2,3},{3,2},{4,5},{5,4},{6,7},{7,6},{8,9},{9,8},{10,11... | collective-permute-start | bytes 3145736 | tf_op jit(solution)/shard_map/ppermute | solution.py:36
  430.1 14.1 %collective-permute-start.43 = (bf16[4,32,2048]{2,1,0:T(8,128)(2,1)}, bf16[4,32,2048]{2,1,0:T(8,128)(2,1)}, u32[]{:S(2)}, u32[]{:S(2)}) collective-permute-start(bf16[4,32,2048]{2,1,0:T(8,128)(2,1)} %fusion.10), channel_id=1, source_target_pairs={{0,2},{1,3},{2,0},{3,1},{4,6},{5,7},{6,4},{7,5},{8,10},{9,11},{10,... | collective-permute-start | bytes 1572872 | tf_op jit(solution)/shard_map/ppermute | solution.py:36
  432.6 24.1 %all-to-all-start.9 = ((bf16[8,16,2944]{2,1,0:T(8,128)(2,1)}), bf16[8,16,2944]{2,1,0:T(8,128)(2,1)}, u32[]{:S(2)}, u32[]{:S(2)}) async-start(bf16[8,16,2944]{2,1,0:T(8,128)(2,1)} %broadcast_in_dim.205), calls=%async_computation.9 | async-start | bytes 1507328 | tf_op jit(solution)/shard_map/all_to_all | solution.py:65
  (103 other events, 690.5 us)

commit v3 on v2

--- a/solution.py
+++ b/solution.py
@@ -897,17 +897,12 @@
     normed_a, d_qkv, pairs, outputs, totals, att = [[None] * 2 for _ in range(6)]
     laid, normed_a[0] = to_heads(gather_end(*started[0]), qkv_w)
 
-    laid, started[1], w_out = after(laid, started[1], w_out)
+    laid, started[1], w_out, w_down = after(laid, started[1], w_out, w_down)
     pairs[0] = send_pairs(laid, 0)
     laid, normed_a[1] = to_heads(gather_end(*started[1]), qkv_w)
+    down_w, down_cross, down_square = row_prep(w_down, a_down, b_down, 256)
     out_w, out_cross, out_square = row_prep(w_out, a_out, b_out, 512)
-    pairs[0], laid, out_square, w_down = after(pairs[0], laid, out_square, w_down)
-
-    outputs[0], totals[0] = attend(pairs[0], tables, kpos, qinfo[0])
-    outputs[0], w_down = after(outputs[0], w_down)
-    fetched = fetch_pairs(outputs[0][:, :, None], 0)
-    down_w, down_cross, down_square = row_prep(w_down, a_down, b_down, 256)
-    fetched, laid, down_square = after(fetched, laid, down_square)
+    pairs[0], laid, down_square, out_square, w_gateup = after(pairs[0], laid, down_square, out_square, w_gateup)
 
     u_out, middle, hidden, d_gu, gu_sum, normed_f, d_mid, du_out, dhid, du_down = [[None] * 2 for _ in range(10)]
 
@@ -915,83 +910,85 @@
         return project_cotangent(whole, down_w, cuts[c].stop - cuts[c].start, cuts[c].start)
 
     pairs[1] = send_pairs(laid, 1)
+    outputs[0], totals[0] = attend(pairs[0], tables, kpos, qinfo[0])
     squares = tensor_sum(jnp.concatenate([down_square, out_square]))
-    fetched, squares = after(fetched, squares)
     down_square, out_square = squares[0:1], squares[1:2]
     down_scale, out_scale = m_down / jnp.sqrt(squares[0]), m_out / jnp.sqrt(squares[1])
+    scaled, w_gateup = after((cot * down_scale).astype(bf16), w_gateup)
+    gu_w, gu_stat, gu_cross = column_prep(w_gateup, a_gateup, b_gateup, m_gateup, LANES, True)
+    started, gu_w = after(gather_start(scaled), gu_w)
+    whole_cot = gather_end(*started)
+    dhid[0], du_down[0] = of_cotangent(whole_cot, 0)
+    pairs[1], outputs[0], dhid[0] = after(pairs[1], outputs[0], dhid[0])
+
+    fetched = fetch_pairs(outputs[0][:, :, None], 0)
+    outputs[1], totals[1] = attend(pairs[1], tables, kpos, qinfo[1])
+    fetched, outputs[1], whole_cot = after(fetched, outputs[1], whole_cot)
+
+    returned = fetch_pairs(outputs[1][:, :, None], 1)
     att[0], split = project_from_pairs(fetched, out_w, 512)
-    moving, scaled, w_gateup = after(scatter_start(*split), (cot * down_scale).astype(bf16), w_gateup)
-    tail, started = scatter_end(*moving), gather_start(scaled)
-    gu_w, gu_stat, gu_cross = column_prep(w_gateup, a_gateup, b_gateup, m_gateup, LANES, True)
-    tail, started, gu_w = after(tail, started, gu_w)
+    moving, whole_cot = after(scatter_start(*split), whole_cot)
+    dhid[1], du_down[1] = of_cotangent(whole_cot, 1)
+    tail, dhid[1] = after(scatter_end(*moving), dhid[1])
     u_out[0] = tail * out_scale
     middle[0] = wide_in[0] + u_out[0]
-    h_f, whole_cot = after(normed(middle[0], gain_ffn), gather_end(*started))
-    pairs[1], h_f = after(pairs[1], h_f)
-    outputs[1], totals[1] = attend(pairs[1], tables, kpos, qinfo[1])
-    started, outputs[1] = after(gather_start(h_f), outputs[1])
-
-    fetched = fetch_pairs(outputs[1][:, :, None], 1)
-    dhid[0], du_down[0] = of_cotangent(whole_cot, 0)
-    hidden[0], d_gu[0], gu_sum[0], normed_f[0] = gated(gather_end(*started), gu_w, dhid[0])
-    d_gu[0], fetched = after(d_gu[0], fetched)
-
-    att[1], split = project_from_pairs(fetched, out_w, 512)
-    moving, d_gu[0], whole_cot = after(scatter_start(*split), d_gu[0], whole_cot)
-    split = project_split([d_gu[0]], gu_w, NT, 512, quarter)
-    dhid[1], du_down[1] = of_cotangent(whole_cot, 1)
-    tail, split, dhid[1] = after(scatter_end(*moving), split, dhid[1])
+    started = gather_start(normed(middle[0], gain_ffn))
+
+    att[1], split = project_from_pairs(returned, out_w, 512)
+    started, split = after(started, split)
+    moving, whole = after(scatter_start(*split), gather_end(*started))
+    hidden[0], d_gu[0], gu_sum[0], normed_f[0] = gated(whole, gu_w, dhid[0])
+    tail, d_gu[0] = after(scatter_end(*moving), d_gu[0])
     u_out[1] = tail * out_scale
     middle[1] = wide_in[1] + u_out[1]
-    h_f, split = after(normed(middle[1], gain_ffn), split)
-    shard, far, near = gather_start(h_f)
-    near, split = after(near, split)
-    started = (shard, far, near)
-    d_mid[0] = cot[cuts[0]] + norm_back(middle[0], gain_ffn, scatter_end(*scatter_start(*split)))
-    behind = gather_start((d_mid[0] * out_scale).astype(bf16))
-    d_att, du_out[0] = back_to_heads(gather_end(*behind), out_w)
-    whole, d_att = after(gather_end(*started), d_att)
-
+    h_f, d_gu[0] = after(normed(middle[1], gain_ffn), d_gu[0])
+    started = gather_start(h_f)
+    split = project_split([d_gu[0]], gu_w, NT, 512, quarter)
+    whole, behind = after(gather_end(*started), scatter_start(*split))
+
+    hidden[1], d_gu[1], gu_sum[1], normed_f[1] = gated(whole, gu_w, dhid[1])
+    tail, d_gu[1] = after(scatter_end(*behind), d_gu[1])
+    d_mid[0] = cot[cuts[0]] + norm_back(middle[0], gain_ffn, tail)
+    scaled, d_gu[1] = after((d_mid[0] * out_scale).astype(bf16), d_gu[1])
+    started, split = after(gather_start(scaled), project_split([d_gu[1]], gu_w, NT, 512, quarter))
+    moving, whole = after(scatter_start(*split), gather_end(*started))
+
+    d_att, du_out[0] = back_to_heads(whole, out_w)
     d_outputs = send_pairs(d_att, 0)[:, :, 0]
-    hidden[1], d_gu[1], gu_sum[1], normed_f[1] = gated(whole, gu_w, dhid[1])
-    d_gu[1], d_outputs = after(d_gu[1], d_outputs)
-    moving, d_outputs = after(scatter_start(*project_split([d_gu[1]], gu_w, NT, 512, quarter)), d_outputs)
+    tail, d_att = after(scatter_end(*moving), d_att)
+    d_mid[1] = cot[cuts[1]] + norm_back(middle[1], gain_ffn, tail)
+    scaled, d_outputs = after((d_mid[1] * out_scale).astype(bf16), d_outputs)
     d_pairs, pair_sums = [None] * 2, [None] * 2
     d_pairs[0], pair_sums[0] = attend_back(pairs[0], outputs[0], d_outputs, totals[0], tables, kpos, qinfo[0])
+    d_pairs[0], scaled, hidden = after(d_pairs[0], scaled, hidden)
     fetched = fetch_pairs(d_pairs[0], 0)
-    d_mid[1] = cot[cuts[1]] + norm_back(middle[1], gain_ffn, scatter_end(*moving))
-    scaled, hidden = after((d_mid[1] * out_scale).astype(bf16), hidden)
-    split = project_split(hidden[::-1], down_w, NN, 512, quarter)
-    started, split, fetched = after(gather_start(scaled), split, fetched)
+    started, split = after(gather_start(scaled), project_split(hidden[::-1], down_w, NN, 512, quarter))
     d_att, du_out[1] = back_to_heads(gather_end(*started), out_w)
-
-    d_att, fetched, out_sum = after(d_att, fetched, sum(jnp.sum(u_out[c] * d_mid[c], axis=(0, 1)) for c in span)[None])
+    d_att, fetched = after(d_att, fetched)
+
+    d_att, att, out_sum = after(d_att, att, sum(jnp.sum(u_out[c] * d_mid[c], axis=(0, 1)) for c in span)[None])
     d_outputs = send_pairs(d_att, 1)[:, :, 0]
-    out_sum, fetched = after(tensor_sum(out_sum), fetched)
-    d_qkv[0] = assemble(fetched)
-    split_in = [project_split([d_qkv[0]], qkv_w, NT, 512, quarter), None]
-    d_outputs, split_in[0], out_sum, d_gu = after(d_outputs, split_in[0], out_sum, d_gu)
+    out_sum = tensor_sum(out_sum)
+    grad_a_out, grad_b_out = row_grads(att, du_out, out_w, a_out, b_out, out_cross, -out_sum / out_square, 512)
+    d_outputs, grad_a_out, d_gu = after(d_outputs, grad_a_out, d_gu)
     d_pairs[1], pair_sums[1] = attend_back(pairs[1], outputs[1], d_outputs, totals[1], tables, kpos, qinfo[1])
 
-    d_pairs[1], split, att, d_gu, split_in[0] = after(d_pairs[1], split, att, d_gu, split_in[0])
-    fetched = fetch_pairs(d_pairs[1], 1)
+    d_pairs[1], split, d_gu = after(d_pairs[1], split, d_gu)
+    returned = fetch_pairs(d_pairs[1], 1)
     moving, d_gu = after(scatter_start(*split), d_gu)
     gu_sums = sum(gu_sum)
     grad_a_gu, grad_b_gu = column_grads(
         normed_f, d_gu, gu_w, a_gateup, b_gateup, gu_stat, m_gateup, gu_sums, gu_cross, LANES
     )
-    tail, grad_a_gu, att = after(scatter_end(*moving), grad_a_gu, att)
+    tail, grad_a_gu, fetched = after(scatter_end(*moving), grad_a_gu, fetched)
     u_down = tail * down_scale
     layer_out = (jnp.concatenate(middle[::-1]) + u_down).astype(bf16)
     down_sum = tensor_sum(jnp.sum(u_down * cot, axis=(0, 1))[None])
-    grad_a_out, grad_b_out = row_grads(att, du_out, out_w, a_out, b_out, out_cross, -out_sum / out_square, 512)
+    d_qkv[0] = assemble(fetched)
     grad_a_down, grad_b_down = row_grads(
         hidden, du_down, down_w, a_down, b_down, down_cross, -down_sum / down_square, 512
     )
-    grad_norm_a = [scatter_end(*scatter_start(*split_in[0])), None]
-    fetched, grad_a_out, grad_a_down, layer_out, grad_norm_a[0] = after(
-        fetched, grad_a_out, grad_a_down, layer_out, grad_norm_a[0]
-    )
+    fetched, d_qkv[0], grad_a_down, layer_out = after(returned, d_qkv[0], grad_a_down, layer_out)
     d_qkv[1] = assemble(fetched)
 
     qkv_sums = 0.0
@@ -1008,17 +1005,15 @@
     vectors = [gu_sums, out_sum[None], down_sum[None], qkv_sums]
     plan = packing(over_all, over_seq, width, seq, rank)
     cut = plan[0][1]
-    packed, d_qkv[1] = after(pack(plan, over_all + over_seq, vectors, seq, rank, width), d_qkv[1])
-    added = exchange(packed)
-    split_in[1] = project_split([d_qkv[1]], qkv_w, NT, 512, quarter)
-    grad_norm_a[1] = scatter_end(*scatter_start(*split_in[1]))
-    grad_in = jnp.concatenate(
-        [d_mid[c] + norm_back(wide_in[c], gain_attn, grad_norm_a[c]) for c in reversed(span)]
-    )
+    packed, d_qkv = after(pack(plan, over_all + over_seq, vectors, seq, rank, width), d_qkv)
+    added, split = after(exchange(packed), project_split(d_qkv[::-1], qkv_w, NT, 512, quarter))
+    moving = scatter_start(*split)
     added = jnp.sum(added.astype(f32), axis=0).astype(bf16)
     shared = added[:, :cut]
     shared = shared.astype(f32) + swap(shared, 1).astype(f32) + swap(shared, 2).astype(f32) + swap(shared, 3).astype(f32)
-    back = seq_gather(jnp.concatenate([shared.astype(bf16), added[:, cut:]], axis=1))
+    joined, moving = after(jnp.concatenate([shared.astype(bf16), added[:, cut:]], axis=1), moving)
+    back = seq_gather(joined)
+    grad_in = jnp.concatenate(d_mid[::-1]) + norm_back(layer_in.astype(f32), gain_attn, scatter_end(*moving))
     g_a_gu, g_b_out, g_b_down, g_a_qkv, g_b_gu, g_a_out, g_a_down, g_b_qkv, s_gu, s_out, s_down, s_qkv = unpack(
         plan, back, over_all + over_seq, [m_gateup, m_out[None], m_down[None], m_qkv]
     )

time: 466 us -> 439 us (0.942)
  starting transfers between devices: 90.5 us -> 74.5 us
  waiting for transfers between devices: 81.6 us -> 74.8 us
    all_to_all x10, starting transfers between devices: 63.7 us -> 51.1 us  [exchange(): return lax.all_to_all(values, 'seq', 0, 0, tiled=True)]
    ppermute x47 -> x45, waiting for transfers between devices: 56.5 us -> 50.6 us  [swap(): return lax.ppermute(values, 'tensor', [(i, i ^ bit) for i in range(size)])]
    pallas_call x5 -> x4, Pallas kernels: 40.1 us -> 35.9 us  [project_split(): pl.pallas_call(partial(project_split_kernel, dims=dims), grid=(out // blo...]
    ppermute x47 -> x45, starting transfers between devices: 26.8 us -> 23.4 us  [swap(): return lax.ppermute(values, 'tensor', [(i, i ^ bit) for i in range(size)])]
    unnamed x158 -> x102, local copies, waits for them, and re-layouts: 9.86 us -> 10.6 us
    convert_element_type x7 -> x6, other arithmetic: 9.84 us -> 10.5 us  [scatter_start(): return (kept, got, (near.astype(f32) + got[1].astype(f32)).astype(bf16))]
  transfers between devices with their start and end apart: 57 -> 55, of which waited for: 25 -> 21; matrix products, arithmetic and copies ran while one was open for 10% -> 9% of each run, Pallas kernels for 38% -> 43%
where the time goes in v3:
time: 439 us; the launch traced here: 431 us
  Pallas kernels  220 us (50%)
  waiting for transfers between devices  74.8 us (17%)
  starting transfers between devices  74.5 us (17%)
  other arithmetic  44.5 us (10%)
  local copies, waits for them, and re-layouts  15.3 us (3%)
    all_to_all x10, starting transfers between devices, exchange(): return lax.all_to_all(values, 'seq', 0, 0, tiled=True)  51.1 us
    ppermute x45, waiting for transfers between devices, swap(): return lax.ppermute(values, 'tensor', [(i, i ^ bit) for i in range(size)])  50.6 us
    pallas_call x4, Pallas kernels, project_split(): pl.pallas_call(partial(project_split_kernel, dims=dims), grid=(out // blo...  35.9 us
    pallas_call x2, Pallas kernels, column_grads(): pl.pallas_call(partial(column_grads_kernel, chunks=chunks, steps=steps),...  28.3 us
    pallas_call x2, Pallas kernels, column_prep(): pl.pallas_call(column_prep_kernel, grid=(out // block,), in_specs=[pl.Blo...  25.5 us
    all_to_all x10, waiting for transfers between devices, exchange(): return lax.all_to_all(values, 'seq', 0, 0, tiled=True)  24.3 us
    pallas_call x2, Pallas kernels, gated(): pl.pallas_call(gated_kernel, grid=(-(-out // block),), in_specs=[pl.Block...  24 us
    ppermute x45, starting transfers between devices, swap(): return lax.ppermute(values, 'tensor', [(i, i ^ bit) for i in range(size)])  23.4 us
  transfers between devices with their start and end apart: 55, of which 21 were waited for; matrix products, arithmetic and copies ran while one was open for 9% of the time, Pallas kernels for 43%

profile of v3, /device:TPU:0, one launch (start us, length us, event | category | flops | bytes accessed | tf_op | source)
XLA Modules:
  0.0 430.6 jit_solution(3603007240162734514)
XLA Ops:
  10.4 8.9 %column_prep.2 = (bf16[2048,1536]{1,0:T(8,128)(2,1)}, f32[3,2,512]{2,1,0:T(2,128)}, f32[3,16,512]{2,1,0:T(8,128)}) custom-call(bf16[3,2048,512]{2,1,0:T(8,128)(2,1)} %w_ref.1, bf16[48,2048]{1,0:T(8,128)(2,1)} %bitcast.195, bf16[2,48,768]{2,1,0:T(8,128)(2,1)} %broadcast_multiply_fusion.1.b_ref, f32[3,1,512]{2,1,0:T(1,128)} %broadcast_in_dim.103.m_ref.refs_8_), custom_call_target="tpu_custom_call" | custom-call | flops 50331648 | bytes 196608 | tf_op jit(solution)/shard_map/column_prep/pallas_call | solution.py:103
  21.8 6.1 %project_to_pairs.4 = (bf16[2,4,3,4,32,128]{5,4,3,2,1,0:T(8,128)(2,1)}, bf16[256,2048]{1,0:T(8,128)(2,1)}) custom-call(bf16[64,2048]{1,0:T(8,128)(2,1)} %bitcast.188, bf16[64,2048]{1,0:T(8,128)(2,1)} %bitcast.4.refs_1_, bf16[64,2048]{1,0:T(8,128)(2,1)} %bitcast.210, bf16[64,2048]{1,0:T(8,128)(2,1)} %bitcast.217, ...), custom_call_target="tpu_custom_call" | custom-call | flops 25165824 | bytes 131072 | tf_op jit(solution)/shard_map/project_to_pairs/pallas_call | solution.py:358
  28.9 6.1 %all-to-all-start = ((bf16[8,1,3,128,128]{4,3,2,1,0:T(8,128)(2,1)}), bf16[8,1,3,128,128]{4,3,2,1,0:T(8,128)(2,1)S(1)}, u32[]{:S(2)}, u32[]{:S(2)}) async-start(bf16[8,1,3,128,128]{4,3,2,1,0:T(8,128)(2,1)} %bitcast.191), calls=%async_computation | async-start | bytes 1572864 | tf_op jit(solution)/shard_map/all_to_all | solution.py:65
  39.9 8.9 %row_prep.2 = (bf16[1408,2048]{1,0:T(8,128)(2,1)}, f32[16,2048]{1,0:T(8,128)}, f32[1,2048]{1,0:T(1,128)}) custom-call(bf16[1408,2048]{1,0:T(8,128)(2,1)} %w_ref.2, bf16[16,1408]{1,0:T(8,128)(2,1)} %bitcast.220, bf16[16,2048]{1,0:T(8,128)(2,1)} %refs_6_.6), custom_call_target="tpu_custom_call" | custom-call | flops 23068672 | bytes 180224 | tf_op jit(solution)/shard_map/row_prep/pallas_call | solution.py:141
  49.7 8.2 %project_to_pairs.5 = (bf16[4,4,3,4,32,128]{5,4,3,2,1,0:T(8,128)(2,1)}, bf16[512,2048]{1,0:T(8,128)(2,1)}) custom-call(bf16[128,2048]{1,0:T(8,128)(2,1)} %bitcast.184, bf16[128,2048]{1,0:T(8,128)(2,1)} %bitcast.200, bf16[128,2048]{1,0:T(8,128)(2,1)} %bitcast.199, bf16[128,2048]{1,0:T(8,128)(2,1)} %bitcast.203, ...), custom_call_target="tpu_custom_call" | custom-call | flops 50331648 | bytes 163840 | tf_op jit(solution)/shard_map/project_to_pairs/pallas_call | solution.py:358
  60.9 6.3 %all-to-all-start.1 = ((bf16[8,2,3,128,128]{4,3,2,1,0:T(8,128)(2,1)}), bf16[8,2,3,128,128]{4,3,2,1,0:T(8,128)(2,1)S(1)}, u32[]{:S(2)}, u32[]{:S(2)}) async-start(bf16[8,2,3,128,128]{4,3,2,1,0:T(8,128)(2,1)} %bitcast.187), calls=%async_computation.1 | async-start | bytes 3145728 | tf_op jit(solution)/shard_map/all_to_all | solution.py:65
  73.3 16.6 %column_prep.3 = (bf16[2048,2816]{1,0:T(8,128)(2,1)}, f32[2,2,1408]{2,1,0:T(2,128)}, f32[2,16,1408]{2,1,0:T(8,128)}) custom-call(bf16[2,2048,1408]{2,1,0:T(8,128)(2,1)} %w_ref.4, bf16[32,2048]{1,0:T(8,128)(2,1)} %bitcast.197, bf16[11,32,256]{2,1,0:T(8,128)(2,1)} %broadcast_multiply_fusion.b_ref, f32[2,1,1408]{2,1,0:T(1,128)} %broadcast_in_dim.107.m_ref.refs_8_), custom_call_target="tpu_custom_call" | custom-call | flops 92274688 | bytes 360448 | tf_op jit(solution)/shard_map/column_prep/pallas_call | solution.py:103
  100.8 5.7 %project_cotangent.2 = (bf16[256,1408]{1,0:T(8,128)(2,1)}, bf16[256,2048]{1,0:T(8,128)(2,1)}) custom-call(bf16[192,2048]{1,0:T(8,128)(2,1)} %bitcast.177, bf16[192,2048]{1,0:T(8,128)(2,1)} %bitcast.27.refs_1_, bf16[192,2048]{1,0:T(8,128)(2,1)} %bitcast.28.refs_2_, bf16[192,2048]{1,0:T(8,128)(2,1)} %bitcast.179, ...), custom_call_target="tpu_custom_call" | custom-call | flops 23068672 | bytes 122880 | tf_op jit(solution)/shard_map/project_cotangent/pallas_call | solution.py:483
  106.5 6.0 %all-to-all-start.2 = ((bf16[8,1,1,128,128]{4,3,2,1,0:T(8,128)(2,1)}), bf16[8,1,1,128,128]{4,3,2,1,0:T(8,128)(2,1)S(1)}, u32[]{:S(2)}, u32[]{:S(2)}) async-start(bf16[8,1,1,128,128]{4,3,2,1,0:T(8,128)(2,1)} %bitcast.31), calls=%async_computation.2 | async-start | bytes 524288 | tf_op jit(solution)/shard_map/all_to_all | solution.py:65
  113.3 5.7 %attend.3 = (bf16[8,2,128,128]{3,2,1,0:T(8,128)(2,1)}, f32[2,1,1024]{2,1,0:T(1,128)}) custom-call(bf16[8,2,3,128,128]{4,3,2,1,0:T(8,128)(2,1)} %copy-done.1, f32[1024,128]{1,0:T(8,128)} %get-tuple-element.470.cos_ref, f32[1024,128]{1,0:T(8,128)} %get-tuple-element.471.sin_ref, s32[1024,1]{1,0:T(8,128)} %copy.57.kpos_ref, s32[2,2,1024]{2,1,0:T(2,128)} %pad_add_fusion.qinfo_ref), custom_call_target="tpu_custom_call" | custom-call | flops 16777216 | bytes 32768 | tf_op jit(solution)/shard_map/attend/pallas_call | solution.py:209
  135.7 7.9 %project_cotangent.3 = (bf16[512,1408]{1,0:T(8,128)(2,1)}, bf16[512,2048]{1,0:T(8,128)(2,1)}) custom-call(bf16[192,2048]{1,0:T(8,128)(2,1)} %bitcast.178, bf16[192,2048]{1,0:T(8,128)(2,1)} %bitcast.39.refs_1_, bf16[192,2048]{1,0:T(8,128)(2,1)} %bitcast.40.refs_2_, bf16[192,2048]{1,0:T(8,128)(2,1)} %bitcast.180, ...), custom_call_target="tpu_custom_call" | custom-call | flops 46137344 | bytes 155648 | tf_op jit(solution)/shard_map/project_cotangent/pallas_call | solution.py:483
  145.5 4.7 %all-to-all-done.3 = bf16[8,2,1,128,128]{4,3,1,2,0:T(8,128)(2,1)S(1)} async-done(((bf16[8,2,1,128,128]{4,3,1,2,0:T(8,128)(2,1)}), bf16[8,2,1,128,128]{4,3,1,2,0:T(8,128)(2,1)S(1)}, u32[]{:S(2)}, u32[]{:S(2)}) %all-to-all-start.3) | async-done | bytes 524320 | tf_op jit(solution)/shard_map/all_to_all | solution.py:65
  151.0 4.7 %project_from_pairs.3 = (bf16[512,512]{1,0:T(8,128)(2,1)}, bf16[128,2048]{1,0:T(8,128)(2,1)}, bf16[128,2048]{1,0:T(8,128)(2,1)}, bf16[2,128,2048]{2,1,0:T(8,128)(2,1)}) custom-call(bf16[4,4,1,4,32,128]{5,4,3,2,1,0:T(8,128)(2,1)} %bitcast.185, bf16[512,2048]{1,0:T(8,128)(2,1)} %get-tuple-element.260.w_ref.refs_4_), custom_call_target="tpu_custom_call" | custom-call | flops 16777216 | bytes 81920 | tf_op jit(solution)/shard_map/project_from_pairs/pallas_call | solution.py:423
  160.6 10.1 %gated.2 = (bf16[256,1408]{1,0:T(8,128)(2,1)}, bf16[256,2816]{1,0:T(8,128)(2,1)}, f32[2,1,1408]{2,1,0:T(1,128)}, bf16[256,2048]{1,0:T(8,128)(2,1)}) custom-call(bf16[64,2048]{1,0:T(8,128)(2,1)} %bitcast.189, bf16[64,2048]{1,0:T(8,128)(2,1)} %bitcast.52.refs_1_, bf16[64,2048]{1,0:T(8,128)(2,1)} %bitcast.211, bf16[64,2048]{1,0:T(8,128)(2,1)} %bitcast.214, ...), custom_call_target="tpu_custom_call" | custom-call | flops 46137344 | bytes 258048 | tf_op jit(solution)/shard_map/gated/pallas_call | solution.py:636
  177.2 7.8 %project_split.4 = (bf16[64,2048]{1,0:T(8,128)(2,1)}, bf16[64,2048]{1,0:T(8,128)(2,1)}, bf16[2,64,2048]{2,1,0:T(8,128)(2,1)}) custom-call(bf16[256,2816]{1,0:T(8,128)(2,1)} %get-tuple-element.381.refs_0_.refs_2_, bf16[2048,2816]{1,0:T(8,128)(2,1)} %get-tuple-element.293.refs_4_.refs_1_), custom_call_target="tpu_custom_call" | custom-call | flops 46137344 | bytes 219136 | tf_op jit(solution)/shard_map/project_split/pallas_call | solution.py:456
  193.2 13.9 %gated.3 = (bf16[512,1408]{1,0:T(8,128)(2,1)}, bf16[512,2816]{1,0:T(8,128)(2,1)}, f32[2,1,1408]{2,1,0:T(1,128)}, bf16[512,2048]{1,0:T(8,128)(2,1)}) custom-call(bf16[128,2048]{1,0:T(8,128)(2,1)} %bitcast.60.refs_0_, bf16[128,2048]{1,0:T(8,128)(2,1)} %bitcast.61.refs_1_, bf16[128,2048]{1,0:T(8,128)(2,1)} %bitcast.62.refs_2_, ...), custom_call_target="tpu_custom_call" | custom-call | flops 92274688 | bytes 335872 | tf_op jit(solution)/shard_map/gated/pallas_call | solution.py:636
  213.1 10.5 %project_split.5 = (bf16[128,2048]{1,0:T(8,128)(2,1)}, bf16[128,2048]{1,0:T(8,128)(2,1)}, bf16[2,128,2048]{2,1,0:T(8,128)(2,1)}) custom-call(bf16[512,2816]{1,0:T(8,128)(2,1)} %get-tuple-element.382.refs_0_.refs_3_, bf16[2048,2816]{1,0:T(8,128)(2,1)} %get-tuple-element.293.refs_4_.refs_1_), custom_call_target="tpu_custom_call" | custom-call | flops 92274688 | bytes 258048 | tf_op jit(solution)/shard_map/project_split/pallas_call | solution.py:456
  238.4 5.7 %collective-permute-done.28 = bf16[4,32,2048]{2,1,0:T(8,128)(2,1)} collective-permute-done((bf16[4,32,2048]{2,1,0:T(8,128)(2,1)}, bf16[4,32,2048]{2,1,0:T(8,128)(2,1)}, u32[]{:S(2)}, u32[]{:S(2)}) %collective-permute-start.28) | collective-permute-done | bytes 524320 | tf_op jit(solution)/shard_map/ppermute | solution.py:36
  249.5 5.4 %attend_back.2 = (bf16[8,1,3,128,128]{4,3,2,1,0:T(8,128)(2,1)}, f32[1,3,128]{2,1,0:T(4,128)}) custom-call(bf16[8,1,3,128,128]{4,3,2,1,0:T(8,128)(2,1)} %copy-done.5, bf16[8,1,128,128]{3,2,1,0:T(8,128)(2,1)} %get-tuple-element.256.o_ref, bf16[8,1,128,128]{3,2,1,0:T(8,128)(2,1)} %bitcast.75.d_ref, f32[1,1,1024]{2,1,0:T(1,128)} %get-tuple-element.335.l_ref, ...), custom_call_target="tpu_custom_call" | custom-call | flops 20971520 | bytes 32768 | tf_op jit(solution)/shard_map/attend_back/pallas_call | solution.py:295
  259.4 8.7 %project_split.6 = (bf16[192,2048]{1,0:T(8,128)(2,1)}, bf16[192,2048]{1,0:T(8,128)(2,1)}, bf16[2,192,2048]{2,1,0:T(8,128)(2,1)}) custom-call(bf16[512,1408]{1,0:T(8,128)(2,1)} %get-tuple-element.341.refs_0_.refs_1_, bf16[256,1408]{1,0:T(8,128)(2,1)} %get-tuple-element.342.refs_1_.refs_0_, bf16[1408,2048]{1,0:T(8,128)(2,1)} %get-tuple-element.253.refs_4_.refs_2_), custom_call_target="tpu_custom_call" | custom-call | flops 69206016 | bytes 173056 | tf_op jit(solution)/shard_map/project_split/pallas_call | solution.py:456
  268.1 5.4 %collective-permute-done.29 = bf16[4,32,2048]{2,1,0:T(8,128)(2,1)} collective-permute-done((bf16[4,32,2048]{2,1,0:T(8,128)(2,1)}, bf16[4,32,2048]{2,1,0:T(8,128)(2,1)}, u32[]{:S(2)}, u32[]{:S(2)}) %collective-permute-start.29) | collective-permute-done | bytes 524320 | tf_op jit(solution)/shard_map/ppermute | solution.py:36
  275.7 5.0 %project_to_pairs.7 = (bf16[4,4,1,4,32,128]{5,4,3,2,1,0:T(8,128)(2,1)}, bf16[512,2048]{1,0:T(8,128)(2,1)}) custom-call(bf16[128,2048]{1,0:T(8,128)(2,1)} %bitcast.186, bf16[128,2048]{1,0:T(8,128)(2,1)} %bitcast.80.refs_1_, bf16[128,2048]{1,0:T(8,128)(2,1)} %bitcast.81.refs_2_, bf16[128,2048]{1,0:T(8,128)(2,1)} %bitcast.82.refs_3_, ...), custom_call_target="tpu_custom_call" | custom-call | flops 16777216 | bytes 98304 | tf_op jit(solution)/shard_map/project_to_pairs/pallas_call | solution.py:358
  280.7 6.0 %all-to-all-start.6 = ((bf16[8,2,1,128,128]{4,3,1,2,0:T(8,128)(2,1)}), bf16[8,2,1,128,128]{4,3,1,2,0:T(8,128)(2,1)}, u32[]{:S(2)}, u32[]{:S(2)}) async-start(bf16[8,2,1,128,128]{4,3,1,2,0:T(8,128)(2,1)} %bitcast.207), calls=%async_computation.6 | async-start | bytes 1048576 | tf_op jit(solution)/shard_map/all_to_all | solution.py:65
  291.1 6.0 %row_grads.2 = (bf16[16,512]{1,0:T(8,128)(2,1)}, bf16[16,2048]{1,0:T(8,128)(2,1)}) custom-call(bf16[256,512]{1,0:T(8,128)(2,1)} %get-tuple-element.355.refs_0_, bf16[512,512]{1,0:T(8,128)(2,1)} %get-tuple-element.356.refs_1_, bf16[256,2048]{1,0:T(8,128)(2,1)} %get-tuple-element.357.refs_2_, bf16[512,2048]{1,0:T(8,128)(2,1)} %get-tuple-element.358.refs_3_, ...), custom_call_target="tpu_custom_call" | custom-call | flops 4194304 | bytes 94208 | tf_op jit(solution)/shard_map/row_grads/pallas_call | solution.py:789
  301.6 8.1 %attend_back.3 = (bf16[8,2,3,128,128]{4,3,2,1,0:T(8,128)(2,1)}, f32[2,3,128]{2,1,0:T(4,128)}) custom-call(bf16[8,2,3,128,128]{4,3,2,1,0:T(8,128)(2,1)} %copy-done.1, bf16[8,2,128,128]{3,2,1,0:T(8,128)(2,1)} %get-tuple-element.258.o_ref, bf16[8,2,128,128]{3,2,1,0:T(8,128)(2,1)} %bitcast.87.d_ref, f32[2,1,1024]{2,1,0:T(1,128)} %get-tuple-element.363.l_ref, ...), custom_call_target="tpu_custom_call" | custom-call | flops 41943040 | bytes 65536 | tf_op jit(solution)/shard_map/attend_back/pallas_call | solution.py:295
  318.1 17.8 %column_grads.2 = (bf16[2,16,1408]{2,1,0:T(8,128)(2,1)}, bf16[32,2048]{1,0:T(8,128)(2,1)}) custom-call(bf16[256,2048]{1,0:T(8,128)(2,1)} %get-tuple-element.379.refs_0_, bf16[512,2048]{1,0:T(8,128)(2,1)} %get-tuple-element.380.refs_1_, bf16[256,2816]{1,0:T(8,128)(2,1)} %get-tuple-element.381.refs_0_.refs_2_, ...), custom_call_target="tpu_custom_call" | custom-call | flops 23068672 | bytes 296960 | tf_op jit(solution)/shard_map/column_grads/pallas_call | solution.py:724
  345.3 8.4 %row_grads.3 = (bf16[16,1408]{1,0:T(8,128)(2,1)}, bf16[16,2048]{1,0:T(8,128)(2,1)}) custom-call(bf16[256,1408]{1,0:T(8,128)(2,1)} %get-tuple-element.342.refs_1_.refs_0_, bf16[512,1408]{1,0:T(8,128)(2,1)} %get-tuple-element.341.refs_0_.refs_1_, bf16[256,2048]{1,0:T(8,128)(2,1)} %get-tuple-element.390.refs_2_, bf16[512,2048]{1,0:T(8,128)(2,1)} %get-tuple-element.391.refs_3_, ...), custom_call_target="tpu_custom_call" | custom-call | flops 11534336 | bytes 173056 | tf_op jit(solution)/shard_map/row_grads/pallas_call | solution.py:789
  356.6 10.5 %column_grads.3 = (bf16[3,16,512]{2,1,0:T(8,128)(2,1)}, bf16[48,2048]{1,0:T(8,128)(2,1)}) custom-call(bf16[256,2048]{1,0:T(8,128)(2,1)} %get-tuple-element.399.refs_0_, bf16[512,2048]{1,0:T(8,128)(2,1)} %get-tuple-element.400.refs_1_, bf16[256,1536]{1,0:T(8,128)(2,1)} %assemble.2.refs_2_.refs_1_, bf16[512,1536]{1,0:T(8,128)(2,1)} %assemble.3.refs_3_.refs_0_, ...), custom_call_target="tpu_custom_call" | custom-call | flops 12582912 | bytes 184320 | tf_op jit(solution)/shard_map/column_grads/pallas_call | solution.py:724
  369.2 5.7 %all-to-all-start.8 = ((bf16[8,16,2944]{2,1,0:T(8,128)(2,1)}), bf16[8,16,2944]{2,1,0:T(8,128)(2,1)S(1)}, u32[]{:S(2)}, u32[]{:S(2)}) async-start(bf16[8,16,2944]{2,1,0:T(8,128)(2,1)} %pack.1), calls=%async_computation.8 | async-start | bytes 1507328 | tf_op jit(solution)/shard_map/all_to_all | solution.py:65
  374.9 8.9 %project_split.7 = (bf16[192,2048]{1,0:T(8,128)(2,1)}, bf16[192,2048]{1,0:T(8,128)(2,1)}, bf16[2,192,2048]{2,1,0:T(8,128)(2,1)}) custom-call(bf16[512,1536]{1,0:T(8,128)(2,1)} %assemble.3.refs_3_.refs_0_, bf16[256,1536]{1,0:T(8,128)(2,1)} %assemble.2.refs_2_.refs_1_, bf16[2048,1536]{1,0:T(8,128)(2,1)} %get-tuple-element.230.refs_4_.refs_2_), custom_call_target="tpu_custom_call" | custom-call | flops 75497472 | bytes 184320 | tf_op jit(solution)/shard_map/project_split/pallas_call | solution.py:456
  383.8 10.7 %all-to-all-done.8 = bf16[8,16,2944]{2,1,0:T(8,128)(2,1)S(1)} async-done(((bf16[8,16,2944]{2,1,0:T(8,128)(2,1)}), bf16[8,16,2944]{2,1,0:T(8,128)(2,1)S(1)}, u32[]{:S(2)}, u32[]{:S(2)}) %all-to-all-start.8) | async-done | bytes 753696 | tf_op jit(solution)/shard_map/all_to_all | solution.py:65
  408.5 13.7 %collective-permute-done.44 = bf16[6,32,2048]{2,1,0:T(8,128)(2,1)} collective-permute-done((bf16[6,32,2048]{2,1,0:T(8,128)(2,1)}, bf16[6,32,2048]{2,1,0:T(8,128)(2,1)}, u32[]{:S(2)}, u32[]{:S(2)}) %collective-permute-start.44) | collective-permute-done | bytes 786464 | tf_op jit(solution)/shard_map/ppermute | solution.py:36
  (308 shorter events, 164.7 us)
Async XLA Ops:
  3.0 16.3 %collective-permute-start.1 = (bf16[2,32,2048]{2,1,0:T(8,128)(2,1)S(1)}, bf16[2,32,2048]{2,1,0:T(8,128)(2,1)S(1)}, u32[]{:S(2)}, u32[]{:S(2)}) collective-permute-start(bf16[2,32,2048]{2,1,0:T(8,128)(2,1)S(1)} %fusion.20), channel_id=1, source_target_pairs={{0,1},{1,0},{2,3},{3,2},{4,5},{5,4},{6,7},{7,6},{8,9},{9,8},{10,11... | collective-permute-start | bytes 786440 | tf_op jit(solution)/shard_map/ppermute | solution.py:36
  3.5 15.8 %collective-permute-start = (bf16[2,32,2048]{2,1,0:T(8,128)(2,1)S(1)}, bf16[2,32,2048]{2,1,0:T(8,128)(2,1)}, u32[]{:S(2)}, u32[]{:S(2)}) collective-permute-start(bf16[2,32,2048]{2,1,0:T(8,128)(2,1)S(1)} %fusion.20), channel_id=1, source_target_pairs={{0,2},{1,3},{2,0},{3,1},{4,6},{5,7},{6,4},{7,5},{8,10},{9,11},{10,... | collective-permute-start | bytes 786440 | tf_op jit(solution)/shard_map/ppermute | solution.py:36
  8.2 19.7 %collective-permute-start.4 = (bf16[4,32,2048]{2,1,0:T(8,128)(2,1)S(1)}, bf16[4,32,2048]{2,1,0:T(8,128)(2,1)S(1)}, u32[]{:S(2)}, u32[]{:S(2)}) collective-permute-start(bf16[4,32,2048]{2,1,0:T(8,128)(2,1)S(1)} %fusion.13), channel_id=1, source_target_pairs={{0,1},{1,0},{2,3},{3,2},{4,5},{5,4},{6,7},{7,6},{8,9},{9,8},{10,11... | collective-permute-start | bytes 1572872 | tf_op jit(solution)/shard_map/ppermute | solution.py:36
  8.4 19.5 %collective-permute-start.3 = (bf16[4,32,2048]{2,1,0:T(8,128)(2,1)S(1)}, bf16[4,32,2048]{2,1,0:T(8,128)(2,1)S(1)}, u32[]{:S(2)}, u32[]{:S(2)}) collective-permute-start(bf16[4,32,2048]{2,1,0:T(8,128)(2,1)S(1)} %fusion.13), channel_id=1, source_target_pairs={{0,2},{1,3},{2,0},{3,1},{4,6},{5,7},{6,4},{7,5},{8,10},{9,11},{10,... | collective-permute-start | bytes 1572872 | tf_op jit(solution)/shard_map/ppermute | solution.py:36
  28.9 29.0 %all-to-all-start = ((bf16[8,1,3,128,128]{4,3,2,1,0:T(8,128)(2,1)}), bf16[8,1,3,128,128]{4,3,2,1,0:T(8,128)(2,1)S(1)}, u32[]{:S(2)}, u32[]{:S(2)}) async-start(bf16[8,1,3,128,128]{4,3,2,1,0:T(8,128)(2,1)} %bitcast.191), calls=%async_computation | async-start | bytes 1572864 | tf_op jit(solution)/shard_map/all_to_all | solution.py:65
  35.0 13.8 %collective-permute-start.5 = (bf16[4,32,2048]{2,1,0:T(8,128)(2,1)}, bf16[4,32,2048]{2,1,0:T(8,128)(2,1)S(1)}, u32[]{:S(2)}, u32[]{:S(2)}) collective-permute-start(bf16[4,32,2048]{2,1,0:T(8,128)(2,1)} %copy-done.24), channel_id=1, source_target_pairs={{0,1},{1,0},{2,3},{3,2},{4,5},{5,4},{6,7},{7,6},{8,9},{9,8},{10,11... | collective-permute-start | bytes 1572872 | tf_op jit(solution)/shard_map/ppermute | solution.py:36
  57.9 9.3 %collective-permute-start.7 = (f32[2,2048]{1,0:T(2,128)S(1)}, f32[2,2048]{1,0:T(2,128)S(1)}, u32[]{:S(2)}, u32[]{:S(2)}) collective-permute-start(f32[2,2048]{1,0:T(2,128)S(1)} %pad_maximum_fusion.3), channel_id=1, source_target_pairs={{0,2},{1,3},{2,0},{3,1},{4,6},{5,7},{6,4},{7,5},{8,10},{9,11},{10,... | collective-permute-start | bytes 49160 | tf_op jit(solution)/shard_map/ppermute | solution.py:36
  60.9 45.6 %all-to-all-start.1 = ((bf16[8,2,3,128,128]{4,3,2,1,0:T(8,128)(2,1)}), bf16[8,2,3,128,128]{4,3,2,1,0:T(8,128)(2,1)S(1)}, u32[]{:S(2)}, u32[]{:S(2)}) async-start(bf16[8,2,3,128,128]{4,3,2,1,0:T(8,128)(2,1)} %bitcast.187), calls=%async_computation.1 | async-start | bytes 3145728 | tf_op jit(solution)/shard_map/all_to_all | solution.py:65
  70.6 19.4 %collective-permute-start.10 = (bf16[6,32,2048]{2,1,0:T(8,128)(2,1)S(1)}, bf16[6,32,2048]{2,1,0:T(8,128)(2,1)}, u32[]{:S(2)}, u32[]{:S(2)}) collective-permute-start(bf16[6,32,2048]{2,1,0:T(8,128)(2,1)S(1)} %get-tuple-element.271), channel_id=1, source_target_pairs={{0,1},{1,0},{2,3},{3,2},{4,5},{5,4},{6,7},{7,6},{8,9},{9,8},{10,11... | collective-permute-start | bytes 2359304 | tf_op jit(solution)/shard_map/ppermute | solution.py:36
  70.6 20.1 %collective-permute-start.9 = (bf16[6,32,2048]{2,1,0:T(8,128)(2,1)S(1)}, bf16[6,32,2048]{2,1,0:T(8,128)(2,1)}, u32[]{:S(2)}, u32[]{:S(2)}) collective-permute-start(bf16[6,32,2048]{2,1,0:T(8,128)(2,1)S(1)} %get-tuple-element.271), channel_id=1, source_target_pairs={{0,2},{1,3},{2,0},{3,1},{4,6},{5,7},{6,4},{7,5},{8,10},{9,11},{10,... | collective-permute-start | bytes 2359304 | tf_op jit(solution)/shard_map/ppermute | solution.py:36
  90.6 9.3 %collective-permute-start.11 = (bf16[6,32,2048]{2,1,0:T(8,128)(2,1)}, bf16[6,32,2048]{2,1,0:T(8,128)(2,1)S(1)}, u32[]{:S(2)}, u32[]{:S(2)}) collective-permute-start(bf16[6,32,2048]{2,1,0:T(8,128)(2,1)} %collective-permute-done.9), channel_id=1, source_target_pairs={{0,1},{1,0},{2,3},{3,2},{4,5},{5,4},{6,7},{7,6},{8,9},{9,8},{10,11... | collective-permute-start | bytes 2359304 | tf_op jit(solution)/shard_map/ppermute | solution.py:36
  106.5 15.6 %all-to-all-start.2 = ((bf16[8,1,1,128,128]{4,3,2,1,0:T(8,128)(2,1)}), bf16[8,1,1,128,128]{4,3,2,1,0:T(8,128)(2,1)S(1)}, u32[]{:S(2)}, u32[]{:S(2)}) async-start(bf16[8,1,1,128,128]{4,3,2,1,0:T(8,128)(2,1)} %bitcast.31), calls=%async_computation.2 | async-start | bytes 524288 | tf_op jit(solution)/shard_map/all_to_all | solution.py:65
  130.2 13.3 %collective-permute-start.13 = (bf16[2,32,2048]{2,1,0:T(8,128)(2,1)S(1)}, bf16[2,32,2048]{2,1,0:T(8,128)(2,1)S(1)}, u32[]{:S(2)}, u32[]{:S(2)}) collective-permute-start(bf16[2,32,2048]{2,1,0:T(8,128)(2,1)S(1)} %fusion.24), channel_id=1, source_target_pairs={{0,2},{1,3},{2,0},{3,1},{4,6},{5,7},{6,4},{7,5},{8,10},{9,11},{10,... | collective-permute-start | bytes 786440 | tf_op jit(solution)/shard_map/ppermute | solution.py:36
  131.8 18.4 %all-to-all-start.3 = ((bf16[8,2,1,128,128]{4,3,1,2,0:T(8,128)(2,1)}), bf16[8,2,1,128,128]{4,3,1,2,0:T(8,128)(2,1)S(1)}, u32[]{:S(2)}, u32[]{:S(2)}) async-start(bf16[8,2,1,128,128]{4,3,1,2,0:T(8,128)(2,1)} %bitcast.44), calls=%async_computation.3 | async-start | bytes 1048576 | tf_op jit(solution)/shard_map/all_to_all | solution.py:65
  144.8 10.9 %collective-permute-start.15 = (bf16[2,32,2048]{2,1,0:T(8,128)(2,1)S(1)}, bf16[2,32,2048]{2,1,0:T(8,128)(2,1)S(1)}, u32[]{:S(2)}, u32[]{:S(2)}) collective-permute-start(bf16[2,32,2048]{2,1,0:T(8,128)(2,1)S(1)} %multiply_convert_fusion.4), channel_id=1, source_target_pairs={{0,1},{1,0},{2,3},{3,2},{4,5},{5,4},{6,7},{7,6},{8,9},{9,8},{10,11... | collective-permute-start | bytes 786440 | tf_op jit(solution)/shard_map/ppermute | solution.py:36
  144.9 10.8 %collective-permute-start.14 = (bf16[2,32,2048]{2,1,0:T(8,128)(2,1)S(1)}, bf16[2,32,2048]{2,1,0:T(8,128)(2,1)}, u32[]{:S(2)}, u32[]{:S(2)}) collective-permute-start(bf16[2,32,2048]{2,1,0:T(8,128)(2,1)S(1)} %multiply_convert_fusion.4), channel_id=1, source_target_pairs={{0,2},{1,3},{2,0},{3,1},{4,6},{5,7},{6,4},{7,5},{8,10},{9,11},{10,... | collective-permute-start | bytes 786440 | tf_op jit(solution)/shard_map/ppermute | solution.py:36
  159.9 14.1 %collective-permute-start.18 = (bf16[4,32,2048]{2,1,0:T(8,128)(2,1)S(1)}, bf16[4,32,2048]{2,1,0:T(8,128)(2,1)}, u32[]{:S(2)}, u32[]{:S(2)}) collective-permute-start(bf16[4,32,2048]{2,1,0:T(8,128)(2,1)S(1)} %fusion.17), channel_id=1, source_target_pairs={{0,2},{1,3},{2,0},{3,1},{4,6},{5,7},{6,4},{7,5},{8,10},{9,11},{10,... | collective-permute-start | bytes 1572872 | tf_op jit(solution)/shard_map/ppermute | solution.py:36
  176.7 13.5 %collective-permute-start.19 = (bf16[4,32,2048]{2,1,0:T(8,128)(2,1)}, bf16[4,32,2048]{2,1,0:T(8,128)(2,1)}, u32[]{:S(2)}, u32[]{:S(2)}) collective-permute-start(bf16[4,32,2048]{2,1,0:T(8,128)(2,1)} %multiply_convert_fusion.2), channel_id=1, source_target_pairs={{0,2},{1,3},{2,0},{3,1},{4,6},{5,7},{6,4},{7,5},{8,10},{9,11},{10,... | collective-permute-start | bytes 1572872 | tf_op jit(solution)/shard_map/ppermute | solution.py:36
  192.7 14.4 %collective-permute-start.23 = (bf16[2,32,2048]{2,1,0:T(8,128)(2,1)}, bf16[2,32,2048]{2,1,0:T(8,128)(2,1)}, u32[]{:S(2)}, u32[]{:S(2)}) collective-permute-start(bf16[2,32,2048]{2,1,0:T(8,128)(2,1)} %fusion.22), channel_id=1, source_target_pairs={{0,2},{1,3},{2,0},{3,1},{4,6},{5,7},{6,4},{7,5},{8,10},{9,11},{10,... | collective-permute-start | bytes 786440 | tf_op jit(solution)/shard_map/ppermute | solution.py:36
  211.4 12.2 %collective-permute-start.25 = (bf16[2,32,2048]{2,1,0:T(8,128)(2,1)}, bf16[2,32,2048]{2,1,0:T(8,128)(2,1)}, u32[]{:S(2)}, u32[]{:S(2)}) collective-permute-start(bf16[2,32,2048]{2,1,0:T(8,128)(2,1)} %multiply_convert_fusion.3), channel_id=1, source_target_pairs={{0,1},{1,0},{2,3},{3,2},{4,5},{5,4},{6,7},{7,6},{8,9},{9,8},{10,11... | collective-permute-start | bytes 786440 | tf_op jit(solution)/shard_map/ppermute | solution.py:36
  211.6 12.0 %collective-permute-start.24 = (bf16[2,32,2048]{2,1,0:T(8,128)(2,1)}, bf16[2,32,2048]{2,1,0:T(8,128)(2,1)}, u32[]{:S(2)}, u32[]{:S(2)}) collective-permute-start(bf16[2,32,2048]{2,1,0:T(8,128)(2,1)} %multiply_convert_fusion.3), channel_id=1, source_target_pairs={{0,2},{1,3},{2,0},{3,1},{4,6},{5,7},{6,4},{7,5},{8,10},{9,11},{10,... | collective-permute-start | bytes 786440 | tf_op jit(solution)/shard_map/ppermute | solution.py:36
  229.9 14.3 %collective-permute-start.28 = (bf16[4,32,2048]{2,1,0:T(8,128)(2,1)}, bf16[4,32,2048]{2,1,0:T(8,128)(2,1)}, u32[]{:S(2)}, u32[]{:S(2)}) collective-permute-start(bf16[4,32,2048]{2,1,0:T(8,128)(2,1)} %fusion.15), channel_id=1, source_target_pairs={{0,2},{1,3},{2,0},{3,1},{4,6},{5,7},{6,4},{7,5},{8,10},{9,11},{10,... | collective-permute-start | bytes 1572872 | tf_op jit(solution)/shard_map/ppermute | solution.py:36
  234.0 15.5 %all-to-all-start.4 = ((bf16[8,1,1,128,128]{4,3,2,1,0:T(8,128)(2,1)}), bf16[8,1,1,128,128]{4,3,2,1,0:T(8,128)(2,1)}, u32[]{:S(2)}, u32[]{:S(2)}) async-start(bf16[8,1,1,128,128]{4,3,2,1,0:T(8,128)(2,1)} %bitcast.218), calls=%async_computation.4 | async-start | bytes 524288 | tf_op jit(solution)/shard_map/all_to_all | solution.py:65
  254.8 25.8 %all-to-all-start.5 = ((bf16[8,1,3,128,128]{4,3,2,1,0:T(8,128)(2,1)}), bf16[8,1,3,128,128]{4,3,2,1,0:T(8,128)(2,1)S(1)}, u32[]{:S(2)}, u32[]{:S(2)}) async-start(bf16[8,1,3,128,128]{4,3,2,1,0:T(8,128)(2,1)} %get-tuple-element.350), calls=%async_computation.5 | async-start | bytes 1572864 | tf_op jit(solution)/shard_map/all_to_all | solution.py:65
  258.8 9.3 %collective-permute-start.30 = (bf16[4,32,2048]{2,1,0:T(8,128)(2,1)}, bf16[4,32,2048]{2,1,0:T(8,128)(2,1)}, u32[]{:S(2)}, u32[]{:S(2)}) collective-permute-start(bf16[4,32,2048]{2,1,0:T(8,128)(2,1)} %multiply_convert_fusion.1), channel_id=1, source_target_pairs={{0,1},{1,0},{2,3},{3,2},{4,5},{5,4},{6,7},{7,6},{8,9},{9,8},{10,11... | collective-permute-start | bytes 1572872 | tf_op jit(solution)/shard_map/ppermute | solution.py:36
  258.8 14.6 %collective-permute-start.29 = (bf16[4,32,2048]{2,1,0:T(8,128)(2,1)}, bf16[4,32,2048]{2,1,0:T(8,128)(2,1)}, u32[]{:S(2)}, u32[]{:S(2)}) collective-permute-start(bf16[4,32,2048]{2,1,0:T(8,128)(2,1)} %multiply_convert_fusion.1), channel_id=1, source_target_pairs={{0,2},{1,3},{2,0},{3,1},{4,6},{5,7},{6,4},{7,5},{8,10},{9,11},{10,... | collective-permute-start | bytes 1572872 | tf_op jit(solution)/shard_map/ppermute | solution.py:36
  280.7 20.9 %all-to-all-start.6 = ((bf16[8,2,1,128,128]{4,3,1,2,0:T(8,128)(2,1)}), bf16[8,2,1,128,128]{4,3,1,2,0:T(8,128)(2,1)}, u32[]{:S(2)}, u32[]{:S(2)}) async-start(bf16[8,2,1,128,128]{4,3,1,2,0:T(8,128)(2,1)} %bitcast.207), calls=%async_computation.6 | async-start | bytes 1048576 | tf_op jit(solution)/shard_map/all_to_all | solution.py:65
  309.7 44.0 %all-to-all-start.7 = ((bf16[8,2,3,128,128]{4,3,2,1,0:T(8,128)(2,1)}), bf16[8,2,3,128,128]{4,3,2,1,0:T(8,128)(2,1)}, u32[]{:S(2)}, u32[]{:S(2)}) async-start(bf16[8,2,3,128,128]{4,3,2,1,0:T(8,128)(2,1)} %get-tuple-element.370), calls=%async_computation.7 | async-start | bytes 3145728 | tf_op jit(solution)/shard_map/all_to_all | solution.py:65
  316.7 20.2 %collective-permute-start.36 = (bf16[6,32,2048]{2,1,0:T(8,128)(2,1)}, bf16[6,32,2048]{2,1,0:T(8,128)(2,1)}, u32[]{:S(2)}, u32[]{:S(2)}) collective-permute-start(bf16[6,32,2048]{2,1,0:T(8,128)(2,1)} %fusion.10), channel_id=1, source_target_pairs={{0,2},{1,3},{2,0},{3,1},{4,6},{5,7},{6,4},{7,5},{8,10},{9,11},{10,... | collective-permute-start | bytes 2359304 | tf_op jit(solution)/shard_map/ppermute | solution.py:36
  369.2 25.3 %all-to-all-start.8 = ((bf16[8,16,2944]{2,1,0:T(8,128)(2,1)}), bf16[8,16,2944]{2,1,0:T(8,128)(2,1)S(1)}, u32[]{:S(2)}, u32[]{:S(2)}) async-start(bf16[8,16,2944]{2,1,0:T(8,128)(2,1)} %pack.1), calls=%async_computation.8 | async-start | bytes 1507328 | tf_op jit(solution)/shard_map/all_to_all | solution.py:65
  402.3 19.9 %collective-permute-start.44 = (bf16[6,32,2048]{2,1,0:T(8,128)(2,1)}, bf16[6,32,2048]{2,1,0:T(8,128)(2,1)}, u32[]{:S(2)}, u32[]{:S(2)}) collective-permute-start(bf16[6,32,2048]{2,1,0:T(8,128)(2,1)} %fusion.8), channel_id=1, source_target_pairs={{0,2},{1,3},{2,0},{3,1},{4,6},{5,7},{6,4},{7,5},{8,10},{9,11},{10,... | collective-permute-start | bytes 2359304 | tf_op jit(solution)/shard_map/ppermute | solution.py:36
  404.2 23.9 %all-to-all-start.9 = ((bf16[8,16,2944]{2,1,0:T(8,128)(2,1)}), bf16[8,16,2944]{2,1,0:T(8,128)(2,1)}, u32[]{:S(2)}, u32[]{:S(2)}) async-start(bf16[8,16,2944]{2,1,0:T(8,128)(2,1)} %broadcast_in_dim.202), calls=%async_computation.9 | async-start | bytes 1507328 | tf_op jit(solution)/shard_map/all_to_all | solution.py:65
  (73 other events, 437.2 us)

commit v4 on v3

--- a/solution.py
+++ b/solution.py
@@ -523,16 +523,17 @@
     return ref.at[j, :, lanes] if len(ref.shape) == 3 else ref.at[j * rank:(j + 1) * rank, lanes]
 
 
-def pack_kernel(*refs, plan, counts, vectors):
-    total = sum(counts)
-    in_refs, sum_refs, out_ref, sums = refs[:total], refs[total:-2], refs[-2], refs[-1]
+def cells(shapes):
+    return [(v, j, c) for v, (members, size) in enumerate(shapes) for j in range(members) for c in range(size // LANES)]
+
+
+def pack_kernel(*refs, plan, count):
+    in_refs, sum_refs, out_ref, sums = refs[:count], refs[count:-2], refs[-2], refs[-1]
     rank = out_ref.shape[1]
     sums[...] = jnp.zeros_like(sums)
-    row = 0
-    for ref in sum_refs:
-        for j in range(ref.shape[0]):
-            sums[row:row + 1, :ref.shape[2]] = ref[j]
-            row += 1
+    for k, (v, j, c) in enumerate(cells([(ref.shape[0], ref.shape[2]) for ref in sum_refs])):
+        at = k // rank * LANES
+        sums[k % rank:k % rank + 1, at:at + LANES] = sum_refs[v][j, :, c * LANES:(c + 1) * LANES]
     base = 0
     for entries, cut in plan:
         sizes = [n for _, _, n in entries]
@@ -560,17 +561,16 @@
             if which is not None:
                 part_of(out_refs[which], j, rank, slice(start, start + n))[...] = values
                 continue
-            row = 0
-            for m_ref, out_ref in zip(m_refs, out_refs[-count:]):
-                members, size = m_ref.shape
-                stop = min(start + n, size)
-                if start < stop:
-                    out_ref[:, start:stop] = values[row:row + members, :stop - start] / m_ref[:, start:stop]
-                row += members
+            for cell, (v, j, c) in enumerate(cells([ref.shape for ref in m_refs])):
+                lane = cell // rank * LANES - start
+                if 0 <= lane < n:
+                    place = (slice(j, j + 1), slice(c * LANES, (c + 1) * LANES))
+                    row = slice(cell % rank, cell % rank + 1)
+                    out_refs[v - count][place] = values[row, lane:lane + LANES] / m_refs[v][place]
         base += cut
 
 
-def packing(over_all, over_seq, width, pieces, rank):
+def packing(over_all, over_seq, vectors, pieces, rank):
     plan, at = [], 0
     for arrays in (over_all, over_seq):
         entries = []
@@ -579,15 +579,16 @@
             entries += [(at, j, v.shape[-1]) for j in range(members)]
             at += 1
         plan.append(entries)
-    plan[1].append((None, 0, width))
+    blocks = len(cells([(v.shape[0], v.shape[2]) for v in vectors]))
+    plan[1].append((None, 0, -(-blocks // rank) * LANES))
     return [(entries, width_of([n for _, _, n in entries], pieces)) for entries in plan]
 
 
-def pack(plan, arrays, vectors, pieces, rank, width):
+def pack(plan, arrays, vectors, pieces, rank):
     return pl.pallas_call(
-        partial(pack_kernel, plan=plan, counts=[len(arrays)], vectors=len(vectors)),
+        partial(pack_kernel, plan=plan, count=len(arrays)),
         out_shape=jax.ShapeDtypeStruct((pieces, rank, sum(cut for _, cut in plan)), bf16),
-        scratch_shapes=[pltpu.VMEM((rank, width), f32)],
+        scratch_shapes=[pltpu.VMEM((rank, plan[1][0][-1][2]), f32)],
         cost_estimate=cost(flops=0, bytes_accessed=4 * sum(v.size for v in arrays), transcendentals=0),
         name="pack",
     )(*arrays, *vectors)
@@ -669,8 +670,15 @@
     return [slice(a, b) for a, b in zip(ends, ends[1:])]
 
 
-def column_grads_kernel(*refs, chunks, steps):
-    x_refs, d_refs, refs = refs[:chunks], refs[chunks:2 * chunks], refs[2 * chunks:]
+def column_grads_kernel(*refs, chunks, steps, joins):
+    x_refs, d_refs, refs = refs[:chunks], list(refs[chunks:2 * chunks]), list(refs[2 * chunks:])
+    if joins:
+        pairs_ref, d_refs[-1] = d_refs[-1], refs.pop(9)
+
+        @pl.when(pl.program_id(0) == 0)
+        def _():
+            join_pairs(pairs_ref, d_refs[-1])
+
     w_ref, a_ref, b_ref, stat_ref, m_ref, sum_ref, cross_ref, gb_ref, ga_ref, ts, dts, es = refs
     members, rank, block = b_ref.shape
     lanes = chunk_lanes(x_refs)
@@ -719,23 +727,32 @@
     first = lambda i: jnp.minimum(i, steps - 1)
     then = lambda i: jnp.maximum(i - steps, 0)
     part = lambda n: pl.BlockSpec((members, n, block), lambda i: (0, 0, first(i)))
+    joins = len(grads[-1].shape) == 6
+    joined = (rows[-1].shape[0], members * out)
     wide = members * block
     ranks = members * rank
-    grad_b, grad_a = pl.pallas_call(
-        partial(column_grads_kernel, chunks=chunks, steps=steps),
+    assert steps == 1 or not joins
+    grad_b, grad_a, *flat = pl.pallas_call(
+        partial(column_grads_kernel, chunks=chunks, steps=steps, joins=joins),
         grid=(steps + width // span,),
         in_specs=[pl.BlockSpec(v.shape, lambda i: (0, 0)) for v in rows]
-        + [pl.BlockSpec((v.shape[0], wide), lambda i: (0, first(i))) for v in grads]
+        + [
+            pl.BlockSpec(v.shape, lambda i: (0,) * 6) if len(v.shape) == 6
+            else pl.BlockSpec((v.shape[0], wide), lambda i: (0, first(i)))
+            for v in grads
+        ]
         + [
             pl.BlockSpec((span, members * out), lambda i: (then(i), 0)),
             pl.BlockSpec((ranks, width), lambda i: (0, 0)),
             part(rank), part(2), part(1), part(1), part(rank),
         ],
-        out_specs=[part(rank), pl.BlockSpec((ranks, span), lambda i: (0, then(i)))],
+        out_specs=[part(rank), pl.BlockSpec((ranks, span), lambda i: (0, then(i)))]
+        + [pl.BlockSpec(joined, lambda i: (0, 0))] * joins,
         out_shape=[
             jax.ShapeDtypeStruct((members, rank, out), bf16),
             jax.ShapeDtypeStruct((ranks, width), bf16),
-        ],
+        ]
+        + [jax.ShapeDtypeStruct(joined, bf16)] * joins,
         scratch_shapes=[
             pltpu.VMEM((ranks, tokens), bf16),
             pltpu.VMEM((ranks, tokens), f32),
@@ -748,7 +765,7 @@
         ),
         name="column_grads",
     )(*rows, *grads, weight, down.transpose(0, 2, 1).reshape(ranks, width), up, stat, magnitude[:, None, :], sums, cross)
-    return grad_a, grad_b
+    return (grad_a, grad_b, *flat)
 
 
 def row_grads_kernel(*refs, chunks):
@@ -897,12 +914,11 @@
     normed_a, d_qkv, pairs, outputs, totals, att = [[None] * 2 for _ in range(6)]
     laid, normed_a[0] = to_heads(gather_end(*started[0]), qkv_w)
 
-    laid, started[1], w_out, w_down = after(laid, started[1], w_out, w_down)
+    laid, started[1], w_down = after(laid, started[1], w_down)
     pairs[0] = send_pairs(laid, 0)
     laid, normed_a[1] = to_heads(gather_end(*started[1]), qkv_w)
     down_w, down_cross, down_square = row_prep(w_down, a_down, b_down, 256)
-    out_w, out_cross, out_square = row_prep(w_out, a_out, b_out, 512)
-    pairs[0], laid, down_square, out_square, w_gateup = after(pairs[0], laid, down_square, out_square, w_gateup)
+    pairs[0], laid, down_square, w_out, w_gateup = after(pairs[0], laid, down_square, w_out, w_gateup)
 
     u_out, middle, hidden, d_gu, gu_sum, normed_f, d_mid, du_out, dhid, du_down = [[None] * 2 for _ in range(10)]
 
@@ -911,25 +927,27 @@
 
     pairs[1] = send_pairs(laid, 1)
     outputs[0], totals[0] = attend(pairs[0], tables, kpos, qinfo[0])
-    squares = tensor_sum(jnp.concatenate([down_square, out_square]))
-    down_square, out_square = squares[0:1], squares[1:2]
-    down_scale, out_scale = m_down / jnp.sqrt(squares[0]), m_out / jnp.sqrt(squares[1])
-    scaled, w_gateup = after((cot * down_scale).astype(bf16), w_gateup)
+    down_square = tensor_sum(down_square)
+    down_scale = m_down / jnp.sqrt(down_square[0])
+    scaled, w_gateup, w_out = after((cot * down_scale).astype(bf16), w_gateup, w_out)
+    out_w, out_cross, out_square = row_prep(w_out, a_out, b_out, 512)
     gu_w, gu_stat, gu_cross = column_prep(w_gateup, a_gateup, b_gateup, m_gateup, LANES, True)
-    started, gu_w = after(gather_start(scaled), gu_w)
+    started, gu_w, out_w = after(gather_start(scaled), gu_w, out_w)
     whole_cot = gather_end(*started)
-    dhid[0], du_down[0] = of_cotangent(whole_cot, 0)
-    pairs[1], outputs[0], dhid[0] = after(pairs[1], outputs[0], dhid[0])
+    pairs[1], outputs[0], whole_cot, out_square = after(pairs[1], outputs[0], whole_cot, out_square)
 
     fetched = fetch_pairs(outputs[0][:, :, None], 0)
     outputs[1], totals[1] = attend(pairs[1], tables, kpos, qinfo[1])
-    fetched, outputs[1], whole_cot = after(fetched, outputs[1], whole_cot)
+    out_square = tensor_sum(out_square)
+    out_scale = m_out / jnp.sqrt(out_square[0])
+    fetched, outputs[1], whole_cot, out_scale = after(fetched, outputs[1], whole_cot, out_scale)
 
     returned = fetch_pairs(outputs[1][:, :, None], 1)
     att[0], split = project_from_pairs(fetched, out_w, 512)
     moving, whole_cot = after(scatter_start(*split), whole_cot)
-    dhid[1], du_down[1] = of_cotangent(whole_cot, 1)
-    tail, dhid[1] = after(scatter_end(*moving), dhid[1])
+    for c in span:
+        dhid[c], du_down[c] = of_cotangent(whole_cot, c)
+    tail, dhid = after(scatter_end(*moving), dhid)
     u_out[0] = tail * out_scale
     middle[0] = wide_in[0] + u_out[0]
     started = gather_start(normed(middle[0], gain_ffn))
@@ -989,23 +1007,22 @@
         hidden, du_down, down_w, a_down, b_down, down_cross, -down_sum / down_square, 512
     )
     fetched, d_qkv[0], grad_a_down, layer_out = after(returned, d_qkv[0], grad_a_down, layer_out)
-    d_qkv[1] = assemble(fetched)
 
     qkv_sums = 0.0
     for c in span:
         choice = jnp.logical_and((mine[c] % heads)[:, None] == jnp.arange(heads)[None, :], live[c][:, None])
         qkv_sums = qkv_sums + jnp.sum(jnp.where(choice[:, None, :, None], pair_sums[c][:, :, None, :], 0.0), axis=0)
     qkv_sums = qkv_sums.reshape(3, 1, feat)
-    grad_a_qkv, grad_b_qkv = column_grads(
-        normed_a, d_qkv, qkv_w, a_qkv, b_qkv, qkv_stat, m_qkv, qkv_sums, qkv_cross, feat
+    grad_a_qkv, grad_b_qkv, d_qkv[1] = column_grads(
+        normed_a, [d_qkv[0], fetched], qkv_w, a_qkv, b_qkv, qkv_stat, m_qkv, qkv_sums, qkv_cross, feat
     )
 
     over_all = [grad_a_gu, grad_b_out, grad_b_down, grad_a_qkv]
     over_seq = [grad_b_gu, grad_a_out, grad_a_down, grad_b_qkv]
     vectors = [gu_sums, out_sum[None], down_sum[None], qkv_sums]
-    plan = packing(over_all, over_seq, width, seq, rank)
+    plan = packing(over_all, over_seq, vectors, seq, rank)
     cut = plan[0][1]
-    packed, d_qkv = after(pack(plan, over_all + over_seq, vectors, seq, rank, width), d_qkv)
+    packed, d_qkv = after(pack(plan, over_all + over_seq, vectors, seq, rank), d_qkv)
     added, split = after(exchange(packed), project_split(d_qkv[::-1], qkv_w, NT, 512, quarter))
     moving = scatter_start(*split)
     added = jnp.sum(added.astype(f32), axis=0).astype(bf16)

time: 439 us -> 434 us (0.989)
  waiting for transfers between devices: 74.8 us -> 65.7 us
  starting transfers between devices: 74.5 us -> 82.4 us
    ppermute x45 -> x48, starting transfers between devices: 23.4 us -> 29.9 us  [swap(): return lax.ppermute(values, 'tensor', [(i, i ^ bit) for i in range(size)])]
    ppermute x45 -> x48, waiting for transfers between devices: 50.6 us -> 46 us  [swap(): return lax.ppermute(values, 'tensor', [(i, i ^ bit) for i in range(size)])]
    all_to_all x10, waiting for transfers between devices: 24.3 us -> 19.8 us  [exchange(): return lax.all_to_all(values, 'seq', 0, 0, tiled=True)]
    unnamed x102 -> x100, local copies, waits for them, and re-layouts: 10.6 us -> 9.64 us
  transfers between devices with their start and end apart: 55 -> 58, of which waited for: 21 -> 21; matrix products, arithmetic and copies ran while one was open for 9% -> 9% of each run, Pallas kernels for 43% -> 43%
where the time goes in v4:
time: 434 us; the launch traced here: 426 us
  Pallas kernels  218 us (50%)
  starting transfers between devices  82.4 us (19%)
  waiting for transfers between devices  65.7 us (15%)
  other arithmetic  44.5 us (10%)
  local copies, waits for them, and re-layouts  13.8 us (3%)
    all_to_all x10, starting transfers between devices, exchange(): return lax.all_to_all(values, 'seq', 0, 0, tiled=True)  52.5 us
    ppermute x48, waiting for transfers between devices, swap(): return lax.ppermute(values, 'tensor', [(i, i ^ bit) for i in range(size)])  46 us
    pallas_call x4, Pallas kernels, project_split(): pl.pallas_call(partial(project_split_kernel, dims=dims), grid=(out // blo...  35.9 us
    ppermute x48, starting transfers between devices, swap(): return lax.ppermute(values, 'tensor', [(i, i ^ bit) for i in range(size)])  29.9 us
    pallas_call x2, Pallas kernels, column_grads(): pl.pallas_call(partial(column_grads_kernel, chunks=chunks, steps=steps, j...  29.2 us
    pallas_call x2, Pallas kernels, column_prep(): pl.pallas_call(column_prep_kernel, grid=(out // block,), in_specs=[pl.Blo...  25.5 us
    pallas_call x2, Pallas kernels, gated(): pl.pallas_call(gated_kernel, grid=(-(-out // block),), in_specs=[pl.Block...  24 us
    pallas_call x4, Pallas kernels, project_to_pairs(): pl.pallas_call(partial(to_pairs_kernel, dims=dims), grid=(parts, steps),...  22.9 us
  transfers between devices with their start and end apart: 58, of which 21 were waited for; matrix products, arithmetic and copies ran while one was open for 9% of the time, Pallas kernels for 43%

profile of v4, /device:TPU:0, one launch (start us, length us, event | category | flops | bytes accessed | tf_op | source)
XLA Modules:
  0.0 425.8 jit_solution(15560278419821094201)
XLA Ops:
  10.4 8.9 %column_prep.2 = (bf16[2048,1536]{1,0:T(8,128)(2,1)}, f32[3,2,512]{2,1,0:T(2,128)}, f32[3,16,512]{2,1,0:T(8,128)}) custom-call(bf16[3,2048,512]{2,1,0:T(8,128)(2,1)} %w_ref.1, bf16[48,2048]{1,0:T(8,128)(2,1)} %bitcast.192, bf16[2,48,768]{2,1,0:T(8,128)(2,1)} %broadcast_multiply_fusion.1.b_ref, f32[3,1,512]{2,1,0:T(1,128)} %broadcast_in_dim.103.m_ref.refs_8_), custom_call_target="tpu_custom_call" | custom-call | flops 50331648 | bytes 196608 | tf_op jit(solution)/shard_map/column_prep/pallas_call | solution.py:103
  21.8 6.1 %project_to_pairs.4 = (bf16[2,4,3,4,32,128]{5,4,3,2,1,0:T(8,128)(2,1)}, bf16[256,2048]{1,0:T(8,128)(2,1)}) custom-call(bf16[64,2048]{1,0:T(8,128)(2,1)} %bitcast.184, bf16[64,2048]{1,0:T(8,128)(2,1)} %bitcast.4.refs_1_, bf16[64,2048]{1,0:T(8,128)(2,1)} %bitcast.207, bf16[64,2048]{1,0:T(8,128)(2,1)} %bitcast.214, ...), custom_call_target="tpu_custom_call" | custom-call | flops 25165824 | bytes 131072 | tf_op jit(solution)/shard_map/project_to_pairs/pallas_call | solution.py:358
  28.9 6.1 %all-to-all-start = ((bf16[8,1,3,128,128]{4,3,2,1,0:T(8,128)(2,1)}), bf16[8,1,3,128,128]{4,3,2,1,0:T(8,128)(2,1)S(1)}, u32[]{:S(2)}, u32[]{:S(2)}) async-start(bf16[8,1,3,128,128]{4,3,2,1,0:T(8,128)(2,1)} %bitcast.188), calls=%async_computation | async-start | bytes 1572864 | tf_op jit(solution)/shard_map/all_to_all | solution.py:65
  35.5 8.9 %row_prep.2 = (bf16[1408,2048]{1,0:T(8,128)(2,1)}, f32[16,2048]{1,0:T(8,128)}, f32[1,2048]{1,0:T(1,128)}) custom-call(bf16[1408,2048]{1,0:T(8,128)(2,1)} %w_ref.2, bf16[16,1408]{1,0:T(8,128)(2,1)} %bitcast.217, bf16[16,2048]{1,0:T(8,128)(2,1)} %refs_6_.6), custom_call_target="tpu_custom_call" | custom-call | flops 23068672 | bytes 180224 | tf_op jit(solution)/shard_map/row_prep/pallas_call | solution.py:141
  45.1 8.2 %project_to_pairs.5 = (bf16[4,4,3,4,32,128]{5,4,3,2,1,0:T(8,128)(2,1)}, bf16[512,2048]{1,0:T(8,128)(2,1)}) custom-call(bf16[128,2048]{1,0:T(8,128)(2,1)} %bitcast.180, bf16[128,2048]{1,0:T(8,128)(2,1)} %bitcast.197, bf16[128,2048]{1,0:T(8,128)(2,1)} %bitcast.196, bf16[128,2048]{1,0:T(8,128)(2,1)} %bitcast.200, ...), custom_call_target="tpu_custom_call" | custom-call | flops 50331648 | bytes 163840 | tf_op jit(solution)/shard_map/project_to_pairs/pallas_call | solution.py:358
  68.6 4.6 %row_prep.3 = (bf16[512,2048]{1,0:T(8,128)(2,1)}, f32[16,2048]{1,0:T(8,128)}, f32[1,2048]{1,0:T(1,128)}) custom-call(bf16[512,2048]{1,0:T(8,128)(2,1)} %w_ref.4, bf16[16,512]{1,0:T(8,128)(2,1)} %bitcast.219, bf16[16,2048]{1,0:T(8,128)(2,1)} %refs_6_.4), custom_call_target="tpu_custom_call" | custom-call | flops 8388608 | bytes 65536 | tf_op jit(solution)/shard_map/row_prep/pallas_call | solution.py:141
  73.2 16.6 %column_prep.3 = (bf16[2048,2816]{1,0:T(8,128)(2,1)}, f32[2,2,1408]{2,1,0:T(2,128)}, f32[2,16,1408]{2,1,0:T(8,128)}) custom-call(bf16[2,2048,1408]{2,1,0:T(8,128)(2,1)} %w_ref.3, bf16[32,2048]{1,0:T(8,128)(2,1)} %bitcast.194, bf16[11,32,256]{2,1,0:T(8,128)(2,1)} %broadcast_multiply_fusion.b_ref, f32[2,1,1408]{2,1,0:T(1,128)} %broadcast_in_dim.107.m_ref.refs_8_), custom_call_target="tpu_custom_call" | custom-call | flops 92274688 | bytes 360448 | tf_op jit(solution)/shard_map/column_prep/pallas_call | solution.py:103
  101.4 5.4 %all-to-all-start.2 = ((bf16[8,1,1,128,128]{4,3,2,1,0:T(8,128)(2,1)}), bf16[8,1,1,128,128]{4,3,2,1,0:T(8,128)(2,1)S(1)}, u32[]{:S(2)}, u32[]{:S(2)}) async-start(bf16[8,1,1,128,128]{4,3,2,1,0:T(8,128)(2,1)} %bitcast.187), calls=%async_computation.2 | async-start | bytes 524288 | tf_op jit(solution)/shard_map/all_to_all | solution.py:65
  107.5 5.7 %attend.3 = (bf16[8,2,128,128]{3,2,1,0:T(8,128)(2,1)}, f32[2,1,1024]{2,1,0:T(1,128)}) custom-call(bf16[8,2,3,128,128]{4,3,2,1,0:T(8,128)(2,1)} %copy-done.1, f32[1024,128]{1,0:T(8,128)} %get-tuple-element.488.cos_ref, f32[1024,128]{1,0:T(8,128)} %get-tuple-element.489.sin_ref, s32[1024,1]{1,0:T(8,128)} %copy.57.kpos_ref, s32[2,2,1024]{2,1,0:T(2,128)} %pad_add_fusion.qinfo_ref), custom_call_target="tpu_custom_call" | custom-call | flops 16777216 | bytes 32768 | tf_op jit(solution)/shard_map/attend/pallas_call | solution.py:209
  129.2 5.7 %project_cotangent.2 = (bf16[256,1408]{1,0:T(8,128)(2,1)}, bf16[256,2048]{1,0:T(8,128)(2,1)}) custom-call(bf16[192,2048]{1,0:T(8,128)(2,1)} %bitcast.173, bf16[192,2048]{1,0:T(8,128)(2,1)} %bitcast.36.refs_1_, bf16[192,2048]{1,0:T(8,128)(2,1)} %bitcast.37.refs_2_, bf16[192,2048]{1,0:T(8,128)(2,1)} %bitcast.175, ...), custom_call_target="tpu_custom_call" | custom-call | flops 23068672 | bytes 122880 | tf_op jit(solution)/shard_map/project_cotangent/pallas_call | solution.py:483
  134.9 7.9 %project_cotangent.3 = (bf16[512,1408]{1,0:T(8,128)(2,1)}, bf16[512,2048]{1,0:T(8,128)(2,1)}) custom-call(bf16[192,2048]{1,0:T(8,128)(2,1)} %bitcast.174, bf16[192,2048]{1,0:T(8,128)(2,1)} %bitcast.36.refs_1_, bf16[192,2048]{1,0:T(8,128)(2,1)} %bitcast.37.refs_2_, bf16[192,2048]{1,0:T(8,128)(2,1)} %bitcast.176, ...), custom_call_target="tpu_custom_call" | custom-call | flops 46137344 | bytes 155648 | tf_op jit(solution)/shard_map/project_cotangent/pallas_call | solution.py:483
  146.5 4.8 %project_from_pairs.3 = (bf16[512,512]{1,0:T(8,128)(2,1)}, bf16[128,2048]{1,0:T(8,128)(2,1)}, bf16[128,2048]{1,0:T(8,128)(2,1)}, bf16[2,128,2048]{2,1,0:T(8,128)(2,1)}) custom-call(bf16[4,4,1,4,32,128]{5,4,3,2,1,0:T(8,128)(2,1)} %bitcast.181, bf16[512,2048]{1,0:T(8,128)(2,1)} %get-tuple-element.272.w_ref.refs_4_), custom_call_target="tpu_custom_call" | custom-call | flops 16777216 | bytes 81920 | tf_op jit(solution)/shard_map/project_from_pairs/pallas_call | solution.py:423
  158.6 10.1 %gated.2 = (bf16[256,1408]{1,0:T(8,128)(2,1)}, bf16[256,2816]{1,0:T(8,128)(2,1)}, f32[2,1,1408]{2,1,0:T(1,128)}, bf16[256,2048]{1,0:T(8,128)(2,1)}) custom-call(bf16[64,2048]{1,0:T(8,128)(2,1)} %bitcast.185, bf16[64,2048]{1,0:T(8,128)(2,1)} %bitcast.48.refs_1_, bf16[64,2048]{1,0:T(8,128)(2,1)} %bitcast.208, bf16[64,2048]{1,0:T(8,128)(2,1)} %bitcast.211, ...), custom_call_target="tpu_custom_call" | custom-call | flops 46137344 | bytes 258048 | tf_op jit(solution)/shard_map/gated/pallas_call | solution.py:637
  175.3 7.8 %project_split.4 = (bf16[64,2048]{1,0:T(8,128)(2,1)}, bf16[64,2048]{1,0:T(8,128)(2,1)}, bf16[2,64,2048]{2,1,0:T(8,128)(2,1)}) custom-call(bf16[256,2816]{1,0:T(8,128)(2,1)} %get-tuple-element.396.refs_0_.refs_2_, bf16[2048,2816]{1,0:T(8,128)(2,1)} %get-tuple-element.308.refs_4_.refs_1_), custom_call_target="tpu_custom_call" | custom-call | flops 46137344 | bytes 219136 | tf_op jit(solution)/shard_map/project_split/pallas_call | solution.py:456
  191.3 13.8 %gated.3 = (bf16[512,1408]{1,0:T(8,128)(2,1)}, bf16[512,2816]{1,0:T(8,128)(2,1)}, f32[2,1,1408]{2,1,0:T(1,128)}, bf16[512,2048]{1,0:T(8,128)(2,1)}) custom-call(bf16[128,2048]{1,0:T(8,128)(2,1)} %bitcast.56.refs_0_, bf16[128,2048]{1,0:T(8,128)(2,1)} %bitcast.57.refs_1_, bf16[128,2048]{1,0:T(8,128)(2,1)} %bitcast.58.refs_2_, ...), custom_call_target="tpu_custom_call" | custom-call | flops 92274688 | bytes 335872 | tf_op jit(solution)/shard_map/gated/pallas_call | solution.py:637
  210.2 10.5 %project_split.5 = (bf16[128,2048]{1,0:T(8,128)(2,1)}, bf16[128,2048]{1,0:T(8,128)(2,1)}, bf16[2,128,2048]{2,1,0:T(8,128)(2,1)}) custom-call(bf16[512,2816]{1,0:T(8,128)(2,1)} %get-tuple-element.397.refs_0_.refs_3_, bf16[2048,2816]{1,0:T(8,128)(2,1)} %get-tuple-element.308.refs_4_.refs_1_), custom_call_target="tpu_custom_call" | custom-call | flops 92274688 | bytes 258048 | tf_op jit(solution)/shard_map/project_split/pallas_call | solution.py:456
  232.0 6.2 %all-to-all-start.4 = ((bf16[8,1,1,128,128]{4,3,2,1,0:T(8,128)(2,1)}), bf16[8,1,1,128,128]{4,3,2,1,0:T(8,128)(2,1)}, u32[]{:S(2)}, u32[]{:S(2)}) async-start(bf16[8,1,1,128,128]{4,3,2,1,0:T(8,128)(2,1)} %bitcast.215), calls=%async_computation.4 | async-start | bytes 524288 | tf_op jit(solution)/shard_map/all_to_all | solution.py:65
  247.2 5.3 %attend_back.2 = (bf16[8,1,3,128,128]{4,3,2,1,0:T(8,128)(2,1)}, f32[1,3,128]{2,1,0:T(4,128)}) custom-call(bf16[8,1,3,128,128]{4,3,2,1,0:T(8,128)(2,1)} %copy-done.5, bf16[8,1,128,128]{3,2,1,0:T(8,128)(2,1)} %get-tuple-element.263.o_ref, bf16[8,1,128,128]{3,2,1,0:T(8,128)(2,1)} %bitcast.71.d_ref, f32[1,1,1024]{2,1,0:T(1,128)} %get-tuple-element.350.l_ref, ...), custom_call_target="tpu_custom_call" | custom-call | flops 20971520 | bytes 32768 | tf_op jit(solution)/shard_map/attend_back/pallas_call | solution.py:295
  252.6 5.3 %all-to-all-start.5 = ((bf16[8,1,3,128,128]{4,3,2,1,0:T(8,128)(2,1)}), bf16[8,1,3,128,128]{4,3,2,1,0:T(8,128)(2,1)S(1)}, u32[]{:S(2)}, u32[]{:S(2)}) async-start(bf16[8,1,3,128,128]{4,3,2,1,0:T(8,128)(2,1)} %get-tuple-element.365), calls=%async_computation.5 | async-start | bytes 1572864 | tf_op jit(solution)/shard_map/all_to_all | solution.py:65
  259.5 8.7 %project_split.6 = (bf16[192,2048]{1,0:T(8,128)(2,1)}, bf16[192,2048]{1,0:T(8,128)(2,1)}, bf16[2,192,2048]{2,1,0:T(8,128)(2,1)}) custom-call(bf16[512,1408]{1,0:T(8,128)(2,1)} %get-tuple-element.356.refs_0_.refs_1_, bf16[256,1408]{1,0:T(8,128)(2,1)} %get-tuple-element.357.refs_1_.refs_0_, bf16[1408,2048]{1,0:T(8,128)(2,1)} %get-tuple-element.287.refs_4_.refs_2_), custom_call_target="tpu_custom_call" | custom-call | flops 69206016 | bytes 173056 | tf_op jit(solution)/shard_map/project_split/pallas_call | solution.py:456
  274.8 5.0 %project_to_pairs.7 = (bf16[4,4,1,4,32,128]{5,4,3,2,1,0:T(8,128)(2,1)}, bf16[512,2048]{1,0:T(8,128)(2,1)}) custom-call(bf16[128,2048]{1,0:T(8,128)(2,1)} %bitcast.182, bf16[128,2048]{1,0:T(8,128)(2,1)} %bitcast.76.refs_1_, bf16[128,2048]{1,0:T(8,128)(2,1)} %bitcast.77.refs_2_, bf16[128,2048]{1,0:T(8,128)(2,1)} %bitcast.78.refs_3_, ...), custom_call_target="tpu_custom_call" | custom-call | flops 16777216 | bytes 98304 | tf_op jit(solution)/shard_map/project_to_pairs/pallas_call | solution.py:358
  279.8 6.0 %all-to-all-start.6 = ((bf16[8,2,1,128,128]{4,3,1,2,0:T(8,128)(2,1)}), bf16[8,2,1,128,128]{4,3,1,2,0:T(8,128)(2,1)}, u32[]{:S(2)}, u32[]{:S(2)}) async-start(bf16[8,2,1,128,128]{4,3,1,2,0:T(8,128)(2,1)} %bitcast.204), calls=%async_computation.6 | async-start | bytes 1048576 | tf_op jit(solution)/shard_map/all_to_all | solution.py:65
  291.1 6.0 %row_grads.2 = (bf16[16,512]{1,0:T(8,128)(2,1)}, bf16[16,2048]{1,0:T(8,128)(2,1)}) custom-call(bf16[256,512]{1,0:T(8,128)(2,1)} %get-tuple-element.370.refs_0_, bf16[512,512]{1,0:T(8,128)(2,1)} %get-tuple-element.371.refs_1_, bf16[256,2048]{1,0:T(8,128)(2,1)} %get-tuple-element.372.refs_2_, bf16[512,2048]{1,0:T(8,128)(2,1)} %get-tuple-element.373.refs_3_, ...), custom_call_target="tpu_custom_call" | custom-call | flops 4194304 | bytes 94208 | tf_op jit(solution)/shard_map/row_grads/pallas_call | solution.py:806
  300.7 8.1 %attend_back.3 = (bf16[8,2,3,128,128]{4,3,2,1,0:T(8,128)(2,1)}, f32[2,3,128]{2,1,0:T(4,128)}) custom-call(bf16[8,2,3,128,128]{4,3,2,1,0:T(8,128)(2,1)} %copy-done.1, bf16[8,2,128,128]{3,2,1,0:T(8,128)(2,1)} %get-tuple-element.270.o_ref, bf16[8,2,128,128]{3,2,1,0:T(8,128)(2,1)} %bitcast.83.d_ref, f32[2,1,1024]{2,1,0:T(1,128)} %get-tuple-element.378.l_ref, ...), custom_call_target="tpu_custom_call" | custom-call | flops 41943040 | bytes 65536 | tf_op jit(solution)/shard_map/attend_back/pallas_call | solution.py:295
  308.9 4.6 %all-to-all-start.7 = ((bf16[8,2,3,128,128]{4,3,2,1,0:T(8,128)(2,1)}), bf16[8,2,3,128,128]{4,3,2,1,0:T(8,128)(2,1)}, u32[]{:S(2)}, u32[]{:S(2)}) async-start(bf16[8,2,3,128,128]{4,3,2,1,0:T(8,128)(2,1)} %get-tuple-element.385), calls=%async_computation.7 | async-start | bytes 3145728 | tf_op jit(solution)/shard_map/all_to_all | solution.py:65
  318.3 17.8 %column_grads.2 = (bf16[2,16,1408]{2,1,0:T(8,128)(2,1)}, bf16[32,2048]{1,0:T(8,128)(2,1)}) custom-call(bf16[256,2048]{1,0:T(8,128)(2,1)} %get-tuple-element.394.refs_0_, bf16[512,2048]{1,0:T(8,128)(2,1)} %get-tuple-element.395.refs_1_, bf16[256,2816]{1,0:T(8,128)(2,1)} %get-tuple-element.396.refs_0_.refs_2_, ...), custom_call_target="tpu_custom_call" | custom-call | flops 23068672 | bytes 296960 | tf_op jit(solution)/shard_map/column_grads/pallas_call | solution.py:735
  344.6 8.4 %row_grads.3 = (bf16[16,1408]{1,0:T(8,128)(2,1)}, bf16[16,2048]{1,0:T(8,128)(2,1)}) custom-call(bf16[256,1408]{1,0:T(8,128)(2,1)} %get-tuple-element.357.refs_1_.refs_0_, bf16[512,1408]{1,0:T(8,128)(2,1)} %get-tuple-element.356.refs_0_.refs_1_, bf16[256,2048]{1,0:T(8,128)(2,1)} %get-tuple-element.405.refs_2_, bf16[512,2048]{1,0:T(8,128)(2,1)} %get-tuple-element.406.refs_3_, ...), custom_call_target="tpu_custom_call" | custom-call | flops 11534336 | bytes 173056 | tf_op jit(solution)/shard_map/row_grads/pallas_call | solution.py:806
  353.0 11.4 %column_grads.3 = (bf16[3,16,512]{2,1,0:T(8,128)(2,1)}, bf16[48,2048]{1,0:T(8,128)(2,1)}, bf16[512,1536]{1,0:T(8,128)(2,1)}) custom-call(bf16[256,2048]{1,0:T(8,128)(2,1)} %get-tuple-element.414.refs_0_, bf16[512,2048]{1,0:T(8,128)(2,1)} %get-tuple-element.415.refs_1_, bf16[256,1536]{1,0:T(8,128)(2,1)} %assemble.1.refs_2_.refs_1_, ...), custom_call_target="tpu_custom_call" | custom-call | flops 12582912 | bytes 184320 | tf_op jit(solution)/shard_map/column_grads/pallas_call | solution.py:735
  366.5 5.9 %all-to-all-start.8 = ((bf16[8,16,2688]{2,1,0:T(8,128)(2,1)}), bf16[8,16,2688]{2,1,0:T(8,128)(2,1)S(1)}, u32[]{:S(2)}, u32[]{:S(2)}) async-start(bf16[8,16,2688]{2,1,0:T(8,128)(2,1)} %pack.1), calls=%async_computation.8 | async-start | bytes 1376256 | tf_op jit(solution)/shard_map/all_to_all | solution.py:65
  372.5 8.9 %project_split.7 = (bf16[192,2048]{1,0:T(8,128)(2,1)}, bf16[192,2048]{1,0:T(8,128)(2,1)}, bf16[2,192,2048]{2,1,0:T(8,128)(2,1)}) custom-call(bf16[512,1536]{1,0:T(8,128)(2,1)} %get-tuple-element.429.refs_0_, bf16[256,1536]{1,0:T(8,128)(2,1)} %assemble.1.refs_2_.refs_1_, bf16[2048,1536]{1,0:T(8,128)(2,1)} %get-tuple-element.238.refs_4_.refs_2_), custom_call_target="tpu_custom_call" | custom-call | flops 75497472 | bytes 184320 | tf_op jit(solution)/shard_map/project_split/pallas_call | solution.py:456
  381.4 9.4 %all-to-all-done.8 = bf16[8,16,2688]{2,1,0:T(8,128)(2,1)S(1)} async-done(((bf16[8,16,2688]{2,1,0:T(8,128)(2,1)}), bf16[8,16,2688]{2,1,0:T(8,128)(2,1)S(1)}, u32[]{:S(2)}, u32[]{:S(2)}) %all-to-all-start.8) | async-done | bytes 688160 | tf_op jit(solution)/shard_map/all_to_all | solution.py:65
  404.8 13.8 %collective-permute-done.47 = bf16[6,32,2048]{2,1,0:T(8,128)(2,1)} collective-permute-done((bf16[6,32,2048]{2,1,0:T(8,128)(2,1)}, bf16[6,32,2048]{2,1,0:T(8,128)(2,1)}, u32[]{:S(2)}, u32[]{:S(2)}) %collective-permute-start.47) | collective-permute-done | bytes 786464 | tf_op jit(solution)/shard_map/ppermute | solution.py:36
  (310 shorter events, 161.8 us)
Async XLA Ops:
  3.0 16.3 %collective-permute-start.1 = (bf16[2,32,2048]{2,1,0:T(8,128)(2,1)S(1)}, bf16[2,32,2048]{2,1,0:T(8,128)(2,1)S(1)}, u32[]{:S(2)}, u32[]{:S(2)}) collective-permute-start(bf16[2,32,2048]{2,1,0:T(8,128)(2,1)S(1)} %fusion.20), channel_id=1, source_target_pairs={{0,1},{1,0},{2,3},{3,2},{4,5},{5,4},{6,7},{7,6},{8,9},{9,8},{10,11... | collective-permute-start | bytes 786440 | tf_op jit(solution)/shard_map/ppermute | solution.py:36
  3.5 15.8 %collective-permute-start = (bf16[2,32,2048]{2,1,0:T(8,128)(2,1)S(1)}, bf16[2,32,2048]{2,1,0:T(8,128)(2,1)}, u32[]{:S(2)}, u32[]{:S(2)}) collective-permute-start(bf16[2,32,2048]{2,1,0:T(8,128)(2,1)S(1)} %fusion.20), channel_id=1, source_target_pairs={{0,2},{1,3},{2,0},{3,1},{4,6},{5,7},{6,4},{7,5},{8,10},{9,11},{10,... | collective-permute-start | bytes 786440 | tf_op jit(solution)/shard_map/ppermute | solution.py:36
  8.2 19.7 %collective-permute-start.4 = (bf16[4,32,2048]{2,1,0:T(8,128)(2,1)S(1)}, bf16[4,32,2048]{2,1,0:T(8,128)(2,1)S(1)}, u32[]{:S(2)}, u32[]{:S(2)}) collective-permute-start(bf16[4,32,2048]{2,1,0:T(8,128)(2,1)S(1)} %fusion.13), channel_id=1, source_target_pairs={{0,1},{1,0},{2,3},{3,2},{4,5},{5,4},{6,7},{7,6},{8,9},{9,8},{10,11... | collective-permute-start | bytes 1572872 | tf_op jit(solution)/shard_map/ppermute | solution.py:36
  8.4 19.5 %collective-permute-start.3 = (bf16[4,32,2048]{2,1,0:T(8,128)(2,1)S(1)}, bf16[4,32,2048]{2,1,0:T(8,128)(2,1)S(1)}, u32[]{:S(2)}, u32[]{:S(2)}) collective-permute-start(bf16[4,32,2048]{2,1,0:T(8,128)(2,1)S(1)} %fusion.13), channel_id=1, source_target_pairs={{0,2},{1,3},{2,0},{3,1},{4,6},{5,7},{6,4},{7,5},{8,10},{9,11},{10,... | collective-permute-start | bytes 1572872 | tf_op jit(solution)/shard_map/ppermute | solution.py:36
  28.9 26.6 %all-to-all-start = ((bf16[8,1,3,128,128]{4,3,2,1,0:T(8,128)(2,1)}), bf16[8,1,3,128,128]{4,3,2,1,0:T(8,128)(2,1)S(1)}, u32[]{:S(2)}, u32[]{:S(2)}) async-start(bf16[8,1,3,128,128]{4,3,2,1,0:T(8,128)(2,1)} %bitcast.188), calls=%async_computation | async-start | bytes 1572864 | tf_op jit(solution)/shard_map/all_to_all | solution.py:65
  35.2 9.1 %collective-permute-start.5 = (bf16[4,32,2048]{2,1,0:T(8,128)(2,1)}, bf16[4,32,2048]{2,1,0:T(8,128)(2,1)S(1)}, u32[]{:S(2)}, u32[]{:S(2)}) collective-permute-start(bf16[4,32,2048]{2,1,0:T(8,128)(2,1)} %copy-done.24), channel_id=1, source_target_pairs={{0,1},{1,0},{2,3},{3,2},{4,5},{5,4},{6,7},{7,6},{8,9},{9,8},{10,11... | collective-permute-start | bytes 1572872 | tf_op jit(solution)/shard_map/ppermute | solution.py:36
  57.4 42.2 %all-to-all-start.1 = ((bf16[8,2,3,128,128]{4,3,2,1,0:T(8,128)(2,1)}), bf16[8,2,3,128,128]{4,3,2,1,0:T(8,128)(2,1)S(1)}, u32[]{:S(2)}, u32[]{:S(2)}) async-start(bf16[8,2,3,128,128]{4,3,2,1,0:T(8,128)(2,1)} %bitcast.183), calls=%async_computation.1 | async-start | bytes 3145728 | tf_op jit(solution)/shard_map/all_to_all | solution.py:65
  65.9 23.9 %collective-permute-start.10 = (bf16[6,32,2048]{2,1,0:T(8,128)(2,1)S(1)}, bf16[6,32,2048]{2,1,0:T(8,128)(2,1)}, u32[]{:S(2)}, u32[]{:S(2)}) collective-permute-start(bf16[6,32,2048]{2,1,0:T(8,128)(2,1)S(1)} %get-tuple-element.283), channel_id=1, source_target_pairs={{0,1},{1,0},{2,3},{3,2},{4,5},{5,4},{6,7},{7,6},{8,9},{9,8},{10,11... | collective-permute-start | bytes 2359304 | tf_op jit(solution)/shard_map/ppermute | solution.py:36
  66.1 23.7 %collective-permute-start.9 = (bf16[6,32,2048]{2,1,0:T(8,128)(2,1)S(1)}, bf16[6,32,2048]{2,1,0:T(8,128)(2,1)}, u32[]{:S(2)}, u32[]{:S(2)}) collective-permute-start(bf16[6,32,2048]{2,1,0:T(8,128)(2,1)S(1)} %get-tuple-element.283), channel_id=1, source_target_pairs={{0,2},{1,3},{2,0},{3,1},{4,6},{5,7},{6,4},{7,5},{8,10},{9,11},{10,... | collective-permute-start | bytes 2359304 | tf_op jit(solution)/shard_map/ppermute | solution.py:36
  89.8 9.1 %collective-permute-start.11 = (bf16[6,32,2048]{2,1,0:T(8,128)(2,1)}, bf16[6,32,2048]{2,1,0:T(8,128)(2,1)S(1)}, u32[]{:S(2)}, u32[]{:S(2)}) collective-permute-start(bf16[6,32,2048]{2,1,0:T(8,128)(2,1)} %collective-permute-done.9), channel_id=1, source_target_pairs={{0,1},{1,0},{2,3},{3,2},{4,5},{5,4},{6,7},{7,6},{8,9},{9,8},{10,11... | collective-permute-start | bytes 2359304 | tf_op jit(solution)/shard_map/ppermute | solution.py:36
  99.6 13.6 %collective-permute-start.14 = (f32[1,2048]{1,0:T(1,128)S(1)}, f32[1,2048]{1,0:T(1,128)S(1)}, u32[]{:S(2)}, u32[]{:S(2)}) collective-permute-start(f32[1,2048]{1,0:T(1,128)S(1)} %copy-done.42), channel_id=1, source_target_pairs={{0,3},{1,2},{2,1},{3,0},{4,7},{5,6},{6,5},{7,4},{8,11},{9,10},{10,... | collective-permute-start | bytes 24584 | tf_op jit(solution)/shard_map/ppermute | solution.py:36
  100.1 13.1 %collective-permute-start.13 = (f32[1,2048]{1,0:T(1,128)S(1)}, f32[1,2048]{1,0:T(1,128)S(1)}, u32[]{:S(2)}, u32[]{:S(2)}) collective-permute-start(f32[1,2048]{1,0:T(1,128)S(1)} %copy-done.42), channel_id=1, source_target_pairs={{0,2},{1,3},{2,0},{3,1},{4,6},{5,7},{6,4},{7,5},{8,10},{9,11},{10,... | collective-permute-start | bytes 24584 | tf_op jit(solution)/shard_map/ppermute | solution.py:36
  101.1 12.1 %collective-permute-start.12 = (f32[1,2048]{1,0:T(1,128)S(1)}, f32[1,2048]{1,0:T(1,128)S(1)}, u32[]{:S(2)}, u32[]{:S(2)}) collective-permute-start(f32[1,2048]{1,0:T(1,128)S(1)} %copy-done.42), channel_id=1, source_target_pairs={{0,1},{1,0},{2,3},{3,2},{4,5},{5,4},{6,7},{7,6},{8,9},{9,8},{10,11... | collective-permute-start | bytes 24584 | tf_op jit(solution)/shard_map/ppermute | solution.py:36
  101.4 15.0 %all-to-all-start.2 = ((bf16[8,1,1,128,128]{4,3,2,1,0:T(8,128)(2,1)}), bf16[8,1,1,128,128]{4,3,2,1,0:T(8,128)(2,1)S(1)}, u32[]{:S(2)}, u32[]{:S(2)}) async-start(bf16[8,1,1,128,128]{4,3,2,1,0:T(8,128)(2,1)} %bitcast.187), calls=%async_computation.2 | async-start | bytes 524288 | tf_op jit(solution)/shard_map/all_to_all | solution.py:65
  124.5 18.2 %collective-permute-start.16 = (bf16[2,32,2048]{2,1,0:T(8,128)(2,1)S(1)}, bf16[2,32,2048]{2,1,0:T(8,128)(2,1)S(1)}, u32[]{:S(2)}, u32[]{:S(2)}) collective-permute-start(bf16[2,32,2048]{2,1,0:T(8,128)(2,1)S(1)} %fusion.24), channel_id=1, source_target_pairs={{0,2},{1,3},{2,0},{3,1},{4,6},{5,7},{6,4},{7,5},{8,10},{9,11},{10,... | collective-permute-start | bytes 786440 | tf_op jit(solution)/shard_map/ppermute | solution.py:36
  125.1 20.5 %all-to-all-start.3 = ((bf16[8,2,1,128,128]{4,3,1,2,0:T(8,128)(2,1)}), bf16[8,2,1,128,128]{4,3,1,2,0:T(8,128)(2,1)S(1)}, u32[]{:S(2)}, u32[]{:S(2)}) async-start(bf16[8,2,1,128,128]{4,3,1,2,0:T(8,128)(2,1)} %bitcast.40), calls=%async_computation.3 | async-start | bytes 1048576 | tf_op jit(solution)/shard_map/all_to_all | solution.py:65
  157.0 14.1 %collective-permute-start.21 = (bf16[4,32,2048]{2,1,0:T(8,128)(2,1)S(1)}, bf16[4,32,2048]{2,1,0:T(8,128)(2,1)}, u32[]{:S(2)}, u32[]{:S(2)}) collective-permute-start(bf16[4,32,2048]{2,1,0:T(8,128)(2,1)S(1)} %fusion.17), channel_id=1, source_target_pairs={{0,2},{1,3},{2,0},{3,1},{4,6},{5,7},{6,4},{7,5},{8,10},{9,11},{10,... | collective-permute-start | bytes 1572872 | tf_op jit(solution)/shard_map/ppermute | solution.py:36
  173.8 13.5 %collective-permute-start.22 = (bf16[4,32,2048]{2,1,0:T(8,128)(2,1)}, bf16[4,32,2048]{2,1,0:T(8,128)(2,1)}, u32[]{:S(2)}, u32[]{:S(2)}) collective-permute-start(bf16[4,32,2048]{2,1,0:T(8,128)(2,1)} %multiply_convert_fusion.2), channel_id=1, source_target_pairs={{0,2},{1,3},{2,0},{3,1},{4,6},{5,7},{6,4},{7,5},{8,10},{9,11},{10,... | collective-permute-start | bytes 1572872 | tf_op jit(solution)/shard_map/ppermute | solution.py:36
  189.8 15.3 %collective-permute-start.26 = (bf16[2,32,2048]{2,1,0:T(8,128)(2,1)}, bf16[2,32,2048]{2,1,0:T(8,128)(2,1)}, u32[]{:S(2)}, u32[]{:S(2)}) collective-permute-start(bf16[2,32,2048]{2,1,0:T(8,128)(2,1)} %fusion.22), channel_id=1, source_target_pairs={{0,2},{1,3},{2,0},{3,1},{4,6},{5,7},{6,4},{7,5},{8,10},{9,11},{10,... | collective-permute-start | bytes 786440 | tf_op jit(solution)/shard_map/ppermute | solution.py:36
  209.4 11.2 %collective-permute-start.28 = (bf16[2,32,2048]{2,1,0:T(8,128)(2,1)}, bf16[2,32,2048]{2,1,0:T(8,128)(2,1)}, u32[]{:S(2)}, u32[]{:S(2)}) collective-permute-start(bf16[2,32,2048]{2,1,0:T(8,128)(2,1)} %multiply_convert_fusion.3), channel_id=1, source_target_pairs={{0,1},{1,0},{2,3},{3,2},{4,5},{5,4},{6,7},{7,6},{8,9},{9,8},{10,11... | collective-permute-start | bytes 786440 | tf_op jit(solution)/shard_map/ppermute | solution.py:36
  209.7 11.0 %collective-permute-start.27 = (bf16[2,32,2048]{2,1,0:T(8,128)(2,1)}, bf16[2,32,2048]{2,1,0:T(8,128)(2,1)}, u32[]{:S(2)}, u32[]{:S(2)}) collective-permute-start(bf16[2,32,2048]{2,1,0:T(8,128)(2,1)} %multiply_convert_fusion.3), channel_id=1, source_target_pairs={{0,2},{1,3},{2,0},{3,1},{4,6},{5,7},{6,4},{7,5},{8,10},{9,11},{10,... | collective-permute-start | bytes 786440 | tf_op jit(solution)/shard_map/ppermute | solution.py:36
  226.9 14.3 %collective-permute-start.31 = (bf16[4,32,2048]{2,1,0:T(8,128)(2,1)}, bf16[4,32,2048]{2,1,0:T(8,128)(2,1)}, u32[]{:S(2)}, u32[]{:S(2)}) collective-permute-start(bf16[4,32,2048]{2,1,0:T(8,128)(2,1)} %fusion.15), channel_id=1, source_target_pairs={{0,2},{1,3},{2,0},{3,1},{4,6},{5,7},{6,4},{7,5},{8,10},{9,11},{10,... | collective-permute-start | bytes 1572872 | tf_op jit(solution)/shard_map/ppermute | solution.py:36
  232.0 15.2 %all-to-all-start.4 = ((bf16[8,1,1,128,128]{4,3,2,1,0:T(8,128)(2,1)}), bf16[8,1,1,128,128]{4,3,2,1,0:T(8,128)(2,1)}, u32[]{:S(2)}, u32[]{:S(2)}) async-start(bf16[8,1,1,128,128]{4,3,2,1,0:T(8,128)(2,1)} %bitcast.215), calls=%async_computation.4 | async-start | bytes 524288 | tf_op jit(solution)/shard_map/all_to_all | solution.py:65
  252.6 27.3 %all-to-all-start.5 = ((bf16[8,1,3,128,128]{4,3,2,1,0:T(8,128)(2,1)}), bf16[8,1,3,128,128]{4,3,2,1,0:T(8,128)(2,1)S(1)}, u32[]{:S(2)}, u32[]{:S(2)}) async-start(bf16[8,1,3,128,128]{4,3,2,1,0:T(8,128)(2,1)} %get-tuple-element.365), calls=%async_computation.5 | async-start | bytes 1572864 | tf_op jit(solution)/shard_map/all_to_all | solution.py:65
  257.9 10.3 %collective-permute-start.33 = (bf16[4,32,2048]{2,1,0:T(8,128)(2,1)}, bf16[4,32,2048]{2,1,0:T(8,128)(2,1)}, u32[]{:S(2)}, u32[]{:S(2)}) collective-permute-start(bf16[4,32,2048]{2,1,0:T(8,128)(2,1)} %multiply_convert_fusion.1), channel_id=1, source_target_pairs={{0,1},{1,0},{2,3},{3,2},{4,5},{5,4},{6,7},{7,6},{8,9},{9,8},{10,11... | collective-permute-start | bytes 1572872 | tf_op jit(solution)/shard_map/ppermute | solution.py:36
  257.9 14.6 %collective-permute-start.32 = (bf16[4,32,2048]{2,1,0:T(8,128)(2,1)}, bf16[4,32,2048]{2,1,0:T(8,128)(2,1)}, u32[]{:S(2)}, u32[]{:S(2)}) collective-permute-start(bf16[4,32,2048]{2,1,0:T(8,128)(2,1)} %multiply_convert_fusion.1), channel_id=1, source_target_pairs={{0,2},{1,3},{2,0},{3,1},{4,6},{5,7},{6,4},{7,5},{8,10},{9,11},{10,... | collective-permute-start | bytes 1572872 | tf_op jit(solution)/shard_map/ppermute | solution.py:36
  279.8 20.9 %all-to-all-start.6 = ((bf16[8,2,1,128,128]{4,3,1,2,0:T(8,128)(2,1)}), bf16[8,2,1,128,128]{4,3,1,2,0:T(8,128)(2,1)}, u32[]{:S(2)}, u32[]{:S(2)}) async-start(bf16[8,2,1,128,128]{4,3,1,2,0:T(8,128)(2,1)} %bitcast.204), calls=%async_computation.6 | async-start | bytes 1048576 | tf_op jit(solution)/shard_map/all_to_all | solution.py:65
  308.9 44.1 %all-to-all-start.7 = ((bf16[8,2,3,128,128]{4,3,2,1,0:T(8,128)(2,1)}), bf16[8,2,3,128,128]{4,3,2,1,0:T(8,128)(2,1)}, u32[]{:S(2)}, u32[]{:S(2)}) async-start(bf16[8,2,3,128,128]{4,3,2,1,0:T(8,128)(2,1)} %get-tuple-element.385), calls=%async_computation.7 | async-start | bytes 3145728 | tf_op jit(solution)/shard_map/all_to_all | solution.py:65
  315.9 20.2 %collective-permute-start.39 = (bf16[6,32,2048]{2,1,0:T(8,128)(2,1)}, bf16[6,32,2048]{2,1,0:T(8,128)(2,1)}, u32[]{:S(2)}, u32[]{:S(2)}) collective-permute-start(bf16[6,32,2048]{2,1,0:T(8,128)(2,1)} %fusion.10), channel_id=1, source_target_pairs={{0,2},{1,3},{2,0},{3,1},{4,6},{5,7},{6,4},{7,5},{8,10},{9,11},{10,... | collective-permute-start | bytes 2359304 | tf_op jit(solution)/shard_map/ppermute | solution.py:36
  366.5 24.3 %all-to-all-start.8 = ((bf16[8,16,2688]{2,1,0:T(8,128)(2,1)}), bf16[8,16,2688]{2,1,0:T(8,128)(2,1)S(1)}, u32[]{:S(2)}, u32[]{:S(2)}) async-start(bf16[8,16,2688]{2,1,0:T(8,128)(2,1)} %pack.1), calls=%async_computation.8 | async-start | bytes 1376256 | tf_op jit(solution)/shard_map/all_to_all | solution.py:65
  398.6 19.9 %collective-permute-start.47 = (bf16[6,32,2048]{2,1,0:T(8,128)(2,1)}, bf16[6,32,2048]{2,1,0:T(8,128)(2,1)}, u32[]{:S(2)}, u32[]{:S(2)}) collective-permute-start(bf16[6,32,2048]{2,1,0:T(8,128)(2,1)} %fusion.8), channel_id=1, source_target_pairs={{0,2},{1,3},{2,0},{3,1},{4,6},{5,7},{6,4},{7,5},{8,10},{9,11},{10,... | collective-permute-start | bytes 2359304 | tf_op jit(solution)/shard_map/ppermute | solution.py:36
  400.5 22.8 %all-to-all-start.9 = ((bf16[8,16,2688]{2,1,0:T(8,128)(2,1)}), bf16[8,16,2688]{2,1,0:T(8,128)(2,1)}, u32[]{:S(2)}, u32[]{:S(2)}) async-start(bf16[8,16,2688]{2,1,0:T(8,128)(2,1)} %broadcast_in_dim.202), calls=%async_computation.9 | async-start | bytes 1376256 | tf_op jit(solution)/shard_map/all_to_all | solution.py:65
  (75 other events, 463.5 us)

commit v5 on v4

--- a/solution.py
+++ b/solution.py
@@ -17,7 +17,8 @@
 bf16 = jnp.bfloat16
 PIECES = (0, 2, 1, 3)
 score_block = 256
-GATED_BLOCKS = 2
+GATED_BLOCKS = 3
+LOG2_E = math.log2(math.e)
 NT = (((1,), (1,)), ((), ()))
 NN = (((1,), (0,)), ((), ()))
 TN = (((0,), (0,)), ((), ()))
@@ -177,7 +178,7 @@
 def weights_t(keys, queries, kpos, qpos, qstart, scale):
     scores = mm(keys, queries, NT)
     allowed = jnp.logical_and(kpos <= qpos, kpos >= qstart)
-    return jnp.where(allowed, jnp.exp(scores * scale), 0.0)
+    return jnp.where(allowed, jnp.exp2(scores * (scale * LOG2_E)), 0.0)
 
 
 def attend_kernel(x_ref, cos_ref, sin_ref, kpos_ref, qinfo_ref, o_ref, l_ref, qs, ks, vt, os, *, scale, block):
@@ -943,7 +944,7 @@
     fetched, outputs[1], whole_cot, out_scale = after(fetched, outputs[1], whole_cot, out_scale)
 
     returned = fetch_pairs(outputs[1][:, :, None], 1)
-    att[0], split = project_from_pairs(fetched, out_w, 512)
+    att[0], split = project_from_pairs(fetched, out_w, 1024)
     moving, whole_cot = after(scatter_start(*split), whole_cot)
     for c in span:
         dhid[c], du_down[c] = of_cotangent(whole_cot, c)
@@ -952,7 +953,7 @@
     middle[0] = wide_in[0] + u_out[0]
     started = gather_start(normed(middle[0], gain_ffn))
 
-    att[1], split = project_from_pairs(returned, out_w, 512)
+    att[1], split = project_from_pairs(returned, out_w, 1024)
     started, split = after(started, split)
     moving, whole = after(scatter_start(*split), gather_end(*started))
     hidden[0], d_gu[0], gu_sum[0], normed_f[0] = gated(whole, gu_w, dhid[0])
@@ -961,7 +962,7 @@
     middle[1] = wide_in[1] + u_out[1]
     h_f, d_gu[0] = after(normed(middle[1], gain_ffn), d_gu[0])
     started = gather_start(h_f)
-    split = project_split([d_gu[0]], gu_w, NT, 512, quarter)
+    split = project_split([d_gu[0]], gu_w, NT, 1024, quarter)
     whole, behind = after(gather_end(*started), scatter_start(*split))
 
     hidden[1], d_gu[1], gu_sum[1], normed_f[1] = gated(whole, gu_w, dhid[1])

time: 434 us -> 431 us (level)
  Pallas kernels: 218 us -> 213 us
  transfers between devices with their start and end apart: 58 -> 58, of which waited for: 21 -> 22; matrix products, arithmetic and copies ran while one was open for 9% -> 9% of each run, Pallas kernels for 43% -> 43%
where the time goes in v5:
time: 431 us; the launch traced here: 424 us
  Pallas kernels  213 us (49%)
  starting transfers between devices  82.3 us (19%)
  waiting for transfers between devices  68.5 us (16%)
  other arithmetic  44.5 us (10%)
  local copies, waits for them, and re-layouts  13.8 us (3%)
    all_to_all x10, starting transfers between devices, exchange(): return lax.all_to_all(values, 'seq', 0, 0, tiled=True)  52.4 us
    ppermute x48, waiting for transfers between devices, swap(): return lax.ppermute(values, 'tensor', [(i, i ^ bit) for i in range(size)])  48.7 us
    pallas_call x4, Pallas kernels, project_split(): pl.pallas_call(partial(project_split_kernel, dims=dims), grid=(out // blo...  35.5 us
    ppermute x48, starting transfers between devices, swap(): return lax.ppermute(values, 'tensor', [(i, i ^ bit) for i in range(size)])  29.9 us
    pallas_call x2, Pallas kernels, column_grads(): pl.pallas_call(partial(column_grads_kernel, chunks=chunks, steps=steps, j...  29.2 us
    pallas_call x2, Pallas kernels, column_prep(): pl.pallas_call(column_prep_kernel, grid=(out // block,), in_specs=[pl.Blo...  25.5 us
    pallas_call x4, Pallas kernels, project_to_pairs(): pl.pallas_call(partial(to_pairs_kernel, dims=dims), grid=(parts, steps),...  22.9 us
    pallas_call x2, Pallas kernels, gated(): pl.pallas_call(gated_kernel, grid=(-(-out // block),), in_specs=[pl.Block...  22.2 us
  transfers between devices with their start and end apart: 58, of which 22 were waited for; matrix products, arithmetic and copies ran while one was open for 9% of the time, Pallas kernels for 43%

profile of v5, /device:TPU:0, one launch (start us, length us, event | category | flops | bytes accessed | tf_op | source)
XLA Modules:
  0.0 423.9 jit_solution(16860523471408895814)
XLA Ops:
  10.4 8.9 %column_prep.2 = (bf16[2048,1536]{1,0:T(8,128)(2,1)}, f32[3,2,512]{2,1,0:T(2,128)}, f32[3,16,512]{2,1,0:T(8,128)}) custom-call(bf16[3,2048,512]{2,1,0:T(8,128)(2,1)} %w_ref.1, bf16[48,2048]{1,0:T(8,128)(2,1)} %bitcast.192, bf16[2,48,768]{2,1,0:T(8,128)(2,1)} %broadcast_multiply_fusion.1.b_ref, f32[3,1,512]{2,1,0:T(1,128)} %broadcast_in_dim.103.m_ref.refs_8_), custom_call_target="tpu_custom_call" | custom-call | flops 50331648 | bytes 196608 | tf_op jit(solution)/shard_map/column_prep/pallas_call | solution.py:104
  21.8 6.1 %project_to_pairs.4 = (bf16[2,4,3,4,32,128]{5,4,3,2,1,0:T(8,128)(2,1)}, bf16[256,2048]{1,0:T(8,128)(2,1)}) custom-call(bf16[64,2048]{1,0:T(8,128)(2,1)} %bitcast.184, bf16[64,2048]{1,0:T(8,128)(2,1)} %bitcast.4.refs_1_, bf16[64,2048]{1,0:T(8,128)(2,1)} %bitcast.207, bf16[64,2048]{1,0:T(8,128)(2,1)} %bitcast.214, ...), custom_call_target="tpu_custom_call" | custom-call | flops 25165824 | bytes 131072 | tf_op jit(solution)/shard_map/project_to_pairs/pallas_call | solution.py:359
  28.9 6.1 %all-to-all-start = ((bf16[8,1,3,128,128]{4,3,2,1,0:T(8,128)(2,1)}), bf16[8,1,3,128,128]{4,3,2,1,0:T(8,128)(2,1)S(1)}, u32[]{:S(2)}, u32[]{:S(2)}) async-start(bf16[8,1,3,128,128]{4,3,2,1,0:T(8,128)(2,1)} %bitcast.188), calls=%async_computation | async-start | bytes 1572864 | tf_op jit(solution)/shard_map/all_to_all | solution.py:66
  35.5 8.9 %row_prep.2 = (bf16[1408,2048]{1,0:T(8,128)(2,1)}, f32[16,2048]{1,0:T(8,128)}, f32[1,2048]{1,0:T(1,128)}) custom-call(bf16[1408,2048]{1,0:T(8,128)(2,1)} %w_ref.2, bf16[16,1408]{1,0:T(8,128)(2,1)} %bitcast.217, bf16[16,2048]{1,0:T(8,128)(2,1)} %refs_6_.6), custom_call_target="tpu_custom_call" | custom-call | flops 23068672 | bytes 180224 | tf_op jit(solution)/shard_map/row_prep/pallas_call | solution.py:142
  45.1 8.2 %project_to_pairs.5 = (bf16[4,4,3,4,32,128]{5,4,3,2,1,0:T(8,128)(2,1)}, bf16[512,2048]{1,0:T(8,128)(2,1)}) custom-call(bf16[128,2048]{1,0:T(8,128)(2,1)} %bitcast.180, bf16[128,2048]{1,0:T(8,128)(2,1)} %bitcast.197, bf16[128,2048]{1,0:T(8,128)(2,1)} %bitcast.196, bf16[128,2048]{1,0:T(8,128)(2,1)} %bitcast.200, ...), custom_call_target="tpu_custom_call" | custom-call | flops 50331648 | bytes 163840 | tf_op jit(solution)/shard_map/project_to_pairs/pallas_call | solution.py:359
  57.4 4.8 %all-to-all-start.1 = ((bf16[8,2,3,128,128]{4,3,2,1,0:T(8,128)(2,1)}), bf16[8,2,3,128,128]{4,3,2,1,0:T(8,128)(2,1)S(1)}, u32[]{:S(2)}, u32[]{:S(2)}) async-start(bf16[8,2,3,128,128]{4,3,2,1,0:T(8,128)(2,1)} %bitcast.183), calls=%async_computation.1 | async-start | bytes 3145728 | tf_op jit(solution)/shard_map/all_to_all | solution.py:66
  68.8 4.6 %row_prep.3 = (bf16[512,2048]{1,0:T(8,128)(2,1)}, f32[16,2048]{1,0:T(8,128)}, f32[1,2048]{1,0:T(1,128)}) custom-call(bf16[512,2048]{1,0:T(8,128)(2,1)} %w_ref.4, bf16[16,512]{1,0:T(8,128)(2,1)} %bitcast.219, bf16[16,2048]{1,0:T(8,128)(2,1)} %refs_6_.4), custom_call_target="tpu_custom_call" | custom-call | flops 8388608 | bytes 65536 | tf_op jit(solution)/shard_map/row_prep/pallas_call | solution.py:142
  73.4 16.6 %column_prep.3 = (bf16[2048,2816]{1,0:T(8,128)(2,1)}, f32[2,2,1408]{2,1,0:T(2,128)}, f32[2,16,1408]{2,1,0:T(8,128)}) custom-call(bf16[2,2048,1408]{2,1,0:T(8,128)(2,1)} %w_ref.3, bf16[32,2048]{1,0:T(8,128)(2,1)} %bitcast.194, bf16[11,32,256]{2,1,0:T(8,128)(2,1)} %broadcast_multiply_fusion.b_ref, f32[2,1,1408]{2,1,0:T(1,128)} %broadcast_in_dim.107.m_ref.refs_8_), custom_call_target="tpu_custom_call" | custom-call | flops 92274688 | bytes 360448 | tf_op jit(solution)/shard_map/column_prep/pallas_call | solution.py:104
  101.7 5.4 %all-to-all-start.2 = ((bf16[8,1,1,128,128]{4,3,2,1,0:T(8,128)(2,1)}), bf16[8,1,1,128,128]{4,3,2,1,0:T(8,128)(2,1)S(1)}, u32[]{:S(2)}, u32[]{:S(2)}) async-start(bf16[8,1,1,128,128]{4,3,2,1,0:T(8,128)(2,1)} %bitcast.187), calls=%async_computation.2 | async-start | bytes 524288 | tf_op jit(solution)/shard_map/all_to_all | solution.py:66
  107.7 5.6 %attend.3 = (bf16[8,2,128,128]{3,2,1,0:T(8,128)(2,1)}, f32[2,1,1024]{2,1,0:T(1,128)}) custom-call(bf16[8,2,3,128,128]{4,3,2,1,0:T(8,128)(2,1)} %copy-done.1, f32[1024,128]{1,0:T(8,128)} %get-tuple-element.488.cos_ref, f32[1024,128]{1,0:T(8,128)} %get-tuple-element.489.sin_ref, s32[1024,1]{1,0:T(8,128)} %copy.57.kpos_ref, s32[2,2,1024]{2,1,0:T(2,128)} %pad_add_fusion.qinfo_ref), custom_call_target="tpu_custom_call" | custom-call | flops 16777216 | bytes 32768 | tf_op jit(solution)/shard_map/attend/pallas_call | solution.py:210
  127.9 5.7 %project_cotangent.2 = (bf16[256,1408]{1,0:T(8,128)(2,1)}, bf16[256,2048]{1,0:T(8,128)(2,1)}) custom-call(bf16[192,2048]{1,0:T(8,128)(2,1)} %bitcast.173, bf16[192,2048]{1,0:T(8,128)(2,1)} %bitcast.36.refs_1_, bf16[192,2048]{1,0:T(8,128)(2,1)} %bitcast.37.refs_2_, bf16[192,2048]{1,0:T(8,128)(2,1)} %bitcast.175, ...), custom_call_target="tpu_custom_call" | custom-call | flops 23068672 | bytes 122880 | tf_op jit(solution)/shard_map/project_cotangent/pallas_call | solution.py:484
  133.6 7.9 %project_cotangent.3 = (bf16[512,1408]{1,0:T(8,128)(2,1)}, bf16[512,2048]{1,0:T(8,128)(2,1)}) custom-call(bf16[192,2048]{1,0:T(8,128)(2,1)} %bitcast.174, bf16[192,2048]{1,0:T(8,128)(2,1)} %bitcast.36.refs_1_, bf16[192,2048]{1,0:T(8,128)(2,1)} %bitcast.37.refs_2_, bf16[192,2048]{1,0:T(8,128)(2,1)} %bitcast.176, ...), custom_call_target="tpu_custom_call" | custom-call | flops 46137344 | bytes 155648 | tf_op jit(solution)/shard_map/project_cotangent/pallas_call | solution.py:484
  157.3 9.2 %gated.2 = (bf16[256,1408]{1,0:T(8,128)(2,1)}, bf16[256,2816]{1,0:T(8,128)(2,1)}, f32[2,1,1408]{2,1,0:T(1,128)}, bf16[256,2048]{1,0:T(8,128)(2,1)}) custom-call(bf16[64,2048]{1,0:T(8,128)(2,1)} %bitcast.185, bf16[64,2048]{1,0:T(8,128)(2,1)} %bitcast.48.refs_1_, bf16[64,2048]{1,0:T(8,128)(2,1)} %bitcast.208, bf16[64,2048]{1,0:T(8,128)(2,1)} %bitcast.211, ...), custom_call_target="tpu_custom_call" | custom-call | flops 46137344 | bytes 258048 | tf_op jit(solution)/shard_map/gated/pallas_call | solution.py:638
  174.1 7.2 %project_split.4 = (bf16[64,2048]{1,0:T(8,128)(2,1)}, bf16[64,2048]{1,0:T(8,128)(2,1)}, bf16[2,64,2048]{2,1,0:T(8,128)(2,1)}) custom-call(bf16[256,2816]{1,0:T(8,128)(2,1)} %get-tuple-element.396.refs_0_.refs_2_, bf16[2048,2816]{1,0:T(8,128)(2,1)} %get-tuple-element.308.refs_4_.refs_1_), custom_call_target="tpu_custom_call" | custom-call | flops 46137344 | bytes 219136 | tf_op jit(solution)/shard_map/project_split/pallas_call | solution.py:457
  190.1 13.1 %gated.3 = (bf16[512,1408]{1,0:T(8,128)(2,1)}, bf16[512,2816]{1,0:T(8,128)(2,1)}, f32[2,1,1408]{2,1,0:T(1,128)}, bf16[512,2048]{1,0:T(8,128)(2,1)}) custom-call(bf16[128,2048]{1,0:T(8,128)(2,1)} %bitcast.56.refs_0_, bf16[128,2048]{1,0:T(8,128)(2,1)} %bitcast.57.refs_1_, bf16[128,2048]{1,0:T(8,128)(2,1)} %bitcast.58.refs_2_, ...), custom_call_target="tpu_custom_call" | custom-call | flops 92274688 | bytes 335872 | tf_op jit(solution)/shard_map/gated/pallas_call | solution.py:638
  208.2 10.7 %project_split.5 = (bf16[128,2048]{1,0:T(8,128)(2,1)}, bf16[128,2048]{1,0:T(8,128)(2,1)}, bf16[2,128,2048]{2,1,0:T(8,128)(2,1)}) custom-call(bf16[512,2816]{1,0:T(8,128)(2,1)} %get-tuple-element.397.refs_0_.refs_3_, bf16[2048,2816]{1,0:T(8,128)(2,1)} %get-tuple-element.308.refs_4_.refs_1_), custom_call_target="tpu_custom_call" | custom-call | flops 92274688 | bytes 258048 | tf_op jit(solution)/shard_map/project_split/pallas_call | solution.py:457
  230.2 6.0 %all-to-all-start.4 = ((bf16[8,1,1,128,128]{4,3,2,1,0:T(8,128)(2,1)}), bf16[8,1,1,128,128]{4,3,2,1,0:T(8,128)(2,1)}, u32[]{:S(2)}, u32[]{:S(2)}) async-start(bf16[8,1,1,128,128]{4,3,2,1,0:T(8,128)(2,1)} %bitcast.215), calls=%async_computation.4 | async-start | bytes 524288 | tf_op jit(solution)/shard_map/all_to_all | solution.py:66
  245.2 5.2 %attend_back.2 = (bf16[8,1,3,128,128]{4,3,2,1,0:T(8,128)(2,1)}, f32[1,3,128]{2,1,0:T(4,128)}) custom-call(bf16[8,1,3,128,128]{4,3,2,1,0:T(8,128)(2,1)} %copy-done.5, bf16[8,1,128,128]{3,2,1,0:T(8,128)(2,1)} %get-tuple-element.263.o_ref, bf16[8,1,128,128]{3,2,1,0:T(8,128)(2,1)} %bitcast.71.d_ref, f32[1,1,1024]{2,1,0:T(1,128)} %get-tuple-element.350.l_ref, ...), custom_call_target="tpu_custom_call" | custom-call | flops 20971520 | bytes 32768 | tf_op jit(solution)/shard_map/attend_back/pallas_call | solution.py:296
  250.5 5.5 %all-to-all-start.5 = ((bf16[8,1,3,128,128]{4,3,2,1,0:T(8,128)(2,1)}), bf16[8,1,3,128,128]{4,3,2,1,0:T(8,128)(2,1)S(1)}, u32[]{:S(2)}, u32[]{:S(2)}) async-start(bf16[8,1,3,128,128]{4,3,2,1,0:T(8,128)(2,1)} %get-tuple-element.365), calls=%async_computation.5 | async-start | bytes 1572864 | tf_op jit(solution)/shard_map/all_to_all | solution.py:66
  257.6 8.7 %project_split.6 = (bf16[192,2048]{1,0:T(8,128)(2,1)}, bf16[192,2048]{1,0:T(8,128)(2,1)}, bf16[2,192,2048]{2,1,0:T(8,128)(2,1)}) custom-call(bf16[512,1408]{1,0:T(8,128)(2,1)} %get-tuple-element.356.refs_0_.refs_1_, bf16[256,1408]{1,0:T(8,128)(2,1)} %get-tuple-element.357.refs_1_.refs_0_, bf16[1408,2048]{1,0:T(8,128)(2,1)} %get-tuple-element.287.refs_4_.refs_2_), custom_call_target="tpu_custom_call" | custom-call | flops 69206016 | bytes 173056 | tf_op jit(solution)/shard_map/project_split/pallas_call | solution.py:457
  272.9 5.0 %project_to_pairs.7 = (bf16[4,4,1,4,32,128]{5,4,3,2,1,0:T(8,128)(2,1)}, bf16[512,2048]{1,0:T(8,128)(2,1)}) custom-call(bf16[128,2048]{1,0:T(8,128)(2,1)} %bitcast.182, bf16[128,2048]{1,0:T(8,128)(2,1)} %bitcast.76.refs_1_, bf16[128,2048]{1,0:T(8,128)(2,1)} %bitcast.77.refs_2_, bf16[128,2048]{1,0:T(8,128)(2,1)} %bitcast.78.refs_3_, ...), custom_call_target="tpu_custom_call" | custom-call | flops 16777216 | bytes 98304 | tf_op jit(solution)/shard_map/project_to_pairs/pallas_call | solution.py:359
  277.9 6.0 %all-to-all-start.6 = ((bf16[8,2,1,128,128]{4,3,1,2,0:T(8,128)(2,1)}), bf16[8,2,1,128,128]{4,3,1,2,0:T(8,128)(2,1)}, u32[]{:S(2)}, u32[]{:S(2)}) async-start(bf16[8,2,1,128,128]{4,3,1,2,0:T(8,128)(2,1)} %bitcast.204), calls=%async_computation.6 | async-start | bytes 1048576 | tf_op jit(solution)/shard_map/all_to_all | solution.py:66
  289.2 6.0 %row_grads.2 = (bf16[16,512]{1,0:T(8,128)(2,1)}, bf16[16,2048]{1,0:T(8,128)(2,1)}) custom-call(bf16[256,512]{1,0:T(8,128)(2,1)} %get-tuple-element.370.refs_0_, bf16[512,512]{1,0:T(8,128)(2,1)} %get-tuple-element.371.refs_1_, bf16[256,2048]{1,0:T(8,128)(2,1)} %get-tuple-element.372.refs_2_, bf16[512,2048]{1,0:T(8,128)(2,1)} %get-tuple-element.373.refs_3_, ...), custom_call_target="tpu_custom_call" | custom-call | flops 4194304 | bytes 94208 | tf_op jit(solution)/shard_map/row_grads/pallas_call | solution.py:807
  298.8 7.9 %attend_back.3 = (bf16[8,2,3,128,128]{4,3,2,1,0:T(8,128)(2,1)}, f32[2,3,128]{2,1,0:T(4,128)}) custom-call(bf16[8,2,3,128,128]{4,3,2,1,0:T(8,128)(2,1)} %copy-done.1, bf16[8,2,128,128]{3,2,1,0:T(8,128)(2,1)} %get-tuple-element.270.o_ref, bf16[8,2,128,128]{3,2,1,0:T(8,128)(2,1)} %bitcast.83.d_ref, f32[2,1,1024]{2,1,0:T(1,128)} %get-tuple-element.378.l_ref, ...), custom_call_target="tpu_custom_call" | custom-call | flops 41943040 | bytes 65536 | tf_op jit(solution)/shard_map/attend_back/pallas_call | solution.py:296
  306.8 4.7 %all-to-all-start.7 = ((bf16[8,2,3,128,128]{4,3,2,1,0:T(8,128)(2,1)}), bf16[8,2,3,128,128]{4,3,2,1,0:T(8,128)(2,1)}, u32[]{:S(2)}, u32[]{:S(2)}) async-start(bf16[8,2,3,128,128]{4,3,2,1,0:T(8,128)(2,1)} %get-tuple-element.385), calls=%async_computation.7 | async-start | bytes 3145728 | tf_op jit(solution)/shard_map/all_to_all | solution.py:66
  316.2 17.8 %column_grads.2 = (bf16[2,16,1408]{2,1,0:T(8,128)(2,1)}, bf16[32,2048]{1,0:T(8,128)(2,1)}) custom-call(bf16[256,2048]{1,0:T(8,128)(2,1)} %get-tuple-element.394.refs_0_, bf16[512,2048]{1,0:T(8,128)(2,1)} %get-tuple-element.395.refs_1_, bf16[256,2816]{1,0:T(8,128)(2,1)} %get-tuple-element.396.refs_0_.refs_2_, ...), custom_call_target="tpu_custom_call" | custom-call | flops 23068672 | bytes 296960 | tf_op jit(solution)/shard_map/column_grads/pallas_call | solution.py:736
  342.5 8.4 %row_grads.3 = (bf16[16,1408]{1,0:T(8,128)(2,1)}, bf16[16,2048]{1,0:T(8,128)(2,1)}) custom-call(bf16[256,1408]{1,0:T(8,128)(2,1)} %get-tuple-element.357.refs_1_.refs_0_, bf16[512,1408]{1,0:T(8,128)(2,1)} %get-tuple-element.356.refs_0_.refs_1_, bf16[256,2048]{1,0:T(8,128)(2,1)} %get-tuple-element.405.refs_2_, bf16[512,2048]{1,0:T(8,128)(2,1)} %get-tuple-element.406.refs_3_, ...), custom_call_target="tpu_custom_call" | custom-call | flops 11534336 | bytes 173056 | tf_op jit(solution)/shard_map/row_grads/pallas_call | solution.py:807
  351.0 11.4 %column_grads.3 = (bf16[3,16,512]{2,1,0:T(8,128)(2,1)}, bf16[48,2048]{1,0:T(8,128)(2,1)}, bf16[512,1536]{1,0:T(8,128)(2,1)}) custom-call(bf16[256,2048]{1,0:T(8,128)(2,1)} %get-tuple-element.414.refs_0_, bf16[512,2048]{1,0:T(8,128)(2,1)} %get-tuple-element.415.refs_1_, bf16[256,1536]{1,0:T(8,128)(2,1)} %assemble.1.refs_2_.refs_1_, ...), custom_call_target="tpu_custom_call" | custom-call | flops 12582912 | bytes 184320 | tf_op jit(solution)/shard_map/column_grads/pallas_call | solution.py:736
  364.4 5.9 %all-to-all-start.8 = ((bf16[8,16,2688]{2,1,0:T(8,128)(2,1)}), bf16[8,16,2688]{2,1,0:T(8,128)(2,1)S(1)}, u32[]{:S(2)}, u32[]{:S(2)}) async-start(bf16[8,16,2688]{2,1,0:T(8,128)(2,1)} %pack.1), calls=%async_computation.8 | async-start | bytes 1376256 | tf_op jit(solution)/shard_map/all_to_all | solution.py:66
  370.4 8.9 %project_split.7 = (bf16[192,2048]{1,0:T(8,128)(2,1)}, bf16[192,2048]{1,0:T(8,128)(2,1)}, bf16[2,192,2048]{2,1,0:T(8,128)(2,1)}) custom-call(bf16[512,1536]{1,0:T(8,128)(2,1)} %get-tuple-element.429.refs_0_, bf16[256,1536]{1,0:T(8,128)(2,1)} %assemble.1.refs_2_.refs_1_, bf16[2048,1536]{1,0:T(8,128)(2,1)} %get-tuple-element.238.refs_4_.refs_2_), custom_call_target="tpu_custom_call" | custom-call | flops 75497472 | bytes 184320 | tf_op jit(solution)/shard_map/project_split/pallas_call | solution.py:457
  379.3 9.4 %all-to-all-done.8 = bf16[8,16,2688]{2,1,0:T(8,128)(2,1)S(1)} async-done(((bf16[8,16,2688]{2,1,0:T(8,128)(2,1)}), bf16[8,16,2688]{2,1,0:T(8,128)(2,1)S(1)}, u32[]{:S(2)}, u32[]{:S(2)}) %all-to-all-start.8) | async-done | bytes 688160 | tf_op jit(solution)/shard_map/all_to_all | solution.py:66
  402.6 13.8 %collective-permute-done.47 = bf16[6,32,2048]{2,1,0:T(8,128)(2,1)} collective-permute-done((bf16[6,32,2048]{2,1,0:T(8,128)(2,1)}, bf16[6,32,2048]{2,1,0:T(8,128)(2,1)}, u32[]{:S(2)}, u32[]{:S(2)}) %collective-permute-start.47) | collective-permute-done | bytes 786464 | tf_op jit(solution)/shard_map/ppermute | solution.py:37
  (310 shorter events, 162.3 us)
Async XLA Ops:
  3.0 16.3 %collective-permute-start.1 = (bf16[2,32,2048]{2,1,0:T(8,128)(2,1)S(1)}, bf16[2,32,2048]{2,1,0:T(8,128)(2,1)S(1)}, u32[]{:S(2)}, u32[]{:S(2)}) collective-permute-start(bf16[2,32,2048]{2,1,0:T(8,128)(2,1)S(1)} %fusion.20), channel_id=1, source_target_pairs={{0,1},{1,0},{2,3},{3,2},{4,5},{5,4},{6,7},{7,6},{8,9},{9,8},{10,11... | collective-permute-start | bytes 786440 | tf_op jit(solution)/shard_map/ppermute | solution.py:37
  3.5 15.8 %collective-permute-start = (bf16[2,32,2048]{2,1,0:T(8,128)(2,1)S(1)}, bf16[2,32,2048]{2,1,0:T(8,128)(2,1)}, u32[]{:S(2)}, u32[]{:S(2)}) collective-permute-start(bf16[2,32,2048]{2,1,0:T(8,128)(2,1)S(1)} %fusion.20), channel_id=1, source_target_pairs={{0,2},{1,3},{2,0},{3,1},{4,6},{5,7},{6,4},{7,5},{8,10},{9,11},{10,... | collective-permute-start | bytes 786440 | tf_op jit(solution)/shard_map/ppermute | solution.py:37
  8.2 19.7 %collective-permute-start.4 = (bf16[4,32,2048]{2,1,0:T(8,128)(2,1)S(1)}, bf16[4,32,2048]{2,1,0:T(8,128)(2,1)S(1)}, u32[]{:S(2)}, u32[]{:S(2)}) collective-permute-start(bf16[4,32,2048]{2,1,0:T(8,128)(2,1)S(1)} %fusion.13), channel_id=1, source_target_pairs={{0,1},{1,0},{2,3},{3,2},{4,5},{5,4},{6,7},{7,6},{8,9},{9,8},{10,11... | collective-permute-start | bytes 1572872 | tf_op jit(solution)/shard_map/ppermute | solution.py:37
  8.4 19.5 %collective-permute-start.3 = (bf16[4,32,2048]{2,1,0:T(8,128)(2,1)S(1)}, bf16[4,32,2048]{2,1,0:T(8,128)(2,1)S(1)}, u32[]{:S(2)}, u32[]{:S(2)}) collective-permute-start(bf16[4,32,2048]{2,1,0:T(8,128)(2,1)S(1)} %fusion.13), channel_id=1, source_target_pairs={{0,2},{1,3},{2,0},{3,1},{4,6},{5,7},{6,4},{7,5},{8,10},{9,11},{10,... | collective-permute-start | bytes 1572872 | tf_op jit(solution)/shard_map/ppermute | solution.py:37
  28.9 26.5 %all-to-all-start = ((bf16[8,1,3,128,128]{4,3,2,1,0:T(8,128)(2,1)}), bf16[8,1,3,128,128]{4,3,2,1,0:T(8,128)(2,1)S(1)}, u32[]{:S(2)}, u32[]{:S(2)}) async-start(bf16[8,1,3,128,128]{4,3,2,1,0:T(8,128)(2,1)} %bitcast.188), calls=%async_computation | async-start | bytes 1572864 | tf_op jit(solution)/shard_map/all_to_all | solution.py:66
  35.2 9.1 %collective-permute-start.5 = (bf16[4,32,2048]{2,1,0:T(8,128)(2,1)}, bf16[4,32,2048]{2,1,0:T(8,128)(2,1)S(1)}, u32[]{:S(2)}, u32[]{:S(2)}) collective-permute-start(bf16[4,32,2048]{2,1,0:T(8,128)(2,1)} %copy-done.24), channel_id=1, source_target_pairs={{0,1},{1,0},{2,3},{3,2},{4,5},{5,4},{6,7},{7,6},{8,9},{9,8},{10,11... | collective-permute-start | bytes 1572872 | tf_op jit(solution)/shard_map/ppermute | solution.py:37
  57.4 42.4 %all-to-all-start.1 = ((bf16[8,2,3,128,128]{4,3,2,1,0:T(8,128)(2,1)}), bf16[8,2,3,128,128]{4,3,2,1,0:T(8,128)(2,1)S(1)}, u32[]{:S(2)}, u32[]{:S(2)}) async-start(bf16[8,2,3,128,128]{4,3,2,1,0:T(8,128)(2,1)} %bitcast.183), calls=%async_computation.1 | async-start | bytes 3145728 | tf_op jit(solution)/shard_map/all_to_all | solution.py:66
  66.1 23.9 %collective-permute-start.10 = (bf16[6,32,2048]{2,1,0:T(8,128)(2,1)S(1)}, bf16[6,32,2048]{2,1,0:T(8,128)(2,1)}, u32[]{:S(2)}, u32[]{:S(2)}) collective-permute-start(bf16[6,32,2048]{2,1,0:T(8,128)(2,1)S(1)} %get-tuple-element.283), channel_id=1, source_target_pairs={{0,1},{1,0},{2,3},{3,2},{4,5},{5,4},{6,7},{7,6},{8,9},{9,8},{10,11... | collective-permute-start | bytes 2359304 | tf_op jit(solution)/shard_map/ppermute | solution.py:37
  66.4 23.7 %collective-permute-start.9 = (bf16[6,32,2048]{2,1,0:T(8,128)(2,1)S(1)}, bf16[6,32,2048]{2,1,0:T(8,128)(2,1)}, u32[]{:S(2)}, u32[]{:S(2)}) collective-permute-start(bf16[6,32,2048]{2,1,0:T(8,128)(2,1)S(1)} %get-tuple-element.283), channel_id=1, source_target_pairs={{0,2},{1,3},{2,0},{3,1},{4,6},{5,7},{6,4},{7,5},{8,10},{9,11},{10,... | collective-permute-start | bytes 2359304 | tf_op jit(solution)/shard_map/ppermute | solution.py:37
  90.0 9.0 %collective-permute-start.11 = (bf16[6,32,2048]{2,1,0:T(8,128)(2,1)}, bf16[6,32,2048]{2,1,0:T(8,128)(2,1)S(1)}, u32[]{:S(2)}, u32[]{:S(2)}) collective-permute-start(bf16[6,32,2048]{2,1,0:T(8,128)(2,1)} %collective-permute-done.9), channel_id=1, source_target_pairs={{0,1},{1,0},{2,3},{3,2},{4,5},{5,4},{6,7},{7,6},{8,9},{9,8},{10,11... | collective-permute-start | bytes 2359304 | tf_op jit(solution)/shard_map/ppermute | solution.py:37
  99.8 13.4 %collective-permute-start.14 = (f32[1,2048]{1,0:T(1,128)S(1)}, f32[1,2048]{1,0:T(1,128)S(1)}, u32[]{:S(2)}, u32[]{:S(2)}) collective-permute-start(f32[1,2048]{1,0:T(1,128)S(1)} %copy-done.42), channel_id=1, source_target_pairs={{0,3},{1,2},{2,1},{3,0},{4,7},{5,6},{6,5},{7,4},{8,11},{9,10},{10,... | collective-permute-start | bytes 24584 | tf_op jit(solution)/shard_map/ppermute | solution.py:37
  100.3 12.9 %collective-permute-start.13 = (f32[1,2048]{1,0:T(1,128)S(1)}, f32[1,2048]{1,0:T(1,128)S(1)}, u32[]{:S(2)}, u32[]{:S(2)}) collective-permute-start(f32[1,2048]{1,0:T(1,128)S(1)} %copy-done.42), channel_id=1, source_target_pairs={{0,2},{1,3},{2,0},{3,1},{4,6},{5,7},{6,4},{7,5},{8,10},{9,11},{10,... | collective-permute-start | bytes 24584 | tf_op jit(solution)/shard_map/ppermute | solution.py:37
  101.4 11.9 %collective-permute-start.12 = (f32[1,2048]{1,0:T(1,128)S(1)}, f32[1,2048]{1,0:T(1,128)S(1)}, u32[]{:S(2)}, u32[]{:S(2)}) collective-permute-start(f32[1,2048]{1,0:T(1,128)S(1)} %copy-done.42), channel_id=1, source_target_pairs={{0,1},{1,0},{2,3},{3,2},{4,5},{5,4},{6,7},{7,6},{8,9},{9,8},{10,11... | collective-permute-start | bytes 24584 | tf_op jit(solution)/shard_map/ppermute | solution.py:37
  101.7 15.0 %all-to-all-start.2 = ((bf16[8,1,1,128,128]{4,3,2,1,0:T(8,128)(2,1)}), bf16[8,1,1,128,128]{4,3,2,1,0:T(8,128)(2,1)S(1)}, u32[]{:S(2)}, u32[]{:S(2)}) async-start(bf16[8,1,1,128,128]{4,3,2,1,0:T(8,128)(2,1)} %bitcast.187), calls=%async_computation.2 | async-start | bytes 524288 | tf_op jit(solution)/shard_map/all_to_all | solution.py:66
  123.5 18.0 %collective-permute-start.16 = (bf16[2,32,2048]{2,1,0:T(8,128)(2,1)S(1)}, bf16[2,32,2048]{2,1,0:T(8,128)(2,1)S(1)}, u32[]{:S(2)}, u32[]{:S(2)}) collective-permute-start(bf16[2,32,2048]{2,1,0:T(8,128)(2,1)S(1)} %fusion.24), channel_id=1, source_target_pairs={{0,2},{1,3},{2,0},{3,1},{4,6},{5,7},{6,4},{7,5},{8,10},{9,11},{10,... | collective-permute-start | bytes 786440 | tf_op jit(solution)/shard_map/ppermute | solution.py:37
  124.1 20.3 %all-to-all-start.3 = ((bf16[8,2,1,128,128]{4,3,1,2,0:T(8,128)(2,1)}), bf16[8,2,1,128,128]{4,3,1,2,0:T(8,128)(2,1)S(1)}, u32[]{:S(2)}, u32[]{:S(2)}) async-start(bf16[8,2,1,128,128]{4,3,1,2,0:T(8,128)(2,1)} %bitcast.40), calls=%async_computation.3 | async-start | bytes 1048576 | tf_op jit(solution)/shard_map/all_to_all | solution.py:66
  155.8 14.1 %collective-permute-start.21 = (bf16[4,32,2048]{2,1,0:T(8,128)(2,1)S(1)}, bf16[4,32,2048]{2,1,0:T(8,128)(2,1)}, u32[]{:S(2)}, u32[]{:S(2)}) collective-permute-start(bf16[4,32,2048]{2,1,0:T(8,128)(2,1)S(1)} %fusion.17), channel_id=1, source_target_pairs={{0,2},{1,3},{2,0},{3,1},{4,6},{5,7},{6,4},{7,5},{8,10},{9,11},{10,... | collective-permute-start | bytes 1572872 | tf_op jit(solution)/shard_map/ppermute | solution.py:37
  172.6 13.5 %collective-permute-start.22 = (bf16[4,32,2048]{2,1,0:T(8,128)(2,1)}, bf16[4,32,2048]{2,1,0:T(8,128)(2,1)}, u32[]{:S(2)}, u32[]{:S(2)}) collective-permute-start(bf16[4,32,2048]{2,1,0:T(8,128)(2,1)} %multiply_convert_fusion.2), channel_id=1, source_target_pairs={{0,2},{1,3},{2,0},{3,1},{4,6},{5,7},{6,4},{7,5},{8,10},{9,11},{10,... | collective-permute-start | bytes 1572872 | tf_op jit(solution)/shard_map/ppermute | solution.py:37
  188.6 14.6 %collective-permute-start.26 = (bf16[2,32,2048]{2,1,0:T(8,128)(2,1)}, bf16[2,32,2048]{2,1,0:T(8,128)(2,1)}, u32[]{:S(2)}, u32[]{:S(2)}) collective-permute-start(bf16[2,32,2048]{2,1,0:T(8,128)(2,1)} %fusion.22), channel_id=1, source_target_pairs={{0,2},{1,3},{2,0},{3,1},{4,6},{5,7},{6,4},{7,5},{8,10},{9,11},{10,... | collective-permute-start | bytes 786440 | tf_op jit(solution)/shard_map/ppermute | solution.py:37
  207.4 11.4 %collective-permute-start.28 = (bf16[2,32,2048]{2,1,0:T(8,128)(2,1)}, bf16[2,32,2048]{2,1,0:T(8,128)(2,1)}, u32[]{:S(2)}, u32[]{:S(2)}) collective-permute-start(bf16[2,32,2048]{2,1,0:T(8,128)(2,1)} %multiply_convert_fusion.3), channel_id=1, source_target_pairs={{0,1},{1,0},{2,3},{3,2},{4,5},{5,4},{6,7},{7,6},{8,9},{9,8},{10,11... | collective-permute-start | bytes 786440 | tf_op jit(solution)/shard_map/ppermute | solution.py:37
  207.7 11.2 %collective-permute-start.27 = (bf16[2,32,2048]{2,1,0:T(8,128)(2,1)}, bf16[2,32,2048]{2,1,0:T(8,128)(2,1)}, u32[]{:S(2)}, u32[]{:S(2)}) collective-permute-start(bf16[2,32,2048]{2,1,0:T(8,128)(2,1)} %multiply_convert_fusion.3), channel_id=1, source_target_pairs={{0,2},{1,3},{2,0},{3,1},{4,6},{5,7},{6,4},{7,5},{8,10},{9,11},{10,... | collective-permute-start | bytes 786440 | tf_op jit(solution)/shard_map/ppermute | solution.py:37
  225.1 14.3 %collective-permute-start.31 = (bf16[4,32,2048]{2,1,0:T(8,128)(2,1)}, bf16[4,32,2048]{2,1,0:T(8,128)(2,1)}, u32[]{:S(2)}, u32[]{:S(2)}) collective-permute-start(bf16[4,32,2048]{2,1,0:T(8,128)(2,1)} %fusion.15), channel_id=1, source_target_pairs={{0,2},{1,3},{2,0},{3,1},{4,6},{5,7},{6,4},{7,5},{8,10},{9,11},{10,... | collective-permute-start | bytes 1572872 | tf_op jit(solution)/shard_map/ppermute | solution.py:37
  230.2 15.0 %all-to-all-start.4 = ((bf16[8,1,1,128,128]{4,3,2,1,0:T(8,128)(2,1)}), bf16[8,1,1,128,128]{4,3,2,1,0:T(8,128)(2,1)}, u32[]{:S(2)}, u32[]{:S(2)}) async-start(bf16[8,1,1,128,128]{4,3,2,1,0:T(8,128)(2,1)} %bitcast.215), calls=%async_computation.4 | async-start | bytes 524288 | tf_op jit(solution)/shard_map/all_to_all | solution.py:66
  250.5 27.4 %all-to-all-start.5 = ((bf16[8,1,3,128,128]{4,3,2,1,0:T(8,128)(2,1)}), bf16[8,1,3,128,128]{4,3,2,1,0:T(8,128)(2,1)S(1)}, u32[]{:S(2)}, u32[]{:S(2)}) async-start(bf16[8,1,3,128,128]{4,3,2,1,0:T(8,128)(2,1)} %get-tuple-element.365), calls=%async_computation.5 | async-start | bytes 1572864 | tf_op jit(solution)/shard_map/all_to_all | solution.py:66
  256.0 10.3 %collective-permute-start.33 = (bf16[4,32,2048]{2,1,0:T(8,128)(2,1)}, bf16[4,32,2048]{2,1,0:T(8,128)(2,1)}, u32[]{:S(2)}, u32[]{:S(2)}) collective-permute-start(bf16[4,32,2048]{2,1,0:T(8,128)(2,1)} %multiply_convert_fusion.1), channel_id=1, source_target_pairs={{0,1},{1,0},{2,3},{3,2},{4,5},{5,4},{6,7},{7,6},{8,9},{9,8},{10,11... | collective-permute-start | bytes 1572872 | tf_op jit(solution)/shard_map/ppermute | solution.py:37
  256.0 14.6 %collective-permute-start.32 = (bf16[4,32,2048]{2,1,0:T(8,128)(2,1)}, bf16[4,32,2048]{2,1,0:T(8,128)(2,1)}, u32[]{:S(2)}, u32[]{:S(2)}) collective-permute-start(bf16[4,32,2048]{2,1,0:T(8,128)(2,1)} %multiply_convert_fusion.1), channel_id=1, source_target_pairs={{0,2},{1,3},{2,0},{3,1},{4,6},{5,7},{6,4},{7,5},{8,10},{9,11},{10,... | collective-permute-start | bytes 1572872 | tf_op jit(solution)/shard_map/ppermute | solution.py:37
  277.9 20.9 %all-to-all-start.6 = ((bf16[8,2,1,128,128]{4,3,1,2,0:T(8,128)(2,1)}), bf16[8,2,1,128,128]{4,3,1,2,0:T(8,128)(2,1)}, u32[]{:S(2)}, u32[]{:S(2)}) async-start(bf16[8,2,1,128,128]{4,3,1,2,0:T(8,128)(2,1)} %bitcast.204), calls=%async_computation.6 | async-start | bytes 1048576 | tf_op jit(solution)/shard_map/all_to_all | solution.py:66
  306.8 44.2 %all-to-all-start.7 = ((bf16[8,2,3,128,128]{4,3,2,1,0:T(8,128)(2,1)}), bf16[8,2,3,128,128]{4,3,2,1,0:T(8,128)(2,1)}, u32[]{:S(2)}, u32[]{:S(2)}) async-start(bf16[8,2,3,128,128]{4,3,2,1,0:T(8,128)(2,1)} %get-tuple-element.385), calls=%async_computation.7 | async-start | bytes 3145728 | tf_op jit(solution)/shard_map/all_to_all | solution.py:66
  313.8 20.2 %collective-permute-start.39 = (bf16[6,32,2048]{2,1,0:T(8,128)(2,1)}, bf16[6,32,2048]{2,1,0:T(8,128)(2,1)}, u32[]{:S(2)}, u32[]{:S(2)}) collective-permute-start(bf16[6,32,2048]{2,1,0:T(8,128)(2,1)} %fusion.10), channel_id=1, source_target_pairs={{0,2},{1,3},{2,0},{3,1},{4,6},{5,7},{6,4},{7,5},{8,10},{9,11},{10,... | collective-permute-start | bytes 2359304 | tf_op jit(solution)/shard_map/ppermute | solution.py:37
  364.4 24.3 %all-to-all-start.8 = ((bf16[8,16,2688]{2,1,0:T(8,128)(2,1)}), bf16[8,16,2688]{2,1,0:T(8,128)(2,1)S(1)}, u32[]{:S(2)}, u32[]{:S(2)}) async-start(bf16[8,16,2688]{2,1,0:T(8,128)(2,1)} %pack.1), calls=%async_computation.8 | async-start | bytes 1376256 | tf_op jit(solution)/shard_map/all_to_all | solution.py:66
  396.5 19.9 %collective-permute-start.47 = (bf16[6,32,2048]{2,1,0:T(8,128)(2,1)}, bf16[6,32,2048]{2,1,0:T(8,128)(2,1)}, u32[]{:S(2)}, u32[]{:S(2)}) collective-permute-start(bf16[6,32,2048]{2,1,0:T(8,128)(2,1)} %fusion.8), channel_id=1, source_target_pairs={{0,2},{1,3},{2,0},{3,1},{4,6},{5,7},{6,4},{7,5},{8,10},{9,11},{10,... | collective-permute-start | bytes 2359304 | tf_op jit(solution)/shard_map/ppermute | solution.py:37
  398.4 22.8 %all-to-all-start.9 = ((bf16[8,16,2688]{2,1,0:T(8,128)(2,1)}), bf16[8,16,2688]{2,1,0:T(8,128)(2,1)}, u32[]{:S(2)}, u32[]{:S(2)}) async-start(bf16[8,16,2688]{2,1,0:T(8,128)(2,1)} %broadcast_in_dim.202), calls=%async_computation.9 | async-start | bytes 1376256 | tf_op jit(solution)/shard_map/all_to_all | solution.py:66
  (75 other events, 465.0 us)

commit v6 on v5

--- a/solution.py
+++ b/solution.py
@@ -724,7 +724,7 @@
 def column_grads(rows, grads, weight, down, up, stat, magnitude, sums, cross, block):
     tokens, width = sum(v.shape[0] for v in rows), rows[0].shape[1]
     members, rank, out = up.shape
-    chunks, steps, span = len(rows), out // block, 512
+    chunks, steps, span = len(rows), out // block, 1024
     first = lambda i: jnp.minimum(i, steps - 1)
     then = lambda i: jnp.maximum(i - steps, 0)
     part = lambda n: pl.BlockSpec((members, n, block), lambda i: (0, 0, first(i)))

time: 431 us -> 430 us (level)
  no operation moved by 1% of the time
where the time goes in v6:
time: 430 us; the launch traced here: 423 us
  Pallas kernels  212 us (49%)
  starting transfers between devices  82.2 us (19%)
  waiting for transfers between devices  68.9 us (16%)
  other arithmetic  44.4 us (10%)
  local copies, waits for them, and re-layouts  13.8 us (3%)
    all_to_all x10, starting transfers between devices, exchange(): return lax.all_to_all(values, 'seq', 0, 0, tiled=True)  52.2 us
    ppermute x48, waiting for transfers between devices, swap(): return lax.ppermute(values, 'tensor', [(i, i ^ bit) for i in range(size)])  49.2 us
    pallas_call x4, Pallas kernels, project_split(): pl.pallas_call(partial(project_split_kernel, dims=dims), grid=(out // blo...  35.5 us
    ppermute x48, starting transfers between devices, swap(): return lax.ppermute(values, 'tensor', [(i, i ^ bit) for i in range(size)])  30 us
    pallas_call x2, Pallas kernels, column_grads(): pl.pallas_call(partial(column_grads_kernel, chunks=chunks, steps=steps, j...  28.1 us
    pallas_call x2, Pallas kernels, column_prep(): pl.pallas_call(column_prep_kernel, grid=(out // block,), in_specs=[pl.Blo...  25.5 us
    pallas_call x4, Pallas kernels, project_to_pairs(): pl.pallas_call(partial(to_pairs_kernel, dims=dims), grid=(parts, steps),...  22.9 us
    pallas_call x2, Pallas kernels, gated(): pl.pallas_call(gated_kernel, grid=(-(-out // block),), in_specs=[pl.Block...  22.2 us
  transfers between devices with their start and end apart: 58, of which 22 were waited for; matrix products, arithmetic and copies ran while one was open for 9% of the time, Pallas kernels for 43%

profile of v6, /device:TPU:0, one launch (start us, length us, event | category | flops | bytes accessed | tf_op | source)
XLA Modules:
  0.0 423.1 jit_solution(6960146087226110312)
XLA Ops:
  10.4 8.9 %column_prep.2 = (bf16[2048,1536]{1,0:T(8,128)(2,1)}, f32[3,2,512]{2,1,0:T(2,128)}, f32[3,16,512]{2,1,0:T(8,128)}) custom-call(bf16[3,2048,512]{2,1,0:T(8,128)(2,1)} %w_ref.1, bf16[48,2048]{1,0:T(8,128)(2,1)} %bitcast.192, bf16[2,48,768]{2,1,0:T(8,128)(2,1)} %broadcast_multiply_fusion.1.b_ref, f32[3,1,512]{2,1,0:T(1,128)} %broadcast_in_dim.103.m_ref.refs_8_), custom_call_target="tpu_custom_call" | custom-call | flops 50331648 | bytes 196608 | tf_op jit(solution)/shard_map/column_prep/pallas_call | solution.py:104
  21.8 6.1 %project_to_pairs.4 = (bf16[2,4,3,4,32,128]{5,4,3,2,1,0:T(8,128)(2,1)}, bf16[256,2048]{1,0:T(8,128)(2,1)}) custom-call(bf16[64,2048]{1,0:T(8,128)(2,1)} %bitcast.184, bf16[64,2048]{1,0:T(8,128)(2,1)} %bitcast.4.refs_1_, bf16[64,2048]{1,0:T(8,128)(2,1)} %bitcast.207, bf16[64,2048]{1,0:T(8,128)(2,1)} %bitcast.214, ...), custom_call_target="tpu_custom_call" | custom-call | flops 25165824 | bytes 131072 | tf_op jit(solution)/shard_map/project_to_pairs/pallas_call | solution.py:359
  28.9 6.1 %all-to-all-start = ((bf16[8,1,3,128,128]{4,3,2,1,0:T(8,128)(2,1)}), bf16[8,1,3,128,128]{4,3,2,1,0:T(8,128)(2,1)S(1)}, u32[]{:S(2)}, u32[]{:S(2)}) async-start(bf16[8,1,3,128,128]{4,3,2,1,0:T(8,128)(2,1)} %bitcast.188), calls=%async_computation | async-start | bytes 1572864 | tf_op jit(solution)/shard_map/all_to_all | solution.py:66
  35.5 8.9 %row_prep.2 = (bf16[1408,2048]{1,0:T(8,128)(2,1)}, f32[16,2048]{1,0:T(8,128)}, f32[1,2048]{1,0:T(1,128)}) custom-call(bf16[1408,2048]{1,0:T(8,128)(2,1)} %w_ref.2, bf16[16,1408]{1,0:T(8,128)(2,1)} %bitcast.217, bf16[16,2048]{1,0:T(8,128)(2,1)} %refs_6_.6), custom_call_target="tpu_custom_call" | custom-call | flops 23068672 | bytes 180224 | tf_op jit(solution)/shard_map/row_prep/pallas_call | solution.py:142
  45.1 8.2 %project_to_pairs.5 = (bf16[4,4,3,4,32,128]{5,4,3,2,1,0:T(8,128)(2,1)}, bf16[512,2048]{1,0:T(8,128)(2,1)}) custom-call(bf16[128,2048]{1,0:T(8,128)(2,1)} %bitcast.180, bf16[128,2048]{1,0:T(8,128)(2,1)} %bitcast.197, bf16[128,2048]{1,0:T(8,128)(2,1)} %bitcast.196, bf16[128,2048]{1,0:T(8,128)(2,1)} %bitcast.200, ...), custom_call_target="tpu_custom_call" | custom-call | flops 50331648 | bytes 163840 | tf_op jit(solution)/shard_map/project_to_pairs/pallas_call | solution.py:359
  57.4 4.8 %all-to-all-start.1 = ((bf16[8,2,3,128,128]{4,3,2,1,0:T(8,128)(2,1)}), bf16[8,2,3,128,128]{4,3,2,1,0:T(8,128)(2,1)S(1)}, u32[]{:S(2)}, u32[]{:S(2)}) async-start(bf16[8,2,3,128,128]{4,3,2,1,0:T(8,128)(2,1)} %bitcast.183), calls=%async_computation.1 | async-start | bytes 3145728 | tf_op jit(solution)/shard_map/all_to_all | solution.py:66
  68.8 4.6 %row_prep.3 = (bf16[512,2048]{1,0:T(8,128)(2,1)}, f32[16,2048]{1,0:T(8,128)}, f32[1,2048]{1,0:T(1,128)}) custom-call(bf16[512,2048]{1,0:T(8,128)(2,1)} %w_ref.4, bf16[16,512]{1,0:T(8,128)(2,1)} %bitcast.219, bf16[16,2048]{1,0:T(8,128)(2,1)} %refs_6_.4), custom_call_target="tpu_custom_call" | custom-call | flops 8388608 | bytes 65536 | tf_op jit(solution)/shard_map/row_prep/pallas_call | solution.py:142
  73.4 16.6 %column_prep.3 = (bf16[2048,2816]{1,0:T(8,128)(2,1)}, f32[2,2,1408]{2,1,0:T(2,128)}, f32[2,16,1408]{2,1,0:T(8,128)}) custom-call(bf16[2,2048,1408]{2,1,0:T(8,128)(2,1)} %w_ref.3, bf16[32,2048]{1,0:T(8,128)(2,1)} %bitcast.194, bf16[11,32,256]{2,1,0:T(8,128)(2,1)} %broadcast_multiply_fusion.b_ref, f32[2,1,1408]{2,1,0:T(1,128)} %broadcast_in_dim.107.m_ref.refs_8_), custom_call_target="tpu_custom_call" | custom-call | flops 92274688 | bytes 360448 | tf_op jit(solution)/shard_map/column_prep/pallas_call | solution.py:104
  101.7 5.4 %all-to-all-start.2 = ((bf16[8,1,1,128,128]{4,3,2,1,0:T(8,128)(2,1)}), bf16[8,1,1,128,128]{4,3,2,1,0:T(8,128)(2,1)S(1)}, u32[]{:S(2)}, u32[]{:S(2)}) async-start(bf16[8,1,1,128,128]{4,3,2,1,0:T(8,128)(2,1)} %bitcast.187), calls=%async_computation.2 | async-start | bytes 524288 | tf_op jit(solution)/shard_map/all_to_all | solution.py:66
  107.7 5.6 %attend.3 = (bf16[8,2,128,128]{3,2,1,0:T(8,128)(2,1)}, f32[2,1,1024]{2,1,0:T(1,128)}) custom-call(bf16[8,2,3,128,128]{4,3,2,1,0:T(8,128)(2,1)} %copy-done.1, f32[1024,128]{1,0:T(8,128)} %get-tuple-element.488.cos_ref, f32[1024,128]{1,0:T(8,128)} %get-tuple-element.489.sin_ref, s32[1024,1]{1,0:T(8,128)} %copy.57.kpos_ref, s32[2,2,1024]{2,1,0:T(2,128)} %pad_add_fusion.qinfo_ref), custom_call_target="tpu_custom_call" | custom-call | flops 16777216 | bytes 32768 | tf_op jit(solution)/shard_map/attend/pallas_call | solution.py:210
  127.9 5.7 %project_cotangent.2 = (bf16[256,1408]{1,0:T(8,128)(2,1)}, bf16[256,2048]{1,0:T(8,128)(2,1)}) custom-call(bf16[192,2048]{1,0:T(8,128)(2,1)} %bitcast.173, bf16[192,2048]{1,0:T(8,128)(2,1)} %bitcast.36.refs_1_, bf16[192,2048]{1,0:T(8,128)(2,1)} %bitcast.37.refs_2_, bf16[192,2048]{1,0:T(8,128)(2,1)} %bitcast.175, ...), custom_call_target="tpu_custom_call" | custom-call | flops 23068672 | bytes 122880 | tf_op jit(solution)/shard_map/project_cotangent/pallas_call | solution.py:484
  133.6 7.9 %project_cotangent.3 = (bf16[512,1408]{1,0:T(8,128)(2,1)}, bf16[512,2048]{1,0:T(8,128)(2,1)}) custom-call(bf16[192,2048]{1,0:T(8,128)(2,1)} %bitcast.174, bf16[192,2048]{1,0:T(8,128)(2,1)} %bitcast.36.refs_1_, bf16[192,2048]{1,0:T(8,128)(2,1)} %bitcast.37.refs_2_, bf16[192,2048]{1,0:T(8,128)(2,1)} %bitcast.176, ...), custom_call_target="tpu_custom_call" | custom-call | flops 46137344 | bytes 155648 | tf_op jit(solution)/shard_map/project_cotangent/pallas_call | solution.py:484
  157.3 9.2 %gated.2 = (bf16[256,1408]{1,0:T(8,128)(2,1)}, bf16[256,2816]{1,0:T(8,128)(2,1)}, f32[2,1,1408]{2,1,0:T(1,128)}, bf16[256,2048]{1,0:T(8,128)(2,1)}) custom-call(bf16[64,2048]{1,0:T(8,128)(2,1)} %bitcast.185, bf16[64,2048]{1,0:T(8,128)(2,1)} %bitcast.48.refs_1_, bf16[64,2048]{1,0:T(8,128)(2,1)} %bitcast.208, bf16[64,2048]{1,0:T(8,128)(2,1)} %bitcast.211, ...), custom_call_target="tpu_custom_call" | custom-call | flops 46137344 | bytes 258048 | tf_op jit(solution)/shard_map/gated/pallas_call | solution.py:638
  174.1 7.2 %project_split.4 = (bf16[64,2048]{1,0:T(8,128)(2,1)}, bf16[64,2048]{1,0:T(8,128)(2,1)}, bf16[2,64,2048]{2,1,0:T(8,128)(2,1)}) custom-call(bf16[256,2816]{1,0:T(8,128)(2,1)} %get-tuple-element.396.refs_0_.refs_2_, bf16[2048,2816]{1,0:T(8,128)(2,1)} %get-tuple-element.308.refs_4_.refs_1_), custom_call_target="tpu_custom_call" | custom-call | flops 46137344 | bytes 219136 | tf_op jit(solution)/shard_map/project_split/pallas_call | solution.py:457
  190.1 13.1 %gated.3 = (bf16[512,1408]{1,0:T(8,128)(2,1)}, bf16[512,2816]{1,0:T(8,128)(2,1)}, f32[2,1,1408]{2,1,0:T(1,128)}, bf16[512,2048]{1,0:T(8,128)(2,1)}) custom-call(bf16[128,2048]{1,0:T(8,128)(2,1)} %bitcast.56.refs_0_, bf16[128,2048]{1,0:T(8,128)(2,1)} %bitcast.57.refs_1_, bf16[128,2048]{1,0:T(8,128)(2,1)} %bitcast.58.refs_2_, ...), custom_call_target="tpu_custom_call" | custom-call | flops 92274688 | bytes 335872 | tf_op jit(solution)/shard_map/gated/pallas_call | solution.py:638
  208.2 10.7 %project_split.5 = (bf16[128,2048]{1,0:T(8,128)(2,1)}, bf16[128,2048]{1,0:T(8,128)(2,1)}, bf16[2,128,2048]{2,1,0:T(8,128)(2,1)}) custom-call(bf16[512,2816]{1,0:T(8,128)(2,1)} %get-tuple-element.397.refs_0_.refs_3_, bf16[2048,2816]{1,0:T(8,128)(2,1)} %get-tuple-element.308.refs_4_.refs_1_), custom_call_target="tpu_custom_call" | custom-call | flops 92274688 | bytes 258048 | tf_op jit(solution)/shard_map/project_split/pallas_call | solution.py:457
  230.2 6.0 %all-to-all-start.4 = ((bf16[8,1,1,128,128]{4,3,2,1,0:T(8,128)(2,1)}), bf16[8,1,1,128,128]{4,3,2,1,0:T(8,128)(2,1)}, u32[]{:S(2)}, u32[]{:S(2)}) async-start(bf16[8,1,1,128,128]{4,3,2,1,0:T(8,128)(2,1)} %bitcast.215), calls=%async_computation.4 | async-start | bytes 524288 | tf_op jit(solution)/shard_map/all_to_all | solution.py:66
  245.2 5.2 %attend_back.2 = (bf16[8,1,3,128,128]{4,3,2,1,0:T(8,128)(2,1)}, f32[1,3,128]{2,1,0:T(4,128)}) custom-call(bf16[8,1,3,128,128]{4,3,2,1,0:T(8,128)(2,1)} %copy-done.5, bf16[8,1,128,128]{3,2,1,0:T(8,128)(2,1)} %get-tuple-element.263.o_ref, bf16[8,1,128,128]{3,2,1,0:T(8,128)(2,1)} %bitcast.71.d_ref, f32[1,1,1024]{2,1,0:T(1,128)} %get-tuple-element.350.l_ref, ...), custom_call_target="tpu_custom_call" | custom-call | flops 20971520 | bytes 32768 | tf_op jit(solution)/shard_map/attend_back/pallas_call | solution.py:296
  250.5 5.5 %all-to-all-start.5 = ((bf16[8,1,3,128,128]{4,3,2,1,0:T(8,128)(2,1)}), bf16[8,1,3,128,128]{4,3,2,1,0:T(8,128)(2,1)S(1)}, u32[]{:S(2)}, u32[]{:S(2)}) async-start(bf16[8,1,3,128,128]{4,3,2,1,0:T(8,128)(2,1)} %get-tuple-element.365), calls=%async_computation.5 | async-start | bytes 1572864 | tf_op jit(solution)/shard_map/all_to_all | solution.py:66
  257.6 8.7 %project_split.6 = (bf16[192,2048]{1,0:T(8,128)(2,1)}, bf16[192,2048]{1,0:T(8,128)(2,1)}, bf16[2,192,2048]{2,1,0:T(8,128)(2,1)}) custom-call(bf16[512,1408]{1,0:T(8,128)(2,1)} %get-tuple-element.356.refs_0_.refs_1_, bf16[256,1408]{1,0:T(8,128)(2,1)} %get-tuple-element.357.refs_1_.refs_0_, bf16[1408,2048]{1,0:T(8,128)(2,1)} %get-tuple-element.287.refs_4_.refs_2_), custom_call_target="tpu_custom_call" | custom-call | flops 69206016 | bytes 173056 | tf_op jit(solution)/shard_map/project_split/pallas_call | solution.py:457
  272.9 5.0 %project_to_pairs.7 = (bf16[4,4,1,4,32,128]{5,4,3,2,1,0:T(8,128)(2,1)}, bf16[512,2048]{1,0:T(8,128)(2,1)}) custom-call(bf16[128,2048]{1,0:T(8,128)(2,1)} %bitcast.182, bf16[128,2048]{1,0:T(8,128)(2,1)} %bitcast.76.refs_1_, bf16[128,2048]{1,0:T(8,128)(2,1)} %bitcast.77.refs_2_, bf16[128,2048]{1,0:T(8,128)(2,1)} %bitcast.78.refs_3_, ...), custom_call_target="tpu_custom_call" | custom-call | flops 16777216 | bytes 98304 | tf_op jit(solution)/shard_map/project_to_pairs/pallas_call | solution.py:359
  277.9 6.0 %all-to-all-start.6 = ((bf16[8,2,1,128,128]{4,3,1,2,0:T(8,128)(2,1)}), bf16[8,2,1,128,128]{4,3,1,2,0:T(8,128)(2,1)}, u32[]{:S(2)}, u32[]{:S(2)}) async-start(bf16[8,2,1,128,128]{4,3,1,2,0:T(8,128)(2,1)} %bitcast.204), calls=%async_computation.6 | async-start | bytes 1048576 | tf_op jit(solution)/shard_map/all_to_all | solution.py:66
  289.2 6.0 %row_grads.2 = (bf16[16,512]{1,0:T(8,128)(2,1)}, bf16[16,2048]{1,0:T(8,128)(2,1)}) custom-call(bf16[256,512]{1,0:T(8,128)(2,1)} %get-tuple-element.370.refs_0_, bf16[512,512]{1,0:T(8,128)(2,1)} %get-tuple-element.371.refs_1_, bf16[256,2048]{1,0:T(8,128)(2,1)} %get-tuple-element.372.refs_2_, bf16[512,2048]{1,0:T(8,128)(2,1)} %get-tuple-element.373.refs_3_, ...), custom_call_target="tpu_custom_call" | custom-call | flops 4194304 | bytes 94208 | tf_op jit(solution)/shard_map/row_grads/pallas_call | solution.py:807
  298.8 7.9 %attend_back.3 = (bf16[8,2,3,128,128]{4,3,2,1,0:T(8,128)(2,1)}, f32[2,3,128]{2,1,0:T(4,128)}) custom-call(bf16[8,2,3,128,128]{4,3,2,1,0:T(8,128)(2,1)} %copy-done.1, bf16[8,2,128,128]{3,2,1,0:T(8,128)(2,1)} %get-tuple-element.270.o_ref, bf16[8,2,128,128]{3,2,1,0:T(8,128)(2,1)} %bitcast.83.d_ref, f32[2,1,1024]{2,1,0:T(1,128)} %get-tuple-element.378.l_ref, ...), custom_call_target="tpu_custom_call" | custom-call | flops 41943040 | bytes 65536 | tf_op jit(solution)/shard_map/attend_back/pallas_call | solution.py:296
  306.8 4.7 %all-to-all-start.7 = ((bf16[8,2,3,128,128]{4,3,2,1,0:T(8,128)(2,1)}), bf16[8,2,3,128,128]{4,3,2,1,0:T(8,128)(2,1)}, u32[]{:S(2)}, u32[]{:S(2)}) async-start(bf16[8,2,3,128,128]{4,3,2,1,0:T(8,128)(2,1)} %get-tuple-element.385), calls=%async_computation.7 | async-start | bytes 3145728 | tf_op jit(solution)/shard_map/all_to_all | solution.py:66
  316.2 17.4 %column_grads.2 = (bf16[2,16,1408]{2,1,0:T(8,128)(2,1)}, bf16[32,2048]{1,0:T(8,128)(2,1)}) custom-call(bf16[256,2048]{1,0:T(8,128)(2,1)} %get-tuple-element.394.refs_0_, bf16[512,2048]{1,0:T(8,128)(2,1)} %get-tuple-element.395.refs_1_, bf16[256,2816]{1,0:T(8,128)(2,1)} %get-tuple-element.396.refs_0_.refs_2_, ...), custom_call_target="tpu_custom_call" | custom-call | flops 23068672 | bytes 296960 | tf_op jit(solution)/shard_map/column_grads/pallas_call | solution.py:736
  342.5 8.4 %row_grads.3 = (bf16[16,1408]{1,0:T(8,128)(2,1)}, bf16[16,2048]{1,0:T(8,128)(2,1)}) custom-call(bf16[256,1408]{1,0:T(8,128)(2,1)} %get-tuple-element.357.refs_1_.refs_0_, bf16[512,1408]{1,0:T(8,128)(2,1)} %get-tuple-element.356.refs_0_.refs_1_, bf16[256,2048]{1,0:T(8,128)(2,1)} %get-tuple-element.405.refs_2_, bf16[512,2048]{1,0:T(8,128)(2,1)} %get-tuple-element.406.refs_3_, ...), custom_call_target="tpu_custom_call" | custom-call | flops 11534336 | bytes 173056 | tf_op jit(solution)/shard_map/row_grads/pallas_call | solution.py:807
  350.9 10.7 %column_grads.3 = (bf16[3,16,512]{2,1,0:T(8,128)(2,1)}, bf16[48,2048]{1,0:T(8,128)(2,1)}, bf16[512,1536]{1,0:T(8,128)(2,1)}) custom-call(bf16[256,2048]{1,0:T(8,128)(2,1)} %get-tuple-element.414.refs_0_, bf16[512,2048]{1,0:T(8,128)(2,1)} %get-tuple-element.415.refs_1_, bf16[256,1536]{1,0:T(8,128)(2,1)} %assemble.1.refs_2_.refs_1_, ...), custom_call_target="tpu_custom_call" | custom-call | flops 12582912 | bytes 184320 | tf_op jit(solution)/shard_map/column_grads/pallas_call | solution.py:736
  363.7 5.7 %all-to-all-start.8 = ((bf16[8,16,2688]{2,1,0:T(8,128)(2,1)}), bf16[8,16,2688]{2,1,0:T(8,128)(2,1)S(1)}, u32[]{:S(2)}, u32[]{:S(2)}) async-start(bf16[8,16,2688]{2,1,0:T(8,128)(2,1)} %pack.1), calls=%async_computation.8 | async-start | bytes 1376256 | tf_op jit(solution)/shard_map/all_to_all | solution.py:66
  369.5 8.9 %project_split.7 = (bf16[192,2048]{1,0:T(8,128)(2,1)}, bf16[192,2048]{1,0:T(8,128)(2,1)}, bf16[2,192,2048]{2,1,0:T(8,128)(2,1)}) custom-call(bf16[512,1536]{1,0:T(8,128)(2,1)} %get-tuple-element.429.refs_0_, bf16[256,1536]{1,0:T(8,128)(2,1)} %assemble.1.refs_2_.refs_1_, bf16[2048,1536]{1,0:T(8,128)(2,1)} %get-tuple-element.238.refs_4_.refs_2_), custom_call_target="tpu_custom_call" | custom-call | flops 75497472 | bytes 184320 | tf_op jit(solution)/shard_map/project_split/pallas_call | solution.py:457
  378.4 9.4 %all-to-all-done.8 = bf16[8,16,2688]{2,1,0:T(8,128)(2,1)S(1)} async-done(((bf16[8,16,2688]{2,1,0:T(8,128)(2,1)}), bf16[8,16,2688]{2,1,0:T(8,128)(2,1)S(1)}, u32[]{:S(2)}, u32[]{:S(2)}) %all-to-all-start.8) | async-done | bytes 688160 | tf_op jit(solution)/shard_map/all_to_all | solution.py:66
  401.9 13.7 %collective-permute-done.47 = bf16[6,32,2048]{2,1,0:T(8,128)(2,1)} collective-permute-done((bf16[6,32,2048]{2,1,0:T(8,128)(2,1)}, bf16[6,32,2048]{2,1,0:T(8,128)(2,1)}, u32[]{:S(2)}, u32[]{:S(2)}) %collective-permute-start.47) | collective-permute-done | bytes 786464 | tf_op jit(solution)/shard_map/ppermute | solution.py:37
  (310 shorter events, 162.9 us)
Async XLA Ops:
  3.0 16.3 %collective-permute-start.1 = (bf16[2,32,2048]{2,1,0:T(8,128)(2,1)S(1)}, bf16[2,32,2048]{2,1,0:T(8,128)(2,1)S(1)}, u32[]{:S(2)}, u32[]{:S(2)}) collective-permute-start(bf16[2,32,2048]{2,1,0:T(8,128)(2,1)S(1)} %fusion.20), channel_id=1, source_target_pairs={{0,1},{1,0},{2,3},{3,2},{4,5},{5,4},{6,7},{7,6},{8,9},{9,8},{10,11... | collective-permute-start | bytes 786440 | tf_op jit(solution)/shard_map/ppermute | solution.py:37
  3.5 15.8 %collective-permute-start = (bf16[2,32,2048]{2,1,0:T(8,128)(2,1)S(1)}, bf16[2,32,2048]{2,1,0:T(8,128)(2,1)}, u32[]{:S(2)}, u32[]{:S(2)}) collective-permute-start(bf16[2,32,2048]{2,1,0:T(8,128)(2,1)S(1)} %fusion.20), channel_id=1, source_target_pairs={{0,2},{1,3},{2,0},{3,1},{4,6},{5,7},{6,4},{7,5},{8,10},{9,11},{10,... | collective-permute-start | bytes 786440 | tf_op jit(solution)/shard_map/ppermute | solution.py:37
  8.2 19.7 %collective-permute-start.4 = (bf16[4,32,2048]{2,1,0:T(8,128)(2,1)S(1)}, bf16[4,32,2048]{2,1,0:T(8,128)(2,1)S(1)}, u32[]{:S(2)}, u32[]{:S(2)}) collective-permute-start(bf16[4,32,2048]{2,1,0:T(8,128)(2,1)S(1)} %fusion.13), channel_id=1, source_target_pairs={{0,1},{1,0},{2,3},{3,2},{4,5},{5,4},{6,7},{7,6},{8,9},{9,8},{10,11... | collective-permute-start | bytes 1572872 | tf_op jit(solution)/shard_map/ppermute | solution.py:37
  8.4 19.5 %collective-permute-start.3 = (bf16[4,32,2048]{2,1,0:T(8,128)(2,1)S(1)}, bf16[4,32,2048]{2,1,0:T(8,128)(2,1)S(1)}, u32[]{:S(2)}, u32[]{:S(2)}) collective-permute-start(bf16[4,32,2048]{2,1,0:T(8,128)(2,1)S(1)} %fusion.13), channel_id=1, source_target_pairs={{0,2},{1,3},{2,0},{3,1},{4,6},{5,7},{6,4},{7,5},{8,10},{9,11},{10,... | collective-permute-start | bytes 1572872 | tf_op jit(solution)/shard_map/ppermute | solution.py:37
  28.9 26.5 %all-to-all-start = ((bf16[8,1,3,128,128]{4,3,2,1,0:T(8,128)(2,1)}), bf16[8,1,3,128,128]{4,3,2,1,0:T(8,128)(2,1)S(1)}, u32[]{:S(2)}, u32[]{:S(2)}) async-start(bf16[8,1,3,128,128]{4,3,2,1,0:T(8,128)(2,1)} %bitcast.188), calls=%async_computation | async-start | bytes 1572864 | tf_op jit(solution)/shard_map/all_to_all | solution.py:66
  35.2 9.1 %collective-permute-start.5 = (bf16[4,32,2048]{2,1,0:T(8,128)(2,1)}, bf16[4,32,2048]{2,1,0:T(8,128)(2,1)S(1)}, u32[]{:S(2)}, u32[]{:S(2)}) collective-permute-start(bf16[4,32,2048]{2,1,0:T(8,128)(2,1)} %copy-done.24), channel_id=1, source_target_pairs={{0,1},{1,0},{2,3},{3,2},{4,5},{5,4},{6,7},{7,6},{8,9},{9,8},{10,11... | collective-permute-start | bytes 1572872 | tf_op jit(solution)/shard_map/ppermute | solution.py:37
  57.4 42.4 %all-to-all-start.1 = ((bf16[8,2,3,128,128]{4,3,2,1,0:T(8,128)(2,1)}), bf16[8,2,3,128,128]{4,3,2,1,0:T(8,128)(2,1)S(1)}, u32[]{:S(2)}, u32[]{:S(2)}) async-start(bf16[8,2,3,128,128]{4,3,2,1,0:T(8,128)(2,1)} %bitcast.183), calls=%async_computation.1 | async-start | bytes 3145728 | tf_op jit(solution)/shard_map/all_to_all | solution.py:66
  66.1 23.9 %collective-permute-start.10 = (bf16[6,32,2048]{2,1,0:T(8,128)(2,1)S(1)}, bf16[6,32,2048]{2,1,0:T(8,128)(2,1)}, u32[]{:S(2)}, u32[]{:S(2)}) collective-permute-start(bf16[6,32,2048]{2,1,0:T(8,128)(2,1)S(1)} %get-tuple-element.283), channel_id=1, source_target_pairs={{0,1},{1,0},{2,3},{3,2},{4,5},{5,4},{6,7},{7,6},{8,9},{9,8},{10,11... | collective-permute-start | bytes 2359304 | tf_op jit(solution)/shard_map/ppermute | solution.py:37
  66.4 23.7 %collective-permute-start.9 = (bf16[6,32,2048]{2,1,0:T(8,128)(2,1)S(1)}, bf16[6,32,2048]{2,1,0:T(8,128)(2,1)}, u32[]{:S(2)}, u32[]{:S(2)}) collective-permute-start(bf16[6,32,2048]{2,1,0:T(8,128)(2,1)S(1)} %get-tuple-element.283), channel_id=1, source_target_pairs={{0,2},{1,3},{2,0},{3,1},{4,6},{5,7},{6,4},{7,5},{8,10},{9,11},{10,... | collective-permute-start | bytes 2359304 | tf_op jit(solution)/shard_map/ppermute | solution.py:37
  90.0 9.0 %collective-permute-start.11 = (bf16[6,32,2048]{2,1,0:T(8,128)(2,1)}, bf16[6,32,2048]{2,1,0:T(8,128)(2,1)S(1)}, u32[]{:S(2)}, u32[]{:S(2)}) collective-permute-start(bf16[6,32,2048]{2,1,0:T(8,128)(2,1)} %collective-permute-done.9), channel_id=1, source_target_pairs={{0,1},{1,0},{2,3},{3,2},{4,5},{5,4},{6,7},{7,6},{8,9},{9,8},{10,11... | collective-permute-start | bytes 2359304 | tf_op jit(solution)/shard_map/ppermute | solution.py:37
  99.8 13.4 %collective-permute-start.14 = (f32[1,2048]{1,0:T(1,128)S(1)}, f32[1,2048]{1,0:T(1,128)S(1)}, u32[]{:S(2)}, u32[]{:S(2)}) collective-permute-start(f32[1,2048]{1,0:T(1,128)S(1)} %copy-done.42), channel_id=1, source_target_pairs={{0,3},{1,2},{2,1},{3,0},{4,7},{5,6},{6,5},{7,4},{8,11},{9,10},{10,... | collective-permute-start | bytes 24584 | tf_op jit(solution)/shard_map/ppermute | solution.py:37
  100.3 12.9 %collective-permute-start.13 = (f32[1,2048]{1,0:T(1,128)S(1)}, f32[1,2048]{1,0:T(1,128)S(1)}, u32[]{:S(2)}, u32[]{:S(2)}) collective-permute-start(f32[1,2048]{1,0:T(1,128)S(1)} %copy-done.42), channel_id=1, source_target_pairs={{0,2},{1,3},{2,0},{3,1},{4,6},{5,7},{6,4},{7,5},{8,10},{9,11},{10,... | collective-permute-start | bytes 24584 | tf_op jit(solution)/shard_map/ppermute | solution.py:37
  101.4 11.9 %collective-permute-start.12 = (f32[1,2048]{1,0:T(1,128)S(1)}, f32[1,2048]{1,0:T(1,128)S(1)}, u32[]{:S(2)}, u32[]{:S(2)}) collective-permute-start(f32[1,2048]{1,0:T(1,128)S(1)} %copy-done.42), channel_id=1, source_target_pairs={{0,1},{1,0},{2,3},{3,2},{4,5},{5,4},{6,7},{7,6},{8,9},{9,8},{10,11... | collective-permute-start | bytes 24584 | tf_op jit(solution)/shard_map/ppermute | solution.py:37
  101.7 15.0 %all-to-all-start.2 = ((bf16[8,1,1,128,128]{4,3,2,1,0:T(8,128)(2,1)}), bf16[8,1,1,128,128]{4,3,2,1,0:T(8,128)(2,1)S(1)}, u32[]{:S(2)}, u32[]{:S(2)}) async-start(bf16[8,1,1,128,128]{4,3,2,1,0:T(8,128)(2,1)} %bitcast.187), calls=%async_computation.2 | async-start | bytes 524288 | tf_op jit(solution)/shard_map/all_to_all | solution.py:66
  123.5 18.0 %collective-permute-start.16 = (bf16[2,32,2048]{2,1,0:T(8,128)(2,1)S(1)}, bf16[2,32,2048]{2,1,0:T(8,128)(2,1)S(1)}, u32[]{:S(2)}, u32[]{:S(2)}) collective-permute-start(bf16[2,32,2048]{2,1,0:T(8,128)(2,1)S(1)} %fusion.24), channel_id=1, source_target_pairs={{0,2},{1,3},{2,0},{3,1},{4,6},{5,7},{6,4},{7,5},{8,10},{9,11},{10,... | collective-permute-start | bytes 786440 | tf_op jit(solution)/shard_map/ppermute | solution.py:37
  124.1 20.3 %all-to-all-start.3 = ((bf16[8,2,1,128,128]{4,3,1,2,0:T(8,128)(2,1)}), bf16[8,2,1,128,128]{4,3,1,2,0:T(8,128)(2,1)S(1)}, u32[]{:S(2)}, u32[]{:S(2)}) async-start(bf16[8,2,1,128,128]{4,3,1,2,0:T(8,128)(2,1)} %bitcast.40), calls=%async_computation.3 | async-start | bytes 1048576 | tf_op jit(solution)/shard_map/all_to_all | solution.py:66
  155.8 14.1 %collective-permute-start.21 = (bf16[4,32,2048]{2,1,0:T(8,128)(2,1)S(1)}, bf16[4,32,2048]{2,1,0:T(8,128)(2,1)}, u32[]{:S(2)}, u32[]{:S(2)}) collective-permute-start(bf16[4,32,2048]{2,1,0:T(8,128)(2,1)S(1)} %fusion.17), channel_id=1, source_target_pairs={{0,2},{1,3},{2,0},{3,1},{4,6},{5,7},{6,4},{7,5},{8,10},{9,11},{10,... | collective-permute-start | bytes 1572872 | tf_op jit(solution)/shard_map/ppermute | solution.py:37
  172.6 13.5 %collective-permute-start.22 = (bf16[4,32,2048]{2,1,0:T(8,128)(2,1)}, bf16[4,32,2048]{2,1,0:T(8,128)(2,1)}, u32[]{:S(2)}, u32[]{:S(2)}) collective-permute-start(bf16[4,32,2048]{2,1,0:T(8,128)(2,1)} %multiply_convert_fusion.2), channel_id=1, source_target_pairs={{0,2},{1,3},{2,0},{3,1},{4,6},{5,7},{6,4},{7,5},{8,10},{9,11},{10,... | collective-permute-start | bytes 1572872 | tf_op jit(solution)/shard_map/ppermute | solution.py:37
  188.6 14.6 %collective-permute-start.26 = (bf16[2,32,2048]{2,1,0:T(8,128)(2,1)}, bf16[2,32,2048]{2,1,0:T(8,128)(2,1)}, u32[]{:S(2)}, u32[]{:S(2)}) collective-permute-start(bf16[2,32,2048]{2,1,0:T(8,128)(2,1)} %fusion.22), channel_id=1, source_target_pairs={{0,2},{1,3},{2,0},{3,1},{4,6},{5,7},{6,4},{7,5},{8,10},{9,11},{10,... | collective-permute-start | bytes 786440 | tf_op jit(solution)/shard_map/ppermute | solution.py:37
  207.4 11.4 %collective-permute-start.28 = (bf16[2,32,2048]{2,1,0:T(8,128)(2,1)}, bf16[2,32,2048]{2,1,0:T(8,128)(2,1)}, u32[]{:S(2)}, u32[]{:S(2)}) collective-permute-start(bf16[2,32,2048]{2,1,0:T(8,128)(2,1)} %multiply_convert_fusion.3), channel_id=1, source_target_pairs={{0,1},{1,0},{2,3},{3,2},{4,5},{5,4},{6,7},{7,6},{8,9},{9,8},{10,11... | collective-permute-start | bytes 786440 | tf_op jit(solution)/shard_map/ppermute | solution.py:37
  207.7 11.2 %collective-permute-start.27 = (bf16[2,32,2048]{2,1,0:T(8,128)(2,1)}, bf16[2,32,2048]{2,1,0:T(8,128)(2,1)}, u32[]{:S(2)}, u32[]{:S(2)}) collective-permute-start(bf16[2,32,2048]{2,1,0:T(8,128)(2,1)} %multiply_convert_fusion.3), channel_id=1, source_target_pairs={{0,2},{1,3},{2,0},{3,1},{4,6},{5,7},{6,4},{7,5},{8,10},{9,11},{10,... | collective-permute-start | bytes 786440 | tf_op jit(solution)/shard_map/ppermute | solution.py:37
  225.1 14.3 %collective-permute-start.31 = (bf16[4,32,2048]{2,1,0:T(8,128)(2,1)}, bf16[4,32,2048]{2,1,0:T(8,128)(2,1)}, u32[]{:S(2)}, u32[]{:S(2)}) collective-permute-start(bf16[4,32,2048]{2,1,0:T(8,128)(2,1)} %fusion.15), channel_id=1, source_target_pairs={{0,2},{1,3},{2,0},{3,1},{4,6},{5,7},{6,4},{7,5},{8,10},{9,11},{10,... | collective-permute-start | bytes 1572872 | tf_op jit(solution)/shard_map/ppermute | solution.py:37
  230.2 15.0 %all-to-all-start.4 = ((bf16[8,1,1,128,128]{4,3,2,1,0:T(8,128)(2,1)}), bf16[8,1,1,128,128]{4,3,2,1,0:T(8,128)(2,1)}, u32[]{:S(2)}, u32[]{:S(2)}) async-start(bf16[8,1,1,128,128]{4,3,2,1,0:T(8,128)(2,1)} %bitcast.215), calls=%async_computation.4 | async-start | bytes 524288 | tf_op jit(solution)/shard_map/all_to_all | solution.py:66
  250.5 27.4 %all-to-all-start.5 = ((bf16[8,1,3,128,128]{4,3,2,1,0:T(8,128)(2,1)}), bf16[8,1,3,128,128]{4,3,2,1,0:T(8,128)(2,1)S(1)}, u32[]{:S(2)}, u32[]{:S(2)}) async-start(bf16[8,1,3,128,128]{4,3,2,1,0:T(8,128)(2,1)} %get-tuple-element.365), calls=%async_computation.5 | async-start | bytes 1572864 | tf_op jit(solution)/shard_map/all_to_all | solution.py:66
  256.0 10.3 %collective-permute-start.33 = (bf16[4,32,2048]{2,1,0:T(8,128)(2,1)}, bf16[4,32,2048]{2,1,0:T(8,128)(2,1)}, u32[]{:S(2)}, u32[]{:S(2)}) collective-permute-start(bf16[4,32,2048]{2,1,0:T(8,128)(2,1)} %multiply_convert_fusion.1), channel_id=1, source_target_pairs={{0,1},{1,0},{2,3},{3,2},{4,5},{5,4},{6,7},{7,6},{8,9},{9,8},{10,11... | collective-permute-start | bytes 1572872 | tf_op jit(solution)/shard_map/ppermute | solution.py:37
  256.0 14.6 %collective-permute-start.32 = (bf16[4,32,2048]{2,1,0:T(8,128)(2,1)}, bf16[4,32,2048]{2,1,0:T(8,128)(2,1)}, u32[]{:S(2)}, u32[]{:S(2)}) collective-permute-start(bf16[4,32,2048]{2,1,0:T(8,128)(2,1)} %multiply_convert_fusion.1), channel_id=1, source_target_pairs={{0,2},{1,3},{2,0},{3,1},{4,6},{5,7},{6,4},{7,5},{8,10},{9,11},{10,... | collective-permute-start | bytes 1572872 | tf_op jit(solution)/shard_map/ppermute | solution.py:37
  277.9 20.9 %all-to-all-start.6 = ((bf16[8,2,1,128,128]{4,3,1,2,0:T(8,128)(2,1)}), bf16[8,2,1,128,128]{4,3,1,2,0:T(8,128)(2,1)}, u32[]{:S(2)}, u32[]{:S(2)}) async-start(bf16[8,2,1,128,128]{4,3,1,2,0:T(8,128)(2,1)} %bitcast.204), calls=%async_computation.6 | async-start | bytes 1048576 | tf_op jit(solution)/shard_map/all_to_all | solution.py:66
  306.8 44.1 %all-to-all-start.7 = ((bf16[8,2,3,128,128]{4,3,2,1,0:T(8,128)(2,1)}), bf16[8,2,3,128,128]{4,3,2,1,0:T(8,128)(2,1)}, u32[]{:S(2)}, u32[]{:S(2)}) async-start(bf16[8,2,3,128,128]{4,3,2,1,0:T(8,128)(2,1)} %get-tuple-element.385), calls=%async_computation.7 | async-start | bytes 3145728 | tf_op jit(solution)/shard_map/all_to_all | solution.py:66
  313.8 20.2 %collective-permute-start.39 = (bf16[6,32,2048]{2,1,0:T(8,128)(2,1)}, bf16[6,32,2048]{2,1,0:T(8,128)(2,1)}, u32[]{:S(2)}, u32[]{:S(2)}) collective-permute-start(bf16[6,32,2048]{2,1,0:T(8,128)(2,1)} %fusion.10), channel_id=1, source_target_pairs={{0,2},{1,3},{2,0},{3,1},{4,6},{5,7},{6,4},{7,5},{8,10},{9,11},{10,... | collective-permute-start | bytes 2359304 | tf_op jit(solution)/shard_map/ppermute | solution.py:37
  363.7 24.0 %all-to-all-start.8 = ((bf16[8,16,2688]{2,1,0:T(8,128)(2,1)}), bf16[8,16,2688]{2,1,0:T(8,128)(2,1)S(1)}, u32[]{:S(2)}, u32[]{:S(2)}) async-start(bf16[8,16,2688]{2,1,0:T(8,128)(2,1)} %pack.1), calls=%async_computation.8 | async-start | bytes 1376256 | tf_op jit(solution)/shard_map/all_to_all | solution.py:66
  395.7 20.0 %collective-permute-start.47 = (bf16[6,32,2048]{2,1,0:T(8,128)(2,1)}, bf16[6,32,2048]{2,1,0:T(8,128)(2,1)}, u32[]{:S(2)}, u32[]{:S(2)}) collective-permute-start(bf16[6,32,2048]{2,1,0:T(8,128)(2,1)} %fusion.8), channel_id=1, source_target_pairs={{0,2},{1,3},{2,0},{3,1},{4,6},{5,7},{6,4},{7,5},{8,10},{9,11},{10,... | collective-permute-start | bytes 2359304 | tf_op jit(solution)/shard_map/ppermute | solution.py:37
  397.7 22.7 %all-to-all-start.9 = ((bf16[8,16,2688]{2,1,0:T(8,128)(2,1)}), bf16[8,16,2688]{2,1,0:T(8,128)(2,1)}, u32[]{:S(2)}, u32[]{:S(2)}) async-start(bf16[8,16,2688]{2,1,0:T(8,128)(2,1)} %broadcast_in_dim.202), calls=%async_computation.9 | async-start | bytes 1376256 | tf_op jit(solution)/shard_map/all_to_all | solution.py:66
  (75 other events, 464.9 us)
